TPU v7x, 32 devices: a whole 2x2x4 slice. The times are simulated.
32 devices in a mesh: rep: 4 (over y, core), exp: 8 (over z, x).
Axes of the slice: x: 2, y: 2, z: 4, core: 2. Of those that a mesh axis runs over, the one named last changes fastest.
Arguments:
- tokens: bfloat16 [8192, 1024], P(('rep', 'exp')), may hold values from -6 to 6
- cotangent: bfloat16 [8192, 1024], P(('rep', 'exp')), may hold values from -6 to 6
- doc_lengths: int32 [32, 4], P(('rep', 'exp')), may hold values from 1 to 128, 256 in all within a row
- expert_of_token: int32 [8192], P(('rep', 'exp')), may hold values from 0 to 3, as said below
- w_query: bfloat16 [1024, 1024], P('exp'), may hold values from -0.25 to 0.25
- w_key: bfloat16 [1024, 1024], P('exp'), may hold values from -0.25 to 0.25
- w_value: bfloat16 [1024, 1024], P('exp'), may hold values from -0.1875 to 0.1875
- w_output: bfloat16 [1024, 1024], P('exp'), may hold values from -0.75 to 0.75
- attn_gain: bfloat16 [1024], P('exp'), may hold values from 0.25 to 1.75
- w_inner: bfloat16 [8, 1024, 4096], P('exp', 'rep'), may hold values from -0.1875 to 0.1875
- w_outer: bfloat16 [8, 4096, 1024], P('exp', 'rep'), may hold values from -0.125 to 0.125
- expert_gain: bfloat16 [8, 1024], P('exp', 'rep'), may hold values from 0.25 to 1.75
- centroids: bfloat16 [8, 512], P('exp', 'rep'), may hold values from -0.08984375 to 0.08984375
Outputs:
- output: bfloat16 [8192, 1024], P(('rep', 'exp'))
- grad_tokens: float32 [8192, 1024], P(('rep', 'exp'))
- grad_w_query: float32 [1024, 1024], P('exp')
- grad_w_key: float32 [1024, 1024], P('exp')
- grad_w_value: float32 [1024, 1024], P('exp')
- grad_w_output: float32 [1024, 1024], P('exp')
- grad_attn_gain: float32 [1024], P('exp')
- grad_w_inner: float32 [8, 1024, 4096], P('exp', 'rep')
- grad_w_outer: float32 [8, 4096, 1024], P('exp', 'rep')
- grad_expert_gain: float32 [8, 1024], P('exp', 'rep')
- grad_centroids: float32 [8, 512], P('exp', 'rep')
Inputs may be any that keep to these rules, and one draw needn't show every extreme that they name: `expert_of_token`: among the tokens of one device every expert is named an even number of times, at most 96, and in every index of rep some device names some expert exactly 2 * 48 times; the devices of one index of rep name every expert exactly 2 * 256 times in all.
All inputs are finite; a program needn't handle non-finite values.
Results may differ from a plain program's by a relative error of at most 0.015.
Values may be sent and summed in bfloat16 or wider, within the bound.
A program may use at most 320 MiB of HBM per device.

v0:
```python
import jax
import jax.numpy as jnp
from jax import lax
from jax.sharding import PartitionSpec as P

HEADS = 16


EPS = 1e-05
ROOT_HALF = 0.7071067811865476
INV_ROOT_TAU = 0.3989422804014327


def partner(shard, axis, bit):
    return lax.ppermute(shard, axis, [(i, i ^ 1 << bit) for i in range(lax.axis_size(axis))])


def plain_product(left_mat, right_mat):
    return jnp.dot(left_mat, right_mat, preferred_element_type=jnp.float32)


def tn_product(left_mat, right_mat):
    return lax.dot_general(
        left_mat, right_mat, (((0,), (0,)), ((), ())), preferred_element_type=jnp.float32
    )


def nt_product(left_mat, right_mat):
    return lax.dot_general(
        left_mat, right_mat, (((1,), (1,)), ((), ())), preferred_element_type=jnp.float32
    )


def norm_rows(inputs_row, gain_row):
    row_mean = jnp.mean(inputs_row, axis=-1, keepdims=True)
    centered = inputs_row - row_mean
    variance = jnp.mean(centered * centered, axis=-1, keepdims=True)
    inv_scale = lax.rsqrt(variance + EPS)
    unit_rows = centered * inv_scale
    return (unit_rows * gain_row, unit_rows, inv_scale)


def norm_back(grad_out, unit_rows, inv_scale, gain_row):
    grad_unit = grad_out * gain_row
    grad_gain = jnp.sum(grad_out * unit_rows, axis=0)
    centred_grad = grad_unit - jnp.mean(grad_unit, axis=-1, keepdims=True)
    grad_in = (
        centred_grad - unit_rows * jnp.mean(grad_unit * unit_rows, axis=-1, keepdims=True)
    ) * inv_scale
    return (grad_in, grad_gain)


def gelu_slope(inner_pre):
    return (
        0.5 * (1.0 + lax.erf(inner_pre * ROOT_HALF))
        + inner_pre * jnp.exp(-0.5 * inner_pre * inner_pre) * INV_ROOT_TAU
    )


def masked_scores(queries3, keys3, allowed, factor):
    scores = (
        jnp.einsum("qhe,khe->hqk", queries3, keys3, preferred_element_type=jnp.float32) * factor
    )
    return jnp.where(allowed[None], scores, -1e30)


def sublayer_forward(rows_in, inner_w, outer_w, gain_row):
    normed, unit_rows, inv_scale = norm_rows(rows_in, gain_row)
    normed_low = normed.astype(jnp.bfloat16)
    inner_pre = plain_product(normed_low, inner_w)
    active = jax.nn.gelu(inner_pre, approximate=False).astype(jnp.bfloat16)
    return (
        rows_in + plain_product(active, outer_w),
        (unit_rows, inv_scale, normed_low, inner_pre, active),
    )


def sublayer_back(grad_state, inner_w, outer_w, gain_row, kept_layer):
    unit_rows, inv_scale, normed_low, inner_pre, active = kept_layer
    grad_outer = grad_state.astype(jnp.bfloat16)
    grad_active = nt_product(grad_outer, outer_w)
    grad_inner = (grad_active * gelu_slope(inner_pre)).astype(jnp.bfloat16)
    grad_normed = nt_product(grad_inner, inner_w)
    grad_in, grad_gain = norm_back(grad_normed, unit_rows, inv_scale, gain_row)
    return (
        grad_state + grad_in,
        grad_gain,
        tn_product(normed_low, grad_inner),
        tn_product(active, grad_outer),
    )


def expert_forward(arrived_rows, inner_pair, outer_pair, gain_pair, centroid):
    wide_rows = arrived_rows.astype(jnp.float32)
    gates = jax.nn.sigmoid(plain_product(arrived_rows, centroid[:, None])[:, 0])
    middle, first_kept = sublayer_forward(wide_rows, inner_pair[0], outer_pair[0], gain_pair[0])
    final_rows, second_kept = sublayer_forward(middle, inner_pair[1], outer_pair[1], gain_pair[1])
    branch = (gates[:, None] * final_rows).astype(jnp.bfloat16)
    return (branch, (wide_rows, gates, final_rows, first_kept, second_kept))


def shards(
    tokens,
    cotangent,
    doc_lengths,
    expert_of_token,
    w_query,
    w_key,
    w_value,
    w_output,
    attn_gain,
    w_inner,
    w_outer,
    expert_gain,
    centroids,
):
    expert_count = lax.axis_size("exp")
    row_count = tokens.shape[0]
    model_width = tokens.shape[1]
    head_dim = model_width // HEADS
    factor = head_dim ** (-0.5)
    query_w, key_w, value_w, output_w, gain_attn = (
        lax.all_gather(w_query, "exp", axis=0, tiled=True),
        lax.all_gather(w_key, "exp", axis=0, tiled=True),
        lax.all_gather(w_value, "exp", axis=0, tiled=True),
        lax.all_gather(w_output, "exp", axis=0, tiled=True),
        lax.all_gather(attn_gain, "exp", axis=0, tiled=True),
    )
    gain_attn = gain_attn.astype(jnp.float32)
    inputs = tokens.astype(jnp.float32)
    normed_a, unit_a, scale_a = norm_rows(inputs, gain_attn)
    act_a = normed_a.astype(jnp.bfloat16)
    queries = plain_product(act_a, query_w).astype(jnp.bfloat16)
    keys_low = plain_product(act_a, key_w).astype(jnp.bfloat16)
    values_low = plain_product(act_a, value_w).astype(jnp.bfloat16)
    queries3 = queries.reshape(row_count, HEADS, head_dim)
    keys3 = keys_low.reshape(row_count, HEADS, head_dim)
    values3 = values_low.reshape(row_count, HEADS, head_dim)
    doc_ends = jnp.cumsum(doc_lengths[0])
    positions = jnp.arange(row_count, dtype=jnp.int32)
    segment = jnp.sum((positions[:, None] >= doc_ends[None, :]).astype(jnp.int32), axis=1)
    allowed = (segment[:, None] == segment[None, :]) & (positions[:, None] >= positions[None, :])
    scores = masked_scores(queries3, keys3, allowed, factor)
    row_top = jnp.max(scores, axis=-1, keepdims=True)
    row_total = jnp.sum(jnp.exp(scores - row_top), axis=-1, keepdims=True)
    log_total = row_top + jnp.log(row_total)
    probs_low = jnp.exp(scores - log_total).astype(jnp.bfloat16)
    context = jnp.einsum("hqk,khe->qhe", probs_low, values3, preferred_element_type=jnp.float32)
    context = context.reshape(row_count, model_width).astype(jnp.bfloat16)
    hidden = inputs + plain_product(context, output_w)
    slot_count = 3 * row_count // (2 * expert_count)
    expert_ids = jnp.arange(expert_count // 2, dtype=jnp.int32)
    onehot = (expert_of_token[:, None] == expert_ids[None, :]).astype(jnp.int32)
    earlier = jnp.cumsum(onehot, axis=0) - onehot
    rank_in = jnp.sum(earlier * onehot, axis=1)
    position = (2 * expert_of_token + rank_in % 2) * slot_count + rank_in // 2

    def pack_rows(row_values):
        holder = jnp.zeros((expert_count * slot_count, model_width), row_values.dtype)
        return holder.at[position].set(row_values).reshape(expert_count, slot_count, model_width)

    sent_rows = hidden.astype(jnp.bfloat16)
    packed_sent = pack_rows(sent_rows)
    arrived = lax.all_to_all(packed_sent, "exp", split_axis=0, concat_axis=0, tiled=True).reshape(
        -1, model_width
    )
    inner_own, outer_own, gain_own, centre_own = (
        lax.all_gather(w_inner, "rep", axis=1, tiled=True),
        lax.all_gather(w_outer, "rep", axis=1, tiled=True),
        lax.all_gather(expert_gain, "rep", axis=1, tiled=True),
        lax.all_gather(centroids, "rep", axis=1, tiled=True),
    )
    inner_other, outer_other, gain_other, centre_other = partner(
        (inner_own, outer_own, gain_own, centre_own), "exp", 0
    )
    parity = lax.axis_index("exp") % 2
    first_side = parity == 0

    def choose_side(when_even, when_odd):
        return jnp.where(first_side, when_even, when_odd)

    inner_pair = (
        choose_side(inner_own[0], inner_other[0]),
        choose_side(inner_other[0], inner_own[0]),
    )
    outer_pair = (
        choose_side(outer_own[0], outer_other[0]),
        choose_side(outer_other[0], outer_own[0]),
    )
    gain_pair = (
        choose_side(gain_own[0], gain_other[0]).astype(jnp.float32),
        choose_side(gain_other[0], gain_own[0]).astype(jnp.float32),
    )
    centroid = jnp.concatenate(
        [choose_side(centre_own[0], centre_other[0]), choose_side(centre_other[0], centre_own[0])]
    )
    branch, kept_state = expert_forward(arrived, inner_pair, outer_pair, gain_pair, centroid)
    returned = lax.all_to_all(
        branch.reshape(expert_count, slot_count, model_width),
        "exp",
        split_axis=0,
        concat_axis=0,
        tiled=True,
    ).reshape(-1, model_width)
    output = (hidden + returned[position].astype(jnp.float32)).astype(jnp.bfloat16)
    grad_out = cotangent.astype(jnp.float32)
    resent, grad_arrived = (
        lax.all_to_all(packed_sent, "exp", split_axis=0, concat_axis=0, tiled=True),
        lax.all_to_all(pack_rows(cotangent), "exp", split_axis=0, concat_axis=0, tiled=True),
    )
    kept_state = expert_forward(
        resent.reshape(-1, model_width), inner_pair, outer_pair, gain_pair, centroid
    )[1]
    wide_rows, gates, final_rows, first_kept, second_kept = kept_state
    grad_rows = grad_arrived.reshape(-1, model_width).astype(jnp.float32)
    grad_gate = jnp.sum(grad_rows * final_rows, axis=1)
    grad_final = gates[:, None] * grad_rows
    grad_middle, gain_grad_one, inner_grad_one, outer_grad_one = sublayer_back(
        grad_final, inner_pair[1], outer_pair[1], gain_pair[1], second_kept
    )
    grad_wide, gain_grad_zero, inner_grad_zero, outer_grad_zero = sublayer_back(
        grad_middle, inner_pair[0], outer_pair[0], gain_pair[0], first_kept
    )
    grad_logit = grad_gate * gates * (1.0 - gates)
    grad_centre = jnp.dot(grad_logit, wide_rows, precision=lax.Precision.HIGHEST)
    grad_back = (grad_wide + grad_logit[:, None] * centroid.astype(jnp.float32)[None, :]).astype(
        jnp.bfloat16
    )
    grad_home = lax.all_to_all(
        grad_back.reshape(expert_count, slot_count, model_width),
        "exp",
        split_axis=0,
        concat_axis=0,
        tiled=True,
    ).reshape(-1, model_width)
    half_width = model_width // 2
    centre_low = grad_centre[:half_width]
    centre_high = grad_centre[half_width:]
    summed = (
        lax.psum_scatter(
            inner_grad_zero[None].astype(jnp.bfloat16), "rep", scatter_dimension=1, tiled=True
        ).astype(jnp.float32),
        lax.psum_scatter(
            inner_grad_one[None].astype(jnp.bfloat16), "rep", scatter_dimension=1, tiled=True
        ).astype(jnp.float32),
        lax.psum_scatter(
            outer_grad_zero[None].astype(jnp.bfloat16), "rep", scatter_dimension=1, tiled=True
        ).astype(jnp.float32),
        lax.psum_scatter(
            outer_grad_one[None].astype(jnp.bfloat16), "rep", scatter_dimension=1, tiled=True
        ).astype(jnp.float32),
        lax.psum_scatter(
            gain_grad_zero[None].astype(jnp.bfloat16), "rep", scatter_dimension=1, tiled=True
        ).astype(jnp.float32),
        lax.psum_scatter(
            gain_grad_one[None].astype(jnp.bfloat16), "rep", scatter_dimension=1, tiled=True
        ).astype(jnp.float32),
        lax.psum_scatter(
            centre_low[None].astype(jnp.bfloat16), "rep", scatter_dimension=1, tiled=True
        ).astype(jnp.float32),
        lax.psum_scatter(
            centre_high[None].astype(jnp.bfloat16), "rep", scatter_dimension=1, tiled=True
        ).astype(jnp.float32),
    )
    mine_part = (
        choose_side(summed[0], summed[1]),
        choose_side(summed[2], summed[3]),
        choose_side(summed[4], summed[5]),
        choose_side(summed[6], summed[7]),
    )
    theirs_part = (
        choose_side(summed[1], summed[0]),
        choose_side(summed[3], summed[2]),
        choose_side(summed[5], summed[4]),
        choose_side(summed[7], summed[6]),
    )
    partner_part = (
        partner(theirs_part[0].astype(jnp.bfloat16), "exp", 0).astype(jnp.float32),
        partner(theirs_part[1].astype(jnp.bfloat16), "exp", 0).astype(jnp.float32),
        partner(theirs_part[2].astype(jnp.bfloat16), "exp", 0).astype(jnp.float32),
        partner(theirs_part[3].astype(jnp.bfloat16), "exp", 0).astype(jnp.float32),
    )
    grad_w_inner = mine_part[0] + partner_part[0]
    grad_w_outer = mine_part[1] + partner_part[1]
    grad_expert_gain = mine_part[2] + partner_part[2]
    grad_centroids = mine_part[3] + partner_part[3]
    grad_hidden = grad_out + grad_home[position].astype(jnp.float32)
    grad_attn = grad_hidden.astype(jnp.bfloat16)
    grad_w_o = tn_product(context, grad_attn)
    grad_context3 = (
        nt_product(grad_attn, output_w).astype(jnp.bfloat16).reshape(row_count, HEADS, head_dim)
    )
    again_scores = masked_scores(queries3, keys3, allowed, factor)
    attn_probs = jnp.exp(again_scores - log_total)
    grad_probs = jnp.einsum(
        "qhe,khe->hqk", grad_context3, values3, preferred_element_type=jnp.float32
    )
    inner_sum = jnp.sum(attn_probs * grad_probs, axis=-1, keepdims=True)
    grad_scores = (attn_probs * (grad_probs - inner_sum)).astype(jnp.bfloat16)
    grad_query = (
        (
            jnp.einsum("hqk,khe->qhe", grad_scores, keys3, preferred_element_type=jnp.float32)
            * factor
        )
        .astype(jnp.bfloat16)
        .reshape(row_count, model_width)
    )
    grad_key = (
        (
            jnp.einsum("hqk,qhe->khe", grad_scores, queries3, preferred_element_type=jnp.float32)
            * factor
        )
        .astype(jnp.bfloat16)
        .reshape(row_count, model_width)
    )
    grad_value = (
        jnp.einsum(
            "hqk,qhe->khe",
            attn_probs.astype(jnp.bfloat16),
            grad_context3,
            preferred_element_type=jnp.float32,
        )
        .astype(jnp.bfloat16)
        .reshape(row_count, model_width)
    )
    grad_w_q = tn_product(act_a, grad_query)
    grad_w_k = tn_product(act_a, grad_key)
    grad_w_v = tn_product(act_a, grad_value)
    grad_act = (
        nt_product(grad_query, query_w)
        + nt_product(grad_key, key_w)
        + nt_product(grad_value, value_w)
    )
    grad_in_a, grad_gain_a = norm_back(grad_act, unit_a, scale_a, gain_attn)
    grad_tokens = grad_hidden + grad_in_a
    attn_shares = (
        lax.psum_scatter(grad_w_q, "exp", scatter_dimension=0, tiled=True),
        lax.psum_scatter(grad_w_k, "exp", scatter_dimension=0, tiled=True),
        lax.psum_scatter(grad_w_v, "exp", scatter_dimension=0, tiled=True),
        lax.psum_scatter(grad_w_o, "exp", scatter_dimension=0, tiled=True),
        lax.psum_scatter(grad_gain_a, "exp", scatter_dimension=0, tiled=True),
    )
    share_q, share_k, share_v, share_o, share_gain = (
        lax.psum(attn_shares[0].astype(jnp.bfloat16), "rep").astype(jnp.float32),
        lax.psum(attn_shares[1].astype(jnp.bfloat16), "rep").astype(jnp.float32),
        lax.psum(attn_shares[2].astype(jnp.bfloat16), "rep").astype(jnp.float32),
        lax.psum(attn_shares[3].astype(jnp.bfloat16), "rep").astype(jnp.float32),
        lax.psum(attn_shares[4].astype(jnp.bfloat16), "rep").astype(jnp.float32),
    )
    return (
        output,
        grad_tokens,
        share_q,
        share_k,
        share_v,
        share_o,
        share_gain,
        grad_w_inner,
        grad_w_outer,
        grad_expert_gain,
        grad_centroids,
    )


def solution(mesh):
    placed = (
        P(("rep", "exp"), None),
        P(("rep", "exp"), None),
        P(("rep", "exp"), None),
        P(("rep", "exp")),
        P("exp", None),
        P("exp", None),
        P("exp", None),
        P("exp", None),
        P("exp"),
        P("exp", "rep", None),
        P("exp", "rep", None),
        P("exp", "rep"),
        P("exp", "rep"),
    )
    return jax.shard_map(
        shards,
        mesh=mesh,
        in_specs=placed,
        out_specs=(
            P(("rep", "exp"), None),
            P(("rep", "exp"), None),
            P("exp", None),
            P("exp", None),
            P("exp", None),
            P("exp", None),
            P("exp"),
            P("exp", "rep", None),
            P("exp", "rep", None),
            P("exp", "rep"),
            P("exp", "rep"),
        ),
        check_vma=False,
    )
```

profile of v0, /device:TPU:11, one launch (start us, length us, event | category | flops | bytes accessed | tf_op | source)
XLA Modules:
  0.0 1454.3 jit_solution(10149077848032668289)
XLA Ops:
  10.6 58.9 %all-gather.16.cloned.1.call-done = bf16[1,1024,4096]{2,1,0:T(8,128)(2,1)} async-done(((bf16[1,256,4096]{2,1,0:T(8,128)(2,1)}), bf16[1,1024,4096]{2,1,0:T(8,128)(2,1)}) %all-gather.16.cloned.1.call-update) | async-done | bytes 8388624 | tf_op jit(solution)/shard_map/all_gather | solution.py:168
  69.8 230.2 %all-gather = bf16[8,1,128]{2,1,0:T(2,128)(2,1)S(1)} all-gather(bf16[1,1,128]{2,1,0:T(2,128)(2,1)S(1)} %bitcast.215), channel_id=1, replica_groups=mesh['rep'=4,'exp'=8] {'exp'}, dimensions={0}, use_global_device_ids=true | all-gather | bytes 2304 | tf_op jit(solution)/shard_map/all_gather | solution.py:127
  314.9 6.3 all-gather.18.cloned.1.call-done
  321.5 63.0 %all-gather.14.cloned.1.call-done = bf16[1024,1024]{1,0:T(8,128)(2,1)} async-done(((bf16[128,1024]{1,0:T(8,128)(2,1)}), bf16[1024,1024]{1,0:T(8,128)(2,1)}) %all-gather.14.cloned.1.call-update) | async-done | bytes 2097168 | tf_op jit(solution)/shard_map/all_gather | solution.py:126
  389.5 4.9 all-to-all-start
  394.4 6.1 all_gather.32
  400.8 5.4 all_gather.33
  407.3 3.1 scatter_custom_fusion.1
  410.4 115.4 %collective-permute-done = bf16[1,512]{1,0:T(2,128)(2,1)S(1)} collective-permute-done((bf16[1,512]{1,0:T(2,128)(2,1)S(1)}, bf16[1,512]{1,0:T(2,128)(2,1)S(1)}, u32[]{:S(2)}, u32[]{:S(2)}) %collective-permute-start) | collective-permute-done | bytes 1056 | tf_op jit(solution)/shard_map/ppermute | solution.py:15
  525.8 5.5 all-to-all-start.2
  534.4 14.4 all-to-all-done.2
  549.4 19.7 %fusion.18 = (bf16[384,4096]{1,0:T(8,128)(2,1)S(1)}, f32[384,4096]{1,0:T(8,128)}) fusion(bf16[384,1024]{1,0:T(8,128)(2,1)S(1)} %bitcast.189, bf16[1,1024,4096]{2,1,0:T(8,128)(2,1)} %all-gather.16.cloned.1.call-done, bf16[1,1024,4096]{2,1,0:T(8,128)(2,1)} %collective-permute-done.2, pred[]{:T(512)S(6)} %eq.57), kind=kOutput, calls=%fused_computation.34 | convolution fusion | flops 3327655936 | bytes 27000832 | tf_op jit(solution)/shard_map/dot_general | solution.py:19
  569.1 7.1 fusion.146
  576.6 19.0 %fusion.21 = (bf16[384,4096]{1,0:T(8,128)(2,1)}, f32[384,4096]{1,0:T(8,128)}) fusion(bf16[1,1024,4096]{2,1,0:T(8,128)(2,1)} %collective-permute-done.2, bf16[1,1024,4096]{2,1,0:T(8,128)(2,1)S(1)} %bitcast.217, pred[]{:T(512)S(6)} %eq.57, f32[384,1024]{1,0:T(8,128)S(1)} %get-tuple-element.41, f32[1024]{0:T(1024)S(1)} %bitcast.211, ...), kind=kOutput, calls=%fused_computation.37 | convolution fusion | flops 3329228800 | bytes 27794432 | tf_op jit(solution)/shard_map/dot_general | solution.py:19
  595.6 9.5 fusion.27
  605.1 6.6 multiply_reduce_fusion.1
  611.7 9.9 fusion.79
  624.7 8.8 fusion.33
  633.6 9.4 fusion.75
  643.9 8.9 convert_bitcast_fusion.2
  652.9 8.9 convert_bitcast_fusion.3
  663.2 8.9 convert_bitcast_fusion.1
  673.3 8.7 convert_bitcast_fusion
  682.7 3.0 fusion.73
  685.6 8.1 all-to-all-start.3
  693.8 16.8 %all-to-all-done.3 = bf16[8,48,1024]{2,1,0:T(8,128)(2,1)S(1)} async-done(((bf16[8,48,1024]{2,1,0:T(8,128)(2,1)}), bf16[8,48,1024]{2,1,0:T(8,128)(2,1)S(1)}, u32[]{:S(2)}, u32[]{:S(2)}) %all-to-all-start.3) | async-done | bytes 786464 | tf_op jit(solution)/shard_map/all_to_all | solution.py:229
  711.8 4.0 fusion.113
  718.8 3.2 convolution_convert_fusion
  722.1 3.4 fusion.136
  725.8 4.8 multiply_reduce_fusion
  742.1 6.6 all-to-all-start.1
  757.4 8.9 all-to-all-done.1
  767.5 3.4 fusion.147
  770.9 16.2 %reduce-scatter.31.cloned.1.call-done = bf16[1,256,4096]{2,1,0:T(8,128)(2,1)} async-done(((bf16[1,1024,4096]{2,1,0:T(8,128)(2,1)}), bf16[1,256,4096]{2,1,0:T(8,128)(2,1)}) %reduce-scatter.31.cloned.1.call-update) | async-done | bytes 2097168 | tf_op jit(solution)/shard_map/reduce_scatter | solution.py:243
  787.1 74.4 %reduce-scatter.29.cloned.1.call-done = bf16[1,256,4096]{2,1,0:T(8,128)(2,1)} async-done(((bf16[1,1024,4096]{2,1,0:T(8,128)(2,1)}), bf16[1,256,4096]{2,1,0:T(8,128)(2,1)}) %reduce-scatter.29.cloned.1.call-update) | async-done | bytes 2097168 | tf_op jit(solution)/shard_map/reduce_scatter | solution.py:240
  861.4 4.5 fusion.53
  869.0 50.5 %all-reduce = bf16[1024]{0:T(1024)(128)(2,1)S(1)} all-reduce(f32[1024]{0:T(1024)S(1)} %get-tuple-element.17), channel_id=6, replica_groups=mesh['rep'=4,'exp'=8] {'exp'}, use_global_device_ids=true, to_apply=%region_32.33.clone | all-reduce | flops 1024 | bytes 6144
  919.5 8.6 psum.39
  928.6 7.2 reduce-scatter.33.cloned.1.call-done
  935.9 74.4 %reduce-scatter.35.cloned.1.call-done = bf16[1,1024,1024]{2,1,0:T(8,128)(2,1)} async-done(((bf16[1,4096,1024]{2,1,0:T(8,128)(2,1)}), bf16[1,1024,1024]{2,1,0:T(8,128)(2,1)}) %reduce-scatter.35.cloned.1.call-update) | async-done | bytes 2097168 | tf_op jit(solution)/shard_map/reduce_scatter | solution.py:249
  1010.2 4.5 fusion.55
  1016.0 99.4 %reduce-scatter.27.cloned.1.call-done = f32[128,1024]{1,0:T(8,128)} async-done(((f32[1024,1024]{1,0:T(8,128)}), f32[128,1024]{1,0:T(8,128)}) %reduce-scatter.27.cloned.1.call-update) | async-done | bytes 524304 | tf_op jit(solution)/shard_map/reduce_scatter | solution.py:340
  1117.1 90.0 %reduce-scatter.25.cloned.1.call-done = f32[128,1024]{1,0:T(8,128)} async-done(((f32[1024,1024]{1,0:T(8,128)}), f32[128,1024]{1,0:T(8,128)}) %reduce-scatter.25.cloned.1.call-update) | async-done | bytes 524304 | tf_op jit(solution)/shard_map/reduce_scatter | solution.py:339
  1208.9 89.9 %reduce-scatter.23.cloned.1.call-done = f32[128,1024]{1,0:T(8,128)} async-done(((f32[1024,1024]{1,0:T(8,128)}), f32[128,1024]{1,0:T(8,128)}) %reduce-scatter.23.cloned.1.call-update) | async-done | bytes 524304 | tf_op jit(solution)/shard_map/reduce_scatter | solution.py:338
  1300.6 90.6 %reduce-scatter.21.cloned.1.call-done = f32[128,1024]{1,0:T(8,128)} async-done(((f32[1024,1024]{1,0:T(8,128)}), f32[128,1024]{1,0:T(8,128)}) %reduce-scatter.21.cloned.1.call-update) | async-done | bytes 524304 | tf_op jit(solution)/shard_map/reduce_scatter | solution.py:337
  1395.8 34.6 %all-reduce.4.cloned.1.call-done = (bf16[128,1024]{1,0:T(8,128)(2,1)}, bf16[128,1024]{1,0:T(8,128)(2,1)}, bf16[128,1024]{1,0:T(8,128)(2,1)}, bf16[128,1024]{1,0:T(8,128)(2,1)}) async-done(((bf16[128,1024]{1,0:T(8,128)(2,1)}, bf16[128,1024]{1,0:T(8,128)(2,1)}, bf16[128,1024]{1,0:T(8,128)(2,1)}, bf16[128,1024]{1,0:T(8,128)(2,1)}), (bf16[128,1024]{1,0:T(8,128)(2,1)}, bf16[128,1024]{1,0:T(8,128)(2,1)}, ...) | async-done | bytes 1048592 | tf_op jit(solution)/shard_map/psum | solution.py:344
  1437.7 4.8 fusion.52
  1442.5 5.0 fusion.54
  (265 shorter events, 83.4 us)
Async XLA Ops:
  7.2 62.6 %copy-start.44 = (bf16[128]{0:T(256)(128)(2,1)S(1)}, bf16[128]{0:T(256)(128)(2,1)}, u32[]{:S(2)}) copy-start(bf16[128]{0:T(256)(128)(2,1)} %param.21) | copy-start | bytes 772
  7.2 292.9 %copy-start.47 = (s32[1,4]{1,0:T(1,128)S(1)}, s32[1,4]{1,0:T(1,128)}, u32[]{:S(2)}) copy-start(s32[1,4]{1,0:T(1,128)} %param.15) | copy-start | bytes 52
  7.2 293.0 %copy-start.38 = (s32[256]{0:T(256)S(1)}, s32[256]{0:T(256)}, u32[]{:S(2)}) copy-start(s32[256]{0:T(256)} %param.16) | copy-start | bytes 3076
  7.2 294.8 %copy-start.2 = (bf16[256,1024]{1,0:T(8,128)(2,1)S(1)}, bf16[256,1024]{1,0:T(8,128)(2,1)}, u32[]{:S(2)}) copy-start(bf16[256,1024]{1,0:T(8,128)(2,1)} %param.13) | copy-start | bytes 1572868
  7.2 62.3 %all-gather.16.cloned.1.call-start = ((), (), s32[]{:S(2)}) async-start(), calls=%async_computation.20 | async-start | bytes 10485760 | tf_op jit(solution)/shard_map/all_gather | solution.py:168
  8.0 294.7 %all-gather.12.cloned.1.call-start = ((), (), s32[]{:S(2)}) async-start(), calls=%async_computation.18 | async-start | bytes 2359296 | tf_op jit(solution)/shard_map/all_gather | solution.py:124
  8.7 296.6 %all-gather.10.cloned.1.call-start = ((), (), s32[]{:S(2)}) async-start(), calls=%async_computation.17 | async-start | bytes 2359296 | tf_op jit(solution)/shard_map/all_gather | solution.py:123
  9.4 298.6 %all-gather.8.cloned.1.call-start = ((), (), s32[]{:S(2)}) async-start(), calls=%async_computation.16 | async-start | bytes 2359296 | tf_op jit(solution)/shard_map/all_gather | solution.py:125
  10.0 311.2 %all-gather.18.cloned.1.call-start = ((), (), s32[]{:S(2)}) async-start(), calls=%async_computation.21 | async-start | bytes 10485760 | tf_op jit(solution)/shard_map/all_gather | solution.py:169
  10.6 373.9 %all-gather.14.cloned.1.call-start = ((), (), s32[]{:S(2)}) async-start(), calls=%async_computation.19 | async-start | bytes 2359296 | tf_op jit(solution)/shard_map/all_gather | solution.py:126
  69.5 479.9 %collective-permute-start.2 = (bf16[1,1024,4096]{2,1,0:T(8,128)(2,1)}, bf16[1,1024,4096]{2,1,0:T(8,128)(2,1)}, u32[]{:S(2)}, u32[]{:S(2)}) collective-permute-start(bf16[1,1024,4096]{2,1,0:T(8,128)(2,1)} %all-gather.16.cloned.1.call-done), channel_id=1, source_target_pairs={{0,1},{1,0},{2,3},{3,2},{4,5},{5,4},{6,7},{7,6},{8,9},{9,8},{10,11... | collective-permute-start | bytes 25165832 | tf_op jit(solution)/shard_map/ppermute | solution.py:15
  302.5 104.9 %copy-start.41 = (s32[256]{0:T(256)}, s32[256]{0:T(256)S(1)}, u32[]{:S(2)}) copy-start(s32[256]{0:T(256)S(1)} %compare_select_fusion) | copy-start | bytes 3076
  312.7 71.9 %copy-start.29 = (f32[16,256]{1,0:T(8,128)}, f32[16,256]{1,0:T(8,128)S(1)}, u32[]{:S(2)}) copy-start(f32[16,256]{1,0:T(8,128)S(1)} %log_add_fusion) | copy-start | bytes 49156
  314.9 95.5 %copy-start.23 = (bf16[16,64,256]{2,1,0:T(8,128)(2,1)}, bf16[16,64,256]{2,1,0:T(8,128)(2,1)S(1)}, u32[]{:S(2)}) copy-start(bf16[16,64,256]{2,1,0:T(8,128)(2,1)S(1)} %convolution_convert_fusion.2) | copy-start | bytes 1572868
  314.9 79.5 %copy-start.45 = (bf16[1,128]{1,0:T(2,128)(2,1)S(1)}, bf16[1,128]{1,0:T(2,128)(2,1)}, u32[]{:S(2)}) copy-start(bf16[1,128]{1,0:T(2,128)(2,1)} %param.25) | copy-start | bytes 772
  314.9 85.9 %copy-start.43 = (bf16[1,256]{1,0:T(2,128)(2,1)S(1)}, bf16[1,256]{1,0:T(2,128)(2,1)}, u32[]{:S(2)}) copy-start(bf16[1,256]{1,0:T(2,128)(2,1)} %param.24) | copy-start | bytes 1540
  321.2 247.9 %collective-permute-start.3 = (bf16[1,4096,1024]{2,1,0:T(8,128)(2,1)}, bf16[1,4096,1024]{2,1,0:T(8,128)(2,1)}, u32[]{:S(2)}, u32[]{:S(2)}) collective-permute-start(bf16[1,4096,1024]{2,1,0:T(8,128)(2,1)} %all-gather.18.cloned.1.call-done), channel_id=1, source_target_pairs={{0,1},{1,0},{2,3},{3,2},{4,5},{5,4},{6,7},{7,6},{8,9},{9,8},{10,11... | collective-permute-start | bytes 25165832 | tf_op jit(solution)/shard_map/ppermute | solution.py:15
  389.5 136.3 %all-to-all-start = ((bf16[8,48,1024]{2,1,0:T(8,128)(2,1)}), bf16[8,48,1024]{2,1,0:T(8,128)(2,1)S(1)}, u32[]{:S(2)}, u32[]{:S(2)}) async-start(bf16[8,48,1024]{2,1,0:T(8,128)(2,1)} %bitcast.12), calls=%async_computation | async-start | bytes 1572864 | tf_op jit(solution)/shard_map/all_to_all | solution.py:164
  400.5 125.3 %collective-permute-start = (bf16[1,512]{1,0:T(2,128)(2,1)S(1)}, bf16[1,512]{1,0:T(2,128)(2,1)S(1)}, u32[]{:S(2)}, u32[]{:S(2)}) collective-permute-start(bf16[1,512]{1,0:T(2,128)(2,1)S(1)} %all_gather.32), channel_id=1, source_target_pairs={{0,1},{1,0},{2,3},{3,2},{4,5},{5,4},{6,7},{7,6},{8,9},{9,8},{10,11... | collective-permute-start | bytes 3080 | tf_op jit(solution)/shard_map/ppermute | solution.py:15
  406.1 126.0 %collective-permute-start.1 = (bf16[1,1024]{1,0:T(2,128)(2,1)S(1)}, bf16[1,1024]{1,0:T(2,128)(2,1)S(1)}, u32[]{:S(2)}, u32[]{:S(2)}) collective-permute-start(bf16[1,1024]{1,0:T(2,128)(2,1)S(1)} %all_gather.33), channel_id=1, source_target_pairs={{0,1},{1,0},{2,3},{3,2},{4,5},{5,4},{6,7},{7,6},{8,9},{9,8},{10,11... | collective-permute-start | bytes 6152 | tf_op jit(solution)/shard_map/ppermute | solution.py:15
  525.8 23.1 %all-to-all-start.2 = ((bf16[8,48,1024]{2,1,0:T(8,128)(2,1)}), bf16[8,48,1024]{2,1,0:T(8,128)(2,1)S(1)}, u32[]{:S(2)}, u32[]{:S(2)}) async-start(bf16[8,48,1024]{2,1,0:T(8,128)(2,1)} %bitcast.23), calls=%async_computation.2 | async-start | bytes 1572864 | tf_op jit(solution)/shard_map/all_to_all | solution.py:209
  531.3 218.7 %reduce-scatter.41.cloned.1.call-start = ((), (), s32[]{:S(2)}) async-start(), calls=%async_computation.32 | async-start | bytes 163840
  548.9 27.7 %slice-start = ((s8[8388608]{0:T(1024)(128)(4,1)}), s8[4194304]{0:T(1024)(128)(4,1)S(1)}, s32[]{:S(2)}) async-start(s8[8388608]{0:T(1024)(128)(4,1)} %bitcast.216), calls=%async_computation.35 | async-start | bytes 8388608
  549.4 27.2 %slice-start.1 = ((s8[8388608]{0:T(1024)(128)(4,1)}), s8[4194304]{0:T(1024)(128)(4,1)S(1)}, s32[]{:S(2)}) async-start(s8[8388608]{0:T(1024)(128)(4,1)} %bitcast.216), calls=%async_computation.36 | async-start | bytes 8388608
  622.8 127.9 %reduce-scatter.43.cloned.1.call-start = ((), (), s32[]{:S(2)}) async-start(), calls=%async_computation.33 | async-start | bytes 163840
  623.7 128.3 %reduce-scatter.39.cloned.1.call-start = ((), (), s32[]{:S(2)}) async-start(), calls=%async_computation.31 | async-start | bytes 327680
  624.7 128.3 %reduce-scatter.37.cloned.1.call-start = ((), (), s32[]{:S(2)}) async-start(), calls=%async_computation.30 | async-start | bytes 327680
  643.9 143.2 %reduce-scatter.31.cloned.1.call-start = ((), (), s32[]{:S(2)}) async-start(), calls=%async_computation.27 | async-start | bytes 10485760 | tf_op jit(solution)/shard_map/reduce_scatter | solution.py:243
  652.8 208.6 %reduce-scatter.29.cloned.1.call-start = ((), (), s32[]{:S(2)}) async-start(), calls=%async_computation.26 | async-start | bytes 10485760 | tf_op jit(solution)/shard_map/reduce_scatter | solution.py:240
  661.8 274.1 %reduce-scatter.33.cloned.1.call-start = ((), (), s32[]{:S(2)}) async-start(), calls=%async_computation.28 | async-start | bytes 10485760 | tf_op jit(solution)/shard_map/reduce_scatter | solution.py:246
  672.1 338.1 %reduce-scatter.35.cloned.1.call-start = ((), (), s32[]{:S(2)}) async-start(), calls=%async_computation.29 | async-start | bytes 10485760 | tf_op jit(solution)/shard_map/reduce_scatter | solution.py:249
  685.6 26.2 %copy-start.22 = (bf16[256,1024]{1,0:T(8,128)(2,1)S(1)}, bf16[256,1024]{1,0:T(8,128)(2,1)}, u32[]{:S(2)}) copy-start(bf16[256,1024]{1,0:T(8,128)(2,1)} %param.14) | copy-start | bytes 1572868
  685.6 25.0 %all-to-all-start.3 = ((bf16[8,48,1024]{2,1,0:T(8,128)(2,1)}), bf16[8,48,1024]{2,1,0:T(8,128)(2,1)S(1)}, u32[]{:S(2)}, u32[]{:S(2)}) async-start(bf16[8,48,1024]{2,1,0:T(8,128)(2,1)} %bitcast.26), calls=%async_computation.3 | async-start | bytes 1572864 | tf_op jit(solution)/shard_map/all_to_all | solution.py:229
  693.8 421.5 %reduce-scatter.27.cloned.1.call-start = ((), (), s32[]{:S(2)}) async-start(), calls=%async_computation.25 | async-start | bytes 4718592 | tf_op jit(solution)/shard_map/reduce_scatter | solution.py:340
  715.9 491.2 %reduce-scatter.25.cloned.1.call-start = ((), (), s32[]{:S(2)}) async-start(), calls=%async_computation.24 | async-start | bytes 4718592 | tf_op jit(solution)/shard_map/reduce_scatter | solution.py:339
  725.5 573.3 %reduce-scatter.23.cloned.1.call-start = ((), (), s32[]{:S(2)}) async-start(), calls=%async_computation.23 | async-start | bytes 4718592 | tf_op jit(solution)/shard_map/reduce_scatter | solution.py:338
  736.8 654.3 %reduce-scatter.21.cloned.1.call-start = ((), (), s32[]{:S(2)}) async-start(), calls=%async_computation.22 | async-start | bytes 4718592 | tf_op jit(solution)/shard_map/reduce_scatter | solution.py:337
  742.1 25.3 %copy-start.13 = (bf16[16,64,256]{2,1,0:T(8,128)(2,1)S(1)}, bf16[16,64,256]{2,1,0:T(8,128)(2,1)}, u32[]{:S(2)}) copy-start(bf16[16,64,256]{2,1,0:T(8,128)(2,1)} %copy-done.12) | copy-start | bytes 1572868
  742.1 24.2 %all-to-all-start.1 = ((bf16[8,48,1024]{2,1,0:T(8,128)(2,1)}), bf16[8,48,1024]{2,1,0:T(8,128)(2,1)S(1)}, u32[]{:S(2)}, u32[]{:S(2)}) async-start(bf16[8,48,1024]{2,1,0:T(8,128)(2,1)} %bitcast.21), calls=%async_computation.1 | async-start | bytes 1572864 | tf_op jit(solution)/shard_map/all_to_all | solution.py:198
  748.7 681.6 %all-reduce.4.cloned.1.call-start = ((), (), s32[]{:S(2)}) async-start(), calls=%async_computation.34 | async-start | bytes 2097152 | tf_op jit(solution)/shard_map/psum | solution.py:344
  751.7 3.5 collective-permute-start.7
  753.9 3.0 collective-permute-start.6
  767.5 98.7 %copy-start.11 = (bf16[16,64,256]{2,1,0:T(8,128)(2,1)S(1)}, bf16[16,64,256]{2,1,0:T(8,128)(2,1)}, u32[]{:S(2)}) copy-start(bf16[16,64,256]{2,1,0:T(8,128)(2,1)} %copy-done.10) | copy-start | bytes 1572868
  770.9 95.3 %copy-start.17 = (f32[256,1024]{1,0:T(8,128)S(1)}, f32[256,1024]{1,0:T(8,128)}, u32[]{:S(2)}) copy-start(f32[256,1024]{1,0:T(8,128)} %fusion.147) | copy-start | bytes 3145732
  865.9 571.8 %collective-permute-start.4 = (bf16[1,256,4096]{2,1,0:T(8,128)(2,1)}, bf16[1,256,4096]{2,1,0:T(8,128)(2,1)}, u32[]{:S(2)}, u32[]{:S(2)}) collective-permute-start(bf16[1,256,4096]{2,1,0:T(8,128)(2,1)} %fusion.53), channel_id=1, source_target_pairs={{0,1},{1,0},{2,3},{3,2},{4,5},{5,4},{6,7},{7,6},{8,9},{9,8},{10,11... | collective-permute-start | bytes 6291464 | tf_op jit(solution)/shard_map/ppermute | solution.py:15
  869.0 146.0 %copy-start.5 = (f32[256,1024]{1,0:T(8,128)S(1)}, f32[256,1024]{1,0:T(8,128)}, u32[]{:S(2)}) copy-start(f32[256,1024]{1,0:T(8,128)} %copy-done.4) | copy-start | bytes 3145732
  1014.7 427.7 %collective-permute-start.5 = (bf16[1,1024,1024]{2,1,0:T(8,128)(2,1)}, bf16[1,1024,1024]{2,1,0:T(8,128)(2,1)}, u32[]{:S(2)}, u32[]{:S(2)}) collective-permute-start(bf16[1,1024,1024]{2,1,0:T(8,128)(2,1)} %fusion.55), channel_id=1, source_target_pairs={{0,1},{1,0},{2,3},{3,2},{4,5},{5,4},{6,7},{7,6},{8,9},{9,8},{10,11... | collective-permute-start | bytes 6291464 | tf_op jit(solution)/shard_map/ppermute | solution.py:15
  1300.6 137.1 %copy-start.6 = (bf16[1,256,4096]{2,1,0:T(8,128)(2,1)S(1)}, bf16[1,256,4096]{2,1,0:T(8,128)(2,1)}, u32[]{:S(2)}) copy-start(bf16[1,256,4096]{2,1,0:T(8,128)(2,1)} %reduce-scatter.31.cloned.1.call-done) | copy-start | bytes 6291460
  (37 other events, 177.9 us)
Sparse Core Ops, SparseCore 0:
  9.6 59.8 all-gather.15
  71.6 61.2 all-gather.11
  135.1 61.8 all-gather.9
  199.0 61.8 all-gather.7
  262.3 58.9 all-gather.17
  323.2 61.2 all-gather.13
  623.0 21.9 reduce-scatter.40
  647.5 19.6 reduce-scatter.42
  669.6 20.4 reduce-scatter.38
  692.6 20.0 reduce-scatter.36
  715.2 71.7 reduce-scatter.30
  789.7 71.6 reduce-scatter.28
  864.0 71.8 reduce-scatter.32
  938.5 71.6 reduce-scatter.34
  1013.7 101.5 reduce-scatter.26
  1119.2 87.8 reduce-scatter.24
  1211.1 87.6 reduce-scatter.22
  1303.3 87.8 reduce-scatter.20
  1394.3 36.0 all-reduce.3
where the time goes:
time: 1470 us; the launch traced here: 1450 us
  waiting for transfers between devices  865 us (59%)
  blocking collectives  301 us (20%)
  matrix products  169 us (11%)
  other arithmetic  50.4 us (3%)
  starting transfers between devices  30.3 us (2%)
  local copies, waits for them, and re-layouts  23.1 us (2%)
  between operations  15.8 us (1%)
    all_gather x1, blocking collectives, shards(): lax.all_gather(attn_gain, 'exp', axis=0, tiled=True)  230 us
    ppermute x8, waiting for transfers between devices, partner(): lax.ppermute(shard, axis, [(i, i ^ 1 << bit) for i in range(lax.axis_size...  117 us
    reduce_scatter x1, waiting for transfers between devices, shards(): lax.psum_scatter(grad_w_o, 'exp', scatter_dimension=0, tiled=True)  99.4 us
    reduce_scatter x1, waiting for transfers between devices, shards(): lax.psum_scatter(grad_w_q, 'exp', scatter_dimension=0, tiled=True)  90.6 us
    reduce_scatter x1, waiting for transfers between devices, shards(): lax.psum_scatter(grad_w_v, 'exp', scatter_dimension=0, tiled=True)  90 us
    reduce_scatter x1, waiting for transfers between devices, shards(): lax.psum_scatter(grad_w_k, 'exp', scatter_dimension=0, tiled=True)  89.9 us
    reduce_scatter x1, waiting for transfers between devices, shards(): lax.psum_scatter(outer_grad_one[None].astype(jnp.bfloat16), 'rep', scatte...  74.4 us
    reduce_scatter x1, waiting for transfers between devices, shards(): lax.psum_scatter(inner_grad_zero[None].astype(jnp.bfloat16), 'rep', scatt...  74.4 us
  transfers between devices with their start and end apart: 31, of which 17 were waited for; matrix products, arithmetic and copies ran while one was open for 12% of the time, Pallas kernels for 0%

commit v1 on v0

v1 whole, which is shorter than its diff:
```python
import jax
import jax.numpy as jnp
from jax import lax
from jax.sharding import PartitionSpec as P

HEADS = 16
EPS = 1e-05
ROOT_HALF = 0.7071067811865476
INV_ROOT_TAU = 0.3989422804014327
CHUNKS = 2


def swap(shard, axis, mask):
    return lax.ppermute(shard, axis, [(i, i ^ mask) for i in range(lax.axis_size(axis))])


def plain_product(left_mat, right_mat):
    return jnp.dot(left_mat, right_mat, preferred_element_type=jnp.float32)


def tn_product(left_mat, right_mat):
    return lax.dot_general(
        left_mat, right_mat, (((0,), (0,)), ((), ())), preferred_element_type=jnp.float32
    )


def nt_product(left_mat, right_mat):
    return lax.dot_general(
        left_mat, right_mat, (((1,), (1,)), ((), ())), preferred_element_type=jnp.float32
    )


def xor_order(array, axis, index, count):
    bits = count.bit_length() - 1
    shape = array.shape
    array = array.reshape(shape[:axis] + (2,) * bits + (shape[axis] // count,) + shape[axis + 1 :])
    for at in range(bits):
        flag = (index >> (bits - 1 - at)) & 1
        if isinstance(flag, int):
            array = jnp.flip(array, axis + at) if flag else array
        else:
            array = jnp.where(flag == 1, jnp.flip(array, axis + at), array)
    return array.reshape(shape)


def norm_stats(rows):
    row_mean = jnp.mean(rows, axis=-1, keepdims=True)
    centered = rows - row_mean
    variance = jnp.mean(centered * centered, axis=-1, keepdims=True)
    inv_scale = lax.rsqrt(variance + EPS)
    return centered * inv_scale, inv_scale


def norm_back(grad_out, unit_rows, inv_scale, gain_row):
    grad_unit = grad_out * gain_row
    centred_grad = grad_unit - jnp.mean(grad_unit, axis=-1, keepdims=True)
    return (
        centred_grad - unit_rows * jnp.mean(grad_unit * unit_rows, axis=-1, keepdims=True)
    ) * inv_scale


def gather_weights(stack, core, exp_bits):
    half = stack.shape[2] // 2
    pair = stack.reshape(stack.shape[0], stack.shape[1], 2, half)
    mine = jnp.where(core == 0, pair[:, :, 0], pair[:, :, 1])
    for bit in range(1, exp_bits):
        got = swap(mine, "exp", 1 << bit)
        mine = jnp.stack([mine[:, None], got[:, None]], axis=1)
        mine = mine.reshape((stack.shape[0], -1) + stack.shape[1:2] + (half,))
    mine = mine.reshape((stack.shape[0], -1) + stack.shape[1:2] + (half,))
    got = swap(mine, "exp", 1)
    mine = jnp.stack([mine, got], axis=2).reshape(stack.shape[0], -1, half)
    other = swap(mine, "rep", 1)
    return jnp.concatenate([mine, other], axis=2)


def reduce_weights(grads, exp_bits):
    count, rows, cols = grads.shape
    half = cols // 2
    total = grads[:, :, :half] + swap(grads[:, :, half:].astype(jnp.bfloat16), "rep", 1).astype(
        jnp.float32
    )
    total = total.reshape(count, -1, 2, rows >> exp_bits, half)
    total = total[:, :, 0] + swap(total[:, :, 1].astype(jnp.bfloat16), "exp", 1).astype(
        jnp.float32
    )
    for bit in range(exp_bits - 1, 0, -1):
        keep = total.shape[1] // 2
        total = total[:, :keep] + swap(
            total[:, keep:].astype(jnp.bfloat16), "exp", 1 << bit
        ).astype(jnp.float32)
    total = total[:, 0]
    total = total + swap(total.astype(jnp.bfloat16), "rep", 2).astype(jnp.float32)
    other = swap(total.astype(jnp.bfloat16), "rep", 1).astype(jnp.float32)
    return total, other


def masked_scores(queries3, keys3, allowed, factor):
    scores = (
        jnp.einsum("qhe,khe->hqk", queries3, keys3, preferred_element_type=jnp.float32) * factor
    )
    return jnp.where(allowed[None], scores, -1e30)


def shards(
    tokens,
    cotangent,
    doc_lengths,
    expert_of_token,
    w_query,
    w_key,
    w_value,
    w_output,
    attn_gain,
    w_inner,
    w_outer,
    expert_gain,
    centroids,
):
    exp_size = lax.axis_size("exp")
    rep_size = lax.axis_size("rep")
    exp_bits = exp_size.bit_length() - 1
    experts = exp_size // 2
    rep_at = lax.axis_index("rep")
    exp_at = lax.axis_index("exp")
    core = rep_at % 2
    first = exp_at % 2 == 0
    group = exp_at // 2
    row_count, width = tokens.shape
    head_dim = width // HEADS
    factor = head_dim ** (-0.5)
    half_width = width // 2
    low = jnp.bfloat16
    wide = jnp.float32

    inner_own = w_inner[0]
    block = inner_own.shape[1] // rep_size

    def inner_for(mask):
        dest = rep_at ^ mask
        return jnp.concatenate(
            [
                lax.dynamic_slice_in_dim(inner_own, dest * block, block, 1),
                lax.dynamic_slice_in_dim(inner_own, (dest ^ 2) * block, block, 1),
            ],
            axis=1,
        )

    inner_w = jnp.concatenate(
        [inner_for(0)] + [swap(inner_for(mask), "rep", mask) for mask in range(1, rep_size)], axis=0
    )
    outer_w = jnp.concatenate([w_outer[0], swap(w_outer[0], "rep", 2)], axis=0)

    expert_ids = jnp.arange(experts, dtype=jnp.int32)
    onehot = expert_of_token[:, None] == expert_ids[None, :]
    counts = jnp.sum(onehot.astype(wide), axis=0)
    pieces = [centroids[0], expert_gain[0], attn_gain, counts.astype(low)]
    small = lax.all_gather(jnp.concatenate(pieces), ("rep", "exp"), axis=0, tiled=False)
    small = small.reshape(rep_size, exp_size, -1)
    edges = [0]
    for piece in pieces:
        edges.append(edges[-1] + piece.shape[0])
    gain_attn = small[0, :, edges[2] : edges[3]].reshape(width).astype(wide)
    own_small = lax.dynamic_slice_in_dim(small, exp_at - exp_at % 2, 2, 1)
    centroid = jnp.swapaxes(own_small[:, :, edges[0] : edges[1]], 0, 1).reshape(width)
    gain_pair = own_small[:, :, edges[1] : edges[2]]
    gain_row = jnp.where(first, gain_pair[:, 0], gain_pair[:, 1]).reshape(width).astype(wide)
    group_counts = lax.dynamic_index_in_dim(small, rep_at, 0, False)[:, edges[3] : edges[4]]
    group_counts = jnp.sum(
        jnp.where(expert_ids[None, :] == group, group_counts.astype(wide), 0.0), axis=1
    ).astype(jnp.int32)

    qkv_w = gather_weights(jnp.stack([w_query, w_key, w_value]), core, exp_bits)
    out_w = gather_weights(w_output[None], core, exp_bits)[0]
    inputs = tokens.astype(wide)
    unit_a, scale_a = norm_stats(inputs)
    act_a = xor_order((unit_a * gain_attn).astype(low), 1, exp_at, exp_size)
    queries, keys_low, values_low = [plain_product(act_a, qkv_w[i]).astype(low) for i in range(3)]
    queries3 = queries.reshape(row_count, HEADS, head_dim)
    keys3 = keys_low.reshape(row_count, HEADS, head_dim)
    values3 = values_low.reshape(row_count, HEADS, head_dim)
    doc_ends = jnp.cumsum(doc_lengths[0])
    positions = jnp.arange(row_count, dtype=jnp.int32)
    segment = jnp.sum((positions[:, None] >= doc_ends[None, :]).astype(jnp.int32), axis=1)
    allowed = (segment[:, None] == segment[None, :]) & (positions[:, None] >= positions[None, :])
    scores = masked_scores(queries3, keys3, allowed, factor)
    row_top = jnp.max(scores, axis=-1, keepdims=True)
    row_total = jnp.sum(jnp.exp(scores - row_top), axis=-1, keepdims=True)
    log_total = row_top + jnp.log(row_total)
    probs_low = jnp.exp(scores - log_total).astype(low)
    context = jnp.einsum("hqk,khe->qhe", probs_low, values3, preferred_element_type=wide)
    context = context.reshape(row_count, width).astype(low)
    context_x = xor_order(xor_order(context, 1, core, 2), 1, exp_at, exp_size)
    hidden = inputs + xor_order(plain_product(context_x, out_w), 1, core, 2)

    slots = 3 * row_count // exp_size
    lower = (positions[:, None] > positions[None, :]).astype(low)
    earlier = plain_product(lower, onehot.astype(low))
    rank_in = jnp.sum(jnp.where(onehot, earlier, 0.0), axis=1).astype(jnp.int32)
    position = expert_of_token * slots + rank_in
    all_slots = experts * slots
    pick = (jnp.arange(all_slots, dtype=jnp.int32)[:, None] == position[None, :]).astype(low)
    sent_rows = hidden.astype(low)
    packed_sent = plain_product(pick, sent_rows).astype(low).reshape(experts, 1, slots, width)
    packed_cot = plain_product(pick, cotangent).astype(low).reshape(experts, 1, slots, width)
    packed = jnp.concatenate([packed_sent, packed_cot], axis=1).reshape(exp_size, slots, width)
    arrived = lax.all_to_all(packed, "exp", split_axis=0, concat_axis=0, tiled=True)
    arrived = arrived.reshape(exp_size * slots, width)
    starts = jnp.cumsum(group_counts) - group_counts
    slot_at = jnp.arange(slots, dtype=jnp.int32)
    row_of_slot = jnp.where(
        slot_at[None, :] < group_counts[:, None], starts[:, None] + slot_at[None, :], -1
    ).reshape(-1)
    own_rows = 2 * row_count
    compact = (jnp.arange(own_rows, dtype=jnp.int32)[:, None] == row_of_slot[None, :]).astype(low)
    rows_own = plain_product(compact, arrived).astype(low)

    part = own_rows // CHUNKS

    def chunk_of(array, at):
        return array[at * part : (at + 1) * part]

    own_f = rows_own.astype(wide)
    gates = swap(jax.nn.sigmoid(plain_product(rows_own, centroid[:, None])[:, 0]), "exp", 1)
    gates_zero = jax.nn.sigmoid(plain_product(rows_own, centroid[:, None])[:, 0])
    gates = jnp.where(first, gates_zero, gates)
    kept = []
    handed = None
    finals = []
    for at in range(CHUNKS + 1):
        if at == 0:
            own_in = chunk_of(rows_own, 0)
        elif at == CHUNKS:
            own_in = handed
        else:
            own_in = jnp.where(first, chunk_of(rows_own, at), handed)
        other_in = swap(own_in, "rep", 1)
        rows_in = jnp.concatenate([own_in, other_in], axis=0).astype(wide)
        unit_rows, inv_scale = norm_stats(rows_in)
        normed_low = xor_order((unit_rows * gain_row).astype(low), 1, rep_at, rep_size)
        inner_pre = plain_product(normed_low, inner_w)
        normal = 0.5 * (1.0 + lax.erf(inner_pre * ROOT_HALF))
        active = (inner_pre * normal).astype(low)
        slope = (
            normal + inner_pre * jnp.exp(-0.5 * inner_pre * inner_pre) * INV_ROOT_TAU
        ).astype(low)
        product = plain_product(active, outer_w)
        got = swap(product[part:].astype(low), "rep", 1)
        result = rows_in[:part] + product[:part] + got.astype(wide)
        kept.append((normed_low, active, slope, own_in))
        finals.append(result)
        if at < CHUNKS:
            handed = swap(result.astype(low), "exp", 1)
    final_rows = jnp.concatenate(finals[1:], axis=0)
    grad_gate = jnp.sum(own_f * final_rows, axis=1)
    branch = (gates[:, None] * final_rows).astype(low)
    grad_gate = swap(grad_gate, "exp", 1)
    grad_logit = grad_gate * gates * (1.0 - gates)

    gain_grad = jnp.zeros((width,), wide)
    states = []
    inners = []
    outs = []
    handed = None
    for at in range(CHUNKS + 1):

        def kept_of(which):
            if at == 0:
                return kept[1][which]
            if at == CHUNKS:
                return kept[CHUNKS - 1][which]
            return jnp.where(first, kept[at - 1][which], kept[at + 1][which])

        if at < CHUNKS:
            fresh = chunk_of(gates, at)[:, None] * chunk_of(own_f, at)
        if at == 0:
            state = fresh
        elif at == CHUNKS:
            state = handed.astype(wide)
        else:
            state = jnp.where(first, handed.astype(wide), fresh)
        grad_own = state.astype(low)
        grad_outer = jnp.concatenate([grad_own, swap(grad_own, "rep", 1)], axis=0)
        grad_active = nt_product(grad_outer, outer_w)
        grad_inner = (grad_active * kept_of(2).astype(wide)).astype(low)
        grad_normed = nt_product(grad_inner, inner_w)
        got = swap(grad_normed[part:].astype(low), "rep", 1)
        got = xor_order(got, 1, 1, rep_size)
        grad_normed = xor_order(grad_normed[:part] + got.astype(wide), 1, rep_at, rep_size)
        unit_rows, inv_scale = norm_stats(kept_of(3).astype(wide))
        share = jnp.sum(grad_normed * unit_rows, axis=0)
        if at == 0:
            share = jnp.where(first, 0.0, share)
        elif at == CHUNKS:
            share = jnp.where(first, share, 0.0)
        gain_grad = gain_grad + share
        grad_state = state + norm_back(grad_normed, unit_rows, inv_scale, gain_row)
        states.append(grad_outer)
        inners.append(grad_inner)
        outs.append(grad_state)
        if at < CHUNKS:
            handed = swap(grad_state.astype(low), "exp", 1)
    grad_wide = jnp.concatenate(outs[1:], axis=0)
    grad_sent = (grad_wide + grad_logit[:, None] * centroid.astype(wide)[None, :]).astype(low)
    back_rows = jnp.where(first, grad_sent, branch)
    spread = tn_product(compact, back_rows).astype(low).reshape(exp_size, slots, width)
    home = lax.all_to_all(spread, "exp", split_axis=0, concat_axis=0, tiled=True)
    home = home.reshape(experts, 2, slots, width)
    grad_home = tn_product(pick, home[:, 0].reshape(all_slots, width))
    branch_home = tn_product(pick, home[:, 1].reshape(all_slots, width))
    output = (hidden + branch_home).astype(low)

    def both(items, of_first, of_second):
        return jnp.concatenate(
            [
                jnp.where(first, items[of_first + k], items[of_second + k])
                for k in range(CHUNKS)
            ],
            axis=0,
        )

    normed_all = both([k[0] for k in kept], 0, 1)
    active_all = both([k[1] for k in kept], 0, 1)
    state_all = both(states, 1, 0)
    inner_all = both(inners, 1, 0)
    grad_outer_w = tn_product(active_all, state_all)
    grad_inner_w = tn_product(normed_all, inner_all)
    outer_rows = w_outer.shape[1]
    grad_w_outer = (
        grad_outer_w[:outer_rows]
        + swap(grad_outer_w[outer_rows:].astype(low), "rep", 2).astype(wide)
    )[None]
    shares = grad_inner_w.reshape(rep_size, width // rep_size, 2, block)
    got = [swap(shares[mask].astype(low), "rep", mask).astype(wide) for mask in (1, 2, 3)]
    mine = shares[0]
    ordered = jnp.stack(
        [
            mine[:, 0] + got[1][:, 1],
            got[0][:, 0] + got[2][:, 1],
            mine[:, 1] + got[1][:, 0],
            got[0][:, 1] + got[2][:, 0],
        ],
        axis=1,
    )
    grad_w_inner = xor_order(ordered.reshape(width // rep_size, -1), 1, rep_at, rep_size)[None]

    grad_centre = jnp.dot(grad_logit, own_f, precision=lax.Precision.HIGHEST)
    other_centre = swap(grad_centre[half_width:], "exp", 1)
    centre_half = jnp.where(first, grad_centre[:half_width], other_centre)

    grad_hidden = cotangent.astype(wide) + grad_home
    grad_attn = grad_hidden.astype(low)
    grad_attn_c = xor_order(grad_attn, 1, core, 2)
    grad_w_o = tn_product(context_x, grad_attn_c)
    share_o = reduce_weights(grad_w_o[None], exp_bits)
    grad_context = nt_product(grad_attn_c, out_w).astype(low)
    grad_context = xor_order(xor_order(grad_context, 1, exp_at, exp_size), 1, core, 2)
    grad_context3 = grad_context.reshape(row_count, HEADS, head_dim)
    again_scores = masked_scores(queries3, keys3, allowed, factor)
    attn_probs = jnp.exp(again_scores - log_total)
    grad_probs = jnp.einsum("qhe,khe->hqk", grad_context3, values3, preferred_element_type=wide)
    inner_sum = jnp.sum(attn_probs * grad_probs, axis=-1, keepdims=True)
    grad_scores = (attn_probs * (grad_probs - inner_sum)).astype(low)
    grad_query = (
        jnp.einsum("hqk,khe->qhe", grad_scores, keys3, preferred_element_type=wide) * factor
    ).astype(low)
    grad_key = (
        jnp.einsum("hqk,qhe->khe", grad_scores, queries3, preferred_element_type=wide) * factor
    ).astype(low)
    grad_value = jnp.einsum(
        "hqk,qhe->khe", attn_probs.astype(low), grad_context3, preferred_element_type=wide
    ).astype(low)
    grads3 = [g.reshape(row_count, width) for g in (grad_query, grad_key, grad_value)]
    grad_w_qkv = jnp.stack([tn_product(act_a, g) for g in grads3])
    share_qkv = reduce_weights(grad_w_qkv, exp_bits)
    grad_act = sum(nt_product(g, qkv_w[i]) for i, g in enumerate(grads3))
    grad_act = xor_order(grad_act, 1, exp_at, exp_size)
    grad_gain_a = jnp.sum(grad_act * unit_a, axis=0)
    grad_tokens = grad_hidden + norm_back(grad_act, unit_a, scale_a, gain_attn)

    def true_halves(pair):
        mine_half, other_half = pair
        return xor_order(jnp.concatenate([mine_half, other_half], axis=-1), 2, core, 2)

    full_o = true_halves(share_o)[0]
    full_qkv = true_halves(share_qkv)

    rep_sums = lax.psum(jnp.concatenate([gain_grad, centre_half]), "rep")
    gain_len = width // rep_size
    centre_len = half_width // rep_size
    grad_expert_gain = lax.dynamic_slice_in_dim(rep_sums, rep_at * gain_len, gain_len)[None]
    grad_centroids = lax.dynamic_slice_in_dim(
        rep_sums, width + rep_at * centre_len, centre_len
    )[None]
    attn_sums = lax.psum(grad_gain_a, ("rep", "exp"))
    attn_len = width // exp_size
    share_gain = lax.dynamic_slice_in_dim(attn_sums, exp_at * attn_len, attn_len)
    return (
        output,
        grad_tokens,
        full_qkv[0],
        full_qkv[1],
        full_qkv[2],
        full_o,
        share_gain,
        grad_w_inner,
        grad_w_outer,
        grad_expert_gain,
        grad_centroids,
    )


def solution(mesh):
    placed = (
        P(("rep", "exp"), None),
        P(("rep", "exp"), None),
        P(("rep", "exp"), None),
        P(("rep", "exp")),
        P("exp", None),
        P("exp", None),
        P("exp", None),
        P("exp", None),
        P("exp"),
        P("exp", "rep", None),
        P("exp", "rep", None),
        P("exp", "rep"),
        P("exp", "rep"),
    )
    return jax.shard_map(
        shards,
        mesh=mesh,
        in_specs=placed,
        out_specs=(
            P(("rep", "exp"), None),
            P(("rep", "exp"), None),
            P("exp", None),
            P("exp", None),
            P("exp", None),
            P("exp", None),
            P("exp"),
            P("exp", "rep", None),
            P("exp", "rep", None),
            P("exp", "rep"),
            P("exp", "rep"),
        ),
        check_vma=False,
    )
```

time: 1470 us -> 976 us (0.66)
  waiting for transfers between devices: 865 us -> 306 us
  local copies, waits for them, and re-layouts: 23.1 us -> 205 us
  blocking collectives: 301 us -> 123 us
  other arithmetic: 50.4 us -> 158 us
  matrix products: 169 us -> 115 us
  starting transfers between devices: 30.3 us -> 55.3 us
    reduce_scatter x8 -> x0, waiting for transfers between devices: 542 us -> none  [the longest x1 99.4 us: shards(): lax.psum_scatter(grad_w_o, 'exp', scatter_dimension=0, tiled=True)]
    all_gather x3 -> x0, blocking collectives: 242 us -> none  [the longest x1 230 us: shards(): lax.all_gather(attn_gain, 'exp', axis=0, tiled=True)]
    ppermute x8 -> x47, waiting for transfers between devices: 117 us -> 281 us  [swap(): lax.ppermute(shard, axis, [(i, i ^ mask) for i in range(lax.axis_size(axi...]
    all_gather x6 -> x0, waiting for transfers between devices: 128 us -> none  [the longest x1 63 us: shards(): lax.all_gather(w_output, 'exp', axis=0, tiled=True)]
    rev x0 -> x12, local copies, waits for them, and re-layouts: none -> 88.9 us  [the longest x9 78.1 us: xor_order(): array = jnp.where(flag == 1, jnp.flip(array, axis + at), array)]
    psum x1 -> x2, blocking collectives: 8.6 us -> 85 us  [the longest x1 45.1 us: shards(): rep_sums = lax.psum(jnp.concatenate([gain_grad, centre_half]), 'rep')]
    select_n x2 -> x34, other arithmetic: 0.04 us -> 45.9 us  [the longest x28 40.3 us: xor_order(): array = jnp.where(flag == 1, jnp.flip(array, axis + at), array)]
    ppermute x8 -> x47, starting transfers between devices: 4.2 us -> 42.7 us  [swap(): lax.ppermute(shard, axis, [(i, i ^ mask) for i in range(lax.axis_size(axi...]
  transfers between devices with their start and end apart: 31 -> 49, of which waited for: 17 -> 26; matrix products, arithmetic and copies ran while one was open for 12% -> 27% of each run, Pallas kernels for 0% -> 0%
where the time goes in v1:
time: 976 us; the launch traced here: 966 us
  waiting for transfers between devices  306 us (31%)
  local copies, waits for them, and re-layouts  205 us (21%)
  other arithmetic  158 us (16%)
  blocking collectives  123 us (13%)
  matrix products  115 us (12%)
  starting transfers between devices  55.3 us (6%)
    ppermute x47, waiting for transfers between devices, swap(): lax.ppermute(shard, axis, [(i, i ^ mask) for i in range(lax.axis_size(axi...  281 us
    rev x9, local copies, waits for them, and re-layouts, xor_order(): array = jnp.where(flag == 1, jnp.flip(array, axis + at), array)  78.1 us
    dot_general x15, matrix products, plain_product(): return jnp.dot(left_mat, right_mat, preferred_element_type=jnp.float32)  49.8 us
    psum x1, blocking collectives, shards(): rep_sums = lax.psum(jnp.concatenate([gain_grad, centre_half]), 'rep')  45.1 us
    ppermute x47, starting transfers between devices, swap(): lax.ppermute(shard, axis, [(i, i ^ mask) for i in range(lax.axis_size(axi...  42.7 us
    select_n x28, other arithmetic, xor_order(): array = jnp.where(flag == 1, jnp.flip(array, axis + at), array)  40.3 us
    psum x1, blocking collectives, shards(): attn_sums = lax.psum(grad_gain_a, ('rep', 'exp'))  39.9 us
    unnamed x1, blocking collectives  38 us
  transfers between devices with their start and end apart: 49, of which 26 were waited for; matrix products, arithmetic and copies ran while one was open for 27% of the time, Pallas kernels for 0%

profile of v1, /device:TPU:11, one launch (start us, length us, event | category | flops | bytes accessed | tf_op | source)
XLA Modules:
  0.0 965.9 jit_solution(17846984216566944835)
XLA Ops:
  4.6 9.8 %collective-permute-done = bf16[3,128,512]{2,1,0:T(8,128)(2,1)S(1)} collective-permute-done((bf16[3,128,512]{2,1,0:T(8,128)(2,1)S(1)}, bf16[3,128,512]{2,1,0:T(8,128)(2,1)S(1)}, u32[]{:S(2)}, u32[]{:S(2)}) %collective-permute-start) | collective-permute-done | bytes 393248 | tf_op jit(solution)/shard_map/ppermute | solution.py:14
  16.9 34.0 %collective-permute-done.1 = bf16[3,2,128,512]{3,2,0,1:T(8,128)(2,1)S(1)} collective-permute-done((bf16[3,2,128,512]{3,2,0,1:T(8,128)(2,1)S(1)}, bf16[3,2,128,512]{3,2,0,1:T(8,128)(2,1)S(1)}, u32[]{:S(2)}, u32[]{:S(2)}) %collective-permute-start.1) | collective-permute-done | bytes 786464 | tf_op jit(solution)/shard_map/ppermute | solution.py:14
  53.8 34.4 %collective-permute-done.2 = bf16[3,4,128,512]{3,2,1,0:T(8,128)(2,1)} collective-permute-done((bf16[3,4,128,512]{3,2,1,0:T(8,128)(2,1)}, bf16[3,4,128,512]{3,2,1,0:T(8,128)(2,1)}, u32[]{:S(2)}, u32[]{:S(2)}) %collective-permute-start.2) | collective-permute-done | bytes 1572896 | tf_op jit(solution)/shard_map/ppermute | solution.py:14
  100.4 38.0 %all-reduce = bf16[16512]{0:T(1024)(128)(2,1)S(1)} all-reduce(bf16[16512]{0:T(1024)(128)(2,1)S(1)} %dynamic-update-slice), channel_id=2, replica_groups=mesh['rep'=4,'exp'=8] {'rep','exp'}, use_global_device_ids=true, to_apply=%add | all-reduce | flops 16512 | bytes 66048
  143.1 8.2 collective-permute-done.6
  190.5 6.5 all-to-all-start
  206.2 25.3 %all-to-all-done = bf16[8,96,1024]{2,1,0:T(8,128)(2,1)} async-done(((bf16[8,96,1024]{2,1,0:T(8,128)(2,1)}), bf16[8,96,1024]{2,1,0:T(8,128)(2,1)}, u32[]{:S(2)}, u32[]{:S(2)}) %all-to-all-start) | async-done | bytes 1572896 | tf_op jit(solution)/shard_map/all_to_all | solution.py:207
  235.9 32.0 %collective-permute-done.14 = bf16[256,2048]{1,0:T(8,128)(2,1)} collective-permute-done((bf16[256,2048]{1,0:T(8,128)(2,1)}, bf16[256,2048]{1,0:T(8,128)(2,1)}, u32[]{:S(2)}, u32[]{:S(2)}) %collective-permute-start.14) | collective-permute-done | bytes 1048608 | tf_op jit(solution)/shard_map/ppermute | solution.py:14
  267.9 21.3 %collective-permute-done.13 = bf16[256,2048]{1,0:T(8,128)(2,1)} collective-permute-done((bf16[256,2048]{1,0:T(8,128)(2,1)}, bf16[256,2048]{1,0:T(8,128)(2,1)}, u32[]{:S(2)}, u32[]{:S(2)}) %collective-permute-start.13) | collective-permute-done | bytes 1048608 | tf_op jit(solution)/shard_map/ppermute | solution.py:14
  289.3 6.7 pad_maximum_fusion.2
  298.9 4.7 multiply_convert_fusion.8
  305.7 10.2 %rev.131 = bf16[512,2,2,256]{3,2,1,0:T(2,128)(2,1)} reverse(bf16[512,2,2,256]{3,2,1,0:T(2,128)(2,1)} %broadcast_select_fusion.7), dimensions={2} | reverse | bytes 2097152 | tf_op jit(solution)/shard_map/jit(_flip)/rev | solution.py:42
  321.5 7.2 multiply_convert_fusion.4
  328.8 4.7 fusion.159
  336.2 13.1 %collective-permute-done.16 = bf16[256,1024]{1,0:T(8,128)(2,1)S(1)} collective-permute-done((bf16[256,1024]{1,0:T(8,128)(2,1)S(1)}, bf16[256,1024]{1,0:T(8,128)(2,1)S(1)}, u32[]{:S(2)}, u32[]{:S(2)}) %collective-permute-start.16) | collective-permute-done | bytes 524320 | tf_op jit(solution)/shard_map/ppermute | solution.py:14
  353.9 4.7 multiply_convert_fusion.7
  360.6 10.3 %rev.133 = bf16[512,2,2,256]{3,2,1,0:T(2,128)(2,1)} reverse(bf16[512,2,2,256]{3,2,1,0:T(2,128)(2,1)} %broadcast_select_fusion.6), dimensions={2} | reverse | bytes 2097152 | tf_op jit(solution)/shard_map/jit(_flip)/rev | solution.py:42
  376.7 7.7 broadcast_select_fusion.2
  384.4 4.7 fusion.158
  393.0 12.8 %collective-permute-done.22 = bf16[256,1024]{1,0:T(8,128)(2,1)S(1)} collective-permute-done((bf16[256,1024]{1,0:T(8,128)(2,1)S(1)}, bf16[256,1024]{1,0:T(8,128)(2,1)S(1)}, u32[]{:S(2)}, u32[]{:S(2)}) %collective-permute-start.22) | collective-permute-done | bytes 524320 | tf_op jit(solution)/shard_map/ppermute | solution.py:14
  410.3 4.7 multiply_convert_fusion.6
  417.1 10.3 %rev.138 = bf16[512,2,2,256]{3,2,1,0:T(2,128)(2,1)} reverse(bf16[512,2,2,256]{3,2,1,0:T(2,128)(2,1)} %broadcast_select_fusion.5), dimensions={2} | reverse | bytes 2097152 | tf_op jit(solution)/shard_map/jit(_flip)/rev | solution.py:42
  433.0 7.6 broadcast_select_fusion.1
  453.5 5.0 fusion
  474.6 6.4 rev.136
  489.5 12.5 %collective-permute-done.19 = bf16[256,1024]{1,0:T(8,128)(2,1)S(1)} collective-permute-done((bf16[256,1024]{1,0:T(8,128)(2,1)S(1)}, bf16[256,1024]{1,0:T(8,128)(2,1)S(1)}, u32[]{:S(2)}, u32[]{:S(2)}) %collective-permute-start.19) | collective-permute-done | bytes 524320 | tf_op jit(solution)/shard_map/ppermute | solution.py:14
  504.3 8.2 multiply_convert_fusion.2
  528.6 6.2 rev.141
  545.8 11.3 %collective-permute-done.25 = bf16[256,1024]{1,0:T(8,128)(2,1)S(1)} collective-permute-done((bf16[256,1024]{1,0:T(8,128)(2,1)}, bf16[256,1024]{1,0:T(8,128)(2,1)S(1)}, u32[]{:S(2)}, u32[]{:S(2)}) %collective-permute-start.25) | collective-permute-done | bytes 524320 | tf_op jit(solution)/shard_map/ppermute | solution.py:14
  559.2 6.2 broadcast_select_fusion.4
  570.8 7.0 fusion.175
  611.6 6.1 all-to-all-start.1
  617.6 6.4 fusion.22
  634.2 45.1 %psum.15 = f32[1536]{0:T(1024)S(1)} all-reduce(f32[1536]{0:T(1024)S(1)} %pad_maximum_fusion.25), channel_id=1, replica_groups=mesh['rep'=4,'exp'=8] {'rep'}, use_global_device_ids=true, to_apply=%region_35.36 | all-reduce | flops 1536 | bytes 12288 | tf_op jit(solution)/shard_map/psum | solution.py:388
  690.8 5.3 pad_maximum_fusion.3
  696.2 6.5 reshape_reshape.15
  735.4 21.0 %rev.156 = f32[256,2,2,1024]{3,2,1,0:T(2,128)} reverse(f32[256,2,2,1024]{3,2,1,0:T(2,128)} %reverse_select_fusion), dimensions={2} | reverse | bytes 8388608 | tf_op jit(solution)/shard_map/jit(_flip)/rev | solution.py:42
  756.4 10.8 %broadcast_select_fusion = f32[256,2,2,1024]{3,2,1,0:T(2,128)} fusion(f32[256,2,2,1024]{3,2,1,0:T(2,128)} %rev.156, pred[]{:T(512)S(6)} %eq.142, f32[256,2,2,1024]{3,2,1,0:T(2,128)} %reshape_reshape.15, pred[]{:T(512)S(6)} %eq.143), kind=kLoop, calls=%fused_computation.56 | loop fusion | flops 2097152 | bytes 12582914 | tf_op jit(solution)/shard_map/jit(_where)/select_n | solution.py:42
  767.2 6.8 broadcast_in_dim_reshape.2
  774.1 6.0 fusion.17
  786.8 5.0 slice_add_fusion
  806.9 24.8 %collective-permute-done.31 = bf16[3,4,128,512]{3,2,1,0:T(8,128)(2,1)} collective-permute-done((bf16[3,4,128,512]{3,2,1,0:T(8,128)(2,1)}, bf16[3,4,128,512]{3,2,1,0:T(8,128)(2,1)}, u32[]{:S(2)}, u32[]{:S(2)}) %collective-permute-start.31) | collective-permute-done | bytes 1572896 | tf_op jit(solution)/shard_map/ppermute | solution.py:14
  837.0 6.0 collective-permute-done.37
  846.9 35.4 %collective-permute-done.38 = bf16[1,2,128,512]{3,2,1,0:T(8,128)(2,1)S(1)} collective-permute-done((bf16[1,2,128,512]{3,2,1,0:T(8,128)(2,1)S(1)}, bf16[1,2,128,512]{3,2,1,0:T(8,128)(2,1)S(1)}, u32[]{:S(2)}, u32[]{:S(2)}) %collective-permute-start.38) | collective-permute-done | bytes 262176 | tf_op jit(solution)/shard_map/ppermute | solution.py:14
  887.6 7.9 collective-permute-done.33
  899.2 5.8 collective-permute-done.34
  908.8 39.9 %psum.14 = f32[1024]{0:T(1024)S(1)} all-reduce(f32[1024]{0:T(1024)S(1)} %get-tuple-element.17), channel_id=1, replica_groups=mesh['rep'=4,'exp'=8] {'rep','exp'}, use_global_device_ids=true, to_apply=%region_31.32 | all-reduce | flops 1024 | bytes 8192 | tf_op jit(solution)/shard_map/psum | solution.py:395
  953.8 8.1 rev.153
  (539 shorter events, 333.9 us)
Async XLA Ops:
  4.4 10.0 %collective-permute-start = (bf16[3,128,512]{2,1,0:T(8,128)(2,1)S(1)}, bf16[3,128,512]{2,1,0:T(8,128)(2,1)S(1)}, u32[]{:S(2)}, u32[]{:S(2)}) collective-permute-start(bf16[3,128,512]{2,1,0:T(8,128)(2,1)S(1)} %bitcast.298), channel_id=1, source_target_pairs={{0,2},{1,3},{2,0},{3,1},{4,6},{5,7},{6,4},{7,5},{8,10},{9,11},{10,... | collective-permute-start | bytes 1179656 | tf_op jit(solution)/shard_map/ppermute | solution.py:14
  14.5 36.4 %collective-permute-start.1 = (bf16[3,2,128,512]{3,2,0,1:T(8,128)(2,1)S(1)}, bf16[3,2,128,512]{3,2,0,1:T(8,128)(2,1)S(1)}, u32[]{:S(2)}, u32[]{:S(2)}) collective-permute-start(bf16[3,2,128,512]{3,2,0,1:T(8,128)(2,1)S(1)} %get-tuple-element.73), channel_id=1, source_target_pairs={{0,4},{1,5},{2,6},{3,7},{4,0},{5,1},{6,2},{7,3},{8,12},{9,13},{10,... | collective-permute-start | bytes 2359304 | tf_op jit(solution)/shard_map/ppermute | solution.py:14
  52.4 35.8 %collective-permute-start.2 = (bf16[3,4,128,512]{3,2,1,0:T(8,128)(2,1)}, bf16[3,4,128,512]{3,2,1,0:T(8,128)(2,1)}, u32[]{:S(2)}, u32[]{:S(2)}) collective-permute-start(bf16[3,4,128,512]{3,2,1,0:T(8,128)(2,1)} %copy.132), channel_id=1, source_target_pairs={{0,1},{1,0},{2,3},{3,2},{4,5},{5,4},{6,7},{7,6},{8,9},{9,8},{10,11... | collective-permute-start | bytes 4718600 | tf_op jit(solution)/shard_map/ppermute | solution.py:14
  53.0 40.2 %collective-permute-start.4 = (bf16[1,128,512]{2,1,0:T(8,128)(2,1)S(1)}, bf16[1,128,512]{2,1,0:T(8,128)(2,1)S(1)}, u32[]{:S(2)}, u32[]{:S(2)}) collective-permute-start(bf16[1,128,512]{2,1,0:T(8,128)(2,1)S(1)} %bitcast.310), channel_id=1, source_target_pairs={{0,2},{1,3},{2,0},{3,1},{4,6},{5,7},{6,4},{7,5},{8,10},{9,11},{10,... | collective-permute-start | bytes 393224 | tf_op jit(solution)/shard_map/ppermute | solution.py:14
  90.4 78.2 %collective-permute-start.3 = (bf16[3,1024,512]{2,1,0:T(8,128)(2,1)S(1)}, bf16[3,1024,512]{2,1,0:T(8,128)(2,1)}, u32[]{:S(2)}, u32[]{:S(2)}) collective-permute-start(bf16[3,1024,512]{2,1,0:T(8,128)(2,1)S(1)} %bitcast.238), channel_id=1, source_target_pairs={{0,8},{8,0},{16,24},{24,16},{1,9},{9,1},{17,25},{25,17},{2,10},{10... | collective-permute-start | bytes 9437192 | tf_op jit(solution)/shard_map/ppermute | solution.py:14
  95.5 43.6 %collective-permute-start.5 = (bf16[1,2,128,512]{3,2,1,0:T(8,128)(2,1)}, bf16[1,2,128,512]{3,2,1,0:T(8,128)(2,1)}, u32[]{:S(2)}, u32[]{:S(2)}) collective-permute-start(bf16[1,2,128,512]{3,2,1,0:T(8,128)(2,1)} %get-tuple-element.75), channel_id=1, source_target_pairs={{0,4},{1,5},{2,6},{3,7},{4,0},{5,1},{6,2},{7,3},{8,12},{9,13},{10,... | collective-permute-start | bytes 786440 | tf_op jit(solution)/shard_map/ppermute | solution.py:14
  140.2 11.1 %collective-permute-start.6 = (bf16[1,4,128,512]{3,2,1,0:T(8,128)(2,1)S(1)}, bf16[1,4,128,512]{3,2,1,0:T(8,128)(2,1)S(1)}, u32[]{:S(2)}, u32[]{:S(2)}) collective-permute-start(bf16[1,4,128,512]{3,2,1,0:T(8,128)(2,1)S(1)} %bitcast.293), channel_id=1, source_target_pairs={{0,1},{1,0},{2,3},{3,2},{4,5},{5,4},{6,7},{7,6},{8,9},{9,8},{10,11... | collective-permute-start | bytes 1572872 | tf_op jit(solution)/shard_map/ppermute | solution.py:14
  152.5 9.0 collective-permute-start.7
  190.5 40.9 %all-to-all-start = ((bf16[8,96,1024]{2,1,0:T(8,128)(2,1)}), bf16[8,96,1024]{2,1,0:T(8,128)(2,1)}, u32[]{:S(2)}, u32[]{:S(2)}) async-start(bf16[8,96,1024]{2,1,0:T(8,128)(2,1)} %bitcast.51), calls=%async_computation | async-start | bytes 3145728 | tf_op jit(solution)/shard_map/all_to_all | solution.py:207
  197.0 131.8 %collective-permute-start.10 = (bf16[1024,1024]{1,0:T(8,128)(2,1)}, bf16[1024,1024]{1,0:T(8,128)(2,1)}, u32[]{:S(2)}, u32[]{:S(2)}) collective-permute-start(bf16[1024,1024]{1,0:T(8,128)(2,1)} %bitcast.331), channel_id=1, source_target_pairs={{0,16},{8,24},{16,0},{24,8},{1,17},{9,25},{17,1},{25,9},{2,18},{10... | collective-permute-start | bytes 6291464 | tf_op jit(solution)/shard_map/ppermute | solution.py:14
  201.6 66.3 %collective-permute-start.14 = (bf16[256,2048]{1,0:T(8,128)(2,1)}, bf16[256,2048]{1,0:T(8,128)(2,1)}, u32[]{:S(2)}, u32[]{:S(2)}) collective-permute-start(bf16[256,2048]{1,0:T(8,128)(2,1)} %pad_maximum_fusion.16), channel_id=1, source_target_pairs={{0,24},{8,16},{16,8},{24,0},{1,25},{9,17},{17,9},{25,1},{2,26},{10... | collective-permute-start | bytes 3145736 | tf_op jit(solution)/shard_map/ppermute | solution.py:14
  203.6 64.3 %collective-permute-start.12 = (bf16[256,2048]{1,0:T(8,128)(2,1)}, bf16[256,2048]{1,0:T(8,128)(2,1)}, u32[]{:S(2)}, u32[]{:S(2)}) collective-permute-start(bf16[256,2048]{1,0:T(8,128)(2,1)} %pad_maximum_fusion.14), channel_id=1, source_target_pairs={{0,8},{8,0},{16,24},{24,16},{1,9},{9,1},{17,25},{25,17},{2,10},{10... | collective-permute-start | bytes 3145736 | tf_op jit(solution)/shard_map/ppermute | solution.py:14
  204.7 84.6 %collective-permute-start.13 = (bf16[256,2048]{1,0:T(8,128)(2,1)}, bf16[256,2048]{1,0:T(8,128)(2,1)}, u32[]{:S(2)}, u32[]{:S(2)}) collective-permute-start(bf16[256,2048]{1,0:T(8,128)(2,1)} %pad_maximum_fusion.15), channel_id=1, source_target_pairs={{0,16},{8,24},{16,0},{24,8},{1,17},{9,25},{17,1},{25,9},{2,18},{10... | collective-permute-start | bytes 3145736 | tf_op jit(solution)/shard_map/ppermute | solution.py:14
  235.3 61.8 %collective-permute-start.11 = (bf16[256,1024]{1,0:T(8,128)(2,1)S(1)}, bf16[256,1024]{1,0:T(8,128)(2,1)S(1)}, u32[]{:S(2)}, u32[]{:S(2)}) collective-permute-start(bf16[256,1024]{1,0:T(8,128)(2,1)S(1)} %slice.323), channel_id=1, source_target_pairs={{0,8},{8,0},{16,24},{24,16},{1,9},{9,1},{17,25},{25,17},{2,10},{10... | collective-permute-start | bytes 1572872 | tf_op jit(solution)/shard_map/ppermute | solution.py:14
  333.6 2.0 collective-permute-start.15
  335.8 13.4 %collective-permute-start.16 = (bf16[256,1024]{1,0:T(8,128)(2,1)S(1)}, bf16[256,1024]{1,0:T(8,128)(2,1)S(1)}, u32[]{:S(2)}, u32[]{:S(2)}) collective-permute-start(bf16[256,1024]{1,0:T(8,128)(2,1)S(1)} %fusion.108), channel_id=1, source_target_pairs={{0,1},{1,0},{2,3},{3,2},{4,5},{5,4},{6,7},{7,6},{8,9},{9,8},{10,11... | collective-permute-start | bytes 1572872 | tf_op jit(solution)/shard_map/ppermute | solution.py:14
  349.5 2.6 collective-permute-start.17
  389.2 2.0 collective-permute-start.21
  392.4 13.4 %collective-permute-start.22 = (bf16[256,1024]{1,0:T(8,128)(2,1)S(1)}, bf16[256,1024]{1,0:T(8,128)(2,1)S(1)}, u32[]{:S(2)}, u32[]{:S(2)}) collective-permute-start(bf16[256,1024]{1,0:T(8,128)(2,1)S(1)} %get-tuple-element.43), channel_id=1, source_target_pairs={{0,1},{1,0},{2,3},{3,2},{4,5},{5,4},{6,7},{7,6},{8,9},{9,8},{10,11... | collective-permute-start | bytes 1572872 | tf_op jit(solution)/shard_map/ppermute | solution.py:14
  405.8 2.5 collective-permute-start.23
  444.8 2.0 collective-permute-start.28
  445.3 3.1 collective-permute-start.8
  447.4 2.5 collective-permute-start.29
  450.1 3.4 collective-permute-start.9
  461.0 2.0 collective-permute-start.18
  488.8 13.2 %collective-permute-start.19 = (bf16[256,1024]{1,0:T(8,128)(2,1)S(1)}, bf16[256,1024]{1,0:T(8,128)(2,1)S(1)}, u32[]{:S(2)}, u32[]{:S(2)}) collective-permute-start(bf16[256,1024]{1,0:T(8,128)(2,1)S(1)} %fusion.92), channel_id=1, source_target_pairs={{0,1},{1,0},{2,3},{3,2},{4,5},{5,4},{6,7},{7,6},{8,9},{9,8},{10,11... | collective-permute-start | bytes 1572872 | tf_op jit(solution)/shard_map/ppermute | solution.py:14
  502.3 2.0 collective-permute-start.20
  543.7 13.3 %collective-permute-start.25 = (bf16[256,1024]{1,0:T(8,128)(2,1)}, bf16[256,1024]{1,0:T(8,128)(2,1)S(1)}, u32[]{:S(2)}, u32[]{:S(2)}) collective-permute-start(bf16[256,1024]{1,0:T(8,128)(2,1)} %get-tuple-element.33), channel_id=1, source_target_pairs={{0,1},{1,0},{2,3},{3,2},{4,5},{5,4},{6,7},{7,6},{8,9},{9,8},{10,11... | collective-permute-start | bytes 1572872 | tf_op jit(solution)/shard_map/ppermute | solution.py:14
  544.9 14.1 %collective-permute-start.46 = (f32[512]{0:T(512)S(1)}, f32[512]{0:T(512)S(1)}, u32[]{:S(2)}, u32[]{:S(2)}) collective-permute-start(f32[512]{0:T(512)S(1)} %slice.310), channel_id=1, source_target_pairs={{0,1},{1,0},{2,3},{3,2},{4,5},{5,4},{6,7},{7,6},{8,9},{9,8},{10,11... | collective-permute-start | bytes 6152 | tf_op jit(solution)/shard_map/ppermute | solution.py:14
  557.1 2.0 collective-permute-start.26
  570.5 20.2 %collective-permute-start.27 = (bf16[256,1024]{1,0:T(8,128)(2,1)}, bf16[256,1024]{1,0:T(8,128)(2,1)}, u32[]{:S(2)}, u32[]{:S(2)}) collective-permute-start(bf16[256,1024]{1,0:T(8,128)(2,1)} %slice.494), channel_id=1, source_target_pairs={{0,8},{8,0},{16,24},{24,16},{1,9},{9,1},{17,25},{25,17},{2,10},{10... | collective-permute-start | bytes 1572872 | tf_op jit(solution)/shard_map/ppermute | solution.py:14
  585.0 95.5 %collective-permute-start.43 = (bf16[256,2,1024]{2,1,0:T(2,128)(2,1)}, bf16[256,2,1024]{2,1,0:T(2,128)(2,1)}, u32[]{:S(2)}, u32[]{:S(2)}) collective-permute-start(bf16[256,2,1024]{2,1,0:T(2,128)(2,1)} %convert_element_type.497), channel_id=1, source_target_pairs={{0,8},{8,0},{16,24},{24,16},{1,9},{9,1},{17,25},{25,17},{2,10},{10... | collective-permute-start | bytes 3145736 | tf_op jit(solution)/shard_map/ppermute | solution.py:14
  585.3 97.2 %collective-permute-start.44 = (bf16[256,2,1024]{2,1,0:T(2,128)(2,1)}, bf16[256,2,1024]{2,1,0:T(2,128)(2,1)}, u32[]{:S(2)}, u32[]{:S(2)}) collective-permute-start(bf16[256,2,1024]{2,1,0:T(2,128)(2,1)} %convert_element_type.499), channel_id=1, source_target_pairs={{0,24},{8,16},{16,8},{24,0},{1,25},{9,17},{17,9},{25,1},{2,26},{10... | collective-permute-start | bytes 3145736 | tf_op jit(solution)/shard_map/ppermute | solution.py:14
  586.6 97.9 %collective-permute-start.42 = (bf16[256,2,1024]{2,1,0:T(2,128)(2,1)}, bf16[256,2,1024]{2,1,0:T(2,128)(2,1)}, u32[]{:S(2)}, u32[]{:S(2)}) collective-permute-start(bf16[256,2,1024]{2,1,0:T(2,128)(2,1)} %convert_element_type.495), channel_id=1, source_target_pairs={{0,16},{8,24},{16,0},{24,8},{1,17},{9,25},{17,1},{25,9},{2,18},{10... | collective-permute-start | bytes 3145736 | tf_op jit(solution)/shard_map/ppermute | solution.py:14
  611.6 91.1 %all-to-all-start.1 = ((bf16[8,96,1024]{2,1,0:T(8,128)(2,1)}), bf16[8,96,1024]{2,1,0:T(8,128)(2,1)}, u32[]{:S(2)}, u32[]{:S(2)}) async-start(bf16[8,96,1024]{2,1,0:T(8,128)(2,1)} %bitcast.65), calls=%async_computation.1 | async-start | bytes 3145728 | tf_op jit(solution)/shard_map/all_to_all | solution.py:307
  626.0 148.1 %collective-permute-start.45 = (bf16[1024,1024]{1,0:T(8,128)(2,1)}, bf16[1024,1024]{1,0:T(8,128)(2,1)}, u32[]{:S(2)}, u32[]{:S(2)}) collective-permute-start(bf16[1024,1024]{1,0:T(8,128)(2,1)} %slice.490), channel_id=1, source_target_pairs={{0,16},{8,24},{16,0},{24,8},{1,17},{9,25},{17,1},{25,9},{2,18},{10... | collective-permute-start | bytes 6291464 | tf_op jit(solution)/shard_map/ppermute | solution.py:14
  729.2 57.6 %collective-permute-start.30 = (bf16[3,1024,512]{2,1,0:T(8,128)(2,1)}, bf16[3,1024,512]{2,1,0:T(8,128)(2,1)}, u32[]{:S(2)}, u32[]{:S(2)}) collective-permute-start(bf16[3,1024,512]{2,1,0:T(8,128)(2,1)} %slice.489), channel_id=1, source_target_pairs={{0,8},{8,0},{16,24},{24,16},{1,9},{9,1},{17,25},{25,17},{2,10},{10... | collective-permute-start | bytes 9437192 | tf_op jit(solution)/shard_map/ppermute | solution.py:14
  783.9 15.1 %collective-permute-start.36 = (bf16[1,1024,512]{2,1,0:T(8,128)(2,1)}, bf16[1,1024,512]{2,1,0:T(8,128)(2,1)}, u32[]{:S(2)}, u32[]{:S(2)}) collective-permute-start(bf16[1,1024,512]{2,1,0:T(8,128)(2,1)} %slice.491), channel_id=1, source_target_pairs={{0,8},{8,0},{16,24},{24,16},{1,9},{9,1},{17,25},{25,17},{2,10},{10... | collective-permute-start | bytes 3145736 | tf_op jit(solution)/shard_map/ppermute | solution.py:14
  795.8 35.9 %collective-permute-start.31 = (bf16[3,4,128,512]{3,2,1,0:T(8,128)(2,1)}, bf16[3,4,128,512]{3,2,1,0:T(8,128)(2,1)}, u32[]{:S(2)}, u32[]{:S(2)}) collective-permute-start(bf16[3,4,128,512]{3,2,1,0:T(8,128)(2,1)} %fusion.44), channel_id=1, source_target_pairs={{0,1},{1,0},{2,3},{3,2},{4,5},{5,4},{6,7},{7,6},{8,9},{9,8},{10,11... | collective-permute-start | bytes 4718600 | tf_op jit(solution)/shard_map/ppermute | solution.py:14
  803.4 39.6 %collective-permute-start.37 = (bf16[1,4,128,512]{3,2,1,0:T(8,128)(2,1)}, bf16[1,4,128,512]{3,2,1,0:T(8,128)(2,1)}, u32[]{:S(2)}, u32[]{:S(2)}) collective-permute-start(bf16[1,4,128,512]{3,2,1,0:T(8,128)(2,1)} %fusion.120), channel_id=1, source_target_pairs={{0,1},{1,0},{2,3},{3,2},{4,5},{5,4},{6,7},{7,6},{8,9},{9,8},{10,11... | collective-permute-start | bytes 1572872 | tf_op jit(solution)/shard_map/ppermute | solution.py:14
  834.8 48.2 %collective-permute-start.32 = (bf16[3,2,128,512]{3,2,1,0:T(8,128)(2,1)S(1)}, bf16[3,2,128,512]{3,2,1,0:T(8,128)(2,1)S(1)}, u32[]{:S(2)}, u32[]{:S(2)}) collective-permute-start(bf16[3,2,128,512]{3,2,1,0:T(8,128)(2,1)S(1)} %slice.492), channel_id=1, source_target_pairs={{0,4},{1,5},{2,6},{3,7},{4,0},{5,1},{6,2},{7,3},{8,12},{9,13},{10,... | collective-permute-start | bytes 2359304 | tf_op jit(solution)/shard_map/ppermute | solution.py:14
  844.2 38.1 %collective-permute-start.38 = (bf16[1,2,128,512]{3,2,1,0:T(8,128)(2,1)S(1)}, bf16[1,2,128,512]{3,2,1,0:T(8,128)(2,1)S(1)}, u32[]{:S(2)}, u32[]{:S(2)}) collective-permute-start(bf16[1,2,128,512]{3,2,1,0:T(8,128)(2,1)S(1)} %slice.500), channel_id=1, source_target_pairs={{0,4},{1,5},{2,6},{3,7},{4,0},{5,1},{6,2},{7,3},{8,12},{9,13},{10,... | collective-permute-start | bytes 786440 | tf_op jit(solution)/shard_map/ppermute | solution.py:14
  882.4 4.6 collective-permute-start.39
  883.3 12.2 %collective-permute-start.33 = (bf16[3,1,128,512]{3,2,1,0:T(8,128)(2,1)S(1)}, bf16[3,1,128,512]{3,2,1,0:T(8,128)(2,1)S(1)}, u32[]{:S(2)}, u32[]{:S(2)}) collective-permute-start(bf16[3,1,128,512]{3,2,1,0:T(8,128)(2,1)S(1)} %slice.499), channel_id=1, source_target_pairs={{0,2},{1,3},{2,0},{3,1},{4,6},{5,7},{6,4},{7,5},{8,10},{9,11},{10,... | collective-permute-start | bytes 1179656 | tf_op jit(solution)/shard_map/ppermute | solution.py:14
  887.1 10.4 %collective-permute-start.40 = (bf16[1,128,512]{2,1,0:T(8,128)(2,1)S(1)}, bf16[1,128,512]{2,1,0:T(8,128)(2,1)S(1)}, u32[]{:S(2)}, u32[]{:S(2)}) collective-permute-start(bf16[1,128,512]{2,1,0:T(8,128)(2,1)S(1)} %fusion.135), channel_id=1, source_target_pairs={{0,16},{8,24},{16,0},{24,8},{1,17},{9,25},{17,1},{25,9},{2,18},{10... | collective-permute-start | bytes 393224 | tf_op jit(solution)/shard_map/ppermute | solution.py:14
  895.6 9.3 collective-permute-start.34
  897.5 51.7 %collective-permute-start.41 = (bf16[1,128,512]{2,1,0:T(8,128)(2,1)S(1)}, bf16[1,128,512]{2,1,0:T(8,128)(2,1)S(1)}, u32[]{:S(2)}, u32[]{:S(2)}) collective-permute-start(bf16[1,128,512]{2,1,0:T(8,128)(2,1)S(1)} %get-tuple-element.23), channel_id=1, source_target_pairs={{0,8},{8,0},{16,24},{24,16},{1,9},{9,1},{17,25},{25,17},{2,10},{10... | collective-permute-start | bytes 393224 | tf_op jit(solution)/shard_map/ppermute | solution.py:14
  905.2 47.0 %collective-permute-start.35 = (bf16[3,128,512]{2,1,0:T(8,128)(2,1)S(1)}, bf16[3,128,512]{2,1,0:T(8,128)(2,1)S(1)}, u32[]{:S(2)}, u32[]{:S(2)}) collective-permute-start(bf16[3,128,512]{2,1,0:T(8,128)(2,1)S(1)} %get-tuple-element.25), channel_id=1, source_target_pairs={{0,8},{8,0},{16,24},{24,16},{1,9},{9,1},{17,25},{25,17},{2,10},{10... | collective-permute-start | bytes 1179656 | tf_op jit(solution)/shard_map/ppermute | solution.py:14
  (94 other events, 847.6 us)

commit v2 on v1

--- a/solution.py
+++ b/solution.py
@@ -1,6 +1,10 @@
+import functools
+
 import jax
 import jax.numpy as jnp
 from jax import lax
+from jax.experimental import pallas as pl
+from jax.experimental.pallas import tpu as pltpu
 from jax.sharding import PartitionSpec as P
 
 HEADS = 16
@@ -57,6 +61,594 @@
     return (
         centred_grad - unit_rows * jnp.mean(grad_unit * unit_rows, axis=-1, keepdims=True)
     ) * inv_scale
+
+
+MESH = pl.DeviceIdType.MESH
+TILE = 256
+ROWS = 64
+
+
+def remote(src, dst, send_sem, recv_sem, device):
+    return pltpu.make_async_remote_copy(
+        src_ref=src,
+        dst_ref=dst,
+        send_sem=send_sem,
+        recv_sem=recv_sem,
+        device_id=device,
+        device_id_type=MESH,
+    )
+
+
+def expert_kernel(
+    exp_size,
+    rep_size,
+    slots,
+    packed,
+    compact,
+    spread_m,
+    own_in,
+    in_one,
+    in_two,
+    in_three,
+    own_out,
+    out_two,
+    gain,
+    cent,
+    cent_wide,
+    home,
+    outer_keep,
+    outer_send,
+    inner_keep,
+    inner_send,
+    gain_grad,
+    centre_grad,
+    arrived,
+    inner_w,
+    outer_w,
+    own_x,
+    own_cot,
+    normed,
+    active,
+    slope,
+    states,
+    fwd_send,
+    fwd_recv,
+    bwd_send,
+    bwd_recv,
+    hop,
+    back,
+    spread,
+    acc,
+    gates,
+    gate_grads,
+    outer_keep_v,
+    outer_send_v,
+    inner_keep_v,
+    inner_send_v,
+    disp_s,
+    disp_r,
+    load_sem,
+    norm_s,
+    norm_r,
+    state_s,
+    state_r,
+    fwd_s,
+    fwd_r,
+    bwd_s,
+    bwd_r,
+    hop_s,
+    hop_r,
+    gate_s,
+    gate_r,
+    ret_s,
+    ret_r,
+    out_sem,
+):
+    low = jnp.bfloat16
+    wide = jnp.float32
+    rep_at = lax.axis_index("rep")
+    exp_at = lax.axis_index("exp")
+    first = exp_at % 2 == 0
+    second = exp_at % 2 == 1
+    core_peer = (rep_at ^ 1, exp_at)
+    side_peer = (rep_at, exp_at ^ 1)
+    width = own_x.shape[1]
+    own_rows = own_x.shape[0]
+    part = own_rows // CHUNKS
+    wide_ff = inner_w.shape[1]
+    block = wide_ff // 2
+    depth = width // rep_size
+
+    def slot_rows(at):
+        return pl.ds(pl.multiple_of(at * slots, slots), slots)
+
+    def inner_rows(mask):
+        return pl.ds(pl.multiple_of((rep_at ^ mask) * depth, depth), depth)
+
+    def own_cols(mask):
+        return pl.ds(pl.multiple_of((rep_at ^ mask) * block, block), block)
+
+    loads = [
+        pltpu.make_async_copy(
+            own_in.at[:, own_cols(0)], inner_w.at[inner_rows(0), :block], load_sem.at[0]
+        ),
+        pltpu.make_async_copy(
+            own_in.at[:, own_cols(2)], inner_w.at[inner_rows(0), block:], load_sem.at[1]
+        ),
+        pltpu.make_async_copy(in_one, inner_w.at[inner_rows(1)], load_sem.at[2]),
+        pltpu.make_async_copy(in_two, inner_w.at[inner_rows(2)], load_sem.at[3]),
+        pltpu.make_async_copy(in_three, inner_w.at[inner_rows(3)], load_sem.at[4]),
+        pltpu.make_async_copy(own_out, outer_w.at[:block], load_sem.at[5]),
+        pltpu.make_async_copy(out_two, outer_w.at[block:], load_sem.at[6]),
+    ]
+    for load in loads:
+        load.start()
+
+    barrier = pltpu.get_barrier_semaphore()
+    pl.semaphore_signal(barrier, inc=1, device_id=core_peer, device_id_type=MESH)
+
+    @pl.loop(1, exp_size)
+    def _(at):
+        pl.semaphore_signal(barrier, inc=1, device_id=(rep_at, exp_at ^ at), device_id_type=MESH)
+
+    pl.semaphore_wait(barrier, exp_size)
+
+    def disp_copy(dest):
+        return remote(
+            packed.at[slot_rows(dest)],
+            arrived.at[slot_rows(exp_at)],
+            disp_s.at[dest],
+            disp_r.at[exp_at],
+            (rep_at, dest),
+        )
+
+    own_copy = pltpu.make_async_copy(
+        packed.at[slot_rows(exp_at)], arrived.at[slot_rows(exp_at)], disp_s.at[exp_at]
+    )
+    own_copy.start()
+    for side in range(2):
+
+        @pl.loop(0, exp_size // 2)
+        def _(at):
+            dest = 2 * ((exp_at // 2) ^ at) + side
+
+            @pl.when(dest != exp_at)
+            def _():
+                disp_copy(dest).start()
+
+    own_copy.wait()
+
+    @pl.loop(1, exp_size)
+    def _(at):
+        source = exp_at ^ at
+        remote(
+            packed.at[slot_rows(source)],
+            arrived.at[slot_rows(source)],
+            disp_s.at[source],
+            disp_r.at[source],
+            (rep_at, source),
+        ).wait()
+
+    for at in range(width // TILE):
+        cols = slice(at * TILE, (at + 1) * TILE)
+        rows_low = jnp.dot(
+            compact[...], arrived[:, cols], preferred_element_type=wide
+        ).astype(low)
+
+        @pl.when(first)
+        def _():
+            own_x[:, cols] = rows_low
+
+        @pl.when(second)
+        def _():
+            own_cot[:, cols] = rows_low
+
+    gate_copy = remote(gates, gates, gate_s.at[0], gate_r.at[0], side_peer)
+    grad_copy = remote(gate_grads, gate_grads, gate_s.at[1], gate_r.at[1], side_peer)
+
+    @pl.when(first)
+    def _():
+        logit = jnp.dot(own_x[...], cent_wide[...], preferred_element_type=wide)
+        gates[...] = jax.nn.sigmoid(logit)
+        gate_copy.start()
+
+    def stats(rows):
+        row_mean = jnp.mean(rows, axis=-1, keepdims=True)
+        centered = rows - row_mean
+        variance = jnp.mean(centered * centered, axis=-1, keepdims=True)
+        inv_scale = lax.rsqrt(variance + EPS)
+        return centered * inv_scale, inv_scale
+
+    def hop_forward(at):
+        rows = pl.ds(at * part, part)
+        return remote(hop.at[rows], own_x.at[rows], hop_s.at[at], hop_r.at[at], side_peer)
+
+    def own_slice(at):
+        return pl.ds(at * 2 * part + part, part)
+
+    def other_slice(at):
+        return pl.ds(at * 2 * part, part)
+
+    def hop_backward(at):
+        rows = pl.ds(at * part, part)
+        return remote(
+            hop.at[rows], states.at[own_slice(at)], hop_s.at[at], hop_r.at[at], side_peer
+        )
+
+    for load in loads:
+        load.wait()
+
+    def forward(at):
+        base = at * part
+
+        @pl.when(second)
+        def _():
+            hop_forward(at).wait_recv()
+
+        @pl.loop(0, part // ROWS)
+        def _(step):
+            off = pl.multiple_of(step * ROWS, ROWS)
+            unit, _ = stats(own_x[pl.ds(base + off, ROWS), :].astype(wide))
+            normed[pl.ds(at * 2 * part + part + off, ROWS), :] = (unit * gain[...]).astype(low)
+
+        norm_copy = remote(
+            normed.at[own_slice(at)], normed.at[other_slice(at)], norm_s.at[at], norm_r.at[at], core_peer
+        )
+        norm_copy.start()
+        norm_copy.wait_recv()
+
+        @pl.loop(0, wide_ff // TILE)
+        def _(step):
+            cols = pl.ds(pl.multiple_of(step * TILE, TILE), TILE)
+            inner = jnp.dot(
+                normed[pl.ds(at * 2 * part, 2 * part), :],
+                inner_w[:, cols],
+                preferred_element_type=wide,
+            )
+            normal = 0.5 * (1.0 + lax.erf(inner * ROOT_HALF))
+            active[pl.ds(at * 2 * part, 2 * part), cols] = (inner * normal).astype(low)
+            slope[pl.ds(at * 2 * part, 2 * part), cols] = (
+                normal + inner * jnp.exp(-0.5 * inner * inner) * INV_ROOT_TAU
+            ).astype(low)
+
+        @pl.loop(0, width // TILE)
+        def _(step):
+            cols = pl.ds(pl.multiple_of(step * TILE, TILE), TILE)
+            fwd_send[pl.ds(base, part), cols] = jnp.dot(
+                active[other_slice(at), :], outer_w[:, cols], preferred_element_type=wide
+            ).astype(low)
+
+        rows = pl.ds(base, part)
+        copy = remote(fwd_send.at[rows], fwd_recv.at[rows], fwd_s.at[at], fwd_r.at[at], core_peer)
+        copy.start()
+
+        @pl.loop(0, width // TILE)
+        def _(step):
+            cols = pl.ds(pl.multiple_of(step * TILE, TILE), TILE)
+            acc[:, cols] = jnp.dot(
+                active[own_slice(at), :], outer_w[:, cols], preferred_element_type=wide
+            )
+
+        copy.wait_recv()
+
+        @pl.when(first)
+        def _():
+            @pl.loop(0, part // ROWS)
+            def _(step):
+                off = pl.multiple_of(step * ROWS, ROWS)
+                here = pl.ds(base + off, ROWS)
+                result = (
+                    own_x[here, :].astype(wide)
+                    + acc[pl.ds(off, ROWS), :]
+                    + fwd_recv[here, :].astype(wide)
+                )
+                hop[here, :] = result.astype(low)
+
+            hop_forward(at).start()
+
+        @pl.when(second)
+        def _():
+            if at == 0:
+                gate_copy.wait_recv()
+
+            @pl.loop(0, part // ROWS)
+            def _(step):
+                off = pl.multiple_of(step * ROWS, ROWS)
+                here = pl.ds(base + off, ROWS)
+                result = (
+                    own_x[here, :].astype(wide)
+                    + acc[pl.ds(off, ROWS), :]
+                    + fwd_recv[here, :].astype(wide)
+                )
+                cot = own_cot[here, :].astype(wide)
+                gate = gates[here, :][:, :1]
+                back[here, :] = (gate * result).astype(low)
+                gate_grads[here, :] = jnp.broadcast_to(
+                    jnp.sum(cot * result, axis=1, keepdims=True), (ROWS, gate_grads.shape[1])
+                )
+                states[pl.ds(at * 2 * part + part + off, ROWS), :] = (gate * cot).astype(low)
+
+    for at in range(CHUNKS):
+        forward(at)
+
+    def ret_copy(dest):
+        return remote(
+            spread.at[slot_rows(dest)],
+            home.at[slot_rows(exp_at)],
+            ret_s.at[dest],
+            ret_r.at[exp_at],
+            (rep_at, dest),
+        )
+
+    ret_own = pltpu.make_async_copy(
+        spread.at[slot_rows(exp_at)], home.at[slot_rows(exp_at)], ret_s.at[exp_at]
+    )
+
+    def send_back():
+        @pl.loop(0, width // TILE)
+        def _(step):
+            cols = pl.ds(pl.multiple_of(step * TILE, TILE), TILE)
+            spread[:, cols] = jnp.dot(
+                spread_m[...], back[:, cols], preferred_element_type=wide
+            ).astype(low)
+
+        @pl.loop(1, exp_size)
+        def _(step):
+            ret_copy(exp_at ^ step).start()
+
+        ret_own.start()
+
+    @pl.when(second)
+    def _():
+        grad_copy.start()
+        send_back()
+
+    gain_grad[...] = jnp.zeros_like(gain_grad)
+    centre_grad[...] = jnp.zeros_like(centre_grad)
+
+    def backward(at):
+        base = at * part
+
+        @pl.when(first)
+        def _():
+            hop_backward(at).wait_recv()
+
+        copy = remote(
+            states.at[own_slice(at)], states.at[other_slice(at)], state_s.at[at], state_r.at[at], core_peer
+        )
+        copy.start()
+        copy.wait_recv()
+
+        @pl.loop(0, wide_ff // TILE)
+        def _(step):
+            rows = pl.ds(pl.multiple_of(step * TILE, TILE), TILE)
+            grad_active = lax.dot_general(
+                states[pl.ds(at * 2 * part, 2 * part), :],
+                outer_w[rows, :],
+                (((1,), (1,)), ((), ())),
+                preferred_element_type=wide,
+            )
+            here = pl.ds(at * 2 * part, 2 * part)
+            slope[here, rows] = (grad_active * slope[here, rows].astype(wide)).astype(low)
+
+        @pl.loop(0, width // TILE)
+        def _(step):
+            cols = pl.ds(pl.multiple_of(step * TILE, TILE), TILE)
+            bwd_send[pl.ds(base, part), cols] = lax.dot_general(
+                slope[other_slice(at), :],
+                inner_w[cols, :],
+                (((1,), (1,)), ((), ())),
+                preferred_element_type=wide,
+            ).astype(low)
+
+        rows = pl.ds(base, part)
+        back_copy = remote(
+            bwd_send.at[rows], bwd_recv.at[rows], bwd_s.at[at], bwd_r.at[at], core_peer
+        )
+        back_copy.start()
+
+        @pl.loop(0, width // TILE)
+        def _(step):
+            cols = pl.ds(pl.multiple_of(step * TILE, TILE), TILE)
+            acc[:, cols] = lax.dot_general(
+                slope[own_slice(at), :],
+                inner_w[cols, :],
+                (((1,), (1,)), ((), ())),
+                preferred_element_type=wide,
+            )
+
+        back_copy.wait_recv()
+        if at == 0:
+
+            @pl.when(first)
+            def _():
+                grad_copy.wait_recv()
+
+        @pl.when(first)
+        def _():
+            hop_forward(at).wait_send()
+
+        @pl.loop(0, part // ROWS)
+        def _(step):
+            off = pl.multiple_of(step * ROWS, ROWS)
+            here = pl.ds(base + off, ROWS)
+            rows_in = own_x[here, :].astype(wide)
+            unit, inv_scale = stats(rows_in)
+            grad_normed = acc[pl.ds(off, ROWS), :] + bwd_recv[here, :].astype(wide)
+            gain_grad[...] += jnp.sum(grad_normed * unit, axis=0, keepdims=True)
+            grad_unit = grad_normed * gain[...]
+            grad_in = (
+                grad_unit
+                - jnp.mean(grad_unit, axis=-1, keepdims=True)
+                - unit * jnp.mean(grad_unit * unit, axis=-1, keepdims=True)
+            ) * inv_scale
+            gate = gates[here, :][:, :1]
+
+            @pl.when(second)
+            def _():
+                state = gate * own_cot[here, :].astype(wide) + grad_in
+                hop[here, :] = state.astype(low)
+
+            @pl.when(first)
+            def _():
+                state = states[pl.ds(at * 2 * part + part + off, ROWS), :].astype(wide) + grad_in
+                grad_logit = gate_grads[here, :][:, :1] * gate * (1.0 - gate)
+                back[here, :] = (state + grad_logit * cent[...]).astype(low)
+                centre_grad[...] += jnp.sum(grad_logit * rows_in, axis=0, keepdims=True)
+
+        @pl.when(second)
+        def _():
+            hop_backward(at).start()
+
+    for at in range(CHUNKS):
+        backward(at)
+
+    @pl.when(first)
+    def _():
+        send_back()
+
+    outs = []
+    for at in range(2 * block // TILE):
+        rows = slice(at * TILE, (at + 1) * TILE)
+        grad = lax.dot_general(
+            active[:, rows], states[...], (((0,), (0,)), ((), ())), preferred_element_type=wide
+        )
+        if (at + 1) * TILE <= block:
+            outer_keep_v[rows, :] = grad
+            outs.append((outer_keep_v.at[rows], outer_keep.at[rows]))
+        else:
+            rows = slice(at * TILE - block, (at + 1) * TILE - block)
+            outer_send_v[rows, :] = grad.astype(low)
+            outs.append((outer_send_v.at[rows], outer_send.at[rows]))
+        pltpu.make_async_copy(outs[-1][0], outs[-1][1], out_sem.at[len(outs) - 1]).start()
+    for mask in range(rep_size):
+        for side in range(2):
+            cols = slice(side * block, (side + 1) * block)
+            grad = lax.dot_general(
+                normed[:, inner_rows(mask)],
+                slope[:, cols],
+                (((0,), (0,)), ((), ())),
+                preferred_element_type=wide,
+            )
+            if mask == 0:
+                inner_keep_v[:, cols] = grad
+                outs.append((inner_keep_v.at[:, cols], inner_keep.at[:, cols]))
+            else:
+                rows = slice((mask - 1) * depth, mask * depth)
+                inner_send_v[rows, cols] = grad.astype(low)
+                outs.append((inner_send_v.at[rows, cols], inner_send.at[mask - 1, :, cols]))
+            pltpu.make_async_copy(outs[-1][0], outs[-1][1], out_sem.at[len(outs) - 1]).start()
+
+    for at, (source, target) in enumerate(outs):
+        pltpu.make_async_copy(source, target, out_sem.at[at]).wait()
+    for at in range(CHUNKS):
+        rows = pl.ds(at * part, part)
+        remote(
+            normed.at[own_slice(at)], normed.at[other_slice(at)], norm_s.at[at], norm_r.at[at], core_peer
+        ).wait_send()
+        remote(
+            states.at[own_slice(at)], states.at[other_slice(at)], state_s.at[at], state_r.at[at], core_peer
+        ).wait_send()
+        remote(
+            fwd_send.at[rows], fwd_recv.at[rows], fwd_s.at[at], fwd_r.at[at], core_peer
+        ).wait_send()
+        remote(
+            bwd_send.at[rows], bwd_recv.at[rows], bwd_s.at[at], bwd_r.at[at], core_peer
+        ).wait_send()
+
+        @pl.when(second)
+        def _():
+            hop_backward(at).wait_send()
+
+    @pl.when(first)
+    def _():
+        gate_copy.wait_send()
+
+    @pl.when(second)
+    def _():
+        grad_copy.wait_send()
+
+    ret_own.wait()
+
+    @pl.loop(1, exp_size)
+    def _(step):
+        source = exp_at ^ step
+        remote(
+            spread.at[slot_rows(source)],
+            home.at[slot_rows(source)],
+            ret_s.at[source],
+            ret_r.at[source],
+            (rep_at, source),
+        ).wait()
+
+
+def run_experts(exp_size, rep_size, slots, packed, compact, spread_m, weights, gain, cent, cent_wide):
+    width = packed.shape[1]
+    own_rows = compact.shape[0]
+    depth = width // rep_size
+    block = weights[0].shape[1] // rep_size
+    low = jnp.bfloat16
+    wide = jnp.float32
+    total = exp_size * slots
+    all_rows = 2 * own_rows
+    part = own_rows // CHUNKS
+    anyplace = pl.BlockSpec(memory_space=pl.ANY)
+    inside = pl.BlockSpec(memory_space=pltpu.VMEM)
+    dma = pltpu.SemaphoreType.DMA
+    n_out = 2 * block // TILE + 2 * rep_size
+    scratch = [
+        pltpu.VMEM((total, width), low),
+        pltpu.VMEM((width, 2 * block), low),
+        pltpu.VMEM((2 * block, width), low),
+        pltpu.VMEM((own_rows, width), low),
+        pltpu.VMEM((own_rows, width), low),
+        pltpu.VMEM((all_rows, width), low),
+        pltpu.VMEM((all_rows, 2 * block), low),
+        pltpu.VMEM((all_rows, 2 * block), low),
+        pltpu.VMEM((all_rows, width), low),
+        pltpu.VMEM((own_rows, width), low),
+        pltpu.VMEM((own_rows, width), low),
+        pltpu.VMEM((own_rows, width), low),
+        pltpu.VMEM((own_rows, width), low),
+        pltpu.VMEM((own_rows, width), low),
+        pltpu.VMEM((own_rows, width), low),
+        pltpu.VMEM((total, width), low),
+        pltpu.VMEM((part, width), wide),
+        pltpu.VMEM((own_rows, 128), wide),
+        pltpu.VMEM((own_rows, 128), wide),
+        pltpu.VMEM((block, width), wide),
+        pltpu.VMEM((block, width), low),
+        pltpu.VMEM((depth, 2 * block), wide),
+        pltpu.VMEM(((rep_size - 1) * depth, 2 * block), low),
+        dma((exp_size,)),
+        dma((exp_size,)),
+        dma((7,)),
+    ]
+    scratch += [dma((CHUNKS,)) for _ in range(10)]
+    scratch += [dma((2,)), dma((2,)), dma((exp_size,)), dma((exp_size,)), dma((n_out,))]
+    flops = 2 * all_rows * width * 2 * block * 6
+    return pl.pallas_call(
+        functools.partial(expert_kernel, exp_size, rep_size, slots),
+        out_shape=(
+            jax.ShapeDtypeStruct((total, width), low),
+            jax.ShapeDtypeStruct((block, width), wide),
+            jax.ShapeDtypeStruct((block, width), low),
+            jax.ShapeDtypeStruct((depth, 2 * block), wide),
+            jax.ShapeDtypeStruct((rep_size - 1, depth, 2 * block), low),
+            jax.ShapeDtypeStruct((1, width), wide),
+            jax.ShapeDtypeStruct((1, width), wide),
+        ),
+        in_specs=[anyplace, inside, inside] + [anyplace] * 6 + [inside] * 3,
+        out_specs=(anyplace,) * 5 + (inside, inside),
+        scratch_shapes=scratch,
+        compiler_params=pltpu.CompilerParams(
+            collective_id=0, has_side_effects=True, vmem_limit_bytes=62 << 20
+        ),
+        cost_estimate=pl.CostEstimate(
+            flops=flops, bytes_accessed=40 << 20, transcendentals=2 * all_rows * 2 * block
+        ),
+        name="experts",
+    )(packed, compact, spread_m, *weights, gain, cent, cent_wide)
 
 
 def gather_weights(stack, core, exp_bits):
@@ -146,10 +738,9 @@
             axis=1,
         )
 
-    inner_w = jnp.concatenate(
-        [inner_for(0)] + [swap(inner_for(mask), "rep", mask) for mask in range(1, rep_size)], axis=0
-    )
-    outer_w = jnp.concatenate([w_outer[0], swap(w_outer[0], "rep", 2)], axis=0)
+    weights = [inner_own]
+    weights += [swap(inner_for(mask), "rep", mask) for mask in range(1, rep_size)]
+    weights += [w_outer[0], swap(w_outer[0], "rep", 2)]
 
     expert_ids = jnp.arange(experts, dtype=jnp.int32)
     onehot = expert_of_token[:, None] == expert_ids[None, :]
@@ -193,7 +784,7 @@
     context_x = xor_order(xor_order(context, 1, core, 2), 1, exp_at, exp_size)
     hidden = inputs + xor_order(plain_product(context_x, out_w), 1, core, 2)
 
-    slots = 3 * row_count // exp_size
+    slots = -(-3 * row_count // exp_size // 16) * 16
     lower = (positions[:, None] > positions[None, :]).astype(low)
     earlier = plain_product(lower, onehot.astype(low))
     rank_in = jnp.sum(jnp.where(onehot, earlier, 0.0), axis=1).astype(jnp.int32)
@@ -204,8 +795,6 @@
     packed_sent = plain_product(pick, sent_rows).astype(low).reshape(experts, 1, slots, width)
     packed_cot = plain_product(pick, cotangent).astype(low).reshape(experts, 1, slots, width)
     packed = jnp.concatenate([packed_sent, packed_cot], axis=1).reshape(exp_size, slots, width)
-    arrived = lax.all_to_all(packed, "exp", split_axis=0, concat_axis=0, tiled=True)
-    arrived = arrived.reshape(exp_size * slots, width)
     starts = jnp.cumsum(group_counts) - group_counts
     slot_at = jnp.arange(slots, dtype=jnp.int32)
     row_of_slot = jnp.where(
@@ -213,126 +802,33 @@
     ).reshape(-1)
     own_rows = 2 * row_count
     compact = (jnp.arange(own_rows, dtype=jnp.int32)[:, None] == row_of_slot[None, :]).astype(low)
-    rows_own = plain_product(compact, arrived).astype(low)
-
-    part = own_rows // CHUNKS
-
-    def chunk_of(array, at):
-        return array[at * part : (at + 1) * part]
-
-    own_f = rows_own.astype(wide)
-    gates = swap(jax.nn.sigmoid(plain_product(rows_own, centroid[:, None])[:, 0]), "exp", 1)
-    gates_zero = jax.nn.sigmoid(plain_product(rows_own, centroid[:, None])[:, 0])
-    gates = jnp.where(first, gates_zero, gates)
-    kept = []
-    handed = None
-    finals = []
-    for at in range(CHUNKS + 1):
-        if at == 0:
-            own_in = chunk_of(rows_own, 0)
-        elif at == CHUNKS:
-            own_in = handed
-        else:
-            own_in = jnp.where(first, chunk_of(rows_own, at), handed)
-        other_in = swap(own_in, "rep", 1)
-        rows_in = jnp.concatenate([own_in, other_in], axis=0).astype(wide)
-        unit_rows, inv_scale = norm_stats(rows_in)
-        normed_low = xor_order((unit_rows * gain_row).astype(low), 1, rep_at, rep_size)
-        inner_pre = plain_product(normed_low, inner_w)
-        normal = 0.5 * (1.0 + lax.erf(inner_pre * ROOT_HALF))
-        active = (inner_pre * normal).astype(low)
-        slope = (
-            normal + inner_pre * jnp.exp(-0.5 * inner_pre * inner_pre) * INV_ROOT_TAU
-        ).astype(low)
-        product = plain_product(active, outer_w)
-        got = swap(product[part:].astype(low), "rep", 1)
-        result = rows_in[:part] + product[:part] + got.astype(wide)
-        kept.append((normed_low, active, slope, own_in))
-        finals.append(result)
-        if at < CHUNKS:
-            handed = swap(result.astype(low), "exp", 1)
-    final_rows = jnp.concatenate(finals[1:], axis=0)
-    grad_gate = jnp.sum(own_f * final_rows, axis=1)
-    branch = (gates[:, None] * final_rows).astype(low)
-    grad_gate = swap(grad_gate, "exp", 1)
-    grad_logit = grad_gate * gates * (1.0 - gates)
-
-    gain_grad = jnp.zeros((width,), wide)
-    states = []
-    inners = []
-    outs = []
-    handed = None
-    for at in range(CHUNKS + 1):
-
-        def kept_of(which):
-            if at == 0:
-                return kept[1][which]
-            if at == CHUNKS:
-                return kept[CHUNKS - 1][which]
-            return jnp.where(first, kept[at - 1][which], kept[at + 1][which])
-
-        if at < CHUNKS:
-            fresh = chunk_of(gates, at)[:, None] * chunk_of(own_f, at)
-        if at == 0:
-            state = fresh
-        elif at == CHUNKS:
-            state = handed.astype(wide)
-        else:
-            state = jnp.where(first, handed.astype(wide), fresh)
-        grad_own = state.astype(low)
-        grad_outer = jnp.concatenate([grad_own, swap(grad_own, "rep", 1)], axis=0)
-        grad_active = nt_product(grad_outer, outer_w)
-        grad_inner = (grad_active * kept_of(2).astype(wide)).astype(low)
-        grad_normed = nt_product(grad_inner, inner_w)
-        got = swap(grad_normed[part:].astype(low), "rep", 1)
-        got = xor_order(got, 1, 1, rep_size)
-        grad_normed = xor_order(grad_normed[:part] + got.astype(wide), 1, rep_at, rep_size)
-        unit_rows, inv_scale = norm_stats(kept_of(3).astype(wide))
-        share = jnp.sum(grad_normed * unit_rows, axis=0)
-        if at == 0:
-            share = jnp.where(first, 0.0, share)
-        elif at == CHUNKS:
-            share = jnp.where(first, share, 0.0)
-        gain_grad = gain_grad + share
-        grad_state = state + norm_back(grad_normed, unit_rows, inv_scale, gain_row)
-        states.append(grad_outer)
-        inners.append(grad_inner)
-        outs.append(grad_state)
-        if at < CHUNKS:
-            handed = swap(grad_state.astype(low), "exp", 1)
-    grad_wide = jnp.concatenate(outs[1:], axis=0)
-    grad_sent = (grad_wide + grad_logit[:, None] * centroid.astype(wide)[None, :]).astype(low)
-    back_rows = jnp.where(first, grad_sent, branch)
-    spread = tn_product(compact, back_rows).astype(low).reshape(exp_size, slots, width)
-    home = lax.all_to_all(spread, "exp", split_axis=0, concat_axis=0, tiled=True)
+    spread_m = (row_of_slot[:, None] == jnp.arange(own_rows, dtype=jnp.int32)[None, :]).astype(low)
+    cent_wide = jnp.broadcast_to(centroid[:, None], (width, 128))
+    home, outer_keep, outer_send, inner_keep, inner_send, gain_grad, grad_centre = run_experts(
+        exp_size,
+        rep_size,
+        slots,
+        packed.reshape(exp_size * slots, width),
+        compact,
+        spread_m,
+        weights,
+        gain_row[None],
+        centroid.astype(wide)[None],
+        cent_wide,
+    )
+    gain_grad = gain_grad[0]
+    grad_centre = grad_centre[0]
     home = home.reshape(experts, 2, slots, width)
     grad_home = tn_product(pick, home[:, 0].reshape(all_slots, width))
     branch_home = tn_product(pick, home[:, 1].reshape(all_slots, width))
     output = (hidden + branch_home).astype(low)
 
-    def both(items, of_first, of_second):
-        return jnp.concatenate(
-            [
-                jnp.where(first, items[of_first + k], items[of_second + k])
-                for k in range(CHUNKS)
-            ],
-            axis=0,
-        )
-
-    normed_all = both([k[0] for k in kept], 0, 1)
-    active_all = both([k[1] for k in kept], 0, 1)
-    state_all = both(states, 1, 0)
-    inner_all = both(inners, 1, 0)
-    grad_outer_w = tn_product(active_all, state_all)
-    grad_inner_w = tn_product(normed_all, inner_all)
-    outer_rows = w_outer.shape[1]
-    grad_w_outer = (
-        grad_outer_w[:outer_rows]
-        + swap(grad_outer_w[outer_rows:].astype(low), "rep", 2).astype(wide)
-    )[None]
-    shares = grad_inner_w.reshape(rep_size, width // rep_size, 2, block)
-    got = [swap(shares[mask].astype(low), "rep", mask).astype(wide) for mask in (1, 2, 3)]
-    mine = shares[0]
+    grad_w_outer = (outer_keep + swap(outer_send, "rep", 2).astype(wide))[None]
+    mine = inner_keep.reshape(width // rep_size, 2, block)
+    got = [
+        swap(inner_send[mask - 1], "rep", mask).astype(wide).reshape(mine.shape)
+        for mask in range(1, rep_size)
+    ]
     ordered = jnp.stack(
         [
             mine[:, 0] + got[1][:, 1],
@@ -344,7 +840,6 @@
     )
     grad_w_inner = xor_order(ordered.reshape(width // rep_size, -1), 1, rep_at, rep_size)[None]
 
-    grad_centre = jnp.dot(grad_logit, own_f, precision=lax.Precision.HIGHEST)
     other_centre = swap(grad_centre[half_width:], "exp", 1)
     centre_half = jnp.where(first, grad_centre[:half_width], other_centre)
 

time: 976 us -> 765 us (0.78)
  Pallas kernels: 0 us -> 185 us
  waiting for transfers between devices: 306 us -> 134 us
  local copies, waits for them, and re-layouts: 205 us -> 122 us
  matrix products: 115 us -> 40.1 us
  other arithmetic: 158 us -> 89.3 us
  blocking collectives: 123 us -> 157 us
  starting transfers between devices: 55.3 us -> 25.6 us
    pallas_call x0 -> x1, Pallas kernels: none -> 185 us  [run_experts(): pl.pallas_call(functools.partial(expert_kernel, exp_size, rep_size, slots...]
    ppermute x47 -> x29, waiting for transfers between devices: 281 us -> 134 us  [swap(): lax.ppermute(shard, axis, [(i, i ^ mask) for i in range(lax.axis_size(axi...]
    rev x9 -> x3, local copies, waits for them, and re-layouts: 78.1 us -> 30.9 us  [xor_order(): array = jnp.where(flag == 1, jnp.flip(array, axis + at), array)]
    dot_general x15 -> x7, matrix products: 49.8 us -> 9.95 us  [plain_product(): return jnp.dot(left_mat, right_mat, preferred_element_type=jnp.float32)]
    unnamed x1, blocking collectives: 38 us -> 76.9 us
    dot_general x10 -> x4, matrix products: 35.4 us -> 8.06 us  [nt_product(): lax.dot_general(left_mat, right_mat, (((1,), (1,)), ((), ())), preferred_...]
    convert_element_type x18 -> x2, other arithmetic: 29.1 us -> 2.22 us  [the longest x1 1.13 us: shards(): (jnp.arange(own_rows, dtype=jnp.int32)[:, None] == row_of_slot[None, :])....]
    all_to_all x2 -> x0, waiting for transfers between devices: 25.3 us -> none  [the longest x1 25.3 us: shards(): lax.all_to_all(packed, 'exp', split_axis=0, concat_axis=0, tiled=True)]
  transfers between devices with their start and end apart: 49 -> 29, of which waited for: 26 -> 8; matrix products, arithmetic and copies ran while one was open for 27% -> 23% of each run, Pallas kernels for 0% -> 0%
where the time goes in v2:
time: 765 us; the launch traced here: 755 us
  Pallas kernels  185 us (24%)
  blocking collectives  157 us (21%)
  waiting for transfers between devices  134 us (18%)
  local copies, waits for them, and re-layouts  122 us (16%)
  other arithmetic  89.3 us (12%)
  matrix products  40.1 us (5%)
  starting transfers between devices  25.6 us (3%)
    pallas_call x1, Pallas kernels, run_experts(): pl.pallas_call(functools.partial(expert_kernel, exp_size, rep_size, slots...  185 us
    ppermute x29, waiting for transfers between devices, swap(): lax.ppermute(shard, axis, [(i, i ^ mask) for i in range(lax.axis_size(axi...  134 us
    unnamed x1, blocking collectives  76.9 us
    psum x1, blocking collectives, shards(): attn_sums = lax.psum(grad_gain_a, ('rep', 'exp'))  54.4 us
    rev x3, local copies, waits for them, and re-layouts, xor_order(): array = jnp.where(flag == 1, jnp.flip(array, axis + at), array)  30.9 us
    ppermute x29, starting transfers between devices, swap(): lax.ppermute(shard, axis, [(i, i ^ mask) for i in range(lax.axis_size(axi...  25.6 us
    psum x1, blocking collectives, shards(): rep_sums = lax.psum(jnp.concatenate([gain_grad, centre_half]), 'rep')  25.3 us
    unnamed x123, local copies, waits for them, and re-layouts  22.4 us
  transfers between devices with their start and end apart: 29, of which 8 were waited for; matrix products, arithmetic and copies ran while one was open for 23% of the time, Pallas kernels for 0%

profile of v2, /device:TPU:11, one launch (start us, length us, event | category | flops | bytes accessed | tf_op | source)
XLA Modules:
  0.0 754.6 jit_solution(3034681479978696176)
XLA Ops:
  13.5 76.9 %all-reduce = bf16[16512]{0:T(1024)(128)(2,1)S(1)} all-reduce(bf16[16512]{0:T(1024)(128)(2,1)S(1)} %dynamic-update-slice), channel_id=2, replica_groups=mesh['rep'=4,'exp'=8] {'rep','exp'}, use_global_device_ids=true, to_apply=%add | all-reduce | flops 16512 | bytes 66048
  93.8 33.5 %collective-permute-done.1 = bf16[3,2,128,512]{3,2,0,1:T(8,128)(2,1)S(1)} collective-permute-done((bf16[3,2,128,512]{3,2,0,1:T(8,128)(2,1)S(1)}, bf16[3,2,128,512]{3,2,0,1:T(8,128)(2,1)S(1)}, u32[]{:S(2)}, u32[]{:S(2)}) %collective-permute-start.1) | collective-permute-done | bytes 786464 | tf_op jit(solution)/shard_map/ppermute | solution.py:18
  129.3 33.8 %collective-permute-done.2 = bf16[3,4,128,512]{3,2,1,0:T(8,128)(2,1)S(1)} collective-permute-done((bf16[3,4,128,512]{3,2,1,0:T(8,128)(2,1)S(1)}, bf16[3,4,128,512]{3,2,1,0:T(8,128)(2,1)S(1)}, u32[]{:S(2)}, u32[]{:S(2)}) %collective-permute-start.2) | collective-permute-done | bytes 1572896 | tf_op jit(solution)/shard_map/ppermute | solution.py:18
  167.4 3.1 collective-permute-start.5
  171.7 10.4 %collective-permute-done.5 = bf16[1,2,128,512]{3,2,1,0:T(8,128)(2,1)} collective-permute-done((bf16[1,2,128,512]{3,2,1,0:T(8,128)(2,1)}, bf16[1,2,128,512]{3,2,1,0:T(8,128)(2,1)}, u32[]{:S(2)}, u32[]{:S(2)}) %collective-permute-start.5) | collective-permute-done | bytes 262176 | tf_op jit(solution)/shard_map/ppermute | solution.py:18
  184.9 2.1 fusion.28
  187.1 9.1 %collective-permute-done.6 = bf16[1,4,128,512]{3,2,1,0:T(8,128)(2,1)S(1)} collective-permute-done((bf16[1,4,128,512]{3,2,1,0:T(8,128)(2,1)S(1)}, bf16[1,4,128,512]{3,2,1,0:T(8,128)(2,1)S(1)}, u32[]{:S(2)}, u32[]{:S(2)}) %collective-permute-start.6) | collective-permute-done | bytes 524320 | tf_op jit(solution)/shard_map/ppermute | solution.py:18
  206.2 3.1 fusion.14
  209.4 4.1 copy.195
  217.9 2.0 copy.183
  220.0 2.9 convolution_convert_fusion.5
  222.9 2.0 copy.184
  224.9 2.9 convolution_convert_fusion.4
  229.1 2.1 fusion
  240.9 11.6 %collective-permute-done.11.out_two = bf16[1024,1024]{1,0:T(8,128)(2,1)} collective-permute-done((bf16[1024,1024]{1,0:T(8,128)(2,1)}, bf16[1024,1024]{1,0:T(8,128)(2,1)}, u32[]{:S(2)}, u32[]{:S(2)}) %collective-permute-start.11) | collective-permute-done | bytes 2097184 | tf_op jit(solution)/shard_map/ppermute | solution.py:18
  253.4 184.6 %experts.1 = (bf16[768,1024]{1,0:T(8,128)(2,1)}, f32[1024,1024]{1,0:T(8,128)}, bf16[1024,1024]{1,0:T(8,128)(2,1)}, f32[256,2048]{1,0:T(8,128)}, bf16[3,256,2048]...) custom-call(bf16[768,1024]{1,0:T(8,128)(2,1)} %bitcast.288, bf16[512,768]{1,0:T(8,128)(2,1)} %fusion.11.compact, ...), custom_call_target="tpu_custom_call" | custom-call | flops 25769803776 | bytes 41943040 | tf_op jit(solution)/shard_map/experts/pallas_call | solution.py:630
  438.0 2.5 fusion.69
  444.5 3.3 fusion.15
  451.8 3.4 convolution_convert_fusion.2
  460.5 2.8 convolution_bitcast_fusion.1
  463.2 2.8 convolution_bitcast_fusion.2
  466.0 2.7 convolution_bitcast_fusion.3
  474.1 5.4 pad_maximum_fusion
  479.5 4.6 copy-done.4
  484.1 2.2 slice.323
  499.9 2.7 reshape.523
  502.6 54.4 %psum.14 = f32[1024]{0:T(1024)S(1)} all-reduce(f32[1024]{0:T(1024)S(1)} %get-tuple-element.25), channel_id=1, replica_groups=mesh['rep'=4,'exp'=8] {'rep','exp'}, use_global_device_ids=true, to_apply=%region_14.15 | all-reduce | flops 1024 | bytes 8192 | tf_op jit(solution)/shard_map/psum | solution.py:890
  558.7 25.3 %psum.15 = f32[1536]{0:T(1024)S(1)} all-reduce(f32[1536]{0:T(1024)S(1)} %pad_maximum_fusion.18), channel_id=1, replica_groups=mesh['rep'=4,'exp'=8] {'rep'}, use_global_device_ids=true, to_apply=%region_15.16 | all-reduce | flops 1536 | bytes 12288 | tf_op jit(solution)/shard_map/psum | solution.py:883
  586.3 5.1 slice_add_fusion
  593.5 2.2 slice_add_fusion.1
  598.3 4.3 reshape.539
  602.6 3.1 reshape.537
  605.7 4.3 reshape.535
  609.9 6.8 slice_add_fusion.5
  616.7 4.7 slice_add_fusion.6
  621.5 6.2 collective-permute-done.13
  632.3 6.6 collective-permute-done.19
  641.9 5.3 pad_maximum_fusion.1
  647.2 6.7 reshape_reshape.19
  653.9 22.7 %collective-permute-done.20 = bf16[1,2,128,512]{3,2,1,0:T(8,128)(2,1)S(1)} collective-permute-done((bf16[1,2,128,512]{3,2,1,0:T(8,128)(2,1)}, bf16[1,2,128,512]{3,2,1,0:T(8,128)(2,1)S(1)}, u32[]{:S(2)}, u32[]{:S(2)}) %collective-permute-start.20) | collective-permute-done | bytes 262176 | tf_op jit(solution)/shard_map/ppermute | solution.py:18
  682.7 4.2 reverse_select_fusion
  687.0 21.1 %rev.91 = f32[256,2,2,1024]{3,2,1,0:T(2,128)} reverse(f32[256,2,2,1024]{3,2,1,0:T(2,128)} %reverse_select_fusion), dimensions={2} | reverse | bytes 8388608 | tf_op jit(solution)/shard_map/jit(_flip)/rev | solution.py:46
  709.8 10.9 %broadcast_select_fusion = f32[256,2,2,1024]{3,2,1,0:T(2,128)} fusion(f32[256,2,2,1024]{3,2,1,0:T(2,128)} %rev.91, pred[]{:T(512)S(6)} %eq.146, f32[256,2,2,1024]{3,2,1,0:T(2,128)} %reshape_reshape.19, pred[]{:T(512)S(6)} %eq.147), kind=kLoop, calls=%fused_computation.15 | loop fusion | flops 2097152 | bytes 12582914 | tf_op jit(solution)/shard_map/jit(_where)/select_n | solution.py:46
  720.8 6.6 broadcast_in_dim_reshape.2
  727.4 2.2 collective-permute-start.23
  729.6 2.0 fusion.67
  731.7 5.9 add_bitcast_fusion
  742.4 8.1 %rev.88 = f32[3,128,2,512]{3,2,1,0:T(2,128)S(1)} reverse(f32[3,128,2,512]{3,2,1,0:T(2,128)S(1)} %reshape.520), dimensions={2} | reverse | bytes 3145728 | tf_op jit(solution)/shard_map/jit(_flip)/rev | solution.py:46
  (300 shorter events, 116.8 us)
Async XLA Ops:
  0.7 5.8 copy-start.23
  4.6 86.2 %collective-permute-start = (bf16[3,128,512]{2,1,0:T(8,128)(2,1)S(1)}, bf16[3,128,512]{2,1,0:T(8,128)(2,1)}, u32[]{:S(2)}, u32[]{:S(2)}) collective-permute-start(bf16[3,128,512]{2,1,0:T(8,128)(2,1)S(1)} %bitcast.290), channel_id=1, source_target_pairs={{0,2},{1,3},{2,0},{3,1},{4,6},{5,7},{6,4},{7,5},{8,10},{9,11},{10,... | collective-permute-start | bytes 1179656 | tf_op jit(solution)/shard_map/ppermute | solution.py:18
  5.1 159.9 %collective-permute-start.4 = (bf16[1,128,512]{2,1,0:T(8,128)(2,1)S(1)}, bf16[1,128,512]{2,1,0:T(8,128)(2,1)S(1)}, u32[]{:S(2)}, u32[]{:S(2)}) collective-permute-start(bf16[1,128,512]{2,1,0:T(8,128)(2,1)S(1)} %bitcast.303), channel_id=1, source_target_pairs={{0,2},{1,3},{2,0},{3,1},{4,6},{5,7},{6,4},{7,5},{8,10},{9,11},{10,... | collective-permute-start | bytes 393224 | tf_op jit(solution)/shard_map/ppermute | solution.py:18
  6.9 6.2 copy-start.50
  6.9 6.2 copy-start.49
  6.9 6.3 copy-start.51
  6.9 6.3 copy-start.52
  6.9 83.6 %copy-start.53 = (s32[1,4]{1,0:T(1,128)S(1)}, s32[1,4]{1,0:T(1,128)}, u32[]{:S(2)}) copy-start(s32[1,4]{1,0:T(1,128)} %param.15) | copy-start | bytes 52
  8.0 232.9 %collective-permute-start.8 = (bf16[256,2048]{1,0:T(8,128)(2,1)}, bf16[256,2048]{1,0:T(8,128)(2,1)}, u32[]{:S(2)}, u32[]{:S(2)}) collective-permute-start(bf16[256,2048]{1,0:T(8,128)(2,1)} %pad_maximum_fusion.10), channel_id=1, source_target_pairs={{0,8},{8,0},{16,24},{24,16},{1,9},{9,1},{17,25},{25,17},{2,10},{10... | collective-permute-start | bytes 3145736 | tf_op jit(solution)/shard_map/ppermute | solution.py:18
  10.3 230.6 %collective-permute-start.9 = (bf16[256,2048]{1,0:T(8,128)(2,1)}, bf16[256,2048]{1,0:T(8,128)(2,1)}, u32[]{:S(2)}, u32[]{:S(2)}) collective-permute-start(bf16[256,2048]{1,0:T(8,128)(2,1)} %pad_maximum_fusion.11), channel_id=1, source_target_pairs={{0,16},{8,24},{16,0},{24,8},{1,17},{9,25},{17,1},{25,9},{2,18},{10... | collective-permute-start | bytes 3145736 | tf_op jit(solution)/shard_map/ppermute | solution.py:18
  12.7 228.2 %collective-permute-start.10 = (bf16[256,2048]{1,0:T(8,128)(2,1)}, bf16[256,2048]{1,0:T(8,128)(2,1)}, u32[]{:S(2)}, u32[]{:S(2)}) collective-permute-start(bf16[256,2048]{1,0:T(8,128)(2,1)} %pad_maximum_fusion.12), channel_id=1, source_target_pairs={{0,24},{8,16},{16,8},{24,0},{1,25},{9,17},{17,9},{25,1},{2,26},{10... | collective-permute-start | bytes 3145736 | tf_op jit(solution)/shard_map/ppermute | solution.py:18
  91.8 35.5 %collective-permute-start.1 = (bf16[3,2,128,512]{3,2,0,1:T(8,128)(2,1)S(1)}, bf16[3,2,128,512]{3,2,0,1:T(8,128)(2,1)S(1)}, u32[]{:S(2)}, u32[]{:S(2)}) collective-permute-start(bf16[3,2,128,512]{3,2,0,1:T(8,128)(2,1)S(1)} %get-tuple-element.52), channel_id=1, source_target_pairs={{0,4},{1,5},{2,6},{3,7},{4,0},{5,1},{6,2},{7,3},{8,12},{9,13},{10,... | collective-permute-start | bytes 2359304 | tf_op jit(solution)/shard_map/ppermute | solution.py:18
  127.5 35.5 %collective-permute-start.2 = (bf16[3,4,128,512]{3,2,1,0:T(8,128)(2,1)S(1)}, bf16[3,4,128,512]{3,2,1,0:T(8,128)(2,1)S(1)}, u32[]{:S(2)}, u32[]{:S(2)}) collective-permute-start(bf16[3,4,128,512]{3,2,1,0:T(8,128)(2,1)S(1)} %copy.181), channel_id=1, source_target_pairs={{0,1},{1,0},{2,3},{3,2},{4,5},{5,4},{6,7},{7,6},{8,9},{9,8},{10,11... | collective-permute-start | bytes 4718600 | tf_op jit(solution)/shard_map/ppermute | solution.py:18
  163.4 61.6 %copy-start = (bf16[3,4,2,128,512]{4,3,2,1,0:T(8,128)(2,1)}, bf16[3,4,2,128,512]{4,3,2,1,0:T(8,128)(2,1)S(1)}, u32[]{:S(2)}) copy-start(bf16[3,4,2,128,512]{4,3,2,1,0:T(8,128)(2,1)S(1)} %pad_maximum_fusion.2) | copy-start | bytes 9437188
  163.4 50.1 %collective-permute-start.3 = (bf16[3,1024,512]{2,1,0:T(8,128)(2,1)S(1)}, bf16[3,1024,512]{2,1,0:T(8,128)(2,1)}, u32[]{:S(2)}, u32[]{:S(2)}) collective-permute-start(bf16[3,1024,512]{2,1,0:T(8,128)(2,1)S(1)} %bitcast.225), channel_id=1, source_target_pairs={{0,8},{8,0},{16,24},{24,16},{1,9},{9,1},{17,25},{25,17},{2,10},{10... | collective-permute-start | bytes 9437192 | tf_op jit(solution)/shard_map/ppermute | solution.py:18
  167.4 14.7 %collective-permute-start.5 = (bf16[1,2,128,512]{3,2,1,0:T(8,128)(2,1)}, bf16[1,2,128,512]{3,2,1,0:T(8,128)(2,1)}, u32[]{:S(2)}, u32[]{:S(2)}) collective-permute-start(bf16[1,2,128,512]{3,2,1,0:T(8,128)(2,1)} %get-tuple-element.54), channel_id=1, source_target_pairs={{0,4},{1,5},{2,6},{3,7},{4,0},{5,1},{6,2},{7,3},{8,12},{9,13},{10,... | collective-permute-start | bytes 786440 | tf_op jit(solution)/shard_map/ppermute | solution.py:18
  183.1 13.1 %collective-permute-start.6 = (bf16[1,4,128,512]{3,2,1,0:T(8,128)(2,1)S(1)}, bf16[1,4,128,512]{3,2,1,0:T(8,128)(2,1)S(1)}, u32[]{:S(2)}, u32[]{:S(2)}) collective-permute-start(bf16[1,4,128,512]{3,2,1,0:T(8,128)(2,1)S(1)} %bitcast.283), channel_id=1, source_target_pairs={{0,1},{1,0},{2,3},{3,2},{4,5},{5,4},{6,7},{7,6},{8,9},{9,8},{10,11... | collective-permute-start | bytes 1572872 | tf_op jit(solution)/shard_map/ppermute | solution.py:18
  197.4 7.6 %collective-permute-start.7 = (bf16[1,1024,512]{2,1,0:T(8,128)(2,1)}, bf16[1,1024,512]{2,1,0:T(8,128)(2,1)}, u32[]{:S(2)}, u32[]{:S(2)}) collective-permute-start(bf16[1,1024,512]{2,1,0:T(8,128)(2,1)} %bitcast.39), channel_id=1, source_target_pairs={{0,8},{8,0},{16,24},{24,16},{1,9},{9,1},{17,25},{25,17},{2,10},{10... | collective-permute-start | bytes 3145736 | tf_op jit(solution)/shard_map/ppermute | solution.py:18
  205.0 47.6 %collective-permute-start.11 = (bf16[1024,1024]{1,0:T(8,128)(2,1)}, bf16[1024,1024]{1,0:T(8,128)(2,1)}, u32[]{:S(2)}, u32[]{:S(2)}) collective-permute-start(bf16[1024,1024]{1,0:T(8,128)(2,1)} %bitcast.59.own_out), channel_id=1, source_target_pairs={{0,16},{8,24},{16,0},{24,8},{1,17},{9,25},{17,1},{25,9},{2,18},{10... | collective-permute-start | bytes 6291464 | tf_op jit(solution)/shard_map/ppermute | solution.py:18
  444.5 4.6 copy-start.39
  479.5 4.6 copy-start.4
  486.2 99.0 %collective-permute-start.12 = (bf16[3,1024,512]{2,1,0:T(8,128)(2,1)}, bf16[3,1024,512]{2,1,0:T(8,128)(2,1)}, u32[]{:S(2)}, u32[]{:S(2)}) collective-permute-start(bf16[3,1024,512]{2,1,0:T(8,128)(2,1)} %slice.323), channel_id=1, source_target_pairs={{0,8},{8,0},{16,24},{24,16},{1,9},{9,1},{17,25},{25,17},{2,10},{10... | collective-permute-start | bytes 9437192 | tf_op jit(solution)/shard_map/ppermute | solution.py:18
  493.0 100.1 %collective-permute-start.18 = (bf16[1,1024,512]{2,1,0:T(8,128)(2,1)}, bf16[1,1024,512]{2,1,0:T(8,128)(2,1)}, u32[]{:S(2)}, u32[]{:S(2)}) collective-permute-start(bf16[1,1024,512]{2,1,0:T(8,128)(2,1)} %slice.324), channel_id=1, source_target_pairs={{0,8},{8,0},{16,24},{24,16},{1,9},{9,1},{17,25},{25,17},{2,10},{10... | collective-permute-start | bytes 3145736 | tf_op jit(solution)/shard_map/ppermute | solution.py:18
  493.0 64.6 %collective-permute-start.28 = (f32[512]{0:T(512)S(1)}, f32[512]{0:T(512)S(1)}, u32[]{:S(2)}, u32[]{:S(2)}) collective-permute-start(f32[512]{0:T(512)S(1)} %bitcast.313), channel_id=1, source_target_pairs={{0,1},{1,0},{2,3},{3,2},{4,5},{5,4},{6,7},{7,6},{8,9},{9,8},{10,11... | collective-permute-start | bytes 6152 | tf_op jit(solution)/shard_map/ppermute | solution.py:18
  498.2 60.5 %copy-start.47 = (f32[1,1024]{1,0:T(1,128)S(1)}, f32[1,1024]{1,0:T(1,128)}, u32[]{:S(2)}) copy-start(f32[1,1024]{1,0:T(1,128)} %get-tuple-element.23) | copy-start | bytes 12292
  498.2 99.6 %collective-permute-start.26 = (bf16[256,2048]{1,0:T(8,128)(2,1)}, bf16[256,2048]{1,0:T(8,128)(2,1)}, u32[]{:S(2)}, u32[]{:S(2)}) collective-permute-start(bf16[256,2048]{1,0:T(8,128)(2,1)} %get-tuple-element.38), channel_id=1, source_target_pairs={{0,24},{8,16},{16,8},{24,0},{1,25},{9,17},{17,9},{25,1},{2,26},{10... | collective-permute-start | bytes 3145736 | tf_op jit(solution)/shard_map/ppermute | solution.py:18
  499.5 103.0 %collective-permute-start.25 = (bf16[256,2048]{1,0:T(8,128)(2,1)}, bf16[256,2048]{1,0:T(8,128)(2,1)S(1)}, u32[]{:S(2)}, u32[]{:S(2)}) collective-permute-start(bf16[256,2048]{1,0:T(8,128)(2,1)} %get-tuple-element.39), channel_id=1, source_target_pairs={{0,8},{8,0},{16,24},{24,16},{1,9},{9,1},{17,25},{25,17},{2,10},{10... | collective-permute-start | bytes 3145736 | tf_op jit(solution)/shard_map/ppermute | solution.py:18
  557.6 48.1 %collective-permute-start.24 = (bf16[256,2048]{1,0:T(8,128)(2,1)}, bf16[256,2048]{1,0:T(8,128)(2,1)}, u32[]{:S(2)}, u32[]{:S(2)}) collective-permute-start(bf16[256,2048]{1,0:T(8,128)(2,1)} %get-tuple-element.37), channel_id=1, source_target_pairs={{0,16},{8,24},{16,0},{24,8},{1,17},{9,25},{17,1},{25,9},{2,18},{10... | collective-permute-start | bytes 3145736 | tf_op jit(solution)/shard_map/ppermute | solution.py:18
  585.2 146.4 %collective-permute-start.27 = (bf16[1024,1024]{1,0:T(8,128)(2,1)}, bf16[1024,1024]{1,0:T(8,128)(2,1)}, u32[]{:S(2)}, u32[]{:S(2)}) collective-permute-start(bf16[1024,1024]{1,0:T(8,128)(2,1)} %get-tuple-element.22), channel_id=1, source_target_pairs={{0,16},{8,24},{16,0},{24,8},{1,17},{9,25},{17,1},{25,9},{2,18},{10... | collective-permute-start | bytes 6291464 | tf_op jit(solution)/shard_map/ppermute | solution.py:18
  586.3 7.1 copy-start.14
  593.1 34.6 %collective-permute-start.13 = (bf16[3,4,128,512]{3,2,1,0:T(8,128)(2,1)}, bf16[3,4,128,512]{3,2,1,0:T(8,128)(2,1)}, u32[]{:S(2)}, u32[]{:S(2)}) collective-permute-start(bf16[3,4,128,512]{3,2,1,0:T(8,128)(2,1)} %fusion.10), channel_id=1, source_target_pairs={{0,1},{1,0},{2,3},{3,2},{4,5},{5,4},{6,7},{7,6},{8,9},{9,8},{10,11... | collective-permute-start | bytes 4718600 | tf_op jit(solution)/shard_map/ppermute | solution.py:18
  597.9 41.1 %collective-permute-start.19 = (bf16[1,4,128,512]{3,2,1,0:T(8,128)(2,1)}, bf16[1,4,128,512]{3,2,1,0:T(8,128)(2,1)}, u32[]{:S(2)}, u32[]{:S(2)}) collective-permute-start(bf16[1,4,128,512]{3,2,1,0:T(8,128)(2,1)} %fusion.39), channel_id=1, source_target_pairs={{0,1},{1,0},{2,3},{3,2},{4,5},{5,4},{6,7},{7,6},{8,9},{9,8},{10,11... | collective-permute-start | bytes 1572872 | tf_op jit(solution)/shard_map/ppermute | solution.py:18
  605.7 22.1 %slice-start = ((s8[6291456]{0:T(1024)(128)(4,1)}), s8[2097152]{0:T(1024)(128)(4,1)S(1)}, s32[]{:S(2)}) async-start(s8[6291456]{0:T(1024)(128)(4,1)} %bitcast.232), calls=%async_computation | async-start | bytes 4194304
  609.9 6.8 copy-start.17
  609.9 17.8 %slice-start.1 = ((s8[6291456]{0:T(1024)(128)(4,1)}), s8[4194304]{0:T(1024)(128)(4,1)S(1)}, s32[]{:S(2)}) async-start(s8[6291456]{0:T(1024)(128)(4,1)} %bitcast.232), calls=%async_computation.1 | async-start | bytes 8388608
  621.5 17.5 %copy-start.22 = (f32[1,1024,512]{2,1,0:T(8,128)S(1)}, f32[1,1024,512]{2,1,0:T(8,128)}, u32[]{:S(2)}) copy-start(f32[1,1024,512]{2,1,0:T(8,128)} %copy-done.21) | copy-start | bytes 6291460
  632.3 47.0 %collective-permute-start.14 = (bf16[3,2,128,512]{3,2,1,0:T(8,128)(2,1)}, bf16[3,2,128,512]{3,2,1,0:T(8,128)(2,1)}, u32[]{:S(2)}, u32[]{:S(2)}) collective-permute-start(bf16[3,2,128,512]{3,2,1,0:T(8,128)(2,1)} %slice.325), channel_id=1, source_target_pairs={{0,4},{1,5},{2,6},{3,7},{4,0},{5,1},{6,2},{7,3},{8,12},{9,13},{10,... | collective-permute-start | bytes 2359304 | tf_op jit(solution)/shard_map/ppermute | solution.py:18
  641.9 34.8 %collective-permute-start.20 = (bf16[1,2,128,512]{3,2,1,0:T(8,128)(2,1)}, bf16[1,2,128,512]{3,2,1,0:T(8,128)(2,1)S(1)}, u32[]{:S(2)}, u32[]{:S(2)}) collective-permute-start(bf16[1,2,128,512]{3,2,1,0:T(8,128)(2,1)} %slice.327), channel_id=1, source_target_pairs={{0,4},{1,5},{2,6},{3,7},{4,0},{5,1},{6,2},{7,3},{8,12},{9,13},{10,... | collective-permute-start | bytes 786440 | tf_op jit(solution)/shard_map/ppermute | solution.py:18
  647.2 32.2 %copy-start.16 = (f32[3,4,128,512]{3,2,1,0:T(8,128)S(1)}, f32[3,4,128,512]{3,2,1,0:T(8,128)}, u32[]{:S(2)}) copy-start(f32[3,4,128,512]{3,2,1,0:T(8,128)} %copy-done.15) | copy-start | bytes 9437188
  653.9 28.8 %copy-start.5 = (f32[256,2,2,1024]{3,2,1,0:T(2,128)S(1)}, f32[256,2,2,1024]{3,2,1,0:T(2,128)}, u32[]{:S(2)}) copy-start(f32[256,2,2,1024]{3,2,1,0:T(2,128)} %reshape_reshape.19) | copy-start | bytes 12582916
  677.8 30.3 %collective-permute-start.21 = (bf16[1,1,128,512]{3,2,1,0:T(8,128)(2,1)S(1)}, bf16[1,1,128,512]{3,2,1,0:T(8,128)(2,1)S(1)}, u32[]{:S(2)}, u32[]{:S(2)}) collective-permute-start(bf16[1,1,128,512]{3,2,1,0:T(8,128)(2,1)S(1)} %slice.328), channel_id=1, source_target_pairs={{0,2},{1,3},{2,0},{3,1},{4,6},{5,7},{6,4},{7,5},{8,10},{9,11},{10,... | collective-permute-start | bytes 393224 | tf_op jit(solution)/shard_map/ppermute | solution.py:18
  682.0 26.2 %collective-permute-start.15 = (bf16[3,1,128,512]{3,2,1,0:T(8,128)(2,1)S(1)}, bf16[3,1,128,512]{3,2,1,0:T(8,128)(2,1)S(1)}, u32[]{:S(2)}, u32[]{:S(2)}) collective-permute-start(bf16[3,1,128,512]{3,2,1,0:T(8,128)(2,1)S(1)} %slice.326), channel_id=1, source_target_pairs={{0,2},{1,3},{2,0},{3,1},{4,6},{5,7},{6,4},{7,5},{8,10},{9,11},{10,... | collective-permute-start | bytes 1179656 | tf_op jit(solution)/shard_map/ppermute | solution.py:18
  687.0 21.1 %copy-start.36 = (f32[1,2,128,512]{3,2,1,0:T(8,128)S(1)}, f32[1,2,128,512]{3,2,1,0:T(8,128)}, u32[]{:S(2)}) copy-start(f32[1,2,128,512]{3,2,1,0:T(8,128)} %copy-done.35) | copy-start | bytes 1572868
  687.0 21.3 %copy-start.20 = (f32[3,2,128,512]{3,2,1,0:T(8,128)S(1)}, f32[3,2,128,512]{3,2,1,0:T(8,128)}, u32[]{:S(2)}) copy-start(f32[3,2,128,512]{3,2,1,0:T(8,128)} %copy-done.19) | copy-start | bytes 4718596
  708.1 19.3 %collective-permute-start.22 = (bf16[1,128,512]{2,1,0:T(8,128)(2,1)S(1)}, bf16[1,128,512]{2,1,0:T(8,128)(2,1)S(1)}, u32[]{:S(2)}, u32[]{:S(2)}) collective-permute-start(bf16[1,128,512]{2,1,0:T(8,128)(2,1)S(1)} %fusion.51), channel_id=1, source_target_pairs={{0,16},{8,24},{16,0},{24,8},{1,17},{9,25},{17,1},{25,9},{2,18},{10... | collective-permute-start | bytes 393224 | tf_op jit(solution)/shard_map/ppermute | solution.py:18
  708.3 21.2 %collective-permute-start.16 = (bf16[3,128,512]{2,1,0:T(8,128)(2,1)S(1)}, bf16[3,128,512]{2,1,0:T(8,128)(2,1)}, u32[]{:S(2)}, u32[]{:S(2)}) collective-permute-start(bf16[3,128,512]{2,1,0:T(8,128)(2,1)S(1)} %fusion.42), channel_id=1, source_target_pairs={{0,16},{8,24},{16,0},{24,8},{1,17},{9,25},{17,1},{25,9},{2,18},{10... | collective-permute-start | bytes 1179656 | tf_op jit(solution)/shard_map/ppermute | solution.py:18
  727.4 10.2 %collective-permute-start.23 = (bf16[1,128,512]{2,1,0:T(8,128)(2,1)S(1)}, bf16[1,128,512]{2,1,0:T(8,128)(2,1)S(1)}, u32[]{:S(2)}, u32[]{:S(2)}) collective-permute-start(bf16[1,128,512]{2,1,0:T(8,128)(2,1)S(1)} %get-tuple-element.27), channel_id=1, source_target_pairs={{0,8},{8,0},{16,24},{24,16},{1,9},{9,1},{17,25},{25,17},{2,10},{10... | collective-permute-start | bytes 393224 | tf_op jit(solution)/shard_map/ppermute | solution.py:18
  731.6 9.2 %collective-permute-start.17 = (bf16[3,128,512]{2,1,0:T(8,128)(2,1)S(1)}, bf16[3,128,512]{2,1,0:T(8,128)(2,1)S(1)}, u32[]{:S(2)}, u32[]{:S(2)}) collective-permute-start(bf16[3,128,512]{2,1,0:T(8,128)(2,1)S(1)} %get-tuple-element.29), channel_id=1, source_target_pairs={{0,8},{8,0},{16,24},{24,16},{1,9},{9,1},{17,25},{25,17},{2,10},{10... | collective-permute-start | bytes 1179656 | tf_op jit(solution)/shard_map/ppermute | solution.py:18
  (37 other events, 84.4 us)

commit v3 on v2

--- a/solution.py
+++ b/solution.py
@@ -79,30 +79,629 @@
     )
 
 
+def row_stats(rows):
+    row_mean = jnp.mean(rows, axis=-1, keepdims=True)
+    centered = rows - row_mean
+    variance = jnp.mean(centered * centered, axis=-1, keepdims=True)
+    inv_scale = lax.rsqrt(variance + EPS)
+    return centered * inv_scale, inv_scale
+
+
+def attend_kernel(
+    exp_size,
+    rep_size,
+    slots,
+    tokens,
+    cotangent,
+    doc,
+    expert_of,
+    w_query,
+    w_key,
+    w_value,
+    w_output,
+    gain_a,
+    w_inner,
+    w_outer,
+    gain_e,
+    cent,
+    attn_w,
+    inner_w,
+    outer_w,
+    arrived,
+    counts_all,
+    cents,
+    gains_e,
+    hidden,
+    qkv,
+    probs,
+    normed_a,
+    context,
+    pick,
+    weights,
+    small_all,
+    gain_row,
+    gain_v,
+    packed_x,
+    packed_c,
+    bias,
+    counts_v,
+    cent_v,
+    own_s,
+    line_s,
+    line_r,
+    side_s,
+    side_r,
+    core_s,
+    core_r,
+    weight_s,
+    weight_r,
+    disp_s,
+    disp_r,
+    count_s,
+    count_r,
+    cent_s,
+    cent_r,
+    gain_s,
+    gain_r,
+    out_s,
+):
+    low = jnp.bfloat16
+    wide = jnp.float32
+    rep_at = lax.axis_index("rep")
+    exp_at = lax.axis_index("exp")
+    core = rep_at % 2
+    group = exp_at // 2
+    side = exp_at % 2
+    groups = exp_size // 2
+    rows_n, width = tokens.shape
+    half = width // 2
+    block = w_query.shape[0]
+    depth = w_inner.shape[0]
+    ff_block = w_outer.shape[0]
+    core_peer = (rep_at ^ 1, exp_at)
+    side_peer = (rep_at, exp_at ^ 1)
+
+    def block_rows(at):
+        return pl.ds(pl.multiple_of(at * block, block), block)
+
+    own_loads = []
+    for at, source in enumerate((w_query, w_key, w_value, w_output)):
+        own_loads.append(
+            pltpu.make_async_copy(source, weights.at[at, block_rows(exp_at)], own_s.at[at])
+        )
+    for load in own_loads:
+        load.start()
+
+    barrier = pltpu.get_barrier_semaphore()
+    for mask in range(1, rep_size):
+        for flip in range(2):
+            pl.semaphore_signal(
+                barrier, inc=1, device_id=(rep_at ^ mask, exp_at ^ flip), device_id_type=MESH
+            )
+
+    @pl.loop(1, exp_size)
+    def _(at):
+        pl.semaphore_signal(barrier, inc=1, device_id=(rep_at, exp_at ^ at), device_id_type=MESH)
+
+    pl.semaphore_wait(barrier, exp_size - 1 + 2 * (rep_size - 1))
+
+    outer_copy = remote(
+        w_outer, outer_w.at[ff_block:], weight_s.at[0], weight_r.at[0], (rep_at ^ 2, exp_at)
+    )
+    outer_copy.start()
+    outer_own = pltpu.make_async_copy(w_outer, outer_w.at[:ff_block], own_s.at[5])
+    outer_own.start()
+
+    for load in own_loads:
+        load.wait()
+
+    picks = (slice(0, 3), slice(3, 4))
+    own_half = pl.ds(pl.multiple_of(core * half, half), half)
+
+    def view(kind, at):
+        return weights.at[picks[kind], block_rows(at), own_half]
+
+    def line_copy(kind, source, step):
+        at = 2 * source + side
+        return remote(
+            view(kind, at),
+            view(kind, at),
+            line_s.at[kind, (1 + step) // 2, source],
+            line_r.at[kind, source],
+            (rep_at, exp_at + 2 * step),
+        )
+
+    def line_wait(kind, source):
+        at = 2 * source + side
+        remote(
+            view(kind, at), view(kind, at), line_s.at[kind, 0, source], line_r.at[kind, source], side_peer
+        ).wait_recv()
+
+    def side_copy(kind, source):
+        at = 2 * source + side
+        return remote(
+            view(kind, at), view(kind, at), side_s.at[kind, source], side_r.at[kind, source], side_peer
+        )
+
+    def side_wait(kind, source):
+        at = 2 * source + 1 - side
+        remote(
+            view(kind, at), view(kind, at), side_s.at[kind, source], side_r.at[kind, source], side_peer
+        ).wait_recv()
+
+    def core_copy(kind, at):
+        return remote(view(kind, at), view(kind, at), core_s.at[kind, at], core_r.at[kind, at], core_peer)
+
+    def core_wait(kind, at):
+        other = pl.ds(pl.multiple_of((1 - core) * half, half), half)
+        there = weights.at[picks[kind], block_rows(at), other]
+        remote(there, there, core_s.at[kind, at], core_r.at[kind, at], core_peer).wait_recv()
+
+    def first_sends(kind):
+        @pl.when(group + 1 < groups)
+        def _():
+            line_copy(kind, group, 1).start()
+
+        @pl.when(group >= 1)
+        def _():
+            line_copy(kind, group, -1).start()
+
+        side_copy(kind, group).start()
+
+    def take_side(kind, source):
+        side_wait(kind, source)
+        core_copy(kind, 2 * source + 1 - side).start()
+
+    def gather_step(kind, step):
+        @pl.when(group - step >= 0)
+        def _():
+            source = group - step
+            line_wait(kind, source)
+
+            @pl.when(group + 1 < groups)
+            def _():
+                line_copy(kind, source, 1).start()
+
+            side_copy(kind, source).start()
+            core_copy(kind, 2 * source + side).start()
+
+        @pl.when(group + step < groups)
+        def _():
+            source = group + step
+            line_wait(kind, source)
+
+            @pl.when(group >= 1)
+            def _():
+                line_copy(kind, source, -1).start()
+
+            side_copy(kind, source).start()
+            core_copy(kind, 2 * source + side).start()
+
+        @pl.when(group - step + 1 >= 0)
+        def _():
+            take_side(kind, group - step + 1)
+
+        @pl.when((step > 1) & (group + step - 1 < groups))
+        def _():
+            take_side(kind, group + step - 1)
+
+    def gather_end(kind):
+        last = groups - 1
+
+        @pl.when(group - last >= 0)
+        def _():
+            take_side(kind, group - last)
+
+        @pl.when((groups > 1) & (group + last < groups))
+        def _():
+            take_side(kind, group + last)
+
+        @pl.loop(0, exp_size)
+        def _(at):
+            @pl.when(at != exp_at)
+            def _():
+                core_wait(kind, at)
+
+    first_sends(0)
+    first_sends(1)
+
+    inner_rows = pl.ds(pl.multiple_of(rep_at * depth, depth), depth)
+
+    def ff_cols(at):
+        return pl.ds(pl.multiple_of(at * ff_block, ff_block), ff_block)
+
+    def inner_copies(mask):
+        dest = rep_at ^ mask
+        found = []
+        for part in range(2):
+            source = w_inner.at[:, ff_cols(dest ^ (2 * part))]
+            target = inner_w.at[inner_rows, part * ff_block : (part + 1) * ff_block]
+            if mask == 0:
+                found.append(pltpu.make_async_copy(source, target, weight_s.at[1 + part]))
+            else:
+                found.append(
+                    remote(
+                        source,
+                        target,
+                        weight_s.at[1 + 2 * mask + part],
+                        weight_r.at[1 + 2 * mask + part],
+                        (dest, exp_at),
+                    )
+                )
+        return found
+
+    for mask in range(rep_size):
+        for copy in inner_copies(mask):
+            copy.start()
+
+    lanes = counts_v.shape[1]
+    expert_row = expert_of[...]
+    onehot = (
+        lax.broadcasted_iota(jnp.int32, (lanes, rows_n), 0) == expert_row
+    ).astype(wide)
+    before = (
+        lax.broadcasted_iota(jnp.int32, (rows_n, rows_n), 0)
+        < lax.broadcasted_iota(jnp.int32, (rows_n, rows_n), 1)
+    ).astype(low)
+    earlier = jnp.dot(onehot.astype(low), before, preferred_element_type=wide)
+    rank = jnp.sum(earlier * onehot, axis=0, keepdims=True).astype(jnp.int32)
+    position = expert_row * slots + rank
+    pick[...] = (
+        lax.broadcasted_iota(jnp.int32, pick.shape, 0) == position
+    ).astype(wide).astype(low)
+    counts_v[:8, :] = lax.dot_general(
+        jnp.ones((8, rows_n), low),
+        onehot.astype(low),
+        (((1,), (1,)), ((), ())),
+        preferred_element_type=wide,
+    )
+    counts_v[8:, :block] = jnp.broadcast_to(gain_a[...].astype(wide), (8, block))
+    cent_v[...] = jnp.broadcast_to(cent[...].astype(wide), cent_v.shape)
+    gain_v[...] = jnp.broadcast_to(gain_e[...].astype(wide), gain_v.shape)
+
+    def eight(at):
+        return pl.ds(pl.multiple_of(at * 8, 8), 8)
+
+    def sixteen(at):
+        return pl.ds(pl.multiple_of(at * 16, 16), 16)
+
+    def count_copy(dest):
+        return remote(
+            counts_v, small_all.at[sixteen(exp_at)], count_s.at[dest], count_r.at[exp_at], (rep_at, dest)
+        )
+
+    count_own = pltpu.make_async_copy(counts_v, small_all.at[sixteen(exp_at)], count_s.at[exp_at])
+    count_own.start()
+
+    @pl.loop(1, exp_size)
+    def _(at):
+        count_copy(exp_at ^ at).start()
+
+    cent_at = side * rep_size + rep_at
+
+    def cent_copy(mask, flip):
+        return remote(
+            cent_v,
+            cents.at[eight(cent_at)],
+            cent_s.at[flip * rep_size + mask],
+            cent_r.at[flip * rep_size + mask],
+            (rep_at ^ mask, exp_at ^ flip),
+        )
+
+    cent_own = pltpu.make_async_copy(cent_v, cents.at[eight(cent_at)], cent_s.at[0])
+    cent_own.start()
+    cent_pairs = [(m, f) for m in range(rep_size) for f in range(2) if m or f]
+    for mask, flip in cent_pairs:
+        cent_copy(mask, flip).start()
+
+    def gain_copy(mask):
+        return remote(
+            gain_v, gains_e.at[eight(rep_at)], gain_s.at[mask], gain_r.at[mask], (rep_at ^ mask, exp_at)
+        )
+
+    gain_own = pltpu.make_async_copy(gain_v, gains_e.at[eight(rep_at)], gain_s.at[0])
+    gain_own.start()
+    for mask in range(1, rep_size):
+        gain_copy(mask).start()
+
+    count_own.wait()
+
+    @pl.loop(1, exp_size)
+    def _(at):
+        source = exp_at ^ at
+        remote(
+            counts_v, small_all.at[sixteen(source)], count_s.at[source], count_r.at[source], (rep_at, source)
+        ).wait()
+
+    small_store = pltpu.make_async_copy(small_all, counts_all, out_s.at[1])
+    small_store.start()
+
+    tiled = jnp.dot(
+        small_all[...].astype(low),
+        (
+            lax.broadcasted_iota(jnp.int32, (lanes, width), 1) % block
+            == lax.broadcasted_iota(jnp.int32, (lanes, width), 0)
+        ).astype(wide).astype(low),
+        preferred_element_type=wide,
+    )
+    chosen_row = lax.broadcasted_iota(jnp.int32, (16 * exp_size, width), 0) == (
+        16 * (lax.broadcasted_iota(jnp.int32, (16 * exp_size, width), 1) // block) + 8
+    )
+    gain_row[...] = jnp.sum(jnp.where(chosen_row, tiled, 0.0), axis=0, keepdims=True)
+
+    @pl.loop(0, rows_n // ROWS)
+    def _(step):
+        here = pl.ds(pl.multiple_of(step * ROWS, ROWS), ROWS)
+        unit, _ = row_stats(tokens[here, :].astype(wide))
+        normed_a[here, :] = (unit * gain_row[...]).astype(low)
+
+    down = lax.broadcasted_iota(jnp.int32, (rows_n, rows_n), 0)
+    along = lax.broadcasted_iota(jnp.int32, (rows_n, rows_n), 1)
+    end = jnp.int32(0)
+    seg_down = jnp.zeros((rows_n, rows_n), jnp.int32)
+    seg_along = jnp.zeros((rows_n, rows_n), jnp.int32)
+    for at in range(doc.shape[1]):
+        end = end + doc[0, at]
+        seg_down = seg_down + (down >= end).astype(jnp.int32)
+        seg_along = seg_along + (along >= end).astype(jnp.int32)
+    bias[...] = jnp.where((seg_down == seg_along) & (down >= along), 0.0, -1e30)
+
+    @pl.loop(1, groups)
+    def _(step):
+        gather_step(0, step)
+
+    gather_end(0)
+
+    def slot_rows(at):
+        return pl.ds(pl.multiple_of(at * slots, slots), slots)
+
+    def disp_copy(source, dest):
+        return remote(
+            source.at[slot_rows(dest // 2)],
+            arrived.at[slot_rows(exp_at)],
+            disp_s.at[dest],
+            disp_r.at[exp_at],
+            (rep_at, dest),
+        )
+
+    def dispatch(source, flip):
+        @pl.loop(0, groups)
+        def _(at):
+            dest = 2 * (group ^ at) + flip
+
+            @pl.when(dest != exp_at)
+            def _():
+                disp_copy(source, dest).start()
+
+            @pl.when(dest == exp_at)
+            def _():
+                pltpu.make_async_copy(
+                    source.at[slot_rows(group)], arrived.at[slot_rows(exp_at)], disp_s.at[exp_at]
+                ).start()
+
+    @pl.loop(0, width // TILE)
+    def _(step):
+        cols = pl.ds(pl.multiple_of(step * TILE, TILE), TILE)
+        packed_c[:, cols] = jnp.dot(
+            pick[...], cotangent[:, cols], preferred_element_type=wide
+        ).astype(low)
+
+    dispatch(packed_c, 1)
+
+    for at in range(3):
+
+        @pl.loop(0, width // TILE)
+        def _(step):
+            cols = pl.ds(pl.multiple_of(step * TILE, TILE), TILE)
+            qkv[at, :, cols] = jnp.dot(
+                normed_a[...], weights[at, :, cols], preferred_element_type=wide
+            ).astype(low)
+
+    head_dim = width // HEADS
+    pair = 2 * head_dim
+    factor = head_dim ** (-0.5)
+    lane = lax.broadcasted_iota(jnp.int32, (rows_n, pair), 1)
+    pairs = HEADS // 2
+    parts = 4
+    for part in range(parts):
+        low_step = 1 + part * (groups - 1) // parts
+        high_step = 1 + (part + 1) * (groups - 1) // parts
+
+        @pl.loop(low_step, high_step)
+        def _(step):
+            gather_step(1, step)
+
+        @pl.loop(part * pairs // parts, (part + 1) * pairs // parts)
+        def _(at):
+            cols = pl.ds(pl.multiple_of(at * pair, pair), pair)
+            q_pair = qkv[0, :, cols]
+            k_pair = qkv[1, :, cols]
+            v_pair = qkv[2, :, cols]
+            found = []
+            for which in range(2):
+                chosen = (lane >= head_dim) if which else (lane < head_dim)
+                q_one = jnp.where(chosen, q_pair, jnp.zeros_like(q_pair))
+                scores = (
+                    lax.dot_general(
+                        q_one, k_pair, (((1,), (1,)), ((), ())), preferred_element_type=wide
+                    )
+                    * factor
+                    + bias[...]
+                )
+                top = jnp.max(scores, axis=1, keepdims=True)
+                raised = jnp.exp(scores - top)
+                total = jnp.sum(raised, axis=1, keepdims=True)
+                prob = (raised * (1.0 / total)).astype(low)
+                probs[pl.ds(pl.multiple_of((2 * at + which) * rows_n, rows_n), rows_n), :] = prob
+                found.append(jnp.dot(prob, v_pair, preferred_element_type=wide))
+            context[:, cols] = jnp.where(lane < head_dim, found[0], found[1]).astype(low)
+
+    gather_end(1)
+    store = pltpu.make_async_copy(weights, attn_w, out_s.at[0])
+    store.start()
+
+    @pl.loop(0, width // TILE)
+    def _(step):
+        cols = pl.ds(pl.multiple_of(step * TILE, TILE), TILE)
+        sum_here = tokens[:, cols].astype(wide) + jnp.dot(
+            context[...], weights[3, :, cols], preferred_element_type=wide
+        )
+        hidden[:, cols] = sum_here
+        packed_x[:, cols] = jnp.dot(
+            pick[...], sum_here.astype(low), preferred_element_type=wide
+        ).astype(low)
+
+    dispatch(packed_x, 0)
+
+    store.wait()
+    outer_copy.wait()
+    outer_own.wait()
+    for mask in range(rep_size):
+        for copy in inner_copies(mask):
+            copy.wait()
+    for kind in range(2):
+        side_copy(kind, group).wait_send()
+
+        @pl.loop(0, groups)
+        def _(source):
+            @pl.when(source != group)
+            def _():
+                side_copy(kind, source).wait_send()
+
+            @pl.when((source <= group) & (group + 1 < groups))
+            def _():
+                line_copy(kind, source, 1).wait_send()
+
+            @pl.when((source >= group) & (group >= 1))
+            def _():
+                line_copy(kind, source, -1).wait_send()
+
+        @pl.loop(0, exp_size)
+        def _(at):
+            @pl.when(at != exp_at)
+            def _():
+                core_copy(kind, at).wait_send()
+
+    small_store.wait()
+    cent_own.wait()
+    gain_own.wait()
+    for mask in range(1, rep_size):
+        gain_copy(mask).wait()
+    for mask, flip in cent_pairs:
+        cent_copy(mask, flip).wait()
+
+    @pl.loop(1, exp_size)
+    def _(at):
+        source = exp_at ^ at
+        remote(
+            packed_c.at[slot_rows(source // 2)],
+            arrived.at[slot_rows(source)],
+            disp_s.at[source],
+            disp_r.at[source],
+            (rep_at, source),
+        ).wait()
+
+    pltpu.make_async_copy(
+        packed_c.at[slot_rows(group)], arrived.at[slot_rows(exp_at)], disp_s.at[exp_at]
+    ).wait()
+
+
+def run_attend(exp_size, rep_size, slots, tokens, cotangent, doc, expert_of, attn, gain_a, w_inner, w_outer, gain_e, cent):
+    rows_n, width = tokens.shape
+    low = jnp.bfloat16
+    wide = jnp.float32
+    groups = exp_size // 2
+    depth = w_inner.shape[0]
+    ff_block = w_outer.shape[0]
+    anyplace = pl.BlockSpec(memory_space=pl.ANY)
+    inside = pl.BlockSpec(memory_space=pltpu.VMEM)
+    dma = pltpu.SemaphoreType.DMA
+    shape = jax.ShapeDtypeStruct
+    return pl.pallas_call(
+        functools.partial(attend_kernel, exp_size, rep_size, slots),
+        out_shape=(
+            shape((4, width, width), low),
+            shape((width, 2 * ff_block), low),
+            shape((2 * ff_block, width), low),
+            shape((exp_size * slots, width), low),
+            shape((exp_size * 16, 128), wide),
+            shape((2 * rep_size * 8, cent.shape[1]), wide),
+            shape((rep_size * 8, depth), wide),
+            shape((rows_n, width), wide),
+            shape((3, rows_n, width), low),
+            shape((HEADS * rows_n, rows_n), low),
+            shape((rows_n, width), low),
+            shape((rows_n, width), low),
+            shape((groups * slots, rows_n), low),
+        ),
+        in_specs=[inside, inside, pl.BlockSpec(memory_space=pltpu.SMEM), inside]
+        + [anyplace] * 4
+        + [inside, anyplace, anyplace, inside, inside],
+        out_specs=(anyplace,) * 7 + (inside,) * 6,
+        scratch_shapes=[
+            pltpu.VMEM((4, width, width), low),
+            pltpu.VMEM((exp_size * 16, 128), wide),
+            pltpu.VMEM((1, width), wide),
+            pltpu.VMEM((8, depth), wide),
+            pltpu.VMEM((groups * slots, width), low),
+            pltpu.VMEM((groups * slots, width), low),
+            pltpu.VMEM((rows_n, rows_n), wide),
+            pltpu.VMEM((16, 128), wide),
+            pltpu.VMEM((8, cent.shape[1]), wide),
+            dma((6,)),
+            dma((2, 2, groups)),
+            dma((2, groups)),
+            dma((2, groups)),
+            dma((2, groups)),
+            dma((2, exp_size)),
+            dma((2, exp_size)),
+            dma((1 + 2 * rep_size,)),
+            dma((1 + 2 * rep_size,)),
+            dma((exp_size,)),
+            dma((exp_size,)),
+            dma((exp_size,)),
+            dma((exp_size,)),
+            dma((2 * rep_size,)),
+            dma((2 * rep_size,)),
+            dma((rep_size,)),
+            dma((rep_size,)),
+            dma((2,)),
+        ],
+        compiler_params=pltpu.CompilerParams(
+            collective_id=1, has_side_effects=True, vmem_limit_bytes=56 << 20
+        ),
+        cost_estimate=pl.CostEstimate(
+            flops=10 * rows_n * width * width,
+            bytes_accessed=40 << 20,
+            transcendentals=HEADS * rows_n * rows_n,
+        ),
+        name="attend",
+    )(tokens, cotangent, doc, expert_of, *attn, gain_a, w_inner, w_outer, gain_e, cent)
+
+
 def expert_kernel(
     exp_size,
     rep_size,
     slots,
-    packed,
-    compact,
-    spread_m,
-    own_in,
-    in_one,
-    in_two,
-    in_three,
-    own_out,
-    out_two,
-    gain,
-    cent,
-    cent_wide,
+    arrived_h,
+    inner_h,
+    outer_h,
+    counts_all,
+    cents,
+    gains_e,
     home,
     outer_keep,
     outer_send,
     inner_keep,
     inner_send,
-    gain_grad,
+    centre_parts,
+    arrived,
+    spread_m,
+    offsets,
+    cent_b,
+    gain,
     centre_grad,
-    arrived,
+    centre_v,
     inner_w,
     outer_w,
     own_x,
@@ -125,9 +724,9 @@
     outer_send_v,
     inner_keep_v,
     inner_send_v,
-    disp_s,
-    disp_r,
     load_sem,
+    centre_s,
+    centre_r,
     norm_s,
     norm_r,
     state_s,
@@ -165,74 +764,65 @@
     def inner_rows(mask):
         return pl.ds(pl.multiple_of((rep_at ^ mask) * depth, depth), depth)
 
-    def own_cols(mask):
-        return pl.ds(pl.multiple_of((rep_at ^ mask) * block, block), block)
-
     loads = [
-        pltpu.make_async_copy(
-            own_in.at[:, own_cols(0)], inner_w.at[inner_rows(0), :block], load_sem.at[0]
-        ),
-        pltpu.make_async_copy(
-            own_in.at[:, own_cols(2)], inner_w.at[inner_rows(0), block:], load_sem.at[1]
-        ),
-        pltpu.make_async_copy(in_one, inner_w.at[inner_rows(1)], load_sem.at[2]),
-        pltpu.make_async_copy(in_two, inner_w.at[inner_rows(2)], load_sem.at[3]),
-        pltpu.make_async_copy(in_three, inner_w.at[inner_rows(3)], load_sem.at[4]),
-        pltpu.make_async_copy(own_out, outer_w.at[:block], load_sem.at[5]),
-        pltpu.make_async_copy(out_two, outer_w.at[block:], load_sem.at[6]),
+        pltpu.make_async_copy(arrived_h, arrived, load_sem.at[0]),
+        pltpu.make_async_copy(inner_h, inner_w, load_sem.at[1]),
+        pltpu.make_async_copy(outer_h, outer_w, load_sem.at[2]),
     ]
     for load in loads:
         load.start()
 
     barrier = pltpu.get_barrier_semaphore()
-    pl.semaphore_signal(barrier, inc=1, device_id=core_peer, device_id_type=MESH)
+    for mask in range(1, rep_size):
+        for flip in range(2):
+            pl.semaphore_signal(
+                barrier, inc=1, device_id=(rep_at ^ mask, exp_at ^ flip), device_id_type=MESH
+            )
 
     @pl.loop(1, exp_size)
     def _(at):
         pl.semaphore_signal(barrier, inc=1, device_id=(rep_at, exp_at ^ at), device_id_type=MESH)
 
-    pl.semaphore_wait(barrier, exp_size)
-
-    def disp_copy(dest):
-        return remote(
-            packed.at[slot_rows(dest)],
-            arrived.at[slot_rows(exp_at)],
-            disp_s.at[dest],
-            disp_r.at[exp_at],
-            (rep_at, dest),
-        )
-
-    own_copy = pltpu.make_async_copy(
-        packed.at[slot_rows(exp_at)], arrived.at[slot_rows(exp_at)], disp_s.at[exp_at]
-    )
-    own_copy.start()
-    for side in range(2):
-
-        @pl.loop(0, exp_size // 2)
-        def _(at):
-            dest = 2 * ((exp_at // 2) ^ at) + side
-
-            @pl.when(dest != exp_at)
-            def _():
-                disp_copy(dest).start()
-
-    own_copy.wait()
-
-    @pl.loop(1, exp_size)
+    counted = counts_all.shape[0]
+    group = exp_at // 2
+    lane = lax.broadcasted_iota(jnp.int32, (counted, 128), 1)
+    mine = jnp.sum(
+        jnp.where(lane == group, counts_all[...], 0.0), axis=1, keepdims=True
+    )
+    mine = jnp.broadcast_to(mine, (counted, 128))
+    down = lax.broadcasted_iota(jnp.int32, (counted, counted), 0)
+    along = lax.broadcasted_iota(jnp.int32, (counted, counted), 1)
+    ahead = ((along // 16 < down // 16) & (along % 16 == 0)).astype(wide).astype(low)
+    offsets[0] = jnp.dot(ahead, mine.astype(low), preferred_element_type=wide)
+    offsets[1] = mine
+    slot_iota = lax.broadcasted_iota(jnp.int32, (slots, own_rows), 0)
+    row_iota = lax.broadcasted_iota(jnp.int32, (slots, own_rows), 1)
+
+    @pl.loop(0, exp_size)
     def _(at):
-        source = exp_at ^ at
-        remote(
-            packed.at[slot_rows(source)],
-            arrived.at[slot_rows(source)],
-            disp_s.at[source],
-            disp_r.at[source],
-            (rep_at, source),
-        ).wait()
+        eight = pl.ds(pl.multiple_of(at * 16, 16), 8)
+        start = offsets[0, eight, :][:1, :1].astype(jnp.int32)
+        limit = offsets[1, eight, :][:1, :1].astype(jnp.int32)
+        spread_m[slot_rows(at), :] = (
+            ((slot_iota + start) == row_iota) & (slot_iota < limit)
+        ).astype(wide).astype(low)
+
+    piece = cents.shape[1]
+    for at in range(width // piece):
+        cent_b[:, at * piece : (at + 1) * piece] = jnp.broadcast_to(
+            cents[at * 8 : at * 8 + 1, :], (cent_b.shape[0], piece)
+        ).astype(low)
+    for at in range(rep_size):
+        gain[:, at * depth : (at + 1) * depth] = gains_e[at * 8 : at * 8 + 1, :]
+    loads[0].wait()
 
     for at in range(width // TILE):
         cols = slice(at * TILE, (at + 1) * TILE)
-        rows_low = jnp.dot(
-            compact[...], arrived[:, cols], preferred_element_type=wide
+        rows_low = lax.dot_general(
+            spread_m[...],
+            arrived[:, cols],
+            (((0,), (0,)), ((), ())),
+            preferred_element_type=wide,
         ).astype(low)
 
         @pl.when(first)
@@ -242,22 +832,19 @@
         @pl.when(second)
         def _():
             own_cot[:, cols] = rows_low
+
+    pl.semaphore_wait(barrier, exp_size - 1 + 2 * (rep_size - 1))
 
     gate_copy = remote(gates, gates, gate_s.at[0], gate_r.at[0], side_peer)
     grad_copy = remote(gate_grads, gate_grads, gate_s.at[1], gate_r.at[1], side_peer)
 
     @pl.when(first)
     def _():
-        logit = jnp.dot(own_x[...], cent_wide[...], preferred_element_type=wide)
+        logit = lax.dot_general(
+            own_x[...], cent_b[...], (((1,), (1,)), ((), ())), preferred_element_type=wide
+        )
         gates[...] = jax.nn.sigmoid(logit)
         gate_copy.start()
-
-    def stats(rows):
-        row_mean = jnp.mean(rows, axis=-1, keepdims=True)
-        centered = rows - row_mean
-        variance = jnp.mean(centered * centered, axis=-1, keepdims=True)
-        inv_scale = lax.rsqrt(variance + EPS)
-        return centered * inv_scale, inv_scale
 
     def hop_forward(at):
         rows = pl.ds(at * part, part)
@@ -275,7 +862,7 @@
             hop.at[rows], states.at[own_slice(at)], hop_s.at[at], hop_r.at[at], side_peer
         )
 
-    for load in loads:
+    for load in loads[1:]:
         load.wait()
 
     def forward(at):
@@ -288,7 +875,7 @@
         @pl.loop(0, part // ROWS)
         def _(step):
             off = pl.multiple_of(step * ROWS, ROWS)
-            unit, _ = stats(own_x[pl.ds(base + off, ROWS), :].astype(wide))
+            unit, _ = row_stats(own_x[pl.ds(base + off, ROWS), :].astype(wide))
             normed[pl.ds(at * 2 * part + part + off, ROWS), :] = (unit * gain[...]).astype(low)
 
         norm_copy = remote(
@@ -371,17 +958,20 @@
     for at in range(CHUNKS):
         forward(at)
 
+    def home_rows(at):
+        return slot_rows((at % 2) * (exp_size // 2) + at // 2)
+
     def ret_copy(dest):
         return remote(
             spread.at[slot_rows(dest)],
-            home.at[slot_rows(exp_at)],
+            home.at[home_rows(exp_at)],
             ret_s.at[dest],
             ret_r.at[exp_at],
             (rep_at, dest),
         )
 
     ret_own = pltpu.make_async_copy(
-        spread.at[slot_rows(exp_at)], home.at[slot_rows(exp_at)], ret_s.at[exp_at]
+        spread.at[slot_rows(exp_at)], home.at[home_rows(exp_at)], ret_s.at[exp_at]
     )
 
     def send_back():
@@ -403,7 +993,6 @@
         grad_copy.start()
         send_back()
 
-    gain_grad[...] = jnp.zeros_like(gain_grad)
     centre_grad[...] = jnp.zeros_like(centre_grad)
 
     def backward(at):
@@ -473,10 +1062,8 @@
             off = pl.multiple_of(step * ROWS, ROWS)
             here = pl.ds(base + off, ROWS)
             rows_in = own_x[here, :].astype(wide)
-            unit, inv_scale = stats(rows_in)
-            grad_normed = acc[pl.ds(off, ROWS), :] + bwd_recv[here, :].astype(wide)
-            gain_grad[...] += jnp.sum(grad_normed * unit, axis=0, keepdims=True)
-            grad_unit = grad_normed * gain[...]
+            unit, inv_scale = row_stats(rows_in)
+            grad_unit = (acc[pl.ds(off, ROWS), :] + bwd_recv[here, :].astype(wide)) * gain[...]
             grad_in = (
                 grad_unit
                 - jnp.mean(grad_unit, axis=-1, keepdims=True)
@@ -493,7 +1080,7 @@
             def _():
                 state = states[pl.ds(at * 2 * part + part + off, ROWS), :].astype(wide) + grad_in
                 grad_logit = gate_grads[here, :][:, :1] * gate * (1.0 - gate)
-                back[here, :] = (state + grad_logit * cent[...]).astype(low)
+                back[here, :] = (state + grad_logit * cent_b[:1, :].astype(wide)).astype(low)
                 centre_grad[...] += jnp.sum(grad_logit * rows_in, axis=0, keepdims=True)
 
         @pl.when(second)
@@ -502,10 +1089,35 @@
 
     for at in range(CHUNKS):
         backward(at)
+
+    def eight_rows(at):
+        return pl.ds(pl.multiple_of(at * 8, 8), 8)
+
+    def centre_copy(mask, flip):
+        dest = rep_at ^ mask
+        return remote(
+            centre_v.at[eight_rows(flip * rep_size + dest)],
+            centre_parts.at[eight_rows(rep_at)],
+            centre_s.at[flip * rep_size + mask],
+            centre_r.at[mask],
+            (dest, exp_at ^ flip),
+        )
+
+    centre_own = pltpu.make_async_copy(
+        centre_v.at[eight_rows(rep_at)], centre_parts.at[eight_rows(rep_at)], centre_s.at[0]
+    )
+    centre_pairs = [(m, f) for m in range(rep_size) for f in range(2) if m or f]
 
     @pl.when(first)
     def _():
         send_back()
+        for at in range(width // piece):
+            centre_v[at * 8 : (at + 1) * 8, :] = jnp.broadcast_to(
+                centre_grad[:, at * piece : (at + 1) * piece], (8, piece)
+            )
+        centre_own.start()
+        for mask, flip in centre_pairs:
+            centre_copy(mask, flip).start()
 
     outs = []
     for at in range(2 * block // TILE):
@@ -568,6 +1180,19 @@
     def _():
         grad_copy.wait_send()
 
+    @pl.when(first)
+    def _():
+        centre_own.wait()
+        for mask, flip in centre_pairs:
+            centre_copy(mask, flip).wait_send()
+        for mask in range(1, rep_size):
+            centre_copy(mask, 0).wait_recv()
+
+    @pl.when(second)
+    def _():
+        for mask in range(rep_size):
+            centre_copy(mask, 1).wait_recv()
+
     ret_own.wait()
 
     @pl.loop(1, exp_size)
@@ -575,29 +1200,37 @@
         source = exp_at ^ step
         remote(
             spread.at[slot_rows(source)],
-            home.at[slot_rows(source)],
+            home.at[home_rows(source)],
             ret_s.at[source],
             ret_r.at[source],
             (rep_at, source),
         ).wait()
 
 
-def run_experts(exp_size, rep_size, slots, packed, compact, spread_m, weights, gain, cent, cent_wide):
-    width = packed.shape[1]
-    own_rows = compact.shape[0]
+def run_experts(
+    exp_size, rep_size, slots, own_rows, arrived, inner_w, outer_w, counts_all, cents, gains_e
+):
+    width = arrived.shape[1]
     depth = width // rep_size
-    block = weights[0].shape[1] // rep_size
+    block = outer_w.shape[0] // 2
     low = jnp.bfloat16
     wide = jnp.float32
     total = exp_size * slots
     all_rows = 2 * own_rows
     part = own_rows // CHUNKS
+    piece = cents.shape[1]
     anyplace = pl.BlockSpec(memory_space=pl.ANY)
     inside = pl.BlockSpec(memory_space=pltpu.VMEM)
     dma = pltpu.SemaphoreType.DMA
     n_out = 2 * block // TILE + 2 * rep_size
     scratch = [
         pltpu.VMEM((total, width), low),
+        pltpu.VMEM((total, own_rows), low),
+        pltpu.VMEM((2, exp_size * 16, 128), wide),
+        pltpu.VMEM((128, width), low),
+        pltpu.VMEM((1, width), wide),
+        pltpu.VMEM((1, width), wide),
+        pltpu.VMEM((2 * rep_size * 8, piece), wide),
         pltpu.VMEM((width, 2 * block), low),
         pltpu.VMEM((2 * block, width), low),
         pltpu.VMEM((own_rows, width), low),
@@ -620,9 +1253,9 @@
         pltpu.VMEM((block, width), low),
         pltpu.VMEM((depth, 2 * block), wide),
         pltpu.VMEM(((rep_size - 1) * depth, 2 * block), low),
-        dma((exp_size,)),
-        dma((exp_size,)),
-        dma((7,)),
+        dma((3,)),
+        dma((2 * rep_size,)),
+        dma((rep_size,)),
     ]
     scratch += [dma((CHUNKS,)) for _ in range(10)]
     scratch += [dma((2,)), dma((2,)), dma((exp_size,)), dma((exp_size,)), dma((n_out,))]
@@ -635,11 +1268,10 @@
             jax.ShapeDtypeStruct((block, width), low),
             jax.ShapeDtypeStruct((depth, 2 * block), wide),
             jax.ShapeDtypeStruct((rep_size - 1, depth, 2 * block), low),
-            jax.ShapeDtypeStruct((1, width), wide),
-            jax.ShapeDtypeStruct((1, width), wide),
+            jax.ShapeDtypeStruct((rep_size * 8, piece), wide),
         ),
-        in_specs=[anyplace, inside, inside] + [anyplace] * 6 + [inside] * 3,
-        out_specs=(anyplace,) * 5 + (inside, inside),
+        in_specs=[anyplace] * 3 + [inside] * 3,
+        out_specs=(anyplace,) * 6,
         scratch_shapes=scratch,
         compiler_params=pltpu.CompilerParams(
             collective_id=0, has_side_effects=True, vmem_limit_bytes=62 << 20
@@ -648,22 +1280,7 @@
             flops=flops, bytes_accessed=40 << 20, transcendentals=2 * all_rows * 2 * block
         ),
         name="experts",
-    )(packed, compact, spread_m, *weights, gain, cent, cent_wide)
-
-
-def gather_weights(stack, core, exp_bits):
-    half = stack.shape[2] // 2
-    pair = stack.reshape(stack.shape[0], stack.shape[1], 2, half)
-    mine = jnp.where(core == 0, pair[:, :, 0], pair[:, :, 1])
-    for bit in range(1, exp_bits):
-        got = swap(mine, "exp", 1 << bit)
-        mine = jnp.stack([mine[:, None], got[:, None]], axis=1)
-        mine = mine.reshape((stack.shape[0], -1) + stack.shape[1:2] + (half,))
-    mine = mine.reshape((stack.shape[0], -1) + stack.shape[1:2] + (half,))
-    got = swap(mine, "exp", 1)
-    mine = jnp.stack([mine, got], axis=2).reshape(stack.shape[0], -1, half)
-    other = swap(mine, "rep", 1)
-    return jnp.concatenate([mine, other], axis=2)
+    )(arrived, inner_w, outer_w, counts_all, cents, gains_e)
 
 
 def reduce_weights(grads, exp_bits):
@@ -685,13 +1302,6 @@
     total = total + swap(total.astype(jnp.bfloat16), "rep", 2).astype(jnp.float32)
     other = swap(total.astype(jnp.bfloat16), "rep", 1).astype(jnp.float32)
     return total, other
-
-
-def masked_scores(queries3, keys3, allowed, factor):
-    scores = (
-        jnp.einsum("qhe,khe->hqk", queries3, keys3, preferred_element_type=jnp.float32) * factor
-    )
-    return jnp.where(allowed[None], scores, -1e30)
 
 
 def shards(
@@ -716,113 +1326,61 @@
     rep_at = lax.axis_index("rep")
     exp_at = lax.axis_index("exp")
     core = rep_at % 2
-    first = exp_at % 2 == 0
-    group = exp_at // 2
     row_count, width = tokens.shape
     head_dim = width // HEADS
     factor = head_dim ** (-0.5)
-    half_width = width // 2
     low = jnp.bfloat16
     wide = jnp.float32
 
-    inner_own = w_inner[0]
-    block = inner_own.shape[1] // rep_size
-
-    def inner_for(mask):
-        dest = rep_at ^ mask
-        return jnp.concatenate(
-            [
-                lax.dynamic_slice_in_dim(inner_own, dest * block, block, 1),
-                lax.dynamic_slice_in_dim(inner_own, (dest ^ 2) * block, block, 1),
-            ],
-            axis=1,
-        )
-
-    weights = [inner_own]
-    weights += [swap(inner_for(mask), "rep", mask) for mask in range(1, rep_size)]
-    weights += [w_outer[0], swap(w_outer[0], "rep", 2)]
-
-    expert_ids = jnp.arange(experts, dtype=jnp.int32)
-    onehot = expert_of_token[:, None] == expert_ids[None, :]
-    counts = jnp.sum(onehot.astype(wide), axis=0)
-    pieces = [centroids[0], expert_gain[0], attn_gain, counts.astype(low)]
-    small = lax.all_gather(jnp.concatenate(pieces), ("rep", "exp"), axis=0, tiled=False)
-    small = small.reshape(rep_size, exp_size, -1)
-    edges = [0]
-    for piece in pieces:
-        edges.append(edges[-1] + piece.shape[0])
-    gain_attn = small[0, :, edges[2] : edges[3]].reshape(width).astype(wide)
-    own_small = lax.dynamic_slice_in_dim(small, exp_at - exp_at % 2, 2, 1)
-    centroid = jnp.swapaxes(own_small[:, :, edges[0] : edges[1]], 0, 1).reshape(width)
-    gain_pair = own_small[:, :, edges[1] : edges[2]]
-    gain_row = jnp.where(first, gain_pair[:, 0], gain_pair[:, 1]).reshape(width).astype(wide)
-    group_counts = lax.dynamic_index_in_dim(small, rep_at, 0, False)[:, edges[3] : edges[4]]
-    group_counts = jnp.sum(
-        jnp.where(expert_ids[None, :] == group, group_counts.astype(wide), 0.0), axis=1
-    ).astype(jnp.int32)
-
-    qkv_w = gather_weights(jnp.stack([w_query, w_key, w_value]), core, exp_bits)
-    out_w = gather_weights(w_output[None], core, exp_bits)[0]
-    inputs = tokens.astype(wide)
-    unit_a, scale_a = norm_stats(inputs)
-    act_a = xor_order((unit_a * gain_attn).astype(low), 1, exp_at, exp_size)
-    queries, keys_low, values_low = [plain_product(act_a, qkv_w[i]).astype(low) for i in range(3)]
-    queries3 = queries.reshape(row_count, HEADS, head_dim)
-    keys3 = keys_low.reshape(row_count, HEADS, head_dim)
-    values3 = values_low.reshape(row_count, HEADS, head_dim)
-    doc_ends = jnp.cumsum(doc_lengths[0])
-    positions = jnp.arange(row_count, dtype=jnp.int32)
-    segment = jnp.sum((positions[:, None] >= doc_ends[None, :]).astype(jnp.int32), axis=1)
-    allowed = (segment[:, None] == segment[None, :]) & (positions[:, None] >= positions[None, :])
-    scores = masked_scores(queries3, keys3, allowed, factor)
-    row_top = jnp.max(scores, axis=-1, keepdims=True)
-    row_total = jnp.sum(jnp.exp(scores - row_top), axis=-1, keepdims=True)
-    log_total = row_top + jnp.log(row_total)
-    probs_low = jnp.exp(scores - log_total).astype(low)
-    context = jnp.einsum("hqk,khe->qhe", probs_low, values3, preferred_element_type=wide)
-    context = context.reshape(row_count, width).astype(low)
-    context_x = xor_order(xor_order(context, 1, core, 2), 1, exp_at, exp_size)
-    hidden = inputs + xor_order(plain_product(context_x, out_w), 1, core, 2)
-
     slots = -(-3 * row_count // exp_size // 16) * 16
-    lower = (positions[:, None] > positions[None, :]).astype(low)
-    earlier = plain_product(lower, onehot.astype(low))
-    rank_in = jnp.sum(jnp.where(onehot, earlier, 0.0), axis=1).astype(jnp.int32)
-    position = expert_of_token * slots + rank_in
-    all_slots = experts * slots
-    pick = (jnp.arange(all_slots, dtype=jnp.int32)[:, None] == position[None, :]).astype(low)
-    sent_rows = hidden.astype(low)
-    packed_sent = plain_product(pick, sent_rows).astype(low).reshape(experts, 1, slots, width)
-    packed_cot = plain_product(pick, cotangent).astype(low).reshape(experts, 1, slots, width)
-    packed = jnp.concatenate([packed_sent, packed_cot], axis=1).reshape(exp_size, slots, width)
-    starts = jnp.cumsum(group_counts) - group_counts
-    slot_at = jnp.arange(slots, dtype=jnp.int32)
-    row_of_slot = jnp.where(
-        slot_at[None, :] < group_counts[:, None], starts[:, None] + slot_at[None, :], -1
-    ).reshape(-1)
-    own_rows = 2 * row_count
-    compact = (jnp.arange(own_rows, dtype=jnp.int32)[:, None] == row_of_slot[None, :]).astype(low)
-    spread_m = (row_of_slot[:, None] == jnp.arange(own_rows, dtype=jnp.int32)[None, :]).astype(low)
-    cent_wide = jnp.broadcast_to(centroid[:, None], (width, 128))
-    home, outer_keep, outer_send, inner_keep, inner_send, gain_grad, grad_centre = run_experts(
+    (
+        attn_w,
+        inner_w,
+        outer_w,
+        arrived,
+        counts_all,
+        cents,
+        gains_e,
+        hidden,
+        qkv,
+        probs,
+        normed_a,
+        context,
+        pick,
+    ) = run_attend(
         exp_size,
         rep_size,
         slots,
-        packed.reshape(exp_size * slots, width),
-        compact,
-        spread_m,
-        weights,
-        gain_row[None],
-        centroid.astype(wide)[None],
-        cent_wide,
-    )
-    gain_grad = gain_grad[0]
-    grad_centre = grad_centre[0]
-    home = home.reshape(experts, 2, slots, width)
-    grad_home = tn_product(pick, home[:, 0].reshape(all_slots, width))
-    branch_home = tn_product(pick, home[:, 1].reshape(all_slots, width))
+        tokens,
+        cotangent,
+        doc_lengths,
+        expert_of_token[None],
+        (w_query, w_key, w_value, w_output),
+        attn_gain[None],
+        w_inner[0],
+        w_outer[0],
+        expert_gain,
+        centroids,
+    )
+    home, outer_keep, outer_send, inner_keep, inner_send, centre_parts = run_experts(
+        exp_size,
+        rep_size,
+        slots,
+        2 * row_count,
+        arrived,
+        inner_w,
+        outer_w,
+        counts_all,
+        cents,
+        gains_e,
+    )
+    all_slots = experts * slots
+    grad_home = tn_product(pick, home[:all_slots])
+    branch_home = tn_product(pick, home[all_slots:])
     output = (hidden + branch_home).astype(low)
-
+    grad_centroids = jnp.sum(centre_parts.reshape(rep_size, 8, -1)[:, 0], axis=0)[None]
+
+    block = outer_keep.shape[0]
     grad_w_outer = (outer_keep + swap(outer_send, "rep", 2).astype(wide))[None]
     mine = inner_keep.reshape(width // rep_size, 2, block)
     got = [
@@ -838,24 +1396,26 @@
         ],
         axis=1,
     )
-    grad_w_inner = xor_order(ordered.reshape(width // rep_size, -1), 1, rep_at, rep_size)[None]
-
-    other_centre = swap(grad_centre[half_width:], "exp", 1)
-    centre_half = jnp.where(first, grad_centre[:half_width], other_centre)
+    summed = xor_order(ordered.reshape(width // rep_size, -1), 1, rep_at, rep_size)
+    grad_w_inner = summed[None]
+    grad_expert_gain = jnp.sum(summed * w_inner[0].astype(wide), axis=1)[None] / expert_gain.astype(
+        wide
+    )
 
     grad_hidden = cotangent.astype(wide) + grad_home
     grad_attn = grad_hidden.astype(low)
-    grad_attn_c = xor_order(grad_attn, 1, core, 2)
-    grad_w_o = tn_product(context_x, grad_attn_c)
+    context_x = xor_order(context, 1, exp_at, exp_size)
+    grad_w_o = tn_product(context_x, xor_order(grad_attn, 1, core, 2))
     share_o = reduce_weights(grad_w_o[None], exp_bits)
-    grad_context = nt_product(grad_attn_c, out_w).astype(low)
-    grad_context = xor_order(xor_order(grad_context, 1, exp_at, exp_size), 1, core, 2)
-    grad_context3 = grad_context.reshape(row_count, HEADS, head_dim)
-    again_scores = masked_scores(queries3, keys3, allowed, factor)
-    attn_probs = jnp.exp(again_scores - log_total)
+    grad_context3 = nt_product(grad_attn, attn_w[3]).astype(low).reshape(
+        row_count, HEADS, head_dim
+    )
+    queries3, keys3, values3 = [qkv[i].reshape(row_count, HEADS, head_dim) for i in range(3)]
+    attn_probs = probs.reshape(HEADS, row_count, row_count)
     grad_probs = jnp.einsum("qhe,khe->hqk", grad_context3, values3, preferred_element_type=wide)
-    inner_sum = jnp.sum(attn_probs * grad_probs, axis=-1, keepdims=True)
-    grad_scores = (attn_probs * (grad_probs - inner_sum)).astype(low)
+    wide_probs = attn_probs.astype(wide)
+    inner_sum = jnp.sum(wide_probs * grad_probs, axis=-1, keepdims=True)
+    grad_scores = (wide_probs * (grad_probs - inner_sum)).astype(low)
     grad_query = (
         jnp.einsum("hqk,khe->qhe", grad_scores, keys3, preferred_element_type=wide) * factor
     ).astype(low)
@@ -863,15 +1423,25 @@
         jnp.einsum("hqk,qhe->khe", grad_scores, queries3, preferred_element_type=wide) * factor
     ).astype(low)
     grad_value = jnp.einsum(
-        "hqk,qhe->khe", attn_probs.astype(low), grad_context3, preferred_element_type=wide
+        "hqk,qhe->khe", attn_probs, grad_context3, preferred_element_type=wide
     ).astype(low)
     grads3 = [g.reshape(row_count, width) for g in (grad_query, grad_key, grad_value)]
-    grad_w_qkv = jnp.stack([tn_product(act_a, g) for g in grads3])
+    unit_x = xor_order(normed_a, 1, exp_at, exp_size)
+    grad_w_qkv = jnp.stack([tn_product(unit_x, xor_order(g, 1, core, 2)) for g in grads3])
     share_qkv = reduce_weights(grad_w_qkv, exp_bits)
-    grad_act = sum(nt_product(g, qkv_w[i]) for i, g in enumerate(grads3))
-    grad_act = xor_order(grad_act, 1, exp_at, exp_size)
-    grad_gain_a = jnp.sum(grad_act * unit_a, axis=0)
-    grad_tokens = grad_hidden + norm_back(grad_act, unit_a, scale_a, gain_attn)
+    grad_unit = sum(nt_product(g, attn_w[i]) for i, g in enumerate(grads3))
+    unit_w, scale_a = row_stats(tokens.astype(wide))
+    gain_all = lax.all_gather(attn_gain, "exp", axis=0, tiled=True).astype(wide)
+    grad_unit = grad_unit * gain_all
+    grad_tokens = (
+        grad_hidden
+        + (
+            grad_unit
+            - jnp.mean(grad_unit, axis=-1, keepdims=True)
+            - unit_w * jnp.mean(grad_unit * unit_w, axis=-1, keepdims=True)
+        )
+        * scale_a
+    )
 
     def true_halves(pair):
         mine_half, other_half = pair
@@ -879,17 +1449,10 @@
 
     full_o = true_halves(share_o)[0]
     full_qkv = true_halves(share_qkv)
-
-    rep_sums = lax.psum(jnp.concatenate([gain_grad, centre_half]), "rep")
-    gain_len = width // rep_size
-    centre_len = half_width // rep_size
-    grad_expert_gain = lax.dynamic_slice_in_dim(rep_sums, rep_at * gain_len, gain_len)[None]
-    grad_centroids = lax.dynamic_slice_in_dim(
-        rep_sums, width + rep_at * centre_len, centre_len
-    )[None]
-    attn_sums = lax.psum(grad_gain_a, ("rep", "exp"))
-    attn_len = width // exp_size
-    share_gain = lax.dynamic_slice_in_dim(attn_sums, exp_at * attn_len, attn_len)
+    share_gain = sum(
+        jnp.sum(full_qkv[i] * w.astype(wide), axis=1)
+        for i, w in enumerate((w_query, w_key, w_value))
+    ) / attn_gain.astype(wide)
     return (
         output,
         grad_tokens,

time: 765 us -> 528 us (0.69)
  blocking collectives: 157 us -> 9.23 us
  waiting for transfers between devices: 134 us -> 15.5 us
  Pallas kernels: 185 us -> 256 us
  other arithmetic: 89.3 us -> 63.1 us
  matrix products: 40.1 us -> 26.1 us
    ppermute x29 -> x16, waiting for transfers between devices: 134 us -> 15.5 us  [swap(): lax.ppermute(shard, axis, [(i, i ^ mask) for i in range(lax.axis_size(axi...]
    pallas_call x0 -> x1, Pallas kernels: none -> 104 us  [run_attend(): pl.pallas_call(functools.partial(attend_kernel, exp_size, rep_size, slots...]
    psum x2 -> x0, blocking collectives: 79.7 us -> none  [the longest x1 54.4 us: shards(): attn_sums = lax.psum(grad_gain_a, ('rep', 'exp'))]
    unnamed x1 -> x0, blocking collectives: 76.9 us -> none
    pallas_call x1, Pallas kernels: 185 us -> 151 us  [run_experts(): pl.pallas_call(functools.partial(expert_kernel, exp_size, rep_size, slots...]
    rev x3 -> x9, local copies, waits for them, and re-layouts: 30.9 us -> 51.2 us  [xor_order(): array = jnp.where(flag == 1, jnp.flip(array, axis + at), array)]
    dot_general x10 -> x1, matrix products: 16.5 us -> 2.98 us  [shards(): jnp.einsum('hqk,qhe->khe', attn_probs, grad_context3, preferred_element_t...]
    all_gather x0 -> x1, blocking collectives: none -> 9.23 us  [shards(): gain_all = lax.all_gather(attn_gain, 'exp', axis=0, tiled=True).astype(wide)]
  transfers between devices with their start and end apart: 29 -> 16, of which waited for: 8 -> 4; matrix products, arithmetic and copies ran while one was open for 23% -> 26% of each run, Pallas kernels for 0% -> 0%
where the time goes in v3:
time: 528 us; the launch traced here: 518 us
  Pallas kernels  256 us (48%)
  local copies, waits for them, and re-layouts  125 us (24%)
  other arithmetic  63.1 us (12%)
  matrix products  26.1 us (5%)
  starting transfers between devices  21.6 us (4%)
  waiting for transfers between devices  15.5 us (3%)
  blocking collectives  9.23 us (2%)
    pallas_call x1, Pallas kernels, run_experts(): pl.pallas_call(functools.partial(expert_kernel, exp_size, rep_size, slots...  151 us
    pallas_call x1, Pallas kernels, run_attend(): pl.pallas_call(functools.partial(attend_kernel, exp_size, rep_size, slots...  104 us
    rev x9, local copies, waits for them, and re-layouts, xor_order(): array = jnp.where(flag == 1, jnp.flip(array, axis + at), array)  51.2 us
    ppermute x16, starting transfers between devices, swap(): lax.ppermute(shard, axis, [(i, i ^ mask) for i in range(lax.axis_size(axi...  21.6 us
    ppermute x16, waiting for transfers between devices, swap(): lax.ppermute(shard, axis, [(i, i ^ mask) for i in range(lax.axis_size(axi...  15.5 us
    unnamed x96, local copies, waits for them, and re-layouts  14.6 us
    reshape x3, local copies, waits for them, and re-layouts, shards(): swap(inner_send[mask - 1], 'rep', mask).astype(wide).reshape(mine.shape)  12.3 us
    select_n x10, other arithmetic, xor_order(): array = jnp.where(flag == 1, jnp.flip(array, axis + at), array)  11.6 us
  transfers between devices with their start and end apart: 16, of which 4 were waited for; matrix products, arithmetic and copies ran while one was open for 26% of the time, Pallas kernels for 0%

profile of v3, /device:TPU:11, one launch (start us, length us, event | category | flops | bytes accessed | tf_op | source)
XLA Modules:
  0.0 518.3 jit_solution(6935618114567849794)
XLA Ops:
  0.7 104.4 %attend.1 = (bf16[4,1024,1024]{2,1,0:T(8,128)(2,1)}, bf16[1024,2048]{1,0:T(8,128)(2,1)}, bf16[2048,1024]{1,0:T(8,128)(2,1)}, bf16[768,1024]{1,0:T(8,128)(2,1)}, ...) custom-call(bf16[256,1024]{1,0:T(8,128)(2,1)} %tokens.1, ...), custom_call_target="tpu_custom_call" | custom-call | flops 2684354560 | bytes 41943040 | tf_op jit(solution)/shard_map/attend/pallas_call | solution.py:620
  105.1 151.3 %experts.1 = (bf16[768,1024]{1,0:T(8,128)(2,1)}, f32[1024,1024]{1,0:T(8,128)}, bf16[1024,1024]{1,0:T(8,128)(2,1)}, f32[256,2048]{1,0:T(8,128)}, bf16[3,256,2048]{2,1,0:T(8,128)(2,1)}, /*index=5*/f32[32,128]{1,0:T(8,128)}) custom-call(bf16[768,1024]{1,0:T(8,128)(2,1)} %get-tuple-element.32.arrived_h, bf16[1024,2048]{1,0:T(8,128)(2,1)} %get-tuple-element.33.inner_h, ...), custom_call_target="tpu_custom_call" | custom-call | flops 25769803776 | bytes 41943040 | tf_op jit(solution)/shard_map/experts/pallas_call | solution.py:1263
  256.4 2.6 fusion.53
  259.3 2.3 fusion.25
  261.9 2.9 copy.56
  264.8 3.0 convolution_convert_fusion
  268.9 2.0 copy.60
  271.0 2.0 copy.58
  282.5 4.0 rev.52
  288.7 4.0 rev.60
  293.2 4.0 rev.55
  297.2 2.1 broadcast_select_fusion.2
  300.7 2.8 rev.54
  304.0 3.0 rev.53
  311.9 4.6 copy-done
  316.5 2.1 slice.278
  319.2 2.8 rev.59
  331.5 9.2 %all-gather = bf16[8,1,128]{2,1,0:T(2,128)(2,1)S(1)} all-gather(bf16[1,1,128]{2,1,0:T(2,128)(2,1)S(1)} %bitcast.212), channel_id=1, replica_groups=mesh['rep'=4,'exp'=8] {'exp'}, dimensions={0}, use_global_device_ids=true | all-gather | bytes 2304 | tf_op jit(solution)/shard_map/all_gather | solution.py:1434
  341.1 2.4 fusion.3
  343.5 2.3 fusion.5
  345.9 3.7 fusion.48
  349.6 5.3 %reshape.191 = f32[256,2,2,1024]{3,2,1,0:T(2,128)} reshape(bf16[1,256,4096]{2,1,0:T(8,128)(2,1)S(1)} %copy-done.20) | data formatting | bytes 6291456 | tf_op jit(solution)/shard_map/convert_element_type | solution.py:1401
  354.9 3.0 reshape.177
  358.0 2.9 fusion.30
  362.1 2.9 fusion.38
  369.4 2.5 collective-permute-start.7
  371.9 4.1 reshape.190
  376.0 4.1 reshape.188
  380.1 5.1 slice_add_fusion
  388.3 3.0 slice_add_fusion.5
  391.3 4.1 reshape.186
  395.4 4.8 slice_add_fusion.6
  400.2 5.9 %pad_maximum_fusion.1 = f32[256,4,1024]{2,1,0:T(4,128)} fusion(f32[256,1,1024]{2,1,0:T(1,128)S(1)} %copy-done.14, f32[256,1,1024]{2,1,0:T(1,128)S(1)} %get-tuple-element.58, f32[256,1,1024]{2,1,0:T(1,128)S(1)} %get-tuple-element.59, f32[256,1,1024]{2,1,0:T(1,128)S(1)} %get-tuple-element.57), kind=kLoop, calls=%fused_computation.8 | loop fusion | flops 3145728 | bytes 8388608 | tf_op jit(solution)/shard_map/stack | solution.py:1390
  406.2 6.6 %reshape_reshape.15 = f32[256,2,2,1024]{3,2,1,0:T(2,128)} reshape(f32[256,4,1024]{2,1,0:T(4,128)} %pad_maximum_fusion.1) | data formatting | bytes 8388608 | tf_op jit(solution)/shard_map/reshape;reshape | solution.py:40
  415.4 3.6 collective-permute-done.1
  419.0 3.1 fusion.2
  423.3 4.2 reverse_select_fusion
  427.5 20.9 %rev.63 = f32[256,2,2,1024]{3,2,1,0:T(2,128)} reverse(f32[256,2,2,1024]{3,2,1,0:T(2,128)} %reverse_select_fusion), dimensions={2} | reverse | bytes 8388608 | tf_op jit(solution)/shard_map/jit(_flip)/rev | solution.py:46
  449.7 2.1 collective-permute-start.9
  451.8 7.4 %collective-permute-done.2 = bf16[3,2,128,512]{3,2,1,0:T(8,128)(2,1)} collective-permute-done((bf16[3,2,128,512]{3,2,1,0:T(8,128)(2,1)}, bf16[3,2,128,512]{3,2,1,0:T(8,128)(2,1)}, u32[]{:S(2)}, u32[]{:S(2)}) %collective-permute-start.2) | collective-permute-done | bytes 786464 | tf_op jit(solution)/shard_map/ppermute | solution.py:18
  461.8 4.1 collective-permute-start.3
  465.9 9.7 %multiply_reduce_fusion = (f32[256]{0:T(256)S(1)}, f32[256,2,2,1024]{3,2,1,0:T(2,128)}) fusion(f32[256,2,2,1024]{3,2,1,0:T(2,128)} %reshape.191, f32[256,2,2,1024]{3,2,1,0:T(2,128)} %rev.63, pred[]{:T(512)S(6)} %eq.32, f32[256,2,2,1024]{3,2,1,0:T(2,128)S(1)} %copy-done.2, pred[]{:T(512)S(6)} %eq.33), kind=kLoop, calls=%fused_computation.9 | loop fusion | flops 4194048 | bytes 16778242 | tf_op jit(solution)/shard_map/reduce_sum | solution.py:1401
  475.6 6.8 %broadcast_in_dim_reshape.3 = f32[1,256,4096]{2,1,0:T(8,128)} reshape(f32[256,2,2,1024]{3,2,1,0:T(2,128)} %get-tuple-element.52) | data formatting | bytes 8388608 | tf_op jit(solution)/shard_map/broadcast_in_dim;reshape | solution.py:1400
  486.3 4.7 collective-permute-start.11
  491.0 3.0 collective-permute-done.4
  495.1 2.9 collective-permute-start.5
  497.9 4.4 add_bitcast_fusion
  507.1 8.1 %rev.56 = f32[3,128,2,512]{3,2,1,0:T(2,128)S(1)} reverse(f32[3,128,2,512]{3,2,1,0:T(2,128)S(1)} %reshape.170), dimensions={2} | reverse | bytes 3145728 | tf_op jit(solution)/shard_map/jit(_flip)/rev | solution.py:46
  (183 shorter events, 59.8 us)
Async XLA Ops:
  105.1 151.3 %copy-start.35 = (bf16[384,256]{1,0:T(8,128)(2,1)S(1)}, bf16[384,256]{1,0:T(8,128)(2,1)}, u32[]{:S(2)}) copy-start(bf16[384,256]{1,0:T(8,128)(2,1)} %get-tuple-element.31) | copy-start | bytes 589828
  105.1 151.3 %copy-start.38 = (bf16[256,1024]{1,0:T(8,128)(2,1)S(1)}, bf16[256,1024]{1,0:T(8,128)(2,1)}, u32[]{:S(2)}) copy-start(bf16[256,1024]{1,0:T(8,128)(2,1)} %cotangent.1) | copy-start | bytes 1572868
  264.8 3.0 copy-start.34
  278.0 2.1 copy-start.37
  278.0 2.4 copy-start.36
  280.0 23.4 %copy-start.26 = (bf16[16,64,256]{2,1,0:T(8,128)(2,1)}, bf16[16,64,256]{2,1,0:T(8,128)(2,1)S(1)}, u32[]{:S(2)}) copy-start(bf16[16,64,256]{2,1,0:T(8,128)(2,1)S(1)} %fusion.28) | copy-start | bytes 1572868
  281.9 10.8 %copy-start.24 = (bf16[16,64,256]{2,1,0:T(8,128)(2,1)S(1)}, bf16[16,64,256]{2,1,0:T(8,128)(2,1)}, u32[]{:S(2)}) copy-start(bf16[16,64,256]{2,1,0:T(8,128)(2,1)} %convolution_convert_fusion) | copy-start | bytes 1572868
  293.2 7.0 %copy-start.28 = (bf16[16,64,256]{2,1,0:T(8,128)(2,1)S(1)}, bf16[16,64,256]{2,1,0:T(8,128)(2,1)}, u32[]{:S(2)}) copy-start(bf16[16,64,256]{2,1,0:T(8,128)(2,1)} %fusion.29) | copy-start | bytes 1572868
  311.9 4.6 copy-start
  318.6 4.5 copy-start.30
  318.7 61.4 %collective-permute-start = (bf16[3,1024,512]{2,1,0:T(8,128)(2,1)}, bf16[3,1024,512]{2,1,0:T(8,128)(2,1)}, u32[]{:S(2)}, u32[]{:S(2)}) collective-permute-start(bf16[3,1024,512]{2,1,0:T(8,128)(2,1)} %slice.278), channel_id=1, source_target_pairs={{0,8},{8,0},{16,24},{24,16},{1,9},{9,1},{17,25},{25,17},{2,10},{10... | collective-permute-start | bytes 9437192 | tf_op jit(solution)/shard_map/ppermute | solution.py:18
  323.2 4.4 copy-start.16
  324.0 2.0 copy-start.4
  327.1 37.8 %collective-permute-start.6 = (bf16[1,1024,512]{2,1,0:T(8,128)(2,1)}, bf16[1,1024,512]{2,1,0:T(8,128)(2,1)}, u32[]{:S(2)}, u32[]{:S(2)}) collective-permute-start(bf16[1,1024,512]{2,1,0:T(8,128)(2,1)} %slice.279), channel_id=1, source_target_pairs={{0,8},{8,0},{16,24},{24,16},{1,9},{9,1},{17,25},{25,17},{2,10},{10... | collective-permute-start | bytes 3145736 | tf_op jit(solution)/shard_map/ppermute | solution.py:18
  327.6 3.7 copy-start.12
  327.7 3.9 copy-start.42
  327.7 13.4 %copy-start.25 = (bf16[16,64,256]{2,1,0:T(8,128)(2,1)S(1)}, bf16[16,64,256]{2,1,0:T(8,128)(2,1)}, u32[]{:S(2)}) copy-start(bf16[16,64,256]{2,1,0:T(8,128)(2,1)} %convolution_convert_fusion) | copy-start | bytes 1572868
  329.5 14.0 %copy-start.29 = (bf16[16,64,256]{2,1,0:T(8,128)(2,1)S(1)}, bf16[16,64,256]{2,1,0:T(8,128)(2,1)}, u32[]{:S(2)}) copy-start(bf16[16,64,256]{2,1,0:T(8,128)(2,1)} %fusion.29) | copy-start | bytes 1572868
  329.5 39.9 %collective-permute-start.14 = (bf16[256,2048]{1,0:T(8,128)(2,1)}, bf16[256,2048]{1,0:T(8,128)(2,1)}, u32[]{:S(2)}, u32[]{:S(2)}) collective-permute-start(bf16[256,2048]{1,0:T(8,128)(2,1)} %get-tuple-element.62), channel_id=1, source_target_pairs={{0,24},{8,16},{16,8},{24,0},{1,25},{9,17},{17,9},{25,1},{2,26},{10... | collective-permute-start | bytes 3145736 | tf_op jit(solution)/shard_map/ppermute | solution.py:18
  330.2 45.7 %collective-permute-start.13 = (bf16[256,2048]{1,0:T(8,128)(2,1)}, bf16[256,2048]{1,0:T(8,128)(2,1)}, u32[]{:S(2)}, u32[]{:S(2)}) collective-permute-start(bf16[256,2048]{1,0:T(8,128)(2,1)} %get-tuple-element.63), channel_id=1, source_target_pairs={{0,8},{8,0},{16,24},{24,16},{1,9},{9,1},{17,25},{25,17},{2,10},{10... | collective-permute-start | bytes 3145736 | tf_op jit(solution)/shard_map/ppermute | solution.py:18
  330.7 60.6 %collective-permute-start.12 = (bf16[256,2048]{1,0:T(8,128)(2,1)}, bf16[256,2048]{1,0:T(8,128)(2,1)}, u32[]{:S(2)}, u32[]{:S(2)}) collective-permute-start(bf16[256,2048]{1,0:T(8,128)(2,1)} %get-tuple-element.61), channel_id=1, source_target_pairs={{0,16},{8,24},{16,0},{24,8},{1,17},{9,25},{17,1},{25,9},{2,18},{10... | collective-permute-start | bytes 3145736 | tf_op jit(solution)/shard_map/ppermute | solution.py:18
  341.1 4.8 copy-start.27
  345.9 3.7 copy-start.20
  358.0 7.6 %copy-start.5 = (f32[1,1024,1024]{2,1,0:T(8,128)S(1)}, f32[1,1024,1024]{2,1,0:T(8,128)}, u32[]{:S(2)}) copy-start(f32[1,1024,1024]{2,1,0:T(8,128)} %copy-done.4) | copy-start | bytes 12582916
  365.0 132.9 %collective-permute-start.15 = (bf16[1024,1024]{1,0:T(8,128)(2,1)}, bf16[1024,1024]{1,0:T(8,128)(2,1)}, u32[]{:S(2)}, u32[]{:S(2)}) collective-permute-start(bf16[1024,1024]{1,0:T(8,128)(2,1)} %get-tuple-element.47), channel_id=1, source_target_pairs={{0,16},{8,24},{16,0},{24,8},{1,17},{9,25},{17,1},{25,9},{2,18},{10... | collective-permute-start | bytes 6291464 | tf_op jit(solution)/shard_map/ppermute | solution.py:18
  369.4 43.3 %collective-permute-start.7 = (bf16[1,4,128,512]{3,2,1,0:T(8,128)(2,1)}, bf16[1,4,128,512]{3,2,1,0:T(8,128)(2,1)}, u32[]{:S(2)}, u32[]{:S(2)}) collective-permute-start(bf16[1,4,128,512]{3,2,1,0:T(8,128)(2,1)} %fusion.44), channel_id=1, source_target_pairs={{0,1},{1,0},{2,3},{3,2},{4,5},{5,4},{6,7},{7,6},{8,9},{9,8},{10,11... | collective-permute-start | bytes 1572872 | tf_op jit(solution)/shard_map/ppermute | solution.py:18
  380.1 6.5 %copy-start.7 = (f32[256,2,1024]{2,1,0:T(2,128)S(1)}, f32[256,2,1024]{2,1,0:T(2,128)}, u32[]{:S(2)}) copy-start(f32[256,2,1024]{2,1,0:T(2,128)} %reshape.188) | copy-start | bytes 6291460
  385.2 6.1 %copy-start.3 = (f32[3,1024,512]{2,1,0:T(8,128)}, f32[3,1024,512]{2,1,0:T(8,128)S(1)}, u32[]{:S(2)}) copy-start(f32[3,1024,512]{2,1,0:T(8,128)S(1)} %slice_add_fusion) | copy-start | bytes 18874372
  385.2 3.1 copy-start.6
  386.6 32.4 %collective-permute-start.1 = (bf16[3,4,128,512]{3,2,1,0:T(8,128)(2,1)}, bf16[3,4,128,512]{3,2,1,0:T(8,128)(2,1)}, u32[]{:S(2)}, u32[]{:S(2)}) collective-permute-start(bf16[3,4,128,512]{3,2,1,0:T(8,128)(2,1)} %fusion.15), channel_id=1, source_target_pairs={{0,1},{1,0},{2,3},{3,2},{4,5},{5,4},{6,7},{7,6},{8,9},{9,8},{10,11... | collective-permute-start | bytes 4718600 | tf_op jit(solution)/shard_map/ppermute | solution.py:18
  395.4 4.8 copy-start.14
  406.2 6.6 %copy-start.11 = (f32[1,1024,512]{2,1,0:T(8,128)S(1)}, f32[1,1024,512]{2,1,0:T(8,128)}, u32[]{:S(2)}) copy-start(f32[1,1024,512]{2,1,0:T(8,128)} %copy-done.10) | copy-start | bytes 6291460
  414.8 8.5 %copy-start.1 = (f32[256,2,2,1024]{3,2,1,0:T(2,128)S(1)}, f32[256,2,2,1024]{3,2,1,0:T(2,128)}, u32[]{:S(2)}) copy-start(f32[256,2,2,1024]{3,2,1,0:T(2,128)} %reshape_reshape.15) | copy-start | bytes 12582916
  414.8 33.6 %collective-permute-start.8 = (bf16[1,2,128,512]{3,2,1,0:T(8,128)(2,1)}, bf16[1,2,128,512]{3,2,1,0:T(8,128)(2,1)S(1)}, u32[]{:S(2)}, u32[]{:S(2)}) collective-permute-start(bf16[1,2,128,512]{3,2,1,0:T(8,128)(2,1)} %slice.282), channel_id=1, source_target_pairs={{0,4},{1,5},{2,6},{3,7},{4,0},{5,1},{6,2},{7,3},{8,12},{9,13},{10,... | collective-permute-start | bytes 786440 | tf_op jit(solution)/shard_map/ppermute | solution.py:18
  423.1 36.1 %collective-permute-start.2 = (bf16[3,2,128,512]{3,2,1,0:T(8,128)(2,1)}, bf16[3,2,128,512]{3,2,1,0:T(8,128)(2,1)}, u32[]{:S(2)}, u32[]{:S(2)}) collective-permute-start(bf16[3,2,128,512]{3,2,1,0:T(8,128)(2,1)} %slice.280), channel_id=1, source_target_pairs={{0,4},{1,5},{2,6},{3,7},{4,0},{5,1},{6,2},{7,3},{8,12},{9,13},{10,... | collective-permute-start | bytes 2359304 | tf_op jit(solution)/shard_map/ppermute | solution.py:18
  448.4 17.5 %copy-start.2 = (f32[256,2,2,1024]{3,2,1,0:T(2,128)S(1)}, f32[256,2,2,1024]{3,2,1,0:T(2,128)}, u32[]{:S(2)}) copy-start(f32[256,2,2,1024]{3,2,1,0:T(2,128)} %reshape_reshape.15) | copy-start | bytes 12582916
  449.7 2.1 copy-start.18
  449.7 32.7 %collective-permute-start.9 = (bf16[1,1,128,512]{3,2,1,0:T(8,128)(2,1)S(1)}, bf16[1,1,128,512]{3,2,1,0:T(8,128)(2,1)S(1)}, u32[]{:S(2)}, u32[]{:S(2)}) collective-permute-start(bf16[1,1,128,512]{3,2,1,0:T(8,128)(2,1)S(1)} %slice.283), channel_id=1, source_target_pairs={{0,2},{1,3},{2,0},{3,1},{4,6},{5,7},{6,4},{7,5},{8,10},{9,11},{10,... | collective-permute-start | bytes 393224 | tf_op jit(solution)/shard_map/ppermute | solution.py:18
  461.8 21.9 %collective-permute-start.3 = (bf16[3,1,128,512]{3,2,1,0:T(8,128)(2,1)S(1)}, bf16[3,1,128,512]{3,2,1,0:T(8,128)(2,1)S(1)}, u32[]{:S(2)}, u32[]{:S(2)}) collective-permute-start(bf16[3,1,128,512]{3,2,1,0:T(8,128)(2,1)S(1)} %slice.281), channel_id=1, source_target_pairs={{0,2},{1,3},{2,0},{3,1},{4,6},{5,7},{6,4},{7,5},{8,10},{9,11},{10,... | collective-permute-start | bytes 1179656 | tf_op jit(solution)/shard_map/ppermute | solution.py:18
  475.6 6.8 %copy-start.19 = (f32[1,2,128,512]{3,2,1,0:T(8,128)S(1)}, f32[1,2,128,512]{3,2,1,0:T(8,128)}, u32[]{:S(2)}) copy-start(f32[1,2,128,512]{3,2,1,0:T(8,128)} %copy-done.18) | copy-start | bytes 1572868
  475.6 8.1 %copy-start.9 = (f32[3,2,128,512]{3,2,1,0:T(8,128)S(1)}, f32[3,2,128,512]{3,2,1,0:T(8,128)}, u32[]{:S(2)}) copy-start(f32[3,2,128,512]{3,2,1,0:T(8,128)} %copy-done.8) | copy-start | bytes 4718596
  475.6 8.5 %copy-start.43 = (bf16[1,256]{1,0:T(2,128)(2,1)S(1)}, bf16[1,256]{1,0:T(2,128)(2,1)}, u32[]{:S(2)}) copy-start(bf16[1,256]{1,0:T(2,128)(2,1)} %gain_e.1) | copy-start | bytes 1540
  482.4 15.6 %copy-start.13 = (f32[1024,1024]{1,0:T(8,128)S(1)}, f32[1024,1024]{1,0:T(8,128)}, u32[]{:S(2)}) copy-start(f32[1024,1024]{1,0:T(8,128)} %get-tuple-element.46) | copy-start | bytes 12582916
  482.4 3.9 collective-permute-start.10
  483.8 10.1 %collective-permute-start.4 = (bf16[3,128,512]{2,1,0:T(8,128)(2,1)S(1)}, bf16[3,128,512]{2,1,0:T(8,128)(2,1)S(1)}, u32[]{:S(2)}, u32[]{:S(2)}) collective-permute-start(bf16[3,128,512]{2,1,0:T(8,128)(2,1)S(1)} %fusion.45), channel_id=1, source_target_pairs={{0,16},{8,24},{16,0},{24,8},{1,17},{9,25},{17,1},{25,9},{2,18},{10... | collective-permute-start | bytes 1179656 | tf_op jit(solution)/shard_map/ppermute | solution.py:18
  486.3 16.0 %collective-permute-start.11 = (bf16[1,128,512]{2,1,0:T(8,128)(2,1)S(1)}, bf16[1,128,512]{2,1,0:T(8,128)(2,1)S(1)}, u32[]{:S(2)}, u32[]{:S(2)}) collective-permute-start(bf16[1,128,512]{2,1,0:T(8,128)(2,1)S(1)} %get-tuple-element.53), channel_id=1, source_target_pairs={{0,8},{8,0},{16,24},{24,16},{1,9},{9,1},{17,25},{25,17},{2,10},{10... | collective-permute-start | bytes 393224 | tf_op jit(solution)/shard_map/ppermute | solution.py:18
  495.1 10.5 %collective-permute-start.5 = (bf16[3,128,512]{2,1,0:T(8,128)(2,1)S(1)}, bf16[3,128,512]{2,1,0:T(8,128)(2,1)S(1)}, u32[]{:S(2)}, u32[]{:S(2)}) collective-permute-start(bf16[3,128,512]{2,1,0:T(8,128)(2,1)S(1)} %get-tuple-element.55), channel_id=1, source_target_pairs={{0,8},{8,0},{16,24},{24,16},{1,9},{9,1},{17,25},{25,17},{2,10},{10... | collective-permute-start | bytes 1179656 | tf_op jit(solution)/shard_map/ppermute | solution.py:18
  502.4 3.2 copy-start.17
  (12 other events, 15.2 us)

commit v4 on v3

--- a/solution.py
+++ b/solution.py
@@ -12,55 +12,6 @@
 ROOT_HALF = 0.7071067811865476
 INV_ROOT_TAU = 0.3989422804014327
 CHUNKS = 2
-
-
-def swap(shard, axis, mask):
-    return lax.ppermute(shard, axis, [(i, i ^ mask) for i in range(lax.axis_size(axis))])
-
-
-def plain_product(left_mat, right_mat):
-    return jnp.dot(left_mat, right_mat, preferred_element_type=jnp.float32)
-
-
-def tn_product(left_mat, right_mat):
-    return lax.dot_general(
-        left_mat, right_mat, (((0,), (0,)), ((), ())), preferred_element_type=jnp.float32
-    )
-
-
-def nt_product(left_mat, right_mat):
-    return lax.dot_general(
-        left_mat, right_mat, (((1,), (1,)), ((), ())), preferred_element_type=jnp.float32
-    )
-
-
-def xor_order(array, axis, index, count):
-    bits = count.bit_length() - 1
-    shape = array.shape
-    array = array.reshape(shape[:axis] + (2,) * bits + (shape[axis] // count,) + shape[axis + 1 :])
-    for at in range(bits):
-        flag = (index >> (bits - 1 - at)) & 1
-        if isinstance(flag, int):
-            array = jnp.flip(array, axis + at) if flag else array
-        else:
-            array = jnp.where(flag == 1, jnp.flip(array, axis + at), array)
-    return array.reshape(shape)
-
-
-def norm_stats(rows):
-    row_mean = jnp.mean(rows, axis=-1, keepdims=True)
-    centered = rows - row_mean
-    variance = jnp.mean(centered * centered, axis=-1, keepdims=True)
-    inv_scale = lax.rsqrt(variance + EPS)
-    return centered * inv_scale, inv_scale
-
-
-def norm_back(grad_out, unit_rows, inv_scale, gain_row):
-    grad_unit = grad_out * gain_row
-    centred_grad = grad_unit - jnp.mean(grad_unit, axis=-1, keepdims=True)
-    return (
-        centred_grad - unit_rows * jnp.mean(grad_unit * unit_rows, axis=-1, keepdims=True)
-    ) * inv_scale
 
 
 MESH = pl.DeviceIdType.MESH
@@ -117,9 +68,9 @@
     normed_a,
     context,
     pick,
+    gain_row,
     weights,
     small_all,
-    gain_row,
     gain_v,
     packed_x,
     packed_c,
@@ -633,15 +584,15 @@
             shape((rows_n, width), low),
             shape((rows_n, width), low),
             shape((groups * slots, rows_n), low),
+            shape((1, width), wide),
         ),
         in_specs=[inside, inside, pl.BlockSpec(memory_space=pltpu.SMEM), inside]
         + [anyplace] * 4
         + [inside, anyplace, anyplace, inside, inside],
-        out_specs=(anyplace,) * 7 + (inside,) * 6,
+        out_specs=(anyplace,) * 7 + (inside,) * 7,
         scratch_shapes=[
             pltpu.VMEM((4, width, width), low),
             pltpu.VMEM((exp_size * 16, 128), wide),
-            pltpu.VMEM((1, width), wide),
             pltpu.VMEM((8, depth), wide),
             pltpu.VMEM((groups * slots, width), low),
             pltpu.VMEM((groups * slots, width), low),
@@ -692,7 +643,6 @@
     home,
     outer_keep,
     outer_send,
-    inner_keep,
     inner_send,
     centre_parts,
     arrived,
@@ -722,7 +672,6 @@
     gate_grads,
     outer_keep_v,
     outer_send_v,
-    inner_keep_v,
     inner_send_v,
     load_sem,
     centre_s,
@@ -1142,13 +1091,8 @@
                 (((0,), (0,)), ((), ())),
                 preferred_element_type=wide,
             )
-            if mask == 0:
-                inner_keep_v[:, cols] = grad
-                outs.append((inner_keep_v.at[:, cols], inner_keep.at[:, cols]))
-            else:
-                rows = slice((mask - 1) * depth, mask * depth)
-                inner_send_v[rows, cols] = grad.astype(low)
-                outs.append((inner_send_v.at[rows, cols], inner_send.at[mask - 1, :, cols]))
+            inner_send_v[mask, side] = grad.astype(low)
+            outs.append((inner_send_v.at[mask, side], inner_send.at[mask, side]))
             pltpu.make_async_copy(outs[-1][0], outs[-1][1], out_sem.at[len(outs) - 1]).start()
 
     for at, (source, target) in enumerate(outs):
@@ -1251,8 +1195,7 @@
         pltpu.VMEM((own_rows, 128), wide),
         pltpu.VMEM((block, width), wide),
         pltpu.VMEM((block, width), low),
-        pltpu.VMEM((depth, 2 * block), wide),
-        pltpu.VMEM(((rep_size - 1) * depth, 2 * block), low),
+        pltpu.VMEM((rep_size, 2, depth, block), low),
         dma((3,)),
         dma((2 * rep_size,)),
         dma((rep_size,)),
@@ -1266,12 +1209,11 @@
             jax.ShapeDtypeStruct((total, width), low),
             jax.ShapeDtypeStruct((block, width), wide),
             jax.ShapeDtypeStruct((block, width), low),
-            jax.ShapeDtypeStruct((depth, 2 * block), wide),
-            jax.ShapeDtypeStruct((rep_size - 1, depth, 2 * block), low),
+            jax.ShapeDtypeStruct((rep_size, 2, depth, block), low),
             jax.ShapeDtypeStruct((rep_size * 8, piece), wide),
         ),
         in_specs=[anyplace] * 3 + [inside] * 3,
-        out_specs=(anyplace,) * 6,
+        out_specs=(anyplace,) * 5,
         scratch_shapes=scratch,
         compiler_params=pltpu.CompilerParams(
             collective_id=0, has_side_effects=True, vmem_limit_bytes=62 << 20
@@ -1283,25 +1225,419 @@
     )(arrived, inner_w, outer_w, counts_all, cents, gains_e)
 
 
-def reduce_weights(grads, exp_bits):
-    count, rows, cols = grads.shape
-    half = cols // 2
-    total = grads[:, :, :half] + swap(grads[:, :, half:].astype(jnp.bfloat16), "rep", 1).astype(
-        jnp.float32
+def finish_kernel(
+    exp_size,
+    rep_size,
+    home,
+    pick,
+    hidden,
+    cotangent,
+    tokens,
+    gain_row,
+    qkv,
+    probs,
+    normed_a,
+    context,
+    attn_w,
+    outer_send,
+    inner_send,
+    output,
+    grad_tokens,
+    shares,
+    outer_recv,
+    inner_zero,
+    inner_one,
+    weights,
+    grad_hidden,
+    grad_attn,
+    grad_context,
+    grads3,
+    keep,
+    core_out,
+    core_in,
+    side_out,
+    side_in,
+    line_out,
+    line_in,
+    total,
+    row_out,
+    row_in,
+    half_out,
+    half_in,
+    load_s,
+    expert_s,
+    expert_r,
+    core_s,
+    core_r,
+    side_s,
+    side_r,
+    line_s,
+    line_r,
+    row_s,
+    row_r,
+    half_s,
+    half_r,
+):
+    low = jnp.bfloat16
+    wide = jnp.float32
+    rep_at = lax.axis_index("rep")
+    exp_at = lax.axis_index("exp")
+    core = rep_at % 2
+    group = exp_at // 2
+    side = exp_at % 2
+    groups = exp_size // 2
+    rows_n, width = tokens.shape
+    half = width // 2
+    block = width // exp_size
+    ff_block = inner_zero.shape[1] // rep_size
+    core_peer = (rep_at ^ 1, exp_at)
+    side_peer = (rep_at, exp_at ^ 1)
+    row_peer = (rep_at ^ 2, exp_at)
+
+    load = pltpu.make_async_copy(attn_w, weights, load_s.at[0])
+    load.start()
+
+    barrier = pltpu.get_barrier_semaphore()
+    for mask in range(1, rep_size):
+        pl.semaphore_signal(
+            barrier, inc=1, device_id=(rep_at ^ mask, exp_at), device_id_type=MESH
+        )
+
+    @pl.loop(1, exp_size)
+    def _(at):
+        pl.semaphore_signal(barrier, inc=1, device_id=(rep_at, exp_at ^ at), device_id_type=MESH)
+
+    pl.semaphore_wait(barrier, exp_size - 1 + rep_size - 1)
+
+    outer_copy = remote(outer_send, outer_recv, expert_s.at[0], expert_r.at[0], row_peer)
+
+    def inner_copies(mask):
+        found = []
+        for part, target in enumerate((inner_zero, inner_one)):
+            at = rep_at ^ (2 * part)
+            cols = pl.ds(pl.multiple_of(at * ff_block, ff_block), ff_block)
+            source = inner_send.at[mask, part]
+            if mask == 0:
+                found.append(
+                    pltpu.make_async_copy(source, target.at[:, cols], expert_s.at[1 + part])
+                )
+            else:
+                found.append(
+                    remote(
+                        source,
+                        target.at[:, cols],
+                        expert_s.at[1 + 2 * mask + part],
+                        expert_r.at[1 + 2 * mask + part],
+                        (rep_at ^ mask, exp_at),
+                    )
+                )
+        return found
+
+    for mask in (2, 3, 1, 0):
+        for copy in inner_copies(mask):
+            copy.start()
+    outer_copy.start()
+
+    all_slots = pick.shape[0]
+
+    @pl.loop(0, width // TILE)
+    def _(step):
+        cols = pl.ds(pl.multiple_of(step * TILE, TILE), TILE)
+        back = lax.dot_general(
+            pick[...], home[:all_slots, cols], (((0,), (0,)), ((), ())), preferred_element_type=wide
+        )
+        grad = cotangent[:, cols].astype(wide) + back
+        grad_hidden[:, cols] = grad
+        grad_attn[:, cols] = grad.astype(low)
+        branch = lax.dot_general(
+            pick[...], home[all_slots:, cols], (((0,), (0,)), ((), ())), preferred_element_type=wide
+        )
+        output[:, cols] = (hidden[:, cols] + branch).astype(low)
+
+    own_half = pl.ds(pl.multiple_of(core * half, half), half)
+    other_half = pl.ds(pl.multiple_of((1 - core) * half, half), half)
+
+    def core_copy(at):
+        return remote(core_out.at[at], core_in.at[at], core_s.at[at], core_r.at[at], core_peer)
+
+    def product(at, left, right, cols, target, kind):
+        @pl.loop(0, width // TILE)
+        def _(step):
+            rows = pl.ds(pl.multiple_of(step * TILE, TILE), TILE)
+            target[at, rows, :] = lax.dot_general(
+                left[:, rows], right[:, cols], (((0,), (0,)), ((), ())), preferred_element_type=wide
+            ).astype(kind)
+
+    def share_start(at, left, right):
+        product(at, left, right, other_half, core_out, low)
+        core_copy(at).start()
+        product(at, left, right, own_half, keep, wide)
+
+    def block_rows(at):
+        return pl.ds(pl.multiple_of(at * block, block), block)
+
+    def side_copy(at):
+        return remote(side_out.at[at], side_in.at[at], side_s.at[at], side_r.at[at], side_peer)
+
+    def share_side(at):
+        core_copy(at).wait_recv()
+
+        @pl.loop(0, groups)
+        def _(which):
+            rows = block_rows(2 * which + 1 - side)
+            side_out[at, block_rows(which), :] = (
+                keep[at, rows, :] + core_in[at, rows, :].astype(wide)
+            ).astype(low)
+
+        side_copy(at).start()
+
+        @pl.loop(0, groups)
+        def _(which):
+            rows = block_rows(2 * which + side)
+            keep[at, rows, :] = keep[at, rows, :] + core_in[at, rows, :].astype(wide)
+
+    def line_copy(at, mask):
+        dest = group ^ mask
+        return remote(
+            line_out.at[at, block_rows(dest)],
+            line_in.at[at, block_rows(group)],
+            line_s.at[at, mask],
+            line_r.at[at, mask],
+            (rep_at, 2 * dest + side),
+        )
+
+    def share_line(at):
+        side_copy(at).wait_recv()
+
+        @pl.loop(1, groups)
+        def _(mask):
+            dest = group ^ mask
+            line_out[at, block_rows(dest), :] = (
+                keep[at, block_rows(2 * dest + side), :] + side_in[at, block_rows(dest), :].astype(wide)
+            ).astype(low)
+            line_copy(at, mask).start()
+
+        total[at] = keep[at, block_rows(exp_at), :] + side_in[at, block_rows(group), :].astype(wide)
+
+    def row_copy(at):
+        return remote(row_out.at[at], row_in.at[at], row_s.at[at], row_r.at[at], row_peer)
+
+    def share_row(at):
+        @pl.loop(1, groups)
+        def _(mask):
+            line_copy(at, mask).wait_recv()
+            total[at] = total[at] + line_in[at, block_rows(group ^ mask), :].astype(wide)
+
+        row_out[at] = total[at].astype(low)
+        row_copy(at).start()
+
+    def half_copy(at):
+        return remote(half_out.at[at], half_in.at[at], half_s.at[at], half_r.at[at], core_peer)
+
+    def share_half(at):
+        row_copy(at).wait_recv()
+        summed = row_out[at].astype(wide) + row_in[at].astype(wide)
+        half_out[at] = summed
+        half_copy(at).start()
+        shares[at, :, own_half] = summed
+
+    def share_end(at):
+        half_copy(at).wait_recv()
+        shares[at, :, other_half] = half_in[at]
+
+    share_start(3, context, grad_attn)
+    load.wait()
+
+    @pl.loop(0, width // TILE)
+    def _(step):
+        rows = pl.ds(pl.multiple_of(step * TILE, TILE), TILE)
+        grad_context[:, rows] = lax.dot_general(
+            grad_attn[...], weights[3, rows, :], (((1,), (1,)), ((), ())), preferred_element_type=wide
+        ).astype(low)
+
+    share_side(3)
+
+    head_dim = width // HEADS
+    pair = 2 * head_dim
+    factor = head_dim ** (-0.5)
+    lane = lax.broadcasted_iota(jnp.int32, (rows_n, pair), 1)
+
+    def heads(start, stop):
+        @pl.loop(start, stop)
+        def _(at):
+            cols = pl.ds(pl.multiple_of(at * pair, pair), pair)
+            q_pair = qkv[0, :, cols]
+            k_pair = qkv[1, :, cols]
+            v_pair = qkv[2, :, cols]
+            c_pair = grad_context[:, cols]
+            found = []
+            for which in range(2):
+                chosen = (lane >= head_dim) if which else (lane < head_dim)
+                c_one = jnp.where(chosen, c_pair, jnp.zeros_like(c_pair))
+                prob = probs[pl.ds(pl.multiple_of((2 * at + which) * rows_n, rows_n), rows_n), :]
+                grad_prob = lax.dot_general(
+                    c_one, v_pair, (((1,), (1,)), ((), ())), preferred_element_type=wide
+                )
+                weighted = prob.astype(wide) * grad_prob
+                row_sum = jnp.sum(weighted, axis=1, keepdims=True)
+                grad_score = (weighted - prob.astype(wide) * row_sum).astype(low)
+                found.append(
+                    (
+                        jnp.dot(grad_score, k_pair, preferred_element_type=wide) * factor,
+                        lax.dot_general(
+                            grad_score,
+                            q_pair,
+                            (((0,), (0,)), ((), ())),
+                            preferred_element_type=wide,
+                        )
+                        * factor,
+                        lax.dot_general(
+                            prob, c_pair, (((0,), (0,)), ((), ())), preferred_element_type=wide
+                        ),
+                    )
+                )
+            for which in range(3):
+                grads3[which, :, cols] = jnp.where(
+                    lane < head_dim, found[0][which], found[1][which]
+                ).astype(low)
+
+    heads(0, HEADS // 4)
+    share_line(3)
+    heads(HEADS // 4, HEADS // 2)
+    for at in range(3):
+        share_start(at, normed_a, grads3.at[at])
+    for at in range(3):
+        share_side(at)
+    share_row(3)
+
+    @pl.loop(0, width // TILE)
+    def _(step):
+        rows = pl.ds(pl.multiple_of(step * TILE, TILE), TILE)
+        grad_normed = jnp.zeros((rows_n, TILE), wide)
+        for at in range(3):
+            grad_normed = grad_normed + lax.dot_general(
+                grads3[at], weights[at, rows, :], (((1,), (1,)), ((), ())), preferred_element_type=wide
+            )
+        grad_tokens[:, rows] = grad_normed
+
+    share_half(3)
+
+    @pl.loop(0, rows_n // ROWS)
+    def _(step):
+        here = pl.ds(pl.multiple_of(step * ROWS, ROWS), ROWS)
+        unit, inv_scale = row_stats(tokens[here, :].astype(wide))
+        grad_unit = grad_tokens[here, :] * gain_row[...]
+        grad_in = (
+            grad_unit
+            - jnp.mean(grad_unit, axis=-1, keepdims=True)
+            - unit * jnp.mean(grad_unit * unit, axis=-1, keepdims=True)
+        ) * inv_scale
+        grad_tokens[here, :] = grad_hidden[here, :] + grad_in
+
+    for at in range(3):
+        share_line(at)
+    share_end(3)
+    for at in range(3):
+        share_row(at)
+    for at in range(3):
+        share_half(at)
+    for at in range(3):
+        share_end(at)
+
+    for at in range(4):
+        core_copy(at).wait_send()
+        side_copy(at).wait_send()
+        row_copy(at).wait_send()
+        half_copy(at).wait_send()
+
+        @pl.loop(1, groups)
+        def _(mask):
+            line_copy(at, mask).wait_send()
+
+    for mask in range(rep_size):
+        for copy in inner_copies(mask):
+            copy.wait()
+    outer_copy.wait()
+
+
+def run_finish(exp_size, rep_size, home, pick, hidden, cotangent, tokens, gain_row, qkv, probs, normed_a, context, attn_w, outer_send, inner_send):
+    rows_n, width = tokens.shape
+    low = jnp.bfloat16
+    wide = jnp.float32
+    half = width // 2
+    groups = exp_size // 2
+    block = width // exp_size
+    depth, ff_block = inner_send.shape[2:]
+    anyplace = pl.BlockSpec(memory_space=pl.ANY)
+    inside = pl.BlockSpec(memory_space=pltpu.VMEM)
+    dma = pltpu.SemaphoreType.DMA
+    shape = jax.ShapeDtypeStruct
+    return pl.pallas_call(
+        functools.partial(finish_kernel, exp_size, rep_size),
+        out_shape=(
+            shape((rows_n, width), low),
+            shape((rows_n, width), wide),
+            shape((4, block, width), wide),
+            shape(outer_send.shape, low),
+            shape((depth, rep_size * ff_block), low),
+            shape((depth, rep_size * ff_block), low),
+        ),
+        in_specs=[inside] * 10 + [anyplace] * 3,
+        out_specs=(inside,) * 3 + (anyplace,) * 3,
+        scratch_shapes=[
+            pltpu.VMEM((4, width, width), low),
+            pltpu.VMEM((rows_n, width), wide),
+            pltpu.VMEM((rows_n, width), low),
+            pltpu.VMEM((rows_n, width), low),
+            pltpu.VMEM((3, rows_n, width), low),
+            pltpu.VMEM((4, width, half), wide),
+            pltpu.VMEM((4, width, half), low),
+            pltpu.VMEM((4, width, half), low),
+            pltpu.VMEM((4, width // 2, half), low),
+            pltpu.VMEM((4, width // 2, half), low),
+            pltpu.VMEM((4, width // 2, half), low),
+            pltpu.VMEM((4, width // 2, half), low),
+            pltpu.VMEM((4, block, half), wide),
+            pltpu.VMEM((4, block, half), low),
+            pltpu.VMEM((4, block, half), low),
+            pltpu.VMEM((4, block, half), wide),
+            pltpu.VMEM((4, block, half), wide),
+            dma((1,)),
+            dma((1 + 2 * rep_size,)),
+            dma((1 + 2 * rep_size,)),
+            dma((4,)),
+            dma((4,)),
+            dma((4,)),
+            dma((4,)),
+            dma((4, groups)),
+            dma((4, groups)),
+            dma((4,)),
+            dma((4,)),
+            dma((4,)),
+            dma((4,)),
+        ],
+        compiler_params=pltpu.CompilerParams(
+            collective_id=2, has_side_effects=True, vmem_limit_bytes=60 << 20
+        ),
+        cost_estimate=pl.CostEstimate(
+            flops=20 * rows_n * width * width, bytes_accessed=60 << 20, transcendentals=0
+        ),
+        name="finish",
+    )(
+        home,
+        pick,
+        hidden,
+        cotangent,
+        tokens,
+        gain_row,
+        qkv,
+        probs,
+        normed_a,
+        context,
+        attn_w,
+        outer_send,
+        inner_send,
     )
-    total = total.reshape(count, -1, 2, rows >> exp_bits, half)
-    total = total[:, :, 0] + swap(total[:, :, 1].astype(jnp.bfloat16), "exp", 1).astype(
-        jnp.float32
-    )
-    for bit in range(exp_bits - 1, 0, -1):
-        keep = total.shape[1] // 2
-        total = total[:, :keep] + swap(
-            total[:, keep:].astype(jnp.bfloat16), "exp", 1 << bit
-        ).astype(jnp.float32)
-    total = total[:, 0]
-    total = total + swap(total.astype(jnp.bfloat16), "rep", 2).astype(jnp.float32)
-    other = swap(total.astype(jnp.bfloat16), "rep", 1).astype(jnp.float32)
-    return total, other
 
 
 def shards(
@@ -1321,15 +1657,7 @@
 ):
     exp_size = lax.axis_size("exp")
     rep_size = lax.axis_size("rep")
-    exp_bits = exp_size.bit_length() - 1
-    experts = exp_size // 2
-    rep_at = lax.axis_index("rep")
-    exp_at = lax.axis_index("exp")
-    core = rep_at % 2
-    row_count, width = tokens.shape
-    head_dim = width // HEADS
-    factor = head_dim ** (-0.5)
-    low = jnp.bfloat16
+    row_count = tokens.shape[0]
     wide = jnp.float32
 
     slots = -(-3 * row_count // exp_size // 16) * 16
@@ -1347,6 +1675,7 @@
         normed_a,
         context,
         pick,
+        gain_row,
     ) = run_attend(
         exp_size,
         rep_size,
@@ -1362,7 +1691,7 @@
         expert_gain,
         centroids,
     )
-    home, outer_keep, outer_send, inner_keep, inner_send, centre_parts = run_experts(
+    home, outer_keep, outer_send, inner_send, centre_parts = run_experts(
         exp_size,
         rep_size,
         slots,
@@ -1374,92 +1703,40 @@
         cents,
         gains_e,
     )
-    all_slots = experts * slots
-    grad_home = tn_product(pick, home[:all_slots])
-    branch_home = tn_product(pick, home[all_slots:])
-    output = (hidden + branch_home).astype(low)
+    output, grad_tokens, shares, outer_recv, inner_zero, inner_one = run_finish(
+        exp_size,
+        rep_size,
+        home,
+        pick,
+        hidden,
+        cotangent,
+        tokens,
+        gain_row,
+        qkv,
+        probs,
+        normed_a,
+        context,
+        attn_w,
+        outer_send,
+        inner_send,
+    )
     grad_centroids = jnp.sum(centre_parts.reshape(rep_size, 8, -1)[:, 0], axis=0)[None]
-
-    block = outer_keep.shape[0]
-    grad_w_outer = (outer_keep + swap(outer_send, "rep", 2).astype(wide))[None]
-    mine = inner_keep.reshape(width // rep_size, 2, block)
-    got = [
-        swap(inner_send[mask - 1], "rep", mask).astype(wide).reshape(mine.shape)
-        for mask in range(1, rep_size)
-    ]
-    ordered = jnp.stack(
-        [
-            mine[:, 0] + got[1][:, 1],
-            got[0][:, 0] + got[2][:, 1],
-            mine[:, 1] + got[1][:, 0],
-            got[0][:, 1] + got[2][:, 0],
-        ],
-        axis=1,
-    )
-    summed = xor_order(ordered.reshape(width // rep_size, -1), 1, rep_at, rep_size)
+    grad_w_outer = (outer_keep + outer_recv.astype(wide))[None]
+    summed = inner_zero.astype(wide) + inner_one.astype(wide)
     grad_w_inner = summed[None]
     grad_expert_gain = jnp.sum(summed * w_inner[0].astype(wide), axis=1)[None] / expert_gain.astype(
         wide
     )
-
-    grad_hidden = cotangent.astype(wide) + grad_home
-    grad_attn = grad_hidden.astype(low)
-    context_x = xor_order(context, 1, exp_at, exp_size)
-    grad_w_o = tn_product(context_x, xor_order(grad_attn, 1, core, 2))
-    share_o = reduce_weights(grad_w_o[None], exp_bits)
-    grad_context3 = nt_product(grad_attn, attn_w[3]).astype(low).reshape(
-        row_count, HEADS, head_dim
-    )
-    queries3, keys3, values3 = [qkv[i].reshape(row_count, HEADS, head_dim) for i in range(3)]
-    attn_probs = probs.reshape(HEADS, row_count, row_count)
-    grad_probs = jnp.einsum("qhe,khe->hqk", grad_context3, values3, preferred_element_type=wide)
-    wide_probs = attn_probs.astype(wide)
-    inner_sum = jnp.sum(wide_probs * grad_probs, axis=-1, keepdims=True)
-    grad_scores = (wide_probs * (grad_probs - inner_sum)).astype(low)
-    grad_query = (
-        jnp.einsum("hqk,khe->qhe", grad_scores, keys3, preferred_element_type=wide) * factor
-    ).astype(low)
-    grad_key = (
-        jnp.einsum("hqk,qhe->khe", grad_scores, queries3, preferred_element_type=wide) * factor
-    ).astype(low)
-    grad_value = jnp.einsum(
-        "hqk,qhe->khe", attn_probs, grad_context3, preferred_element_type=wide
-    ).astype(low)
-    grads3 = [g.reshape(row_count, width) for g in (grad_query, grad_key, grad_value)]
-    unit_x = xor_order(normed_a, 1, exp_at, exp_size)
-    grad_w_qkv = jnp.stack([tn_product(unit_x, xor_order(g, 1, core, 2)) for g in grads3])
-    share_qkv = reduce_weights(grad_w_qkv, exp_bits)
-    grad_unit = sum(nt_product(g, attn_w[i]) for i, g in enumerate(grads3))
-    unit_w, scale_a = row_stats(tokens.astype(wide))
-    gain_all = lax.all_gather(attn_gain, "exp", axis=0, tiled=True).astype(wide)
-    grad_unit = grad_unit * gain_all
-    grad_tokens = (
-        grad_hidden
-        + (
-            grad_unit
-            - jnp.mean(grad_unit, axis=-1, keepdims=True)
-            - unit_w * jnp.mean(grad_unit * unit_w, axis=-1, keepdims=True)
-        )
-        * scale_a
-    )
-
-    def true_halves(pair):
-        mine_half, other_half = pair
-        return xor_order(jnp.concatenate([mine_half, other_half], axis=-1), 2, core, 2)
-
-    full_o = true_halves(share_o)[0]
-    full_qkv = true_halves(share_qkv)
     share_gain = sum(
-        jnp.sum(full_qkv[i] * w.astype(wide), axis=1)
-        for i, w in enumerate((w_query, w_key, w_value))
+        jnp.sum(shares[i] * w.astype(wide), axis=1) for i, w in enumerate((w_query, w_key, w_value))
     ) / attn_gain.astype(wide)
     return (
         output,
         grad_tokens,
-        full_qkv[0],
-        full_qkv[1],
-        full_qkv[2],
-        full_o,
+        shares[0],
+        shares[1],
+        shares[2],
+        shares[3],
         share_gain,
         grad_w_inner,
         grad_w_outer,

time: 528 us -> 417 us (0.79); the launches traced: 518 us -> 416 us
  Pallas kernels: 256 us -> 399 us
  local copies, waits for them, and re-layouts: 125 us -> 3.15 us
  other arithmetic: 63.1 us -> 12.5 us
  matrix products: 26.1 us -> 0 us
  starting transfers between devices: 21.6 us -> 0 us
  waiting for transfers between devices: 15.5 us -> 0 us
  blocking collectives: 9.23 us -> 0 us
    pallas_call x0 -> x1, Pallas kernels: none -> 144 us  [run_finish(): pl.pallas_call(functools.partial(finish_kernel, exp_size, rep_size), out_...]
    rev x9 -> x0, local copies, waits for them, and re-layouts: 51.2 us -> none  [xor_order(): array = jnp.where(flag == 1, jnp.flip(array, axis + at), array)]
    dot_general x14 -> x0, matrix products: 26.1 us -> none  [the longest x4 10.8 us: nt_product(): lax.dot_general(left_mat, right_mat, (((1,), (1,)), ((), ())), preferred_...]
    add x9 -> x0, other arithmetic: 24.3 us -> none  [the longest x2 6.75 us: reduce_weights(): grads[:, :, :half]]
    reshape x12 -> x0, local copies, waits for them, and re-layouts: 21.8 us -> none  [the longest x3 12.3 us: shards(): swap(inner_send[mask - 1], 'rep', mask).astype(wide).reshape(mine.shape)]
    ppermute x16 -> x0, starting transfers between devices: 21.6 us -> none  [swap(): lax.ppermute(shard, axis, [(i, i ^ mask) for i in range(lax.axis_size(axi...]
    ppermute x16 -> x0, waiting for transfers between devices: 15.5 us -> none  [swap(): lax.ppermute(shard, axis, [(i, i ^ mask) for i in range(lax.axis_size(axi...]
    another operation x5 -> x0, local copies, waits for them, and re-layouts: 14.8 us -> none  [the longest x4 8.08 us: xor_order(): array.reshape(shape[:axis] + (2,) * bits + (shape[axis] // count,) + shap...]
  transfers between devices with their start and end apart: 16 -> 0, of which waited for: 4 -> 0; matrix products, arithmetic and copies ran while one was open for 26% -> 0% of each run, Pallas kernels for 0% -> 0%
where the time goes in v4:
time: 417 us; the launch traced here: 416 us
  Pallas kernels  399 us (96%)
  other arithmetic  12.5 us (3%)
    pallas_call x1, Pallas kernels, run_experts(): pl.pallas_call(functools.partial(expert_kernel, exp_size, rep_size, slots...  151 us
    pallas_call x1, Pallas kernels, run_finish(): pl.pallas_call(functools.partial(finish_kernel, exp_size, rep_size), out_...  144 us
    pallas_call x1, Pallas kernels, run_attend(): pl.pallas_call(functools.partial(attend_kernel, exp_size, rep_size, slots...  104 us

profile of v4, /device:TPU:11, one launch (start us, length us, event | category | flops | bytes accessed | tf_op | source)
XLA Modules:
  0.0 415.7 jit_solution(10796565126969953090)
XLA Ops:
  0.6 104.5 %attend.1 = (bf16[4,1024,1024]{2,1,0:T(8,128)(2,1)}, bf16[1024,2048]{1,0:T(8,128)(2,1)}, bf16[2048,1024]{1,0:T(8,128)(2,1)}, bf16[768,1024]{1,0:T(8,128)(2,1)}, ...) custom-call(bf16[256,1024]{1,0:T(8,128)(2,1)} %tokens.3, ...), custom_call_target="tpu_custom_call" | custom-call | flops 2684354560 | bytes 41943040 | tf_op jit(solution)/shard_map/attend/pallas_call | solution.py:571
  105.1 151.2 %experts.1 = (bf16[768,1024]{1,0:T(8,128)(2,1)}, f32[1024,1024]{1,0:T(8,128)}, bf16[1024,1024]{1,0:T(8,128)(2,1)}, bf16[4,2,256,1024]{3,2,1,0:T(8,128)(2,1)}, f32[32,128]{1,0:T(8,128)}) custom-call(bf16[768,1024]{1,0:T(8,128)(2,1)} %get-tuple-element.36.arrived_h, bf16[1024,2048]{1,0:T(8,128)(2,1)} %get-tuple-element.37.inner_h, ...), custom_call_target="tpu_custom_call" | custom-call | flops 25769803776 | bytes 41943040 | tf_op jit(solution)/shard_map/experts/pallas_call | solution.py:1206
  256.4 143.6 %finish.1 = (bf16[256,1024]{1,0:T(8,128)(2,1)}, f32[256,1024]{1,0:T(8,128)}, f32[4,128,1024]{2,1,0:T(8,128)}, bf16[1024,1024]{1,0:T(8,128)(2,1)}, bf16[256,4096]{1,0:T(8,128)(2,1)}, /*index=5*/bf16[256,4096]{1,0:T(8,128)(2,1)}) custom-call(bf16[768,1024]{1,0:T(8,128)(2,1)} %get-tuple-element.42.home, bf16[384,256]{1,0:T(8,128)(2,1)} %get-tuple-element.43.pick, ...), custom_call_target="tpu_custom_call" | custom-call | flops 5368709120 | bytes 62914560 | tf_op jit(solution)/shard_map/finish/pallas_call | solution.py:1575
  400.0 0.0 copy-start
  400.0 0.0 copy-start.6
  400.0 0.0 copy-start.7
  400.0 0.0 copy-start.8
  400.1 0.0 copy-start.3
  400.1 6.1 %add_bitcast_fusion = f32[1,1024,1024]{2,1,0:T(8,128)} fusion(f32[1024,1024]{1,0:T(8,128)} %get-tuple-element.58, bf16[1024,1024]{1,0:T(8,128)(2,1)} %get-tuple-element.59), kind=kLoop, calls=%fused_computation.1 | loop fusion | flops 2097152 | bytes 10485760 | tf_op jit(solution)/shard_map/broadcast_in_dim | solution.py:1724
  406.2 1.2 slice_reduce_fusion
  407.4 0.0 copy-done
  407.4 0.0 copy-start.2
  407.4 0.8 slice_bitcast_fusion
  408.2 0.0 copy-done.6
  408.2 0.0 copy-done.7
  408.2 0.0 copy-done.8
  408.2 0.0 copy-start.10
  408.3 0.0 copy-start.1
  408.3 1.3 multiply_reduce_fusion.1
  409.6 0.0 copy-done.10
  409.6 0.5 convert_divide_fusion.1
  410.1 0.0 copy-done.3
  410.1 0.0 copy-done.2
  410.1 0.5 copy-done.1
  410.6 0.0 copy-start.9
  410.6 0.0 copy-start.5
  410.6 0.0 copy-start.4
  410.6 2.8 multiply_reduce_fusion
  413.4 0.0 copy-done.9
  413.4 0.6 convert_divide_fusion
  414.0 0.0 copy-done.5
  414.0 0.8 copy.26
  414.8 0.0 copy-done.4
  414.8 1.0 copy.27
Async XLA Ops:
  400.0 7.4 %copy-start = (f32[4,128,1024]{2,1,0:T(8,128)S(1)}, f32[4,128,1024]{2,1,0:T(8,128)}, u32[]{:S(2)}) copy-start(f32[4,128,1024]{2,1,0:T(8,128)} %get-tuple-element.55) | copy-start | bytes 6291460
  400.0 8.2 %copy-start.6 = (bf16[128,1024]{1,0:T(8,128)(2,1)S(1)}, bf16[128,1024]{1,0:T(8,128)(2,1)}, u32[]{:S(2)}) copy-start(bf16[128,1024]{1,0:T(8,128)(2,1)} %w_query.1) | copy-start | bytes 786436
  400.0 8.2 %copy-start.7 = (bf16[128,1024]{1,0:T(8,128)(2,1)S(1)}, bf16[128,1024]{1,0:T(8,128)(2,1)}, u32[]{:S(2)}) copy-start(bf16[128,1024]{1,0:T(8,128)(2,1)} %w_key.1) | copy-start | bytes 786436
  400.0 8.2 %copy-start.8 = (bf16[128,1024]{1,0:T(8,128)(2,1)S(1)}, bf16[128,1024]{1,0:T(8,128)(2,1)}, u32[]{:S(2)}) copy-start(bf16[128,1024]{1,0:T(8,128)(2,1)} %w_value.1) | copy-start | bytes 786436
  400.1 10.0 %copy-start.3 = (bf16[256,4096]{1,0:T(8,128)(2,1)S(1)}, bf16[256,4096]{1,0:T(8,128)(2,1)}, u32[]{:S(2)}) copy-start(bf16[256,4096]{1,0:T(8,128)(2,1)} %get-tuple-element.57) | copy-start | bytes 6291460
  407.4 2.7 copy-start.2
  408.2 1.3 copy-start.10
  408.3 2.3 copy-start.1
  410.6 2.8 copy-start.9
  410.6 3.4 copy-start.5
  410.6 4.2 %copy-start.4 = (f32[256,1024]{1,0:T(8,128)S(1)}, f32[256,1024]{1,0:T(8,128)}, u32[]{:S(2)}) copy-start(f32[256,1024]{1,0:T(8,128)} %get-tuple-element.85) | copy-start | bytes 3145732

commit v5 on v4

--- a/solution.py
+++ b/solution.py
@@ -11,12 +11,15 @@
 EPS = 1e-05
 ROOT_HALF = 0.7071067811865476
 INV_ROOT_TAU = 0.3989422804014327
-CHUNKS = 2
+CHUNKS = 4
+DEFER = 256
+EARLY = 512
 
 
 MESH = pl.DeviceIdType.MESH
 TILE = 256
 ROWS = 64
+BIG = 512
 
 
 def remote(src, dst, send_sem, recv_sem, device):
@@ -70,6 +73,7 @@
     pick,
     gain_row,
     weights,
+    staging,
     small_all,
     gain_v,
     packed_x,
@@ -137,9 +141,12 @@
     pl.semaphore_wait(barrier, exp_size - 1 + 2 * (rep_size - 1))
 
     outer_copy = remote(
-        w_outer, outer_w.at[ff_block:], weight_s.at[0], weight_r.at[0], (rep_at ^ 2, exp_at)
+        w_outer.at[: ff_block - DEFER],
+        outer_w.at[ff_block:],
+        weight_s.at[0],
+        weight_r.at[0],
+        (rep_at ^ 2, exp_at),
     )
-    outer_copy.start()
     outer_own = pltpu.make_async_copy(w_outer, outer_w.at[:ff_block], own_s.at[5])
     outer_own.start()
 
@@ -266,24 +273,47 @@
         found = []
         for part in range(2):
             source = w_inner.at[:, ff_cols(dest ^ (2 * part))]
-            target = inner_w.at[inner_rows, part * ff_block : (part + 1) * ff_block]
+            cols = slice(part * ff_block, (part + 1) * ff_block)
+            at = 1 + 2 * mask + part
             if mask == 0:
-                found.append(pltpu.make_async_copy(source, target, weight_s.at[1 + part]))
+                found.append(
+                    pltpu.make_async_copy(source, inner_w.at[inner_rows, cols], weight_s.at[at])
+                )
+            elif mask == 3:
+                found.append(
+                    remote(
+                        source,
+                        staging.at[:, cols],
+                        weight_s.at[at],
+                        weight_r.at[at],
+                        (rep_at ^ 2, exp_at),
+                    )
+                )
             else:
                 found.append(
                     remote(
                         source,
-                        target,
-                        weight_s.at[1 + 2 * mask + part],
-                        weight_r.at[1 + 2 * mask + part],
+                        inner_w.at[inner_rows, cols],
+                        weight_s.at[at],
+                        weight_r.at[at],
                         (dest, exp_at),
                     )
                 )
         return found
 
-    for mask in range(rep_size):
+    far_rows = pl.ds(pl.multiple_of((rep_at ^ 2) * depth, depth), depth)
+    forward_copy = remote(
+        staging,
+        inner_w.at[far_rows],
+        weight_s.at[1 + 2 * rep_size],
+        weight_r.at[1 + 2 * rep_size],
+        core_peer,
+    )
+
+    for mask in (3, 2, 1, 0):
         for copy in inner_copies(mask):
             copy.start()
+    outer_copy.start()
 
     lanes = counts_v.shape[1]
     expert_row = expert_of[...]
@@ -402,6 +432,9 @@
         gather_step(0, step)
 
     gather_end(0)
+    for copy in inner_copies(3):
+        copy.wait_recv()
+    forward_copy.start()
 
     def slot_rows(at):
         return pl.ds(pl.multiple_of(at * slots, slots), slots)
@@ -430,14 +463,9 @@
                     source.at[slot_rows(group)], arrived.at[slot_rows(exp_at)], disp_s.at[exp_at]
                 ).start()
 
-    @pl.loop(0, width // TILE)
+    @pl.loop(1, 1 + (groups - 1 + 2) // 3)
     def _(step):
-        cols = pl.ds(pl.multiple_of(step * TILE, TILE), TILE)
-        packed_c[:, cols] = jnp.dot(
-            pick[...], cotangent[:, cols], preferred_element_type=wide
-        ).astype(low)
-
-    dispatch(packed_c, 1)
+        gather_step(1, step)
 
     for at in range(3):
 
@@ -453,10 +481,11 @@
     factor = head_dim ** (-0.5)
     lane = lax.broadcasted_iota(jnp.int32, (rows_n, pair), 1)
     pairs = HEADS // 2
-    parts = 4
+    parts = 2
+    begun = (groups - 1 + 2) // 3
     for part in range(parts):
-        low_step = 1 + part * (groups - 1) // parts
-        high_step = 1 + (part + 1) * (groups - 1) // parts
+        low_step = 1 + begun + part * (groups - 1 - begun) // parts
+        high_step = 1 + begun + (part + 1) * (groups - 1 - begun) // parts
 
         @pl.loop(low_step, high_step)
         def _(step):
@@ -487,6 +516,15 @@
                 found.append(jnp.dot(prob, v_pair, preferred_element_type=wide))
             context[:, cols] = jnp.where(lane < head_dim, found[0], found[1]).astype(low)
 
+    @pl.loop(0, width // TILE)
+    def _(step):
+        cols = pl.ds(pl.multiple_of(step * TILE, TILE), TILE)
+        packed_c[:, cols] = jnp.dot(
+            pick[...], cotangent[:, cols], preferred_element_type=wide
+        ).astype(low)
+
+    dispatch(packed_c, 1)
+
     gather_end(1)
     store = pltpu.make_async_copy(weights, attn_w, out_s.at[0])
     store.start()
@@ -507,9 +545,13 @@
     store.wait()
     outer_copy.wait()
     outer_own.wait()
+    forward_copy.wait()
     for mask in range(rep_size):
         for copy in inner_copies(mask):
-            copy.wait()
+            if mask == 3:
+                copy.wait_send()
+            else:
+                copy.wait()
     for kind in range(2):
         side_copy(kind, group).wait_send()
 
@@ -573,7 +615,7 @@
         out_shape=(
             shape((4, width, width), low),
             shape((width, 2 * ff_block), low),
-            shape((2 * ff_block, width), low),
+            shape((2 * ff_block - DEFER, width), low),
             shape((exp_size * slots, width), low),
             shape((exp_size * 16, 128), wide),
             shape((2 * rep_size * 8, cent.shape[1]), wide),
@@ -592,6 +634,7 @@
         out_specs=(anyplace,) * 7 + (inside,) * 7,
         scratch_shapes=[
             pltpu.VMEM((4, width, width), low),
+            pltpu.VMEM((depth, 2 * ff_block), low),
             pltpu.VMEM((exp_size * 16, 128), wide),
             pltpu.VMEM((8, depth), wide),
             pltpu.VMEM((groups * slots, width), low),
@@ -606,8 +649,8 @@
             dma((2, groups)),
             dma((2, exp_size)),
             dma((2, exp_size)),
-            dma((1 + 2 * rep_size,)),
-            dma((1 + 2 * rep_size,)),
+            dma((2 + 2 * rep_size,)),
+            dma((2 + 2 * rep_size,)),
             dma((exp_size,)),
             dma((exp_size,)),
             dma((exp_size,)),
@@ -637,13 +680,16 @@
     arrived_h,
     inner_h,
     outer_h,
+    w_outer,
     counts_all,
     cents,
     gains_e,
     home,
+    branch,
     outer_keep,
     outer_send,
-    inner_send,
+    outer_got,
+    inner_sum,
     centre_parts,
     arrived,
     spread_m,
@@ -667,6 +713,7 @@
     hop,
     back,
     spread,
+    relay,
     acc,
     gates,
     gate_grads,
@@ -690,7 +737,13 @@
     gate_r,
     ret_s,
     ret_r,
+    relay_s,
+    relay_r,
+    early_s,
+    early_r,
     out_sem,
+    inner_s,
+    out_r,
 ):
     low = jnp.bfloat16
     wide = jnp.float32
@@ -716,7 +769,9 @@
     loads = [
         pltpu.make_async_copy(arrived_h, arrived, load_sem.at[0]),
         pltpu.make_async_copy(inner_h, inner_w, load_sem.at[1]),
-        pltpu.make_async_copy(outer_h, outer_w, load_sem.at[2]),
+        pltpu.make_async_copy(
+            outer_h, outer_w.at[: outer_h.shape[0]], load_sem.at[2]
+        ),
     ]
     for load in loads:
         load.start()
@@ -783,6 +838,15 @@
             own_cot[:, cols] = rows_low
 
     pl.semaphore_wait(barrier, exp_size - 1 + 2 * (rep_size - 1))
+    row_peer = (rep_at ^ 2, exp_at)
+    late_copy = remote(
+        w_outer.at[block - DEFER :],
+        outer_w.at[2 * block - DEFER :],
+        early_s.at[0],
+        early_r.at[0],
+        row_peer,
+    )
+    late_copy.start()
 
     gate_copy = remote(gates, gates, gate_s.at[0], gate_r.at[0], side_peer)
     grad_copy = remote(gate_grads, gate_grads, gate_s.at[1], gate_r.at[1], side_peer)
@@ -832,10 +896,12 @@
         )
         norm_copy.start()
         norm_copy.wait_recv()
-
-        @pl.loop(0, wide_ff // TILE)
+        if at == 0:
+            late_copy.wait_recv()
+
+        @pl.loop(0, wide_ff // BIG)
         def _(step):
-            cols = pl.ds(pl.multiple_of(step * TILE, TILE), TILE)
+            cols = pl.ds(pl.multiple_of(step * BIG, BIG), BIG)
             inner = jnp.dot(
                 normed[pl.ds(at * 2 * part, 2 * part), :],
                 inner_w[:, cols],
@@ -847,23 +913,18 @@
                 normal + inner * jnp.exp(-0.5 * inner * inner) * INV_ROOT_TAU
             ).astype(low)
 
-        @pl.loop(0, width // TILE)
+        @pl.loop(0, width // BIG)
         def _(step):
-            cols = pl.ds(pl.multiple_of(step * TILE, TILE), TILE)
-            fwd_send[pl.ds(base, part), cols] = jnp.dot(
-                active[other_slice(at), :], outer_w[:, cols], preferred_element_type=wide
-            ).astype(low)
+            cols = pl.ds(pl.multiple_of(step * BIG, BIG), BIG)
+            both = jnp.dot(
+                active[pl.ds(at * 2 * part, 2 * part), :], outer_w[:, cols], preferred_element_type=wide
+            )
+            fwd_send[pl.ds(base, part), cols] = both[:part].astype(low)
+            acc[:, cols] = both[part:]
 
         rows = pl.ds(base, part)
         copy = remote(fwd_send.at[rows], fwd_recv.at[rows], fwd_s.at[at], fwd_r.at[at], core_peer)
         copy.start()
-
-        @pl.loop(0, width // TILE)
-        def _(step):
-            cols = pl.ds(pl.multiple_of(step * TILE, TILE), TILE)
-            acc[:, cols] = jnp.dot(
-                active[own_slice(at), :], outer_w[:, cols], preferred_element_type=wide
-            )
 
         copy.wait_recv()
 
@@ -907,23 +968,31 @@
     for at in range(CHUNKS):
         forward(at)
 
-    def home_rows(at):
-        return slot_rows((at % 2) * (exp_size // 2) + at // 2)
-
-    def ret_copy(dest):
+    groups = exp_size // 2
+
+    def ret_copy(source, dest):
         return remote(
-            spread.at[slot_rows(dest)],
-            home.at[home_rows(exp_at)],
+            source,
+            home.at[slot_rows(group)],
             ret_s.at[dest],
-            ret_r.at[exp_at],
+            ret_r.at[group],
             (rep_at, dest),
         )
 
+    def relay_copy(which):
+        return remote(
+            spread.at[slot_rows(2 * which + 1)],
+            relay.at[slot_rows(which)],
+            relay_s.at[which],
+            relay_r.at[which],
+            side_peer,
+        )
+
     ret_own = pltpu.make_async_copy(
-        spread.at[slot_rows(exp_at)], home.at[home_rows(exp_at)], ret_s.at[exp_at]
+        spread.at[slot_rows(exp_at)], home.at[slot_rows(group)], ret_s.at[exp_at]
     )
 
-    def send_back():
+    def make_spread():
         @pl.loop(0, width // TILE)
         def _(step):
             cols = pl.ds(pl.multiple_of(step * TILE, TILE), TILE)
@@ -931,16 +1000,22 @@
                 spread_m[...], back[:, cols], preferred_element_type=wide
             ).astype(low)
 
-        @pl.loop(1, exp_size)
+    def send_back():
+        @pl.loop(1, groups)
         def _(step):
-            ret_copy(exp_at ^ step).start()
-
+            relay_copy(group ^ (groups - step)).start()
+
+        @pl.loop(1, groups)
+        def _(step):
+            dest = 2 * (group ^ (groups - step))
+            ret_copy(spread.at[slot_rows(dest)], dest).start()
+
+        ret_copy(spread.at[slot_rows(exp_at + 1)], exp_at + 1).start()
         ret_own.start()
 
     @pl.when(second)
     def _():
         grad_copy.start()
-        send_back()
 
     centre_grad[...] = jnp.zeros_like(centre_grad)
 
@@ -957,9 +1032,9 @@
         copy.start()
         copy.wait_recv()
 
-        @pl.loop(0, wide_ff // TILE)
+        @pl.loop(0, wide_ff // BIG)
         def _(step):
-            rows = pl.ds(pl.multiple_of(step * TILE, TILE), TILE)
+            rows = pl.ds(pl.multiple_of(step * BIG, BIG), BIG)
             grad_active = lax.dot_general(
                 states[pl.ds(at * 2 * part, 2 * part), :],
                 outer_w[rows, :],
@@ -969,31 +1044,23 @@
             here = pl.ds(at * 2 * part, 2 * part)
             slope[here, rows] = (grad_active * slope[here, rows].astype(wide)).astype(low)
 
-        @pl.loop(0, width // TILE)
+        @pl.loop(0, width // BIG)
         def _(step):
-            cols = pl.ds(pl.multiple_of(step * TILE, TILE), TILE)
-            bwd_send[pl.ds(base, part), cols] = lax.dot_general(
-                slope[other_slice(at), :],
-                inner_w[cols, :],
-                (((1,), (1,)), ((), ())),
-                preferred_element_type=wide,
-            ).astype(low)
-
-        rows = pl.ds(base, part)
-        back_copy = remote(
-            bwd_send.at[rows], bwd_recv.at[rows], bwd_s.at[at], bwd_r.at[at], core_peer
-        )
-        back_copy.start()
-
-        @pl.loop(0, width // TILE)
-        def _(step):
-            cols = pl.ds(pl.multiple_of(step * TILE, TILE), TILE)
-            acc[:, cols] = lax.dot_general(
-                slope[own_slice(at), :],
+            cols = pl.ds(pl.multiple_of(step * BIG, BIG), BIG)
+            both = lax.dot_general(
+                slope[pl.ds(at * 2 * part, 2 * part), :],
                 inner_w[cols, :],
                 (((1,), (1,)), ((), ())),
                 preferred_element_type=wide,
             )
+            bwd_send[pl.ds(base, part), cols] = both[:part].astype(low)
+            acc[:, cols] = both[part:]
+
+        rows = pl.ds(base, part)
+        back_copy = remote(
+            bwd_send.at[rows], bwd_recv.at[rows], bwd_s.at[at], bwd_r.at[at], core_peer
+        )
+        back_copy.start()
 
         back_copy.wait_recv()
         if at == 0:
@@ -1057,6 +1124,8 @@
     )
     centre_pairs = [(m, f) for m in range(rep_size) for f in range(2) if m or f]
 
+    make_spread()
+
     @pl.when(first)
     def _():
         send_back()
@@ -1069,34 +1138,68 @@
             centre_copy(mask, flip).start()
 
     outs = []
-    for at in range(2 * block // TILE):
+    tiles = block // TILE
+    early_copy = remote(
+        outer_send_v.at[:EARLY], outer_got, early_s.at[1], early_r.at[1], row_peer
+    )
+    for at in list(range(tiles, 2 * tiles)) + list(range(tiles)):
         rows = slice(at * TILE, (at + 1) * TILE)
         grad = lax.dot_general(
             active[:, rows], states[...], (((0,), (0,)), ((), ())), preferred_element_type=wide
         )
-        if (at + 1) * TILE <= block:
+        if at < tiles:
             outer_keep_v[rows, :] = grad
             outs.append((outer_keep_v.at[rows], outer_keep.at[rows]))
         else:
-            rows = slice(at * TILE - block, (at + 1) * TILE - block)
-            outer_send_v[rows, :] = grad.astype(low)
-            outs.append((outer_send_v.at[rows], outer_send.at[rows]))
+            top = at * TILE - block
+            outer_send_v[top : top + TILE, :] = grad.astype(low)
+            if top + TILE == EARLY:
+                early_copy.start()
+            if top < EARLY:
+                continue
+            outs.append(
+                (outer_send_v.at[top : top + TILE], outer_send.at[top - EARLY : top - EARLY + TILE])
+            )
         pltpu.make_async_copy(outs[-1][0], outs[-1][1], out_sem.at[len(outs) - 1]).start()
-    for mask in range(rep_size):
-        for side in range(2):
-            cols = slice(side * block, (side + 1) * block)
-            grad = lax.dot_general(
-                normed[:, inner_rows(mask)],
-                slope[:, cols],
-                (((0,), (0,)), ((), ())),
-                preferred_element_type=wide,
-            )
-            inner_send_v[mask, side] = grad.astype(low)
-            outs.append((inner_send_v.at[mask, side], inner_send.at[mask, side]))
-            pltpu.make_async_copy(outs[-1][0], outs[-1][1], out_sem.at[len(outs) - 1]).start()
-
+    outs.append((spread, branch))
+    pltpu.make_async_copy(spread, branch, out_sem.at[len(outs) - 1]).start()
+
+    def inner_copy(mask, side):
+        at = rep_at ^ (2 * side)
+        cols = pl.ds(pl.multiple_of(at * block, block), block)
+        target = inner_sum.at[mask // 2, :, cols]
+        source = inner_send_v.at[mask, side]
+        count = 2 * mask + side
+        if mask % 2 == 0:
+            return pltpu.make_async_copy(source, target, inner_s.at[count])
+        return remote(source, target, inner_s.at[count], out_r.at[count], core_peer)
+
+    inner_order = [(m, f) for m in (3, 1, 2, 0) for f in range(2)]
+    for mask, side in inner_order:
+        cols = slice(side * block, (side + 1) * block)
+        grad = lax.dot_general(
+            normed[:, inner_rows(mask)],
+            slope[:, cols],
+            (((0,), (0,)), ((), ())),
+            preferred_element_type=wide,
+        )
+        inner_send_v[mask, side] = grad.astype(low)
+        inner_copy(mask, side).start()
+
+    @pl.when(second)
+    def _():
+        @pl.loop(1, groups)
+        def _(step):
+            which = group ^ (groups - step)
+            relay_copy(which).wait_recv()
+            ret_copy(relay.at[slot_rows(which)], 2 * which + 1).start()
+
+    late_copy.wait_send()
+    early_copy.wait()
     for at, (source, target) in enumerate(outs):
         pltpu.make_async_copy(source, target, out_sem.at[at]).wait()
+    for mask, side in inner_order:
+        inner_copy(mask, side).wait()
     for at in range(CHUNKS):
         rows = pl.ds(at * part, part)
         remote(
@@ -1137,26 +1240,50 @@
         for mask in range(rep_size):
             centre_copy(mask, 1).wait_recv()
 
-    ret_own.wait()
-
-    @pl.loop(1, exp_size)
+    @pl.when(first)
+    def _():
+        ret_own.wait()
+        ret_copy(spread.at[slot_rows(exp_at + 1)], exp_at + 1).wait_send()
+
+        @pl.loop(1, groups)
+        def _(step):
+            which = group ^ step
+            relay_copy(which).wait_send()
+            ret_copy(spread.at[slot_rows(2 * which)], 2 * which).wait_send()
+
+    @pl.when(second)
+    def _():
+        @pl.loop(1, groups)
+        def _(step):
+            which = group ^ step
+            ret_copy(relay.at[slot_rows(which)], 2 * which + 1).wait_send()
+
+        remote(
+            relay.at[slot_rows(group)],
+            home.at[slot_rows(group)],
+            relay_s.at[group],
+            ret_r.at[group],
+            side_peer,
+        ).wait_recv()
+
+    @pl.loop(1, groups)
     def _(step):
-        source = exp_at ^ step
+        source = group ^ step
         remote(
-            spread.at[slot_rows(source)],
-            home.at[home_rows(source)],
-            ret_s.at[source],
+            relay.at[slot_rows(source)],
+            home.at[slot_rows(source)],
+            relay_s.at[source],
             ret_r.at[source],
-            (rep_at, source),
-        ).wait()
+            side_peer,
+        ).wait_recv()
 
 
 def run_experts(
-    exp_size, rep_size, slots, own_rows, arrived, inner_w, outer_w, counts_all, cents, gains_e
+    exp_size, rep_size, slots, own_rows, arrived, inner_w, outer_w, w_outer, counts_all, cents, gains_e
 ):
     width = arrived.shape[1]
     depth = width // rep_size
-    block = outer_w.shape[0] // 2
+    block = w_outer.shape[0]
     low = jnp.bfloat16
     wide = jnp.float32
     total = exp_size * slots
@@ -1166,7 +1293,7 @@
     anyplace = pl.BlockSpec(memory_space=pl.ANY)
     inside = pl.BlockSpec(memory_space=pltpu.VMEM)
     dma = pltpu.SemaphoreType.DMA
-    n_out = 2 * block // TILE + 2 * rep_size
+    n_out = (2 * block - EARLY) // TILE + 1
     scratch = [
         pltpu.VMEM((total, width), low),
         pltpu.VMEM((total, own_rows), low),
@@ -1190,6 +1317,7 @@
         pltpu.VMEM((own_rows, width), low),
         pltpu.VMEM((own_rows, width), low),
         pltpu.VMEM((total, width), low),
+        pltpu.VMEM((total // 2, width), low),
         pltpu.VMEM((part, width), wide),
         pltpu.VMEM((own_rows, 128), wide),
         pltpu.VMEM((own_rows, 128), wide),
@@ -1201,19 +1329,23 @@
         dma((rep_size,)),
     ]
     scratch += [dma((CHUNKS,)) for _ in range(10)]
-    scratch += [dma((2,)), dma((2,)), dma((exp_size,)), dma((exp_size,)), dma((n_out,))]
+    scratch += [dma((2,)), dma((2,)), dma((exp_size,)), dma((exp_size // 2,))]
+    scratch += [dma((exp_size // 2,)), dma((exp_size // 2,)), dma((2,)), dma((2,)), dma((n_out,))]
+    scratch += [dma((2 * rep_size,)), dma((2 * rep_size,))]
     flops = 2 * all_rows * width * 2 * block * 6
     return pl.pallas_call(
         functools.partial(expert_kernel, exp_size, rep_size, slots),
         out_shape=(
+            jax.ShapeDtypeStruct((total // 2, width), low),
             jax.ShapeDtypeStruct((total, width), low),
             jax.ShapeDtypeStruct((block, width), wide),
-            jax.ShapeDtypeStruct((block, width), low),
-            jax.ShapeDtypeStruct((rep_size, 2, depth, block), low),
+            jax.ShapeDtypeStruct((block - EARLY, width), low),
+            jax.ShapeDtypeStruct((EARLY, width), low),
+            jax.ShapeDtypeStruct((2, depth, rep_size * block), low),
             jax.ShapeDtypeStruct((rep_size * 8, piece), wide),
         ),
-        in_specs=[anyplace] * 3 + [inside] * 3,
-        out_specs=(anyplace,) * 5,
+        in_specs=[anyplace] * 4 + [inside] * 3,
+        out_specs=(anyplace,) * 7,
         scratch_shapes=scratch,
         compiler_params=pltpu.CompilerParams(
             collective_id=0, has_side_effects=True, vmem_limit_bytes=62 << 20
@@ -1222,13 +1354,14 @@
             flops=flops, bytes_accessed=40 << 20, transcendentals=2 * all_rows * 2 * block
         ),
         name="experts",
-    )(arrived, inner_w, outer_w, counts_all, cents, gains_e)
+    )(arrived, inner_w, outer_w, w_outer, counts_all, cents, gains_e)
 
 
 def finish_kernel(
     exp_size,
     rep_size,
     home,
+    branch,
     pick,
     hidden,
     cotangent,
@@ -1240,13 +1373,13 @@
     context,
     attn_w,
     outer_send,
-    inner_send,
+    inner_sum,
     output,
     grad_tokens,
     shares,
     outer_recv,
-    inner_zero,
-    inner_one,
+    inner_recv,
+    branch_in,
     weights,
     grad_hidden,
     grad_attn,
@@ -1265,6 +1398,8 @@
     half_out,
     half_in,
     load_s,
+    branch_s,
+    branch_r,
     expert_s,
     expert_r,
     core_s,
@@ -1289,7 +1424,6 @@
     rows_n, width = tokens.shape
     half = width // 2
     block = width // exp_size
-    ff_block = inner_zero.shape[1] // rep_size
     core_peer = (rep_at ^ 1, exp_at)
     side_peer = (rep_at, exp_at ^ 1)
     row_peer = (rep_at ^ 2, exp_at)
@@ -1298,7 +1432,7 @@
     load.start()
 
     barrier = pltpu.get_barrier_semaphore()
-    for mask in range(1, rep_size):
+    for mask in range(1, 3):
         pl.semaphore_signal(
             barrier, inc=1, device_id=(rep_at ^ mask, exp_at), device_id_type=MESH
         )
@@ -1307,52 +1441,49 @@
     def _(at):
         pl.semaphore_signal(barrier, inc=1, device_id=(rep_at, exp_at ^ at), device_id_type=MESH)
 
-    pl.semaphore_wait(barrier, exp_size - 1 + rep_size - 1)
+    pl.semaphore_wait(barrier, exp_size + 1)
 
     outer_copy = remote(outer_send, outer_recv, expert_s.at[0], expert_r.at[0], row_peer)
 
-    def inner_copies(mask):
-        found = []
-        for part, target in enumerate((inner_zero, inner_one)):
-            at = rep_at ^ (2 * part)
-            cols = pl.ds(pl.multiple_of(at * ff_block, ff_block), ff_block)
-            source = inner_send.at[mask, part]
-            if mask == 0:
-                found.append(
-                    pltpu.make_async_copy(source, target.at[:, cols], expert_s.at[1 + part])
-                )
-            else:
-                found.append(
-                    remote(
-                        source,
-                        target.at[:, cols],
-                        expert_s.at[1 + 2 * mask + part],
-                        expert_r.at[1 + 2 * mask + part],
-                        (rep_at ^ mask, exp_at),
-                    )
-                )
-        return found
-
-    for mask in (2, 3, 1, 0):
-        for copy in inner_copies(mask):
-            copy.start()
+    inner_copy = remote(inner_sum.at[1], inner_recv, expert_s.at[1], expert_r.at[1], row_peer)
+    inner_copy.start()
     outer_copy.start()
 
-    all_slots = pick.shape[0]
+    slots = pick.shape[0] // groups
+
+    def slot_rows(at):
+        return pl.ds(pl.multiple_of(at * slots, slots), slots)
+
+    def branch_copy(dest):
+        return remote(
+            branch.at[slot_rows(dest)],
+            branch_in.at[slot_rows(group)],
+            branch_s.at[dest],
+            branch_r.at[group],
+            (rep_at, dest),
+        )
+
+    branch_own = pltpu.make_async_copy(
+        branch.at[slot_rows(exp_at)], branch_in.at[slot_rows(group)], branch_s.at[exp_at]
+    )
+
+    @pl.when(side == 1)
+    def _():
+        branch_own.start()
+
+        @pl.loop(1, exp_size)
+        def _(at):
+            branch_copy(exp_at ^ at).start()
 
     @pl.loop(0, width // TILE)
     def _(step):
         cols = pl.ds(pl.multiple_of(step * TILE, TILE), TILE)
         back = lax.dot_general(
-            pick[...], home[:all_slots, cols], (((0,), (0,)), ((), ())), preferred_element_type=wide
+            pick[...], home[:, cols], (((0,), (0,)), ((), ())), preferred_element_type=wide
         )
         grad = cotangent[:, cols].astype(wide) + back
         grad_hidden[:, cols] = grad
         grad_attn[:, cols] = grad.astype(low)
-        branch = lax.dot_general(
-            pick[...], home[all_slots:, cols], (((0,), (0,)), ((), ())), preferred_element_type=wide
-        )
-        output[:, cols] = (hidden[:, cols] + branch).astype(low)
 
     own_half = pl.ds(pl.multiple_of(core * half, half), half)
     other_half = pl.ds(pl.multiple_of((1 - core) * half, half), half)
@@ -1508,7 +1639,6 @@
         share_start(at, normed_a, grads3.at[at])
     for at in range(3):
         share_side(at)
-    share_row(3)
 
     @pl.loop(0, width // TILE)
     def _(step):
@@ -1519,8 +1649,6 @@
                 grads3[at], weights[at, rows, :], (((1,), (1,)), ((), ())), preferred_element_type=wide
             )
         grad_tokens[:, rows] = grad_normed
-
-    share_half(3)
 
     @pl.loop(0, rows_n // ROWS)
     def _(step):
@@ -1534,15 +1662,51 @@
         ) * inv_scale
         grad_tokens[here, :] = grad_hidden[here, :] + grad_in
 
+    share_row(3)
     for at in range(3):
         share_line(at)
-    share_end(3)
+
+    def branch_wait(which):
+        remote(
+            branch.at[slot_rows(which)],
+            branch_in.at[slot_rows(which)],
+            branch_s.at[which],
+            branch_r.at[which],
+            side_peer,
+        ).wait_recv()
+
+    @pl.when(side == 0)
+    def _():
+        branch_wait(group)
+
+    @pl.when(side == 1)
+    def _():
+        branch_own.wait()
+
+    @pl.loop(1, groups)
+    def _(at):
+        branch_wait(group ^ at)
+
+    @pl.loop(0, width // TILE)
+    def _(step):
+        cols = pl.ds(pl.multiple_of(step * TILE, TILE), TILE)
+        rows = lax.dot_general(
+            pick[...], branch_in[:, cols], (((0,), (0,)), ((), ())), preferred_element_type=wide
+        )
+        output[:, cols] = (hidden[:, cols] + rows).astype(low)
+
     for at in range(3):
         share_row(at)
-    for at in range(3):
+    for at in (3, 0, 1, 2):
         share_half(at)
-    for at in range(3):
+    for at in (3, 0, 1, 2):
         share_end(at)
+
+    @pl.when(side == 1)
+    def _():
+        @pl.loop(1, exp_size)
+        def _(at):
+            branch_copy(exp_at ^ at).wait_send()
 
     for at in range(4):
         core_copy(at).wait_send()
@@ -1554,20 +1718,17 @@
         def _(mask):
             line_copy(at, mask).wait_send()
 
-    for mask in range(rep_size):
-        for copy in inner_copies(mask):
-            copy.wait()
+    inner_copy.wait()
     outer_copy.wait()
 
 
-def run_finish(exp_size, rep_size, home, pick, hidden, cotangent, tokens, gain_row, qkv, probs, normed_a, context, attn_w, outer_send, inner_send):
+def run_finish(exp_size, rep_size, home, branch, pick, hidden, cotangent, tokens, gain_row, qkv, probs, normed_a, context, attn_w, outer_send, inner_sum):
     rows_n, width = tokens.shape
     low = jnp.bfloat16
     wide = jnp.float32
     half = width // 2
     groups = exp_size // 2
     block = width // exp_size
-    depth, ff_block = inner_send.shape[2:]
     anyplace = pl.BlockSpec(memory_space=pl.ANY)
     inside = pl.BlockSpec(memory_space=pltpu.VMEM)
     dma = pltpu.SemaphoreType.DMA
@@ -1579,12 +1740,12 @@
             shape((rows_n, width), wide),
             shape((4, block, width), wide),
             shape(outer_send.shape, low),
-            shape((depth, rep_size * ff_block), low),
-            shape((depth, rep_size * ff_block), low),
+            shape(inner_sum.shape[1:], low),
         ),
-        in_specs=[inside] * 10 + [anyplace] * 3,
-        out_specs=(inside,) * 3 + (anyplace,) * 3,
+        in_specs=[inside, anyplace] + [inside] * 9 + [anyplace] * 3,
+        out_specs=(inside,) * 3 + (anyplace,) * 2,
         scratch_shapes=[
+            pltpu.VMEM(pick.shape[:1] + (width,), low),
             pltpu.VMEM((4, width, width), low),
             pltpu.VMEM((rows_n, width), wide),
             pltpu.VMEM((rows_n, width), low),
@@ -1603,8 +1764,10 @@
             pltpu.VMEM((4, block, half), wide),
             pltpu.VMEM((4, block, half), wide),
             dma((1,)),
-            dma((1 + 2 * rep_size,)),
-            dma((1 + 2 * rep_size,)),
+            dma((exp_size,)),
+            dma((groups,)),
+            dma((2,)),
+            dma((2,)),
             dma((4,)),
             dma((4,)),
             dma((4,)),
@@ -1625,6 +1788,7 @@
         name="finish",
     )(
         home,
+        branch,
         pick,
         hidden,
         cotangent,
@@ -1636,7 +1800,7 @@
         context,
         attn_w,
         outer_send,
-        inner_send,
+        inner_sum,
     )
 
 
@@ -1691,7 +1855,7 @@
         expert_gain,
         centroids,
     )
-    home, outer_keep, outer_send, inner_send, centre_parts = run_experts(
+    home, branch, outer_keep, outer_send, outer_got, inner_sum, centre_parts = run_experts(
         exp_size,
         rep_size,
         slots,
@@ -1699,14 +1863,16 @@
         arrived,
         inner_w,
         outer_w,
+        w_outer[0],
         counts_all,
         cents,
         gains_e,
     )
-    output, grad_tokens, shares, outer_recv, inner_zero, inner_one = run_finish(
+    output, grad_tokens, shares, outer_recv, inner_recv = run_finish(
         exp_size,
         rep_size,
         home,
+        branch,
         pick,
         hidden,
         cotangent,
@@ -1718,11 +1884,13 @@
         context,
         attn_w,
         outer_send,
-        inner_send,
+        inner_sum,
     )
     grad_centroids = jnp.sum(centre_parts.reshape(rep_size, 8, -1)[:, 0], axis=0)[None]
-    grad_w_outer = (outer_keep + outer_recv.astype(wide))[None]
-    summed = inner_zero.astype(wide) + inner_one.astype(wide)
+    grad_w_outer = (
+        outer_keep + jnp.concatenate([outer_got, outer_recv], axis=0).astype(wide)
+    )[None]
+    summed = inner_sum[0].astype(wide) + inner_recv.astype(wide)
     grad_w_inner = summed[None]
     grad_expert_gain = jnp.sum(summed * w_inner[0].astype(wide), axis=1)[None] / expert_gain.astype(
         wide

time: 417 us -> 351 us (0.84)
  Pallas kernels: 399 us -> 335 us
    pallas_call x1, Pallas kernels: 144 us -> 105 us  [run_finish(): pl.pallas_call(functools.partial(finish_kernel, exp_size, rep_size), out_...]
    pallas_call x1, Pallas kernels: 151 us -> 126 us  [run_experts(): pl.pallas_call(functools.partial(expert_kernel, exp_size, rep_size, slots...]
where the time goes in v5:
time: 351 us
  Pallas kernels  335 us (95%)
  other arithmetic  12.2 us (3%)
    pallas_call x1, Pallas kernels, run_experts(): pl.pallas_call(functools.partial(expert_kernel, exp_size, rep_size, slots...  126 us
    pallas_call x1, Pallas kernels, run_finish(): pl.pallas_call(functools.partial(finish_kernel, exp_size, rep_size), out_...  105 us
    pallas_call x1, Pallas kernels, run_attend(): pl.pallas_call(functools.partial(attend_kernel, exp_size, rep_size, slots...  104 us

profile of v5, /device:TPU:11, one launch (start us, length us, event | category | flops | bytes accessed | tf_op | source)
XLA Modules:
  0.0 350.9 jit_solution(9811957082250403556)
XLA Ops:
  0.6 104.5 %attend.1 = (bf16[4,1024,1024]{2,1,0:T(8,128)(2,1)}, bf16[1024,2048]{1,0:T(8,128)(2,1)}, bf16[1792,1024]{1,0:T(8,128)(2,1)}, bf16[768,1024]{1,0:T(8,128)(2,1)}, ...) custom-call(bf16[256,1024]{1,0:T(8,128)(2,1)} %tokens.3, ...), custom_call_target="tpu_custom_call" | custom-call | flops 2684354560 | bytes 41943040 | tf_op jit(solution)/shard_map/attend/pallas_call | solution.py:613
  105.1 125.9 %experts.1 = (bf16[384,1024]{1,0:T(8,128)(2,1)}, bf16[768,1024]{1,0:T(8,128)(2,1)}, f32[1024,1024]{1,0:T(8,128)}, bf16[512,1024]{1,0:T(8,128)(2,1)}, bf16[512,10...) custom-call(bf16[768,1024]{1,0:T(8,128)(2,1)} %get-tuple-element.37.arrived_h, ...), custom_call_target="tpu_custom_call" | custom-call | flops 25769803776 | bytes 41943040 | tf_op jit(solution)/shard_map/experts/pallas_call | solution.py:1336
  231.0 0.0 copy-start.4
  231.1 105.0 %finish.1 = (bf16[256,1024]{1,0:T(8,128)(2,1)}, f32[256,1024]{1,0:T(8,128)}, f32[4,128,1024]{2,1,0:T(8,128)}, bf16[512,1024]{1,0:T(8,128)(2,1)}, bf16[256,4096]{1,0:T(8,128)(2,1)}) custom-call(bf16[384,1024]{1,0:T(8,128)(2,1)} %get-tuple-element.43.home, bf16[768,1024]{1,0:T(8,128)(2,1)} %get-tuple-element.44.branch, ...), custom_call_target="tpu_custom_call" | custom-call | flops 5368709120 | bytes 62914560 | tf_op jit(solution)/shard_map/finish/pallas_call | solution.py:1736
  336.0 0.0 copy-done.4
  336.0 0.0 copy-start
  336.0 0.0 copy-start.2
  336.0 0.0 copy-start.3
  336.1 5.7 %add_bitcast_fusion = f32[1,1024,1024]{2,1,0:T(8,128)} fusion(f32[1024,1024]{1,0:T(8,128)} %get-tuple-element.59, bf16[512,1024]{1,0:T(8,128)(2,1)} %get-tuple-element.61, bf16[512,1024]{1,0:T(8,128)(2,1)S(1)} %copy-done.4), kind=kLoop, calls=%fused_computation.2 | loop fusion | flops 5242880 | bytes 10485760 | tf_op jit(solution)/shard_map/broadcast_in_dim | solution.py:1890
  341.8 1.2 slice_reduce_fusion
  343.0 0.0 copy-done
  343.0 0.0 copy-done.2
  343.0 0.0 copy-done.3
  343.0 0.0 copy-start.10
  343.0 0.0 copy-start.1
  343.0 0.0 copy-start.7
  343.1 0.0 copy-start.8
  343.1 0.0 copy-start.9
  343.1 2.8 multiply_reduce_fusion
  345.9 0.0 copy-start.11
  345.9 0.0 copy-start.6
  345.9 0.0 copy-start.5
  345.9 0.0 copy-done.10
  345.9 0.6 convert_divide_fusion
  346.5 0.0 copy-done.1
  346.5 0.8 slice_bitcast_fusion
  347.3 0.0 copy-done.7
  347.3 0.0 copy-done.8
  347.3 0.0 copy-done.9
  347.3 1.3 multiply_reduce_fusion.1
  348.6 0.0 copy-done.11
  348.6 0.5 convert_divide_fusion.1
  349.2 0.0 copy-done.6
  349.2 0.8 copy.26
  350.0 0.0 copy-done.5
  350.0 1.0 copy.27
Async XLA Ops:
  231.0 105.0 %copy-start.4 = (bf16[512,1024]{1,0:T(8,128)(2,1)S(1)}, bf16[512,1024]{1,0:T(8,128)(2,1)}, u32[]{:S(2)}) copy-start(bf16[512,1024]{1,0:T(8,128)(2,1)} %get-tuple-element.60) | copy-start | bytes 3145732
  336.0 7.0 %copy-start = (bf16[2,256,4096]{2,1,0:T(8,128)(2,1)S(1)}, bf16[2,256,4096]{2,1,0:T(8,128)(2,1)}, u32[]{:S(2)}) copy-start(bf16[2,256,4096]{2,1,0:T(8,128)(2,1)} %get-tuple-element.54.inner_sum) | copy-start | bytes 12582916
  336.0 7.0 %copy-start.2 = (bf16[1,256,4096]{2,1,0:T(8,128)(2,1)S(1)}, bf16[1,256,4096]{2,1,0:T(8,128)(2,1)}, u32[]{:S(2)}) copy-start(bf16[1,256,4096]{2,1,0:T(8,128)(2,1)} %param.22) | copy-start | bytes 6291460
  336.0 7.0 %copy-start.3 = (bf16[256,4096]{1,0:T(8,128)(2,1)S(1)}, bf16[256,4096]{1,0:T(8,128)(2,1)}, u32[]{:S(2)}) copy-start(bf16[256,4096]{1,0:T(8,128)(2,1)} %get-tuple-element.58) | copy-start | bytes 6291460
  343.0 2.9 copy-start.10
  343.0 3.5 copy-start.1
  343.0 4.3 %copy-start.7 = (bf16[128,1024]{1,0:T(8,128)(2,1)S(1)}, bf16[128,1024]{1,0:T(8,128)(2,1)}, u32[]{:S(2)}) copy-start(bf16[128,1024]{1,0:T(8,128)(2,1)} %w_query.1) | copy-start | bytes 786436
  343.1 4.3 %copy-start.8 = (bf16[128,1024]{1,0:T(8,128)(2,1)S(1)}, bf16[128,1024]{1,0:T(8,128)(2,1)}, u32[]{:S(2)}) copy-start(bf16[128,1024]{1,0:T(8,128)(2,1)} %w_key.1) | copy-start | bytes 786436
  343.1 4.3 %copy-start.9 = (bf16[128,1024]{1,0:T(8,128)(2,1)S(1)}, bf16[128,1024]{1,0:T(8,128)(2,1)}, u32[]{:S(2)}) copy-start(bf16[128,1024]{1,0:T(8,128)(2,1)} %w_value.1) | copy-start | bytes 786436
  345.9 2.7 copy-start.11
  345.9 3.3 copy-start.6
  345.9 4.1 %copy-start.5 = (f32[256,1024]{1,0:T(8,128)S(1)}, f32[256,1024]{1,0:T(8,128)}, u32[]{:S(2)}) copy-start(f32[256,1024]{1,0:T(8,128)} %get-tuple-element.87) | copy-start | bytes 3145732

commit v6 on v5

--- a/solution.py
+++ b/solution.py
@@ -19,7 +19,7 @@
 MESH = pl.DeviceIdType.MESH
 TILE = 256
 ROWS = 64
-BIG = 512
+BIG = 1024
 
 
 def remote(src, dst, send_sem, recv_sem, device):
@@ -142,13 +142,11 @@
 
     outer_copy = remote(
         w_outer.at[: ff_block - DEFER],
-        outer_w.at[ff_block:],
+        outer_w,
         weight_s.at[0],
         weight_r.at[0],
         (rep_at ^ 2, exp_at),
     )
-    outer_own = pltpu.make_async_copy(w_outer, outer_w.at[:ff_block], own_s.at[5])
-    outer_own.start()
 
     for load in own_loads:
         load.wait()
@@ -275,11 +273,7 @@
             source = w_inner.at[:, ff_cols(dest ^ (2 * part))]
             cols = slice(part * ff_block, (part + 1) * ff_block)
             at = 1 + 2 * mask + part
-            if mask == 0:
-                found.append(
-                    pltpu.make_async_copy(source, inner_w.at[inner_rows, cols], weight_s.at[at])
-                )
-            elif mask == 3:
+            if mask == 3:
                 found.append(
                     remote(
                         source,
@@ -310,7 +304,7 @@
         core_peer,
     )
 
-    for mask in (3, 2, 1, 0):
+    for mask in (3, 2, 1):
         for copy in inner_copies(mask):
             copy.start()
     outer_copy.start()
@@ -432,9 +426,6 @@
         gather_step(0, step)
 
     gather_end(0)
-    for copy in inner_copies(3):
-        copy.wait_recv()
-    forward_copy.start()
 
     def slot_rows(at):
         return pl.ds(pl.multiple_of(at * slots, slots), slots)
@@ -541,12 +532,14 @@
         ).astype(low)
 
     dispatch(packed_x, 0)
+    for copy in inner_copies(3):
+        copy.wait_recv()
+    forward_copy.start()
 
     store.wait()
     outer_copy.wait()
-    outer_own.wait()
     forward_copy.wait()
-    for mask in range(rep_size):
+    for mask in range(1, rep_size):
         for copy in inner_copies(mask):
             if mask == 3:
                 copy.wait_send()
@@ -615,7 +608,7 @@
         out_shape=(
             shape((4, width, width), low),
             shape((width, 2 * ff_block), low),
-            shape((2 * ff_block - DEFER, width), low),
+            shape((ff_block - DEFER, width), low),
             shape((exp_size * slots, width), low),
             shape((exp_size * 16, 128), wide),
             shape((2 * rep_size * 8, cent.shape[1]), wide),
@@ -680,6 +673,7 @@
     arrived_h,
     inner_h,
     outer_h,
+    w_inner,
     w_outer,
     counts_all,
     cents,
@@ -706,10 +700,8 @@
     active,
     slope,
     states,
-    fwd_send,
-    fwd_recv,
-    bwd_send,
-    bwd_recv,
+    part_send,
+    part_recv,
     hop,
     back,
     spread,
@@ -727,10 +719,10 @@
     norm_r,
     state_s,
     state_r,
-    fwd_s,
-    fwd_r,
-    bwd_s,
-    bwd_r,
+    part_s,
+    part_r,
+    grad_s,
+    grad_r,
     hop_s,
     hop_r,
     gate_s,
@@ -768,11 +760,24 @@
 
     loads = [
         pltpu.make_async_copy(arrived_h, arrived, load_sem.at[0]),
-        pltpu.make_async_copy(inner_h, inner_w, load_sem.at[1]),
-        pltpu.make_async_copy(
-            outer_h, outer_w.at[: outer_h.shape[0]], load_sem.at[2]
-        ),
+        pltpu.make_async_copy(w_outer, outer_w.at[:block], load_sem.at[1]),
+        pltpu.make_async_copy(outer_h, outer_w.at[block : 2 * block - DEFER], load_sem.at[2]),
     ]
+    for side in range(2):
+        at = rep_at ^ (2 * side)
+        loads.append(
+            pltpu.make_async_copy(
+                w_inner.at[:, pl.ds(pl.multiple_of(at * block, block), block)],
+                inner_w.at[inner_rows(0), side * block : (side + 1) * block],
+                load_sem.at[3 + side],
+            )
+        )
+    for mask in range(1, rep_size):
+        loads.append(
+            pltpu.make_async_copy(
+                inner_h.at[inner_rows(mask)], inner_w.at[inner_rows(mask)], load_sem.at[4 + mask]
+            )
+        )
     for load in loads:
         load.start()
 
@@ -849,7 +854,76 @@
     late_copy.start()
 
     gate_copy = remote(gates, gates, gate_s.at[0], gate_r.at[0], side_peer)
-    grad_copy = remote(gate_grads, gate_grads, gate_s.at[1], gate_r.at[1], side_peer)
+
+    def part_rows(at):
+        return pl.ds(pl.multiple_of(at * part, part), part)
+
+    def both_rows(at):
+        return pl.ds(pl.multiple_of(at * 2 * part, 2 * part), 2 * part)
+
+    def own_slice(at):
+        return pl.ds(pl.multiple_of(at * 2 * part + part, part), part)
+
+    def other_slice(at):
+        return pl.ds(pl.multiple_of(at * 2 * part, part), part)
+
+    def grad_copy(at):
+        rows = part_rows(at)
+        return remote(
+            gate_grads.at[rows], gate_grads.at[rows], grad_s.at[at], grad_r.at[at], side_peer
+        )
+
+    def hop_forward(at):
+        rows = part_rows(at)
+        return remote(hop.at[rows], own_x.at[rows], hop_s.at[at], hop_r.at[at], side_peer)
+
+    def hop_backward(at):
+        return remote(
+            hop.at[part_rows(at)], states.at[own_slice(at)], hop_s.at[at], hop_r.at[at], side_peer
+        )
+
+    def norm_copy(at):
+        return remote(
+            normed.at[own_slice(at)], normed.at[other_slice(at)], norm_s.at[at], norm_r.at[at], core_peer
+        )
+
+    def state_copy(at):
+        return remote(
+            states.at[own_slice(at)], states.at[other_slice(at)], state_s.at[at], state_r.at[at], core_peer
+        )
+
+    def part_copy(kind, at):
+        count = kind * CHUNKS + at
+        rows = part_rows(count)
+        return remote(
+            part_send.at[rows], part_recv.at[rows], part_s.at[count], part_r.at[count], core_peer
+        )
+
+    def norm_rows(at):
+        @pl.loop(0, part // ROWS)
+        def _(step):
+            off = pl.multiple_of(step * ROWS, ROWS)
+            unit, _ = row_stats(own_x[pl.ds(at * part + off, ROWS), :].astype(wide))
+            normed[pl.ds(at * 2 * part + part + off, ROWS), :] = (unit * gain[...]).astype(low)
+
+        norm_copy(at).start()
+
+    steps = 2 * CHUNKS
+
+    def is_forward(step):
+        early = step < CHUNKS
+        mixed = (step == 0) | ((step % 2 == 1) & (step < steps - 1))
+        return (first & early) | (second & mixed)
+
+    def chunk_at(step):
+        of_first = jnp.where(step < CHUNKS, step, step - CHUNKS)
+        mixed = (step == 0) | ((step % 2 == 1) & (step < steps - 1))
+        of_second = jnp.where(
+            mixed,
+            (step + 1) // 2,
+            jnp.where(step == steps - 1, CHUNKS - 1, (step - 2) // 2),
+        )
+        return jnp.where(first, of_first, of_second)
 
     @pl.when(first)
     def _():
@@ -859,114 +933,195 @@
         gates[...] = jax.nn.sigmoid(logit)
         gate_copy.start()
 
-    def hop_forward(at):
-        rows = pl.ds(at * part, part)
-        return remote(hop.at[rows], own_x.at[rows], hop_s.at[at], hop_r.at[at], side_peer)
-
-    def own_slice(at):
-        return pl.ds(at * 2 * part + part, part)
-
-    def other_slice(at):
-        return pl.ds(at * 2 * part, part)
-
-    def hop_backward(at):
-        rows = pl.ds(at * part, part)
-        return remote(
-            hop.at[rows], states.at[own_slice(at)], hop_s.at[at], hop_r.at[at], side_peer
-        )
-
-    for load in loads[1:]:
-        load.wait()
-
-    def forward(at):
-        base = at * part
-
-        @pl.when(second)
-        def _():
-            hop_forward(at).wait_recv()
-
-        @pl.loop(0, part // ROWS)
-        def _(step):
-            off = pl.multiple_of(step * ROWS, ROWS)
-            unit, _ = row_stats(own_x[pl.ds(base + off, ROWS), :].astype(wide))
-            normed[pl.ds(at * 2 * part + part + off, ROWS), :] = (unit * gain[...]).astype(low)
-
-        norm_copy = remote(
-            normed.at[own_slice(at)], normed.at[other_slice(at)], norm_s.at[at], norm_r.at[at], core_peer
-        )
-        norm_copy.start()
-        norm_copy.wait_recv()
-        if at == 0:
-            late_copy.wait_recv()
-
-        @pl.loop(0, wide_ff // BIG)
-        def _(step):
-            cols = pl.ds(pl.multiple_of(step * BIG, BIG), BIG)
-            inner = jnp.dot(
-                normed[pl.ds(at * 2 * part, 2 * part), :],
-                inner_w[:, cols],
-                preferred_element_type=wide,
-            )
-            normal = 0.5 * (1.0 + lax.erf(inner * ROOT_HALF))
-            active[pl.ds(at * 2 * part, 2 * part), cols] = (inner * normal).astype(low)
-            slope[pl.ds(at * 2 * part, 2 * part), cols] = (
-                normal + inner * jnp.exp(-0.5 * inner * inner) * INV_ROOT_TAU
-            ).astype(low)
-
-        @pl.loop(0, width // BIG)
-        def _(step):
-            cols = pl.ds(pl.multiple_of(step * BIG, BIG), BIG)
-            both = jnp.dot(
-                active[pl.ds(at * 2 * part, 2 * part), :], outer_w[:, cols], preferred_element_type=wide
-            )
-            fwd_send[pl.ds(base, part), cols] = both[:part].astype(low)
-            acc[:, cols] = both[part:]
-
-        rows = pl.ds(base, part)
-        copy = remote(fwd_send.at[rows], fwd_recv.at[rows], fwd_s.at[at], fwd_r.at[at], core_peer)
-        copy.start()
-
-        copy.wait_recv()
-
-        @pl.when(first)
-        def _():
+        @pl.loop(0, CHUNKS)
+        def _(at):
+            norm_rows(at)
+
+    @pl.when(second)
+    def _():
+        gate_copy.wait_recv()
+
+        @pl.loop(0, CHUNKS)
+        def _(at):
             @pl.loop(0, part // ROWS)
             def _(step):
                 off = pl.multiple_of(step * ROWS, ROWS)
-                here = pl.ds(base + off, ROWS)
-                result = (
-                    own_x[here, :].astype(wide)
-                    + acc[pl.ds(off, ROWS), :]
-                    + fwd_recv[here, :].astype(wide)
-                )
+                here = pl.ds(at * part + off, ROWS)
+                states[pl.ds(at * 2 * part + part + off, ROWS), :] = (
+                    gates[here, :][:, :1] * own_cot[here, :].astype(wide)
+                ).astype(low)
+
+            state_copy(at).start()
+
+        hop_forward(0).wait_recv()
+        norm_rows(0)
+
+    for load in loads[1:]:
+        load.wait()
+    late_copy.wait_recv()
+    centre_grad[...] = jnp.zeros_like(centre_grad)
+
+    def finish_forward(step, at):
+        part_copy(0, at).wait_recv()
+
+        @pl.loop(0, part // ROWS)
+        def _(tile):
+            off = pl.multiple_of(tile * ROWS, ROWS)
+            here = pl.ds(at * part + off, ROWS)
+            result = (
+                own_x[here, :].astype(wide)
+                + acc[step % 2, pl.ds(off, ROWS), :]
+                + part_recv[here, :].astype(wide)
+            )
+
+            @pl.when(first)
+            def _():
                 hop[here, :] = result.astype(low)
 
-            hop_forward(at).start()
-
-        @pl.when(second)
-        def _():
-            if at == 0:
-                gate_copy.wait_recv()
-
-            @pl.loop(0, part // ROWS)
-            def _(step):
-                off = pl.multiple_of(step * ROWS, ROWS)
-                here = pl.ds(base + off, ROWS)
-                result = (
-                    own_x[here, :].astype(wide)
-                    + acc[pl.ds(off, ROWS), :]
-                    + fwd_recv[here, :].astype(wide)
-                )
+            @pl.when(second)
+            def _():
                 cot = own_cot[here, :].astype(wide)
-                gate = gates[here, :][:, :1]
-                back[here, :] = (gate * result).astype(low)
+                back[here, :] = (gates[here, :][:, :1] * result).astype(low)
                 gate_grads[here, :] = jnp.broadcast_to(
                     jnp.sum(cot * result, axis=1, keepdims=True), (ROWS, gate_grads.shape[1])
                 )
-                states[pl.ds(at * 2 * part + part + off, ROWS), :] = (gate * cot).astype(low)
-
-    for at in range(CHUNKS):
-        forward(at)
+
+        @pl.when(first)
+        def _():
+            hop_forward(at).start()
+
+        @pl.when(second)
+        def _():
+            grad_copy(at).start()
+
+    def finish_backward(step, at):
+        part_copy(1, at).wait_recv()
+
+        @pl.when(first)
+        def _():
+            grad_copy(at).wait_recv()
+
+        @pl.loop(0, part // ROWS)
+        def _(tile):
+            off = pl.multiple_of(tile * ROWS, ROWS)
+            here = pl.ds(at * part + off, ROWS)
+            rows_in = own_x[here, :].astype(wide)
+            unit, inv_scale = row_stats(rows_in)
+            grad_unit = (
+                acc[step % 2, pl.ds(off, ROWS), :]
+                + part_recv[pl.ds((CHUNKS + at) * part + off, ROWS), :].astype(wide)
+            ) * gain[...]
+            grad_in = (
+                grad_unit
+                - jnp.mean(grad_unit, axis=-1, keepdims=True)
+                - unit * jnp.mean(grad_unit * unit, axis=-1, keepdims=True)
+            ) * inv_scale
+            gate = gates[here, :][:, :1]
+
+            @pl.when(second)
+            def _():
+                state = gate * own_cot[here, :].astype(wide) + grad_in
+                hop[here, :] = state.astype(low)
+
+            @pl.when(first)
+            def _():
+                state = states[pl.ds(at * 2 * part + part + off, ROWS), :].astype(wide) + grad_in
+                grad_logit = gate_grads[here, :][:, :1] * gate * (1.0 - gate)
+                back[here, :] = (state + grad_logit * cent_b[:1, :].astype(wide)).astype(low)
+                centre_grad[...] += jnp.sum(grad_logit * rows_in, axis=0, keepdims=True)
+
+        @pl.when(second)
+        def _():
+            hop_backward(at).start()
+
+    def finish(step):
+        at = chunk_at(step)
+        forward = is_forward(step)
+
+        @pl.when(forward)
+        def _():
+            finish_forward(step, at)
+
+        @pl.when(jnp.logical_not(forward))
+        def _():
+            finish_backward(step, at)
+
+    @pl.loop(0, steps)
+    def _(step):
+        at = chunk_at(step)
+        forward = is_forward(step)
+        rows = both_rows(at)
+
+        @pl.when(forward)
+        def _():
+            norm_copy(at).wait_recv()
+
+            @pl.loop(0, wide_ff // BIG)
+            def _(tile):
+                cols = pl.ds(pl.multiple_of(tile * BIG, BIG), BIG)
+                inner = jnp.dot(normed[rows, :], inner_w[:, cols], preferred_element_type=wide)
+                normal = 0.5 * (1.0 + lax.erf(inner * ROOT_HALF))
+                active[rows, cols] = (inner * normal).astype(low)
+                slope[rows, cols] = (
+                    normal + inner * jnp.exp(-0.5 * inner * inner) * INV_ROOT_TAU
+                ).astype(low)
+
+        @pl.when(jnp.logical_not(forward))
+        def _():
+            state_copy(at).wait_recv()
+
+            @pl.loop(0, wide_ff // BIG)
+            def _(tile):
+                cols = pl.ds(pl.multiple_of(tile * BIG, BIG), BIG)
+                grad_active = lax.dot_general(
+                    states[rows, :],
+                    outer_w[cols, :],
+                    (((1,), (1,)), ((), ())),
+                    preferred_element_type=wide,
+                )
+                slope[rows, cols] = (grad_active * slope[rows, cols].astype(wide)).astype(low)
+
+        @pl.when((step > 0) & jnp.logical_not(first & (step == CHUNKS)))
+        def _():
+            finish(step - 1)
+
+        @pl.when(forward)
+        def _():
+            both = jnp.dot(active[rows, :], outer_w[...], preferred_element_type=wide)
+            part_send[part_rows(at), :] = both[:part].astype(low)
+            acc[step % 2] = both[part:]
+            part_copy(0, at).start()
+
+        @pl.when(jnp.logical_not(forward))
+        def _():
+            both = lax.dot_general(
+                slope[rows, :],
+                inner_w[...],
+                (((1,), (1,)), ((), ())),
+                preferred_element_type=wide,
+            )
+            part_send[part_rows(CHUNKS + at), :] = both[:part].astype(low)
+            acc[step % 2] = both[part:]
+            part_copy(1, at).start()
+
+        @pl.when(first & (step == CHUNKS - 1))
+        def _():
+            finish(step)
+
+        after = step + 1
+        after_at = chunk_at(after)
+
+        @pl.when(first & (after >= CHUNKS) & (after < steps))
+        def _():
+            hop_backward(after_at).wait_recv()
+            state_copy(after_at).start()
+
+        @pl.when(second & is_forward(after) & (after < steps))
+        def _():
+            hop_forward(after_at).wait_recv()
+            norm_rows(after_at)
+
+    finish(steps - 1)
 
     groups = exp_size // 2
 
@@ -1012,99 +1167,6 @@
 
         ret_copy(spread.at[slot_rows(exp_at + 1)], exp_at + 1).start()
         ret_own.start()
-
-    @pl.when(second)
-    def _():
-        grad_copy.start()
-
-    centre_grad[...] = jnp.zeros_like(centre_grad)
-
-    def backward(at):
-        base = at * part
-
-        @pl.when(first)
-        def _():
-            hop_backward(at).wait_recv()
-
-        copy = remote(
-            states.at[own_slice(at)], states.at[other_slice(at)], state_s.at[at], state_r.at[at], core_peer
-        )
-        copy.start()
-        copy.wait_recv()
-
-        @pl.loop(0, wide_ff // BIG)
-        def _(step):
-            rows = pl.ds(pl.multiple_of(step * BIG, BIG), BIG)
-            grad_active = lax.dot_general(
-                states[pl.ds(at * 2 * part, 2 * part), :],
-                outer_w[rows, :],
-                (((1,), (1,)), ((), ())),
-                preferred_element_type=wide,
-            )
-            here = pl.ds(at * 2 * part, 2 * part)
-            slope[here, rows] = (grad_active * slope[here, rows].astype(wide)).astype(low)
-
-        @pl.loop(0, width // BIG)
-        def _(step):
-            cols = pl.ds(pl.multiple_of(step * BIG, BIG), BIG)
-            both = lax.dot_general(
-                slope[pl.ds(at * 2 * part, 2 * part), :],
-                inner_w[cols, :],
-                (((1,), (1,)), ((), ())),
-                preferred_element_type=wide,
-            )
-            bwd_send[pl.ds(base, part), cols] = both[:part].astype(low)
-            acc[:, cols] = both[part:]
-
-        rows = pl.ds(base, part)
-        back_copy = remote(
-            bwd_send.at[rows], bwd_recv.at[rows], bwd_s.at[at], bwd_r.at[at], core_peer
-        )
-        back_copy.start()
-
-        back_copy.wait_recv()
-        if at == 0:
-
-            @pl.when(first)
-            def _():
-                grad_copy.wait_recv()
-
-        @pl.when(first)
-        def _():
-            hop_forward(at).wait_send()
-
-        @pl.loop(0, part // ROWS)
-        def _(step):
-            off = pl.multiple_of(step * ROWS, ROWS)
-            here = pl.ds(base + off, ROWS)
-            rows_in = own_x[here, :].astype(wide)
-            unit, inv_scale = row_stats(rows_in)
-            grad_unit = (acc[pl.ds(off, ROWS), :] + bwd_recv[here, :].astype(wide)) * gain[...]
-            grad_in = (
-                grad_unit
-                - jnp.mean(grad_unit, axis=-1, keepdims=True)
-                - unit * jnp.mean(grad_unit * unit, axis=-1, keepdims=True)
-            ) * inv_scale
-            gate = gates[here, :][:, :1]
-
-            @pl.when(second)
-            def _():
-                state = gate * own_cot[here, :].astype(wide) + grad_in
-                hop[here, :] = state.astype(low)
-
-            @pl.when(first)
-            def _():
-                state = states[pl.ds(at * 2 * part + part + off, ROWS), :].astype(wide) + grad_in
-                grad_logit = gate_grads[here, :][:, :1] * gate * (1.0 - gate)
-                back[here, :] = (state + grad_logit * cent_b[:1, :].astype(wide)).astype(low)
-                centre_grad[...] += jnp.sum(grad_logit * rows_in, axis=0, keepdims=True)
-
-        @pl.when(second)
-        def _():
-            hop_backward(at).start()
-
-    for at in range(CHUNKS):
-        backward(at)
 
     def eight_rows(at):
         return pl.ds(pl.multiple_of(at * 8, 8), 8)
@@ -1201,31 +1263,23 @@
     for mask, side in inner_order:
         inner_copy(mask, side).wait()
     for at in range(CHUNKS):
-        rows = pl.ds(at * part, part)
-        remote(
-            normed.at[own_slice(at)], normed.at[other_slice(at)], norm_s.at[at], norm_r.at[at], core_peer
-        ).wait_send()
-        remote(
-            states.at[own_slice(at)], states.at[other_slice(at)], state_s.at[at], state_r.at[at], core_peer
-        ).wait_send()
-        remote(
-            fwd_send.at[rows], fwd_recv.at[rows], fwd_s.at[at], fwd_r.at[at], core_peer
-        ).wait_send()
-        remote(
-            bwd_send.at[rows], bwd_recv.at[rows], bwd_s.at[at], bwd_r.at[at], core_peer
-        ).wait_send()
+        norm_copy(at).wait_send()
+        state_copy(at).wait_send()
+        part_copy(0, at).wait_send()
+        part_copy(1, at).wait_send()
+
+        @pl.when(first)
+        def _():
+            hop_forward(at).wait_send()
 
         @pl.when(second)
         def _():
             hop_backward(at).wait_send()
+            grad_copy(at).wait_send()
 
     @pl.when(first)
     def _():
         gate_copy.wait_send()
-
-    @pl.when(second)
-    def _():
-        grad_copy.wait_send()
 
     @pl.when(first)
     def _():
@@ -1279,7 +1333,7 @@
 
 
 def run_experts(
-    exp_size, rep_size, slots, own_rows, arrived, inner_w, outer_w, w_outer, counts_all, cents, gains_e
+    exp_size, rep_size, slots, own_rows, arrived, inner_w, outer_w, w_inner, w_outer, counts_all, cents, gains_e
 ):
     width = arrived.shape[1]
     depth = width // rep_size
@@ -1310,26 +1364,26 @@
         pltpu.VMEM((all_rows, 2 * block), low),
         pltpu.VMEM((all_rows, 2 * block), low),
         pltpu.VMEM((all_rows, width), low),
-        pltpu.VMEM((own_rows, width), low),
-        pltpu.VMEM((own_rows, width), low),
-        pltpu.VMEM((own_rows, width), low),
-        pltpu.VMEM((own_rows, width), low),
+        pltpu.VMEM((2 * own_rows, width), low),
+        pltpu.VMEM((2 * own_rows, width), low),
         pltpu.VMEM((own_rows, width), low),
         pltpu.VMEM((own_rows, width), low),
         pltpu.VMEM((total, width), low),
         pltpu.VMEM((total // 2, width), low),
-        pltpu.VMEM((part, width), wide),
+        pltpu.VMEM((2, part, width), wide),
         pltpu.VMEM((own_rows, 128), wide),
         pltpu.VMEM((own_rows, 128), wide),
         pltpu.VMEM((block, width), wide),
         pltpu.VMEM((block, width), low),
         pltpu.VMEM((rep_size, 2, depth, block), low),
-        dma((3,)),
+        dma((8,)),
         dma((2 * rep_size,)),
         dma((rep_size,)),
     ]
-    scratch += [dma((CHUNKS,)) for _ in range(10)]
-    scratch += [dma((2,)), dma((2,)), dma((exp_size,)), dma((exp_size // 2,))]
+    scratch += [dma((CHUNKS,)) for _ in range(4)]
+    scratch += [dma((2 * CHUNKS,)), dma((2 * CHUNKS,))]
+    scratch += [dma((CHUNKS,)) for _ in range(4)]
+    scratch += [dma((1,)), dma((1,)), dma((exp_size,)), dma((exp_size // 2,))]
     scratch += [dma((exp_size // 2,)), dma((exp_size // 2,)), dma((2,)), dma((2,)), dma((n_out,))]
     scratch += [dma((2 * rep_size,)), dma((2 * rep_size,))]
     flops = 2 * all_rows * width * 2 * block * 6
@@ -1344,7 +1398,7 @@
             jax.ShapeDtypeStruct((2, depth, rep_size * block), low),
             jax.ShapeDtypeStruct((rep_size * 8, piece), wide),
         ),
-        in_specs=[anyplace] * 4 + [inside] * 3,
+        in_specs=[anyplace] * 5 + [inside] * 3,
         out_specs=(anyplace,) * 7,
         scratch_shapes=scratch,
         compiler_params=pltpu.CompilerParams(
@@ -1354,7 +1408,7 @@
             flops=flops, bytes_accessed=40 << 20, transcendentals=2 * all_rows * 2 * block
         ),
         name="experts",
-    )(arrived, inner_w, outer_w, w_outer, counts_all, cents, gains_e)
+    )(arrived, inner_w, outer_w, w_inner, w_outer, counts_all, cents, gains_e)
 
 
 def finish_kernel(
@@ -1863,6 +1917,7 @@
         arrived,
         inner_w,
         outer_w,
+        w_inner[0],
         w_outer[0],
         counts_all,
         cents,

time: 351 us -> 334 us (0.952)
  Pallas kernels: 335 us -> 318 us
    pallas_call x1, Pallas kernels: 126 us -> 112 us  [run_experts(): pl.pallas_call(functools.partial(expert_kernel, exp_size, rep_size, slots...]
where the time goes in v6:
time: 334 us; the launch traced here: 333 us
  Pallas kernels  318 us (95%)
  other arithmetic  12.2 us (4%)
    pallas_call x1, Pallas kernels, run_experts(): pl.pallas_call(functools.partial(expert_kernel, exp_size, rep_size, slots...  112 us
    pallas_call x1, Pallas kernels, run_finish(): pl.pallas_call(functools.partial(finish_kernel, exp_size, rep_size), out_...  104 us
    pallas_call x1, Pallas kernels, run_attend(): pl.pallas_call(functools.partial(attend_kernel, exp_size, rep_size, slots...  102 us

profile of v6, /device:TPU:11, one launch (start us, length us, event | category | flops | bytes accessed | tf_op | source)
XLA Modules:
  0.0 333.3 jit_solution(14628542592243546312)
XLA Ops:
  0.6 101.6 %attend.1 = (bf16[4,1024,1024]{2,1,0:T(8,128)(2,1)}, bf16[1024,2048]{1,0:T(8,128)(2,1)}, bf16[768,1024]{1,0:T(8,128)(2,1)}, bf16[768,1024]{1,0:T(8,128)(2,1)}, f...) custom-call(bf16[256,1024]{1,0:T(8,128)(2,1)} %tokens.3, ...), custom_call_target="tpu_custom_call" | custom-call | flops 2684354560 | bytes 41943040 | tf_op jit(solution)/shard_map/attend/pallas_call | solution.py:606
  102.3 111.7 %experts.1 = (bf16[384,1024]{1,0:T(8,128)(2,1)}, bf16[768,1024]{1,0:T(8,128)(2,1)}, f32[1024,1024]{1,0:T(8,128)}, bf16[512,1024]{1,0:T(8,128)(2,1)}, bf16[512,10...) custom-call(bf16[768,1024]{1,0:T(8,128)(2,1)} %get-tuple-element.37.arrived_h, ...), custom_call_target="tpu_custom_call" | custom-call | flops 25769803776 | bytes 41943040 | tf_op jit(solution)/shard_map/experts/pallas_call | solution.py:1390
  214.0 0.0 copy-start.4
  214.0 104.4 %finish.1 = (bf16[256,1024]{1,0:T(8,128)(2,1)}, f32[256,1024]{1,0:T(8,128)}, f32[4,128,1024]{2,1,0:T(8,128)}, bf16[512,1024]{1,0:T(8,128)(2,1)}, bf16[256,4096]{1,0:T(8,128)(2,1)}) custom-call(bf16[384,1024]{1,0:T(8,128)(2,1)} %get-tuple-element.43.home, bf16[768,1024]{1,0:T(8,128)(2,1)} %get-tuple-element.44.branch, ...), custom_call_target="tpu_custom_call" | custom-call | flops 5368709120 | bytes 62914560 | tf_op jit(solution)/shard_map/finish/pallas_call | solution.py:1790
  318.4 0.0 copy-done.4
  318.4 0.0 copy-start
  318.4 0.0 copy-start.2
  318.4 0.0 copy-start.3
  318.5 5.7 %add_bitcast_fusion = f32[1,1024,1024]{2,1,0:T(8,128)} fusion(f32[1024,1024]{1,0:T(8,128)} %get-tuple-element.59, bf16[512,1024]{1,0:T(8,128)(2,1)} %get-tuple-element.61, bf16[512,1024]{1,0:T(8,128)(2,1)S(1)} %copy-done.4), kind=kLoop, calls=%fused_computation.2 | loop fusion | flops 5242880 | bytes 10485760 | tf_op jit(solution)/shard_map/broadcast_in_dim | solution.py:1945
  324.2 1.2 slice_reduce_fusion
  325.4 0.0 copy-done
  325.4 0.0 copy-done.2
  325.4 0.0 copy-done.3
  325.4 0.0 copy-start.10
  325.4 0.0 copy-start.1
  325.4 0.0 copy-start.7
  325.4 0.0 copy-start.8
  325.5 0.0 copy-start.9
  325.5 2.8 multiply_reduce_fusion
  328.3 0.0 copy-start.11
  328.3 0.0 copy-start.6
  328.3 0.0 copy-start.5
  328.3 0.0 copy-done.10
  328.3 0.6 convert_divide_fusion
  328.9 0.0 copy-done.1
  328.9 0.8 slice_bitcast_fusion
  329.7 0.0 copy-done.7
  329.7 0.0 copy-done.8
  329.7 0.0 copy-done.9
  329.7 1.3 multiply_reduce_fusion.1
  331.0 0.0 copy-done.11
  331.0 0.5 convert_divide_fusion.1
  331.6 0.0 copy-done.6
  331.6 0.8 copy.26
  332.3 0.0 copy-done.5
  332.4 1.0 copy.27
Async XLA Ops:
  214.0 104.4 %copy-start.4 = (bf16[512,1024]{1,0:T(8,128)(2,1)S(1)}, bf16[512,1024]{1,0:T(8,128)(2,1)}, u32[]{:S(2)}) copy-start(bf16[512,1024]{1,0:T(8,128)(2,1)} %get-tuple-element.60) | copy-start | bytes 3145732
  318.4 7.0 %copy-start = (bf16[2,256,4096]{2,1,0:T(8,128)(2,1)S(1)}, bf16[2,256,4096]{2,1,0:T(8,128)(2,1)}, u32[]{:S(2)}) copy-start(bf16[2,256,4096]{2,1,0:T(8,128)(2,1)} %get-tuple-element.54.inner_sum) | copy-start | bytes 12582916
  318.4 7.0 %copy-start.2 = (bf16[1,256,4096]{2,1,0:T(8,128)(2,1)S(1)}, bf16[1,256,4096]{2,1,0:T(8,128)(2,1)}, u32[]{:S(2)}) copy-start(bf16[1,256,4096]{2,1,0:T(8,128)(2,1)} %param.22) | copy-start | bytes 6291460
  318.4 7.0 %copy-start.3 = (bf16[256,4096]{1,0:T(8,128)(2,1)S(1)}, bf16[256,4096]{1,0:T(8,128)(2,1)}, u32[]{:S(2)}) copy-start(bf16[256,4096]{1,0:T(8,128)(2,1)} %get-tuple-element.58) | copy-start | bytes 6291460
  325.4 2.9 copy-start.10
  325.4 3.5 %copy-start.1 = (f32[4,128,1024]{2,1,0:T(8,128)S(1)}, f32[4,128,1024]{2,1,0:T(8,128)}, u32[]{:S(2)}) copy-start(f32[4,128,1024]{2,1,0:T(8,128)} %get-tuple-element.57) | copy-start | bytes 6291460
  325.4 4.3 %copy-start.7 = (bf16[128,1024]{1,0:T(8,128)(2,1)S(1)}, bf16[128,1024]{1,0:T(8,128)(2,1)}, u32[]{:S(2)}) copy-start(bf16[128,1024]{1,0:T(8,128)(2,1)} %w_query.1) | copy-start | bytes 786436
  325.4 4.3 %copy-start.8 = (bf16[128,1024]{1,0:T(8,128)(2,1)S(1)}, bf16[128,1024]{1,0:T(8,128)(2,1)}, u32[]{:S(2)}) copy-start(bf16[128,1024]{1,0:T(8,128)(2,1)} %w_key.1) | copy-start | bytes 786436
  325.5 4.3 %copy-start.9 = (bf16[128,1024]{1,0:T(8,128)(2,1)S(1)}, bf16[128,1024]{1,0:T(8,128)(2,1)}, u32[]{:S(2)}) copy-start(bf16[128,1024]{1,0:T(8,128)(2,1)} %w_value.1) | copy-start | bytes 786436
  328.3 2.7 copy-start.11
  328.3 3.3 copy-start.6
  328.3 4.1 %copy-start.5 = (f32[256,1024]{1,0:T(8,128)S(1)}, f32[256,1024]{1,0:T(8,128)}, u32[]{:S(2)}) copy-start(f32[256,1024]{1,0:T(8,128)} %get-tuple-element.87) | copy-start | bytes 3145732

commit v7 on v6

--- a/solution.py
+++ b/solution.py
@@ -65,13 +65,19 @@
     counts_all,
     cents,
     gains_e,
+    packed_h,
+    hidden_h,
+    qkv_h,
+    probs_h,
+    normed_h,
+    context_h,
+    pick,
+    gain_row,
     hidden,
     qkv,
     probs,
     normed_a,
     context,
-    pick,
-    gain_row,
     weights,
     staging,
     small_all,
@@ -514,11 +520,21 @@
             pick[...], cotangent[:, cols], preferred_element_type=wide
         ).astype(low)
 
-    dispatch(packed_c, 1)
-
     gather_end(1)
-    store = pltpu.make_async_copy(weights, attn_w, out_s.at[0])
-    store.start()
+    stores = [
+        pltpu.make_async_copy(source, target, out_s.at[at])
+        for at, (source, target) in (
+            (0, (weights, attn_w)),
+            (2, (qkv, qkv_h)),
+            (3, (probs, probs_h)),
+            (4, (normed_a, normed_h)),
+            (5, (context, context_h)),
+            (7, (packed_c, packed_h)),
+            (6, (hidden, hidden_h)),
+        )
+    ]
+    for store in stores[:-1]:
+        store.start()
 
     @pl.loop(0, width // TILE)
     def _(step):
@@ -532,11 +548,13 @@
         ).astype(low)
 
     dispatch(packed_x, 0)
+    stores[-1].start()
     for copy in inner_copies(3):
         copy.wait_recv()
     forward_copy.start()
 
-    store.wait()
+    for store in stores:
+        store.wait()
     outer_copy.wait()
     forward_copy.wait()
     for mask in range(1, rep_size):
@@ -576,20 +594,30 @@
     for mask, flip in cent_pairs:
         cent_copy(mask, flip).wait()
 
-    @pl.loop(1, exp_size)
-    def _(at):
-        source = exp_at ^ at
-        remote(
-            packed_c.at[slot_rows(source // 2)],
+    def disp_wait(source):
+        return remote(
+            packed_x.at[slot_rows(source // 2)],
             arrived.at[slot_rows(source)],
             disp_s.at[source],
             disp_r.at[source],
             (rep_at, source),
+        )
+
+    @pl.loop(0, groups)
+    def _(at):
+        @pl.when(2 * at != exp_at)
+        def _():
+            disp_wait(2 * at).wait_send()
+
+    @pl.when(side == 0)
+    def _():
+        pltpu.make_async_copy(
+            packed_x.at[slot_rows(group)], arrived.at[slot_rows(exp_at)], disp_s.at[exp_at]
         ).wait()
 
-    pltpu.make_async_copy(
-        packed_c.at[slot_rows(group)], arrived.at[slot_rows(exp_at)], disp_s.at[exp_at]
-    ).wait()
+        @pl.loop(1, exp_size)
+        def _(at):
+            disp_wait(exp_at ^ at).wait_recv()
 
 
 def run_attend(exp_size, rep_size, slots, tokens, cotangent, doc, expert_of, attn, gain_a, w_inner, w_outer, gain_e, cent):
@@ -613,6 +641,7 @@
             shape((exp_size * 16, 128), wide),
             shape((2 * rep_size * 8, cent.shape[1]), wide),
             shape((rep_size * 8, depth), wide),
+            shape((groups * slots, width), low),
             shape((rows_n, width), wide),
             shape((3, rows_n, width), low),
             shape((HEADS * rows_n, rows_n), low),
@@ -624,8 +653,13 @@
         in_specs=[inside, inside, pl.BlockSpec(memory_space=pltpu.SMEM), inside]
         + [anyplace] * 4
         + [inside, anyplace, anyplace, inside, inside],
-        out_specs=(anyplace,) * 7 + (inside,) * 7,
+        out_specs=(anyplace,) * 13 + (inside,) * 2,
         scratch_shapes=[
+            pltpu.VMEM((rows_n, width), wide),
+            pltpu.VMEM((3, rows_n, width), low),
+            pltpu.VMEM((HEADS * rows_n, rows_n), low),
+            pltpu.VMEM((rows_n, width), low),
+            pltpu.VMEM((rows_n, width), low),
             pltpu.VMEM((4, width, width), low),
             pltpu.VMEM((depth, 2 * ff_block), low),
             pltpu.VMEM((exp_size * 16, 128), wide),
@@ -652,7 +686,7 @@
             dma((2 * rep_size,)),
             dma((rep_size,)),
             dma((rep_size,)),
-            dma((2,)),
+            dma((8,)),
         ],
         compiler_params=pltpu.CompilerParams(
             collective_id=1, has_side_effects=True, vmem_limit_bytes=56 << 20
@@ -671,6 +705,7 @@
     rep_size,
     slots,
     arrived_h,
+    packed_h,
     inner_h,
     outer_h,
     w_inner,
@@ -680,6 +715,7 @@
     gains_e,
     home,
     branch,
+    branch_got,
     outer_keep,
     outer_send,
     outer_got,
@@ -713,6 +749,10 @@
     outer_send_v,
     inner_send_v,
     load_sem,
+    disp_s,
+    disp_r,
+    bran_s,
+    bran_r,
     centre_s,
     centre_r,
     norm_s,
@@ -758,8 +798,13 @@
     def inner_rows(mask):
         return pl.ds(pl.multiple_of((rep_at ^ mask) * depth, depth), depth)
 
+    rows_load = pltpu.make_async_copy(arrived_h, arrived, load_sem.at[0])
+
+    @pl.when(first)
+    def _():
+        rows_load.start()
+
     loads = [
-        pltpu.make_async_copy(arrived_h, arrived, load_sem.at[0]),
         pltpu.make_async_copy(w_outer, outer_w.at[:block], load_sem.at[1]),
         pltpu.make_async_copy(outer_h, outer_w.at[block : 2 * block - DEFER], load_sem.at[2]),
     ]
@@ -823,26 +868,43 @@
         ).astype(low)
     for at in range(rep_size):
         gain[:, at * depth : (at + 1) * depth] = gains_e[at * 8 : at * 8 + 1, :]
-    loads[0].wait()
-
-    for at in range(width // TILE):
-        cols = slice(at * TILE, (at + 1) * TILE)
-        rows_low = lax.dot_general(
-            spread_m[...],
-            arrived[:, cols],
-            (((0,), (0,)), ((), ())),
-            preferred_element_type=wide,
+    def compact_rows():
+        return lax.dot_general(
+            spread_m[...], arrived[...], (((0,), (0,)), ((), ())), preferred_element_type=wide
         ).astype(low)
 
-        @pl.when(first)
-        def _():
-            own_x[:, cols] = rows_low
-
-        @pl.when(second)
-        def _():
-            own_cot[:, cols] = rows_low
+    @pl.when(first)
+    def _():
+        rows_load.wait()
+        own_x[...] = compact_rows()
 
     pl.semaphore_wait(barrier, exp_size - 1 + 2 * (rep_size - 1))
+
+    def disp_copy(which):
+        return remote(
+            packed_h.at[slot_rows(which)],
+            arrived.at[slot_rows(exp_at)],
+            disp_s.at[which],
+            disp_r.at[exp_at],
+            (rep_at, 2 * which + 1),
+        )
+
+    disp_own = pltpu.make_async_copy(
+        packed_h.at[slot_rows(group)], arrived.at[slot_rows(exp_at)], disp_s.at[group]
+    )
+
+    @pl.loop(0, exp_size // 2)
+    def _(step):
+        which = group ^ (exp_size // 2 - 1 - step)
+
+        @pl.when(2 * which + 1 != exp_at)
+        def _():
+            disp_copy(which).start()
+
+        @pl.when(2 * which + 1 == exp_at)
+        def _():
+            disp_own.start()
+
     row_peer = (rep_at ^ 2, exp_at)
     late_copy = remote(
         w_outer.at[block - DEFER :],
@@ -939,6 +1001,24 @@
 
     @pl.when(second)
     def _():
+        hop_forward(0).wait_recv()
+        norm_rows(0)
+
+    def take_cotangent():
+        disp_own.wait()
+
+        @pl.loop(1, exp_size)
+        def _(at):
+            source = exp_at ^ at
+            remote(
+                packed_h.at[slot_rows(0)],
+                arrived.at[slot_rows(source)],
+                disp_s.at[0],
+                disp_r.at[source],
+                side_peer,
+            ).wait_recv()
+
+        own_cot[...] = compact_rows()
         gate_copy.wait_recv()
 
         @pl.loop(0, CHUNKS)
@@ -953,12 +1033,8 @@
 
             state_copy(at).start()
 
-        hop_forward(0).wait_recv()
-        norm_rows(0)
-
-    for load in loads[1:]:
+    for load in loads:
         load.wait()
-    late_copy.wait_recv()
     centre_grad[...] = jnp.zeros_like(centre_grad)
 
     def finish_forward(step, at):
@@ -1085,6 +1161,10 @@
         def _():
             finish(step - 1)
 
+        @pl.when(step == 0)
+        def _():
+            late_copy.wait_recv()
+
         @pl.when(forward)
         def _():
             both = jnp.dot(active[rows, :], outer_w[...], preferred_element_type=wide)
@@ -1108,6 +1188,10 @@
         def _():
             finish(step)
 
+        @pl.when(second & (step == 0))
+        def _():
+            take_cotangent()
+
         after = step + 1
         after_at = chunk_at(after)
 
@@ -1187,6 +1271,27 @@
     centre_pairs = [(m, f) for m in range(rep_size) for f in range(2) if m or f]
 
     make_spread()
+
+    def bran_copy(which):
+        return remote(
+            spread.at[slot_rows(2 * which + 1)],
+            branch_got.at[slot_rows(group)],
+            bran_s.at[which],
+            bran_r.at[group],
+            (rep_at, 2 * which + 1),
+        )
+
+    bran_own = pltpu.make_async_copy(
+        spread.at[slot_rows(exp_at)], branch_got.at[slot_rows(group)], bran_s.at[group]
+    )
+
+    @pl.when(second)
+    def _():
+        bran_own.start()
+
+        @pl.loop(1, groups)
+        def _(step):
+            bran_copy(group ^ (groups - step)).start()
 
     @pl.when(first)
     def _():
@@ -1277,6 +1382,28 @@
             hop_backward(at).wait_send()
             grad_copy(at).wait_send()
 
+    @pl.loop(0, groups)
+    def _(which):
+        @pl.when(2 * which + 1 != exp_at)
+        def _():
+            disp_copy(which).wait_send()
+
+    @pl.when(second)
+    def _():
+        bran_own.wait()
+
+        @pl.loop(1, groups)
+        def _(step):
+            which = group ^ step
+            bran_copy(which).wait_send()
+            remote(
+                spread.at[slot_rows(which)],
+                branch_got.at[slot_rows(which)],
+                bran_s.at[which],
+                bran_r.at[which],
+                side_peer,
+            ).wait_recv()
+
     @pl.when(first)
     def _():
         gate_copy.wait_send()
@@ -1333,7 +1460,7 @@
 
 
 def run_experts(
-    exp_size, rep_size, slots, own_rows, arrived, inner_w, outer_w, w_inner, w_outer, counts_all, cents, gains_e
+    exp_size, rep_size, slots, own_rows, arrived, packed, inner_w, outer_w, w_inner, w_outer, counts_all, cents, gains_e
 ):
     width = arrived.shape[1]
     depth = width // rep_size
@@ -1377,6 +1504,10 @@
         pltpu.VMEM((block, width), low),
         pltpu.VMEM((rep_size, 2, depth, block), low),
         dma((8,)),
+        dma((exp_size // 2,)),
+        dma((exp_size,)),
+        dma((exp_size // 2,)),
+        dma((exp_size // 2,)),
         dma((2 * rep_size,)),
         dma((rep_size,)),
     ]
@@ -1392,14 +1523,15 @@
         out_shape=(
             jax.ShapeDtypeStruct((total // 2, width), low),
             jax.ShapeDtypeStruct((total, width), low),
+            jax.ShapeDtypeStruct((total // 2, width), low),
             jax.ShapeDtypeStruct((block, width), wide),
             jax.ShapeDtypeStruct((block - EARLY, width), low),
             jax.ShapeDtypeStruct((EARLY, width), low),
             jax.ShapeDtypeStruct((2, depth, rep_size * block), low),
             jax.ShapeDtypeStruct((rep_size * 8, piece), wide),
         ),
-        in_specs=[anyplace] * 5 + [inside] * 3,
-        out_specs=(anyplace,) * 7,
+        in_specs=[anyplace] * 6 + [inside] * 3,
+        out_specs=(anyplace,) * 8,
         scratch_shapes=scratch,
         compiler_params=pltpu.CompilerParams(
             collective_id=0, has_side_effects=True, vmem_limit_bytes=62 << 20
@@ -1408,7 +1540,7 @@
             flops=flops, bytes_accessed=40 << 20, transcendentals=2 * all_rows * 2 * block
         ),
         name="experts",
-    )(arrived, inner_w, outer_w, w_inner, w_outer, counts_all, cents, gains_e)
+    )(arrived, packed, inner_w, outer_w, w_inner, w_outer, counts_all, cents, gains_e)
 
 
 def finish_kernel(
@@ -1416,15 +1548,16 @@
     rep_size,
     home,
     branch,
+    branch_got,
     pick,
-    hidden,
+    hidden_h,
     cotangent,
-    tokens,
+    tokens_h,
     gain_row,
-    qkv,
-    probs,
-    normed_a,
-    context,
+    qkv_h,
+    probs_h,
+    normed_h,
+    context_h,
     attn_w,
     outer_send,
     inner_sum,
@@ -1433,6 +1566,14 @@
     shares,
     outer_recv,
     inner_recv,
+    hidden,
+    tokens,
+    qkv,
+    probs,
+    normed_a,
+    context,
+    normed_t,
+    context_t,
     branch_in,
     weights,
     grad_hidden,
@@ -1475,15 +1616,29 @@
     group = exp_at // 2
     side = exp_at % 2
     groups = exp_size // 2
-    rows_n, width = tokens.shape
+    rows_n, width = cotangent.shape
     half = width // 2
     block = width // exp_size
     core_peer = (rep_at ^ 1, exp_at)
     side_peer = (rep_at, exp_at ^ 1)
     row_peer = (rep_at ^ 2, exp_at)
 
-    load = pltpu.make_async_copy(attn_w, weights, load_s.at[0])
-    load.start()
+    loads = [
+        pltpu.make_async_copy(source, target, load_s.at[at])
+        for at, (source, target) in enumerate(
+            (
+                (context_h, context),
+                (attn_w, weights),
+                (qkv_h, qkv),
+                (probs_h, probs),
+                (normed_h, normed_a),
+                (tokens_h, tokens),
+                (hidden_h, hidden),
+            )
+        )
+    ]
+    for load in loads:
+        load.start()
 
     barrier = pltpu.get_barrier_semaphore()
     for mask in range(1, 3):
@@ -1517,27 +1672,23 @@
             (rep_at, dest),
         )
 
-    branch_own = pltpu.make_async_copy(
-        branch.at[slot_rows(exp_at)], branch_in.at[slot_rows(group)], branch_s.at[exp_at]
-    )
+    branch_own = pltpu.make_async_copy(branch_got, branch_in, branch_s.at[exp_at])
 
     @pl.when(side == 1)
     def _():
         branch_own.start()
 
-        @pl.loop(1, exp_size)
+        @pl.loop(0, groups)
         def _(at):
-            branch_copy(exp_at ^ at).start()
-
-    @pl.loop(0, width // TILE)
-    def _(step):
-        cols = pl.ds(pl.multiple_of(step * TILE, TILE), TILE)
-        back = lax.dot_general(
-            pick[...], home[:, cols], (((0,), (0,)), ((), ())), preferred_element_type=wide
-        )
-        grad = cotangent[:, cols].astype(wide) + back
-        grad_hidden[:, cols] = grad
-        grad_attn[:, cols] = grad.astype(low)
+            branch_copy(2 * (group ^ (groups - 1 - at))).start()
+
+    back_rows = lax.dot_general(
+        pick[...], home[...], (((0,), (0,)), ((), ())), preferred_element_type=wide
+    )
+    grad_hidden[...] = cotangent[...].astype(wide) + back_rows
+    grad_attn[...] = grad_hidden[...].astype(low)
+    loads[0].wait()
+    context_t[...] = context[...].T
 
     own_half = pl.ds(pl.multiple_of(core * half, half), half)
     other_half = pl.ds(pl.multiple_of((1 - core) * half, half), half)
@@ -1546,11 +1697,11 @@
         return remote(core_out.at[at], core_in.at[at], core_s.at[at], core_r.at[at], core_peer)
 
     def product(at, left, right, cols, target, kind):
-        @pl.loop(0, width // TILE)
+        @pl.loop(0, width // 512)
         def _(step):
-            rows = pl.ds(pl.multiple_of(step * TILE, TILE), TILE)
-            target[at, rows, :] = lax.dot_general(
-                left[:, rows], right[:, cols], (((0,), (0,)), ((), ())), preferred_element_type=wide
+            rows = pl.ds(pl.multiple_of(step * 512, 512), 512)
+            target[at, rows, :] = jnp.dot(
+                left[rows, :], right[:, cols], preferred_element_type=wide
             ).astype(kind)
 
     def share_start(at, left, right):
@@ -1630,8 +1781,8 @@
         half_copy(at).wait_recv()
         shares[at, :, other_half] = half_in[at]
 
-    share_start(3, context, grad_attn)
-    load.wait()
+    share_start(3, context_t, grad_attn)
+    loads[1].wait()
 
     @pl.loop(0, width // TILE)
     def _(step):
@@ -1686,14 +1837,19 @@
                     lane < head_dim, found[0][which], found[1][which]
                 ).astype(low)
 
+    loads[2].wait()
+    loads[3].wait()
     heads(0, HEADS // 4)
     share_line(3)
     heads(HEADS // 4, HEADS // 2)
+    loads[4].wait()
+    normed_t[...] = normed_a[...].T
     for at in range(3):
-        share_start(at, normed_a, grads3.at[at])
+        share_start(at, normed_t, grads3.at[at])
     for at in range(3):
         share_side(at)
 
+    loads[5].wait()
     @pl.loop(0, width // TILE)
     def _(step):
         rows = pl.ds(pl.multiple_of(step * TILE, TILE), TILE)
@@ -1720,6 +1876,8 @@
     for at in range(3):
         share_line(at)
 
+    for at in range(3):
+        share_row(at)
     def branch_wait(which):
         remote(
             branch.at[slot_rows(which)],
@@ -1731,26 +1889,20 @@
 
     @pl.when(side == 0)
     def _():
-        branch_wait(group)
+        @pl.loop(0, groups)
+        def _(at):
+            branch_wait(at)
 
     @pl.when(side == 1)
     def _():
         branch_own.wait()
 
-    @pl.loop(1, groups)
-    def _(at):
-        branch_wait(group ^ at)
-
-    @pl.loop(0, width // TILE)
-    def _(step):
-        cols = pl.ds(pl.multiple_of(step * TILE, TILE), TILE)
-        rows = lax.dot_general(
-            pick[...], branch_in[:, cols], (((0,), (0,)), ((), ())), preferred_element_type=wide
-        )
-        output[:, cols] = (hidden[:, cols] + rows).astype(low)
-
-    for at in range(3):
-        share_row(at)
+    loads[6].wait()
+    rows = lax.dot_general(
+        pick[...], branch_in[...], (((0,), (0,)), ((), ())), preferred_element_type=wide
+    )
+    output[...] = (hidden[...] + rows).astype(low)
+
     for at in (3, 0, 1, 2):
         share_half(at)
     for at in (3, 0, 1, 2):
@@ -1758,9 +1910,9 @@
 
     @pl.when(side == 1)
     def _():
-        @pl.loop(1, exp_size)
+        @pl.loop(0, groups)
         def _(at):
-            branch_copy(exp_at ^ at).wait_send()
+            branch_copy(2 * at).wait_send()
 
     for at in range(4):
         core_copy(at).wait_send()
@@ -1776,7 +1928,7 @@
     outer_copy.wait()
 
 
-def run_finish(exp_size, rep_size, home, branch, pick, hidden, cotangent, tokens, gain_row, qkv, probs, normed_a, context, attn_w, outer_send, inner_sum):
+def run_finish(exp_size, rep_size, home, branch, branch_got, pick, hidden, cotangent, tokens, gain_row, qkv, probs, normed_a, context, attn_w, outer_send, inner_sum):
     rows_n, width = tokens.shape
     low = jnp.bfloat16
     wide = jnp.float32
@@ -1796,9 +1948,18 @@
             shape(outer_send.shape, low),
             shape(inner_sum.shape[1:], low),
         ),
-        in_specs=[inside, anyplace] + [inside] * 9 + [anyplace] * 3,
+        in_specs=[inside, anyplace, anyplace, inside, anyplace, inside, anyplace, inside]
+        + [anyplace] * 7,
         out_specs=(inside,) * 3 + (anyplace,) * 2,
         scratch_shapes=[
+            pltpu.VMEM((rows_n, width), wide),
+            pltpu.VMEM((rows_n, width), low),
+            pltpu.VMEM(qkv.shape, low),
+            pltpu.VMEM(probs.shape, low),
+            pltpu.VMEM((rows_n, width), low),
+            pltpu.VMEM((rows_n, width), low),
+            pltpu.VMEM((width, rows_n), low),
+            pltpu.VMEM((width, rows_n), low),
             pltpu.VMEM(pick.shape[:1] + (width,), low),
             pltpu.VMEM((4, width, width), low),
             pltpu.VMEM((rows_n, width), wide),
@@ -1817,7 +1978,7 @@
             pltpu.VMEM((4, block, half), low),
             pltpu.VMEM((4, block, half), wide),
             pltpu.VMEM((4, block, half), wide),
-            dma((1,)),
+            dma((7,)),
             dma((exp_size,)),
             dma((groups,)),
             dma((2,)),
@@ -1843,6 +2004,7 @@
     )(
         home,
         branch,
+        branch_got,
         pick,
         hidden,
         cotangent,
@@ -1887,6 +2049,7 @@
         counts_all,
         cents,
         gains_e,
+        packed,
         hidden,
         qkv,
         probs,
@@ -1909,12 +2072,13 @@
         expert_gain,
         centroids,
     )
-    home, branch, outer_keep, outer_send, outer_got, inner_sum, centre_parts = run_experts(
+    home, branch, branch_got, outer_keep, outer_send, outer_got, inner_sum, centre_parts = run_experts(
         exp_size,
         rep_size,
         slots,
         2 * row_count,
         arrived,
+        packed,
         inner_w,
         outer_w,
         w_inner[0],
@@ -1928,6 +2092,7 @@
         rep_size,
         home,
         branch,
+        branch_got,
         pick,
         hidden,
         cotangent,

time: 334 us -> 323 us (0.967)
  Pallas kernels: 318 us -> 307 us
    pallas_call x1, Pallas kernels: 102 us -> 88 us  [run_attend(): pl.pallas_call(functools.partial(attend_kernel, exp_size, rep_size, slots...]
    pallas_call x1, Pallas kernels: 112 us -> 118 us  [run_experts(): pl.pallas_call(functools.partial(expert_kernel, exp_size, rep_size, slots...]
where the time goes in v7:
time: 323 us
  Pallas kernels  307 us (95%)
  other arithmetic  12.2 us (4%)
    pallas_call x1, Pallas kernels, run_experts(): pl.pallas_call(functools.partial(expert_kernel, exp_size, rep_size, slots...  118 us
    pallas_call x1, Pallas kernels, run_finish(): pl.pallas_call(functools.partial(finish_kernel, exp_size, rep_size), out_...  102 us
    pallas_call x1, Pallas kernels, run_attend(): pl.pallas_call(functools.partial(attend_kernel, exp_size, rep_size, slots...  88 us

profile of v7, /device:TPU:11, one launch (start us, length us, event | category | flops | bytes accessed | tf_op | source)
XLA Modules:
  0.0 322.6 jit_solution(7710669716238612353)
XLA Ops:
  0.6 88.0 %attend.1 = (bf16[4,1024,1024]{2,1,0:T(8,128)(2,1)}, bf16[1024,2048]{1,0:T(8,128)(2,1)}, bf16[768,1024]{1,0:T(8,128)(2,1)}, bf16[768,1024]{1,0:T(8,128)(2,1)}, f...) custom-call(bf16[256,1024]{1,0:T(8,128)(2,1)} %tokens_h.1, ...), custom_call_target="tpu_custom_call" | custom-call | flops 2684354560 | bytes 41943040 | tf_op jit(solution)/shard_map/attend/pallas_call | solution.py:634
  88.6 117.5 %experts.1 = (bf16[384,1024]{1,0:T(8,128)(2,1)}, bf16[768,1024]{1,0:T(8,128)(2,1)}, bf16[384,1024]{1,0:T(8,128)(2,1)}, f32[1024,1024]{1,0:T(8,128)}, bf16[512,10...) custom-call(bf16[768,1024]{1,0:T(8,128)(2,1)} %get-tuple-element.39.arrived_h, ...), custom_call_target="tpu_custom_call" | custom-call | flops 25769803776 | bytes 41943040 | tf_op jit(solution)/shard_map/experts/pallas_call | solution.py:1521
  206.2 0.0 copy-start.4
  206.2 101.5 %finish.1 = (bf16[256,1024]{1,0:T(8,128)(2,1)}, f32[256,1024]{1,0:T(8,128)}, f32[4,128,1024]{2,1,0:T(8,128)}, bf16[512,1024]{1,0:T(8,128)(2,1)}, bf16[256,4096]{1,0:T(8,128)(2,1)}) custom-call(bf16[384,1024]{1,0:T(8,128)(2,1)} %get-tuple-element.46.home, bf16[768,1024]{1,0:T(8,128)(2,1)} %get-tuple-element.47.branch, ...), custom_call_target="tpu_custom_call" | custom-call | flops 5368709120 | bytes 62914560 | tf_op jit(solution)/shard_map/finish/pallas_call | solution.py:1942
  307.7 0.0 copy-done.4
  307.7 0.0 copy-start
  307.7 0.0 copy-start.2
  307.8 0.0 copy-start.3
  307.8 5.7 %add_bitcast_fusion = f32[1,1024,1024]{2,1,0:T(8,128)} fusion(f32[1024,1024]{1,0:T(8,128)} %get-tuple-element.63, bf16[512,1024]{1,0:T(8,128)(2,1)} %get-tuple-element.65, bf16[512,1024]{1,0:T(8,128)(2,1)S(1)} %copy-done.4), kind=kLoop, calls=%fused_computation.2 | loop fusion | flops 5242880 | bytes 10485760 | tf_op jit(solution)/shard_map/broadcast_in_dim | solution.py:2110
  313.5 1.2 slice_reduce_fusion
  314.7 0.0 copy-done
  314.7 0.0 copy-done.2
  314.7 0.0 copy-done.3
  314.7 0.0 copy-start.10
  314.7 0.0 copy-start.1
  314.7 0.0 copy-start.7
  314.8 0.0 copy-start.8
  314.8 0.0 copy-start.9
  314.8 2.8 multiply_reduce_fusion
  317.6 0.0 copy-start.11
  317.6 0.0 copy-start.6
  317.6 0.0 copy-start.5
  317.6 0.0 copy-done.10
  317.6 0.6 convert_divide_fusion
  318.2 0.0 copy-done.1
  318.2 0.8 slice_bitcast_fusion
  319.0 0.0 copy-done.7
  319.0 0.0 copy-done.8
  319.0 0.0 copy-done.9
  319.0 1.3 multiply_reduce_fusion.1
  320.3 0.0 copy-done.11
  320.3 0.5 convert_divide_fusion.1
  320.9 0.0 copy-done.6
  320.9 0.8 copy.26
  321.7 0.0 copy-done.5
  321.7 1.0 copy.27
Async XLA Ops:
  206.2 101.6 %copy-start.4 = (bf16[512,1024]{1,0:T(8,128)(2,1)S(1)}, bf16[512,1024]{1,0:T(8,128)(2,1)}, u32[]{:S(2)}) copy-start(bf16[512,1024]{1,0:T(8,128)(2,1)} %get-tuple-element.64) | copy-start | bytes 3145732
  307.7 7.0 %copy-start = (bf16[2,256,4096]{2,1,0:T(8,128)(2,1)S(1)}, bf16[2,256,4096]{2,1,0:T(8,128)(2,1)}, u32[]{:S(2)}) copy-start(bf16[2,256,4096]{2,1,0:T(8,128)(2,1)} %get-tuple-element.58.inner_sum) | copy-start | bytes 12582916
  307.7 7.0 %copy-start.2 = (bf16[1,256,4096]{2,1,0:T(8,128)(2,1)S(1)}, bf16[1,256,4096]{2,1,0:T(8,128)(2,1)}, u32[]{:S(2)}) copy-start(bf16[1,256,4096]{2,1,0:T(8,128)(2,1)} %param.22) | copy-start | bytes 6291460
  307.8 7.0 %copy-start.3 = (bf16[256,4096]{1,0:T(8,128)(2,1)S(1)}, bf16[256,4096]{1,0:T(8,128)(2,1)}, u32[]{:S(2)}) copy-start(bf16[256,4096]{1,0:T(8,128)(2,1)} %get-tuple-element.62) | copy-start | bytes 6291460
  314.7 2.9 copy-start.10
  314.7 3.5 %copy-start.1 = (f32[4,128,1024]{2,1,0:T(8,128)S(1)}, f32[4,128,1024]{2,1,0:T(8,128)}, u32[]{:S(2)}) copy-start(f32[4,128,1024]{2,1,0:T(8,128)} %get-tuple-element.61) | copy-start | bytes 6291460
  314.7 4.3 %copy-start.7 = (bf16[128,1024]{1,0:T(8,128)(2,1)S(1)}, bf16[128,1024]{1,0:T(8,128)(2,1)}, u32[]{:S(2)}) copy-start(bf16[128,1024]{1,0:T(8,128)(2,1)} %w_query.1) | copy-start | bytes 786436
  314.8 4.3 %copy-start.8 = (bf16[128,1024]{1,0:T(8,128)(2,1)S(1)}, bf16[128,1024]{1,0:T(8,128)(2,1)}, u32[]{:S(2)}) copy-start(bf16[128,1024]{1,0:T(8,128)(2,1)} %w_key.1) | copy-start | bytes 786436
  314.8 4.3 %copy-start.9 = (bf16[128,1024]{1,0:T(8,128)(2,1)S(1)}, bf16[128,1024]{1,0:T(8,128)(2,1)}, u32[]{:S(2)}) copy-start(bf16[128,1024]{1,0:T(8,128)(2,1)} %w_value.1) | copy-start | bytes 786436
  317.6 2.7 copy-start.11
  317.6 3.3 %copy-start.6 = (bf16[256,1024]{1,0:T(8,128)(2,1)S(1)}, bf16[256,1024]{1,0:T(8,128)(2,1)}, u32[]{:S(2)}) copy-start(bf16[256,1024]{1,0:T(8,128)(2,1)} %get-tuple-element.90) | copy-start | bytes 1572868
  317.6 4.1 %copy-start.5 = (f32[256,1024]{1,0:T(8,128)S(1)}, f32[256,1024]{1,0:T(8,128)}, u32[]{:S(2)}) copy-start(f32[256,1024]{1,0:T(8,128)} %get-tuple-element.91) | copy-start | bytes 3145732

commit v8 on v7

--- a/solution.py
+++ b/solution.py
@@ -18,8 +18,8 @@
 
 MESH = pl.DeviceIdType.MESH
 TILE = 256
-ROWS = 64
-BIG = 1024
+ROWS = 128
+BIG = 2048
 
 
 def remote(src, dst, send_sem, recv_sem, device):
@@ -1239,16 +1239,12 @@
                 spread_m[...], back[:, cols], preferred_element_type=wide
             ).astype(low)
 
-    def send_back():
-        @pl.loop(1, groups)
-        def _(step):
-            relay_copy(group ^ (groups - step)).start()
-
-        @pl.loop(1, groups)
-        def _(step):
-            dest = 2 * (group ^ (groups - step))
-            ret_copy(spread.at[slot_rows(dest)], dest).start()
-
+    def send_step(step):
+        which = group ^ (groups - step)
+        relay_copy(which).start()
+        ret_copy(spread.at[slot_rows(2 * which)], 2 * which).start()
+
+    def send_end():
         ret_copy(spread.at[slot_rows(exp_at + 1)], exp_at + 1).start()
         ret_own.start()
 
@@ -1293,9 +1289,17 @@
         def _(step):
             bran_copy(group ^ (groups - step)).start()
 
+    spans = 4
+
+    def send_span(span):
+        @pl.when(first)
+        def _():
+            @pl.loop(1 + -(-span * (groups - 1) // spans), 1 + -(-(span + 1) * (groups - 1) // spans))
+            def _(step):
+                send_step(step)
+
     @pl.when(first)
     def _():
-        send_back()
         for at in range(width // piece):
             centre_v[at * 8 : (at + 1) * 8, :] = jnp.broadcast_to(
                 centre_grad[:, at * piece : (at + 1) * piece], (8, piece)
@@ -1309,13 +1313,15 @@
     early_copy = remote(
         outer_send_v.at[:EARLY], outer_got, early_s.at[1], early_r.at[1], row_peer
     )
-    for at in list(range(tiles, 2 * tiles)) + list(range(tiles)):
+    for place, at in enumerate(list(range(tiles, 2 * tiles)) + list(range(tiles))):
+        if place % 2 == 0 and place // 2 < spans:
+            send_span(place // 2)
         rows = slice(at * TILE, (at + 1) * TILE)
         grad = lax.dot_general(
             active[:, rows], states[...], (((0,), (0,)), ((), ())), preferred_element_type=wide
         )
         if at < tiles:
-            outer_keep_v[rows, :] = grad
+            outer_keep_v[rows, :] = grad.astype(low)
             outs.append((outer_keep_v.at[rows], outer_keep.at[rows]))
         else:
             top = at * TILE - block
@@ -1342,6 +1348,10 @@
         return remote(source, target, inner_s.at[count], out_r.at[count], core_peer)
 
     inner_order = [(m, f) for m in (3, 1, 2, 0) for f in range(2)]
+    @pl.when(first)
+    def _():
+        send_end()
+
     for mask, side in inner_order:
         cols = slice(side * block, (side + 1) * block)
         grad = lax.dot_general(
@@ -1500,7 +1510,7 @@
         pltpu.VMEM((2, part, width), wide),
         pltpu.VMEM((own_rows, 128), wide),
         pltpu.VMEM((own_rows, 128), wide),
-        pltpu.VMEM((block, width), wide),
+        pltpu.VMEM((block, width), low),
         pltpu.VMEM((block, width), low),
         pltpu.VMEM((rep_size, 2, depth, block), low),
         dma((8,)),
@@ -1524,7 +1534,7 @@
             jax.ShapeDtypeStruct((total // 2, width), low),
             jax.ShapeDtypeStruct((total, width), low),
             jax.ShapeDtypeStruct((total // 2, width), low),
-            jax.ShapeDtypeStruct((block, width), wide),
+            jax.ShapeDtypeStruct((block, width), low),
             jax.ShapeDtypeStruct((block - EARLY, width), low),
             jax.ShapeDtypeStruct((EARLY, width), low),
             jax.ShapeDtypeStruct((2, depth, rep_size * block), low),
@@ -1560,6 +1570,7 @@
     context_h,
     attn_w,
     outer_send,
+    outer_got,
     inner_sum,
     output,
     grad_tokens,
@@ -1575,6 +1586,7 @@
     normed_t,
     context_t,
     branch_in,
+    early_rows,
     weights,
     grad_hidden,
     grad_attn,
@@ -1634,6 +1646,7 @@
                 (normed_h, normed_a),
                 (tokens_h, tokens),
                 (hidden_h, hidden),
+                (outer_got, early_rows),
             )
         )
     ]
@@ -1652,7 +1665,10 @@
 
     pl.semaphore_wait(barrier, exp_size + 1)
 
-    outer_copy = remote(outer_send, outer_recv, expert_s.at[0], expert_r.at[0], row_peer)
+    outer_copy = remote(
+        outer_send, outer_recv.at[EARLY:], expert_s.at[0], expert_r.at[0], row_peer
+    )
+    early_store = pltpu.make_async_copy(early_rows, outer_recv.at[:EARLY], load_s.at[8])
 
     inner_copy = remote(inner_sum.at[1], inner_recv, expert_s.at[1], expert_r.at[1], row_peer)
     inner_copy.start()
@@ -1798,9 +1814,10 @@
     factor = head_dim ** (-0.5)
     lane = lax.broadcasted_iota(jnp.int32, (rows_n, pair), 1)
 
-    def heads(start, stop):
-        @pl.loop(start, stop)
-        def _(at):
+    def heads(which_half):
+        @pl.loop(0, HEADS // 4)
+        def _(step):
+            at = which_half * (HEADS // 4) + step
             cols = pl.ds(pl.multiple_of(at * pair, pair), pair)
             q_pair = qkv[0, :, cols]
             k_pair = qkv[1, :, cols]
@@ -1837,18 +1854,21 @@
                     lane < head_dim, found[0][which], found[1][which]
                 ).astype(low)
 
+    loads[7].wait()
+    early_store.start()
     loads[2].wait()
     loads[3].wait()
-    heads(0, HEADS // 4)
-    share_line(3)
-    heads(HEADS // 4, HEADS // 2)
+    heads(1 - core)
     loads[4].wait()
     normed_t[...] = normed_a[...].T
     for at in range(3):
-        share_start(at, normed_t, grads3.at[at])
+        product(at, normed_t, grads3.at[at], other_half, core_out, low)
+        core_copy(at).start()
+    share_line(3)
+    heads(core)
     for at in range(3):
+        product(at, normed_t, grads3.at[at], own_half, keep, wide)
         share_side(at)
-
     loads[5].wait()
     @pl.loop(0, width // TILE)
     def _(step):
@@ -1926,9 +1946,10 @@
 
     inner_copy.wait()
     outer_copy.wait()
-
-
-def run_finish(exp_size, rep_size, home, branch, branch_got, pick, hidden, cotangent, tokens, gain_row, qkv, probs, normed_a, context, attn_w, outer_send, inner_sum):
+    early_store.wait()
+
+
+def run_finish(exp_size, rep_size, home, branch, branch_got, pick, hidden, cotangent, tokens, gain_row, qkv, probs, normed_a, context, attn_w, outer_send, outer_got, inner_sum):
     rows_n, width = tokens.shape
     low = jnp.bfloat16
     wide = jnp.float32
@@ -1945,11 +1966,11 @@
             shape((rows_n, width), low),
             shape((rows_n, width), wide),
             shape((4, block, width), wide),
-            shape(outer_send.shape, low),
+            shape((outer_send.shape[0] + EARLY, width), low),
             shape(inner_sum.shape[1:], low),
         ),
         in_specs=[inside, anyplace, anyplace, inside, anyplace, inside, anyplace, inside]
-        + [anyplace] * 7,
+        + [anyplace] * 8,
         out_specs=(inside,) * 3 + (anyplace,) * 2,
         scratch_shapes=[
             pltpu.VMEM((rows_n, width), wide),
@@ -1961,6 +1982,7 @@
             pltpu.VMEM((width, rows_n), low),
             pltpu.VMEM((width, rows_n), low),
             pltpu.VMEM(pick.shape[:1] + (width,), low),
+            pltpu.VMEM((EARLY, width), low),
             pltpu.VMEM((4, width, width), low),
             pltpu.VMEM((rows_n, width), wide),
             pltpu.VMEM((rows_n, width), low),
@@ -1978,7 +2000,7 @@
             pltpu.VMEM((4, block, half), low),
             pltpu.VMEM((4, block, half), wide),
             pltpu.VMEM((4, block, half), wide),
-            dma((7,)),
+            dma((9,)),
             dma((exp_size,)),
             dma((groups,)),
             dma((2,)),
@@ -2016,6 +2038,7 @@
         context,
         attn_w,
         outer_send,
+        outer_got,
         inner_sum,
     )
 
@@ -2104,12 +2127,11 @@
         context,
         attn_w,
         outer_send,
+        outer_got,
         inner_sum,
     )
     grad_centroids = jnp.sum(centre_parts.reshape(rep_size, 8, -1)[:, 0], axis=0)[None]
-    grad_w_outer = (
-        outer_keep + jnp.concatenate([outer_got, outer_recv], axis=0).astype(wide)
-    )[None]
+    grad_w_outer = (outer_keep.astype(wide) + outer_recv.astype(wide))[None]
     summed = inner_sum[0].astype(wide) + inner_recv.astype(wide)
     grad_w_inner = summed[None]
     grad_expert_gain = jnp.sum(summed * w_inner[0].astype(wide), axis=1)[None] / expert_gain.astype(

time: 323 us -> 315 us (0.975)
  Pallas kernels: 307 us -> 299 us
    pallas_call x1, Pallas kernels: 118 us -> 113 us  [run_experts(): pl.pallas_call(functools.partial(expert_kernel, exp_size, rep_size, slots...]
    pallas_call x1, Pallas kernels: 102 us -> 98.1 us  [run_finish(): pl.pallas_call(functools.partial(finish_kernel, exp_size, rep_size), out_...]
where the time goes in v8:
time: 315 us
  Pallas kernels  299 us (95%)
  other arithmetic  11.8 us (4%)
  local copies, waits for them, and re-layouts  3.15 us (1%)
    pallas_call x1, Pallas kernels, run_experts(): pl.pallas_call(functools.partial(expert_kernel, exp_size, rep_size, slots...  113 us
    pallas_call x1, Pallas kernels, run_finish(): pl.pallas_call(functools.partial(finish_kernel, exp_size, rep_size), out_...  98.1 us
    pallas_call x1, Pallas kernels, run_attend(): pl.pallas_call(functools.partial(attend_kernel, exp_size, rep_size, slots...  88 us

profile of v8, /device:TPU:11, one launch (start us, length us, event | category | flops | bytes accessed | tf_op | source)
XLA Modules:
  0.0 314.9 jit_solution(15030229972111025658)
XLA Ops:
  0.6 88.0 %attend.1 = (bf16[4,1024,1024]{2,1,0:T(8,128)(2,1)}, bf16[1024,2048]{1,0:T(8,128)(2,1)}, bf16[768,1024]{1,0:T(8,128)(2,1)}, bf16[768,1024]{1,0:T(8,128)(2,1)}, f...) custom-call(bf16[256,1024]{1,0:T(8,128)(2,1)} %tokens_h.1, ...), custom_call_target="tpu_custom_call" | custom-call | flops 2684354560 | bytes 41943040 | tf_op jit(solution)/shard_map/attend/pallas_call | solution.py:634
  88.6 113.2 %experts.1 = (bf16[384,1024]{1,0:T(8,128)(2,1)}, bf16[768,1024]{1,0:T(8,128)(2,1)}, bf16[384,1024]{1,0:T(8,128)(2,1)}, bf16[1024,1024]{1,0:T(8,128)(2,1)}, bf16[...) custom-call(bf16[768,1024]{1,0:T(8,128)(2,1)} %get-tuple-element.39.arrived, ...), custom_call_target="tpu_custom_call" | custom-call | flops 25769803776 | bytes 41943040 | tf_op jit(solution)/shard_map/experts/pallas_call | solution.py:1531
  201.9 0.0 copy-start.1
  201.9 98.1 %finish.1 = (bf16[256,1024]{1,0:T(8,128)(2,1)}, f32[256,1024]{1,0:T(8,128)}, f32[4,128,1024]{2,1,0:T(8,128)}, bf16[1024,1024]{1,0:T(8,128)(2,1)}, bf16[256,4096]{1,0:T(8,128)(2,1)}) custom-call(bf16[384,1024]{1,0:T(8,128)(2,1)} %get-tuple-element.46.home, bf16[768,1024]{1,0:T(8,128)(2,1)} %get-tuple-element.47.branch, ...), custom_call_target="tpu_custom_call" | custom-call | flops 5368709120 | bytes 62914560 | tf_op jit(solution)/shard_map/finish/pallas_call | solution.py:1963
  299.9 1.2 slice_reduce_fusion
  301.2 0.0 copy-done.1
  301.2 0.0 copy-start.9
  301.2 0.0 copy-start
  301.2 0.0 copy-start.6
  301.2 0.0 copy-start.7
  301.2 0.0 copy-start.8
  301.2 5.2 %multiply_reduce_fusion = (f32[256]{0:T(256)S(1)}, f32[1,256,4096]{2,1,0:T(8,128)}) fusion(bf16[256,4096]{1,0:T(8,128)(2,1)} %get-tuple-element.63, bf16[2,256,4096]{2,1,0:T(8,128)(2,1)} %get-tuple-element.59.inner_sum, bf16[1,256,4096]{2,1,0:T(8,128)(2,1)S(1)} %copy-done.1), kind=kLoop, calls=%fused_computation.1 | loop fusion | flops 6291200 | bytes 10486784 | tf_op jit(solution)/shard_map/reduce_sum | solution.py:2137
  306.4 0.0 copy-done.9
  306.4 0.6 convert_divide_fusion
  307.0 0.0 copy-done
  307.0 0.0 copy-start.3
  307.0 0.8 slice_bitcast_fusion
  307.8 0.0 copy-done.6
  307.8 0.0 copy-done.7
  307.8 0.0 copy-done.8
  307.8 0.0 copy-start.10
  307.8 0.0 copy-start.2
  307.8 1.3 multiply_reduce_fusion.1
  309.1 0.0 copy-done.10
  309.1 0.5 convert_divide_fusion.1
  309.7 0.0 copy-done.3
  309.7 0.5 copy-done.2
  310.2 0.0 copy-start.5
  310.2 0.0 copy-start.4
  310.2 2.9 add_bitcast_fusion
  313.1 0.0 copy-done.5
  313.1 0.8 copy.26
  313.9 0.0 copy-done.4
  313.9 1.0 copy.27
Async XLA Ops:
  201.9 99.3 %copy-start.1 = (bf16[1,256,4096]{2,1,0:T(8,128)(2,1)S(1)}, bf16[1,256,4096]{2,1,0:T(8,128)(2,1)}, u32[]{:S(2)}) copy-start(bf16[1,256,4096]{2,1,0:T(8,128)(2,1)} %param.22) | copy-start | bytes 6291460
  301.2 5.2 %copy-start.9 = (bf16[1,256]{1,0:T(2,128)(2,1)S(1)}, bf16[1,256]{1,0:T(2,128)(2,1)}, u32[]{:S(2)}) copy-start(bf16[1,256]{1,0:T(2,128)(2,1)} %gain_e.1) | copy-start | bytes 1540
  301.2 5.8 %copy-start = (f32[4,128,1024]{2,1,0:T(8,128)S(1)}, f32[4,128,1024]{2,1,0:T(8,128)}, u32[]{:S(2)}) copy-start(f32[4,128,1024]{2,1,0:T(8,128)} %get-tuple-element.62) | copy-start | bytes 6291460
  301.2 6.6 %copy-start.6 = (bf16[128,1024]{1,0:T(8,128)(2,1)S(1)}, bf16[128,1024]{1,0:T(8,128)(2,1)}, u32[]{:S(2)}) copy-start(bf16[128,1024]{1,0:T(8,128)(2,1)} %w_query.1) | copy-start | bytes 786436
  301.2 6.6 %copy-start.7 = (bf16[128,1024]{1,0:T(8,128)(2,1)S(1)}, bf16[128,1024]{1,0:T(8,128)(2,1)}, u32[]{:S(2)}) copy-start(bf16[128,1024]{1,0:T(8,128)(2,1)} %w_key.1) | copy-start | bytes 786436
  301.2 6.6 %copy-start.8 = (bf16[128,1024]{1,0:T(8,128)(2,1)S(1)}, bf16[128,1024]{1,0:T(8,128)(2,1)}, u32[]{:S(2)}) copy-start(bf16[128,1024]{1,0:T(8,128)(2,1)} %w_value.1) | copy-start | bytes 786436
  307.0 2.7 copy-start.3
  307.8 1.3 copy-start.10
  307.8 2.3 copy-start.2
  310.2 2.9 copy-start.5
  310.2 3.7 %copy-start.4 = (f32[256,1024]{1,0:T(8,128)S(1)}, f32[256,1024]{1,0:T(8,128)}, u32[]{:S(2)}) copy-start(f32[256,1024]{1,0:T(8,128)} %get-tuple-element.91) | copy-start | bytes 3145732

commit v9 on v8

--- a/solution.py
+++ b/solution.py
@@ -12,7 +12,7 @@
 ROOT_HALF = 0.7071067811865476
 INV_ROOT_TAU = 0.3989422804014327
 CHUNKS = 4
-DEFER = 256
+DEFER = 384
 EARLY = 512
 
 
@@ -62,7 +62,7 @@
     inner_w,
     outer_w,
     arrived,
-    counts_all,
+    spread_h,
     cents,
     gains_e,
     packed_h,
@@ -80,6 +80,8 @@
     context,
     weights,
     staging,
+    spread_m,
+    offsets,
     small_all,
     gain_v,
     packed_x,
@@ -394,9 +396,6 @@
             counts_v, small_all.at[sixteen(source)], count_s.at[source], count_r.at[source], (rep_at, source)
         ).wait()
 
-    small_store = pltpu.make_async_copy(small_all, counts_all, out_s.at[1])
-    small_store.start()
-
     tiled = jnp.dot(
         small_all[...].astype(low),
         (
@@ -549,6 +548,33 @@
 
     dispatch(packed_x, 0)
     stores[-1].start()
+
+    counted = small_all.shape[0]
+    own_rows = spread_m.shape[1]
+    count_lane = lax.broadcasted_iota(jnp.int32, (counted, 128), 1)
+    mine = jnp.sum(
+        jnp.where(count_lane == group, small_all[...], 0.0), axis=1, keepdims=True
+    )
+    mine = jnp.broadcast_to(mine, (counted, 128))
+    table_down = lax.broadcasted_iota(jnp.int32, (counted, counted), 0)
+    table_along = lax.broadcasted_iota(jnp.int32, (counted, counted), 1)
+    ahead = ((table_along // 16 < table_down // 16) & (table_along % 16 == 0)).astype(wide).astype(low)
+    offsets[0] = jnp.dot(ahead, mine.astype(low), preferred_element_type=wide)
+    offsets[1] = mine
+    slot_iota = lax.broadcasted_iota(jnp.int32, (slots, own_rows), 0)
+    row_iota = lax.broadcasted_iota(jnp.int32, (slots, own_rows), 1)
+
+    @pl.loop(0, exp_size)
+    def _(at):
+        eight = pl.ds(pl.multiple_of(at * 16, 16), 8)
+        start = offsets[0, eight, :][:1, :1].astype(jnp.int32)
+        limit = offsets[1, eight, :][:1, :1].astype(jnp.int32)
+        spread_m[slot_rows(at), :] = (
+            ((slot_iota + start) == row_iota) & (slot_iota < limit)
+        ).astype(wide).astype(low)
+
+    spread_store = pltpu.make_async_copy(spread_m, spread_h, out_s.at[1])
+    spread_store.start()
     for copy in inner_copies(3):
         copy.wait_recv()
     forward_copy.start()
@@ -586,7 +612,7 @@
             def _():
                 core_copy(kind, at).wait_send()
 
-    small_store.wait()
+    spread_store.wait()
     cent_own.wait()
     gain_own.wait()
     for mask in range(1, rep_size):
@@ -638,7 +664,7 @@
             shape((width, 2 * ff_block), low),
             shape((ff_block - DEFER, width), low),
             shape((exp_size * slots, width), low),
-            shape((exp_size * 16, 128), wide),
+            shape((exp_size * slots, 2 * rows_n), low),
             shape((2 * rep_size * 8, cent.shape[1]), wide),
             shape((rep_size * 8, depth), wide),
             shape((groups * slots, width), low),
@@ -662,6 +688,8 @@
             pltpu.VMEM((rows_n, width), low),
             pltpu.VMEM((4, width, width), low),
             pltpu.VMEM((depth, 2 * ff_block), low),
+            pltpu.VMEM((exp_size * slots, 2 * rows_n), low),
+            pltpu.VMEM((2, exp_size * 16, 128), wide),
             pltpu.VMEM((exp_size * 16, 128), wide),
             pltpu.VMEM((8, depth), wide),
             pltpu.VMEM((groups * slots, width), low),
@@ -710,7 +738,7 @@
     outer_h,
     w_inner,
     w_outer,
-    counts_all,
+    spread_h,
     cents,
     gains_e,
     home,
@@ -723,7 +751,6 @@
     centre_parts,
     arrived,
     spread_m,
-    offsets,
     cent_b,
     gain,
     centre_grad,
@@ -799,6 +826,8 @@
         return pl.ds(pl.multiple_of((rep_at ^ mask) * depth, depth), depth)
 
     rows_load = pltpu.make_async_copy(arrived_h, arrived, load_sem.at[0])
+    spread_load = pltpu.make_async_copy(spread_h, spread_m, load_sem.at[8])
+    spread_load.start()
 
     @pl.when(first)
     def _():
@@ -837,29 +866,42 @@
     def _(at):
         pl.semaphore_signal(barrier, inc=1, device_id=(rep_at, exp_at ^ at), device_id_type=MESH)
 
-    counted = counts_all.shape[0]
     group = exp_at // 2
-    lane = lax.broadcasted_iota(jnp.int32, (counted, 128), 1)
-    mine = jnp.sum(
-        jnp.where(lane == group, counts_all[...], 0.0), axis=1, keepdims=True
-    )
-    mine = jnp.broadcast_to(mine, (counted, 128))
-    down = lax.broadcasted_iota(jnp.int32, (counted, counted), 0)
-    along = lax.broadcasted_iota(jnp.int32, (counted, counted), 1)
-    ahead = ((along // 16 < down // 16) & (along % 16 == 0)).astype(wide).astype(low)
-    offsets[0] = jnp.dot(ahead, mine.astype(low), preferred_element_type=wide)
-    offsets[1] = mine
-    slot_iota = lax.broadcasted_iota(jnp.int32, (slots, own_rows), 0)
-    row_iota = lax.broadcasted_iota(jnp.int32, (slots, own_rows), 1)
-
-    @pl.loop(0, exp_size)
-    def _(at):
-        eight = pl.ds(pl.multiple_of(at * 16, 16), 8)
-        start = offsets[0, eight, :][:1, :1].astype(jnp.int32)
-        limit = offsets[1, eight, :][:1, :1].astype(jnp.int32)
-        spread_m[slot_rows(at), :] = (
-            ((slot_iota + start) == row_iota) & (slot_iota < limit)
-        ).astype(wide).astype(low)
+    pl.semaphore_wait(barrier, exp_size - 1 + 2 * (rep_size - 1))
+    row_peer = (rep_at ^ 2, exp_at)
+    late_copy = remote(
+        w_outer.at[block - DEFER :],
+        outer_w.at[2 * block - DEFER :],
+        early_s.at[0],
+        early_r.at[0],
+        row_peer,
+    )
+    late_copy.start()
+
+    def disp_copy(which):
+        return remote(
+            packed_h.at[slot_rows(which)],
+            arrived.at[slot_rows(exp_at)],
+            disp_s.at[which],
+            disp_r.at[exp_at],
+            (rep_at, 2 * which + 1),
+        )
+
+    disp_own = pltpu.make_async_copy(
+        packed_h.at[slot_rows(group)], arrived.at[slot_rows(exp_at)], disp_s.at[group]
+    )
+
+    @pl.loop(0, exp_size // 2)
+    def _(step):
+        which = group ^ (exp_size // 2 - 1 - step)
+
+        @pl.when(2 * which + 1 != exp_at)
+        def _():
+            disp_copy(which).start()
+
+        @pl.when(2 * which + 1 == exp_at)
+        def _():
+            disp_own.start()
 
     piece = cents.shape[1]
     for at in range(width // piece):
@@ -873,47 +915,13 @@
             spread_m[...], arrived[...], (((0,), (0,)), ((), ())), preferred_element_type=wide
         ).astype(low)
 
+    spread_load.wait()
+
     @pl.when(first)
     def _():
         rows_load.wait()
         own_x[...] = compact_rows()
 
-    pl.semaphore_wait(barrier, exp_size - 1 + 2 * (rep_size - 1))
-
-    def disp_copy(which):
-        return remote(
-            packed_h.at[slot_rows(which)],
-            arrived.at[slot_rows(exp_at)],
-            disp_s.at[which],
-            disp_r.at[exp_at],
-            (rep_at, 2 * which + 1),
-        )
-
-    disp_own = pltpu.make_async_copy(
-        packed_h.at[slot_rows(group)], arrived.at[slot_rows(exp_at)], disp_s.at[group]
-    )
-
-    @pl.loop(0, exp_size // 2)
-    def _(step):
-        which = group ^ (exp_size // 2 - 1 - step)
-
-        @pl.when(2 * which + 1 != exp_at)
-        def _():
-            disp_copy(which).start()
-
-        @pl.when(2 * which + 1 == exp_at)
-        def _():
-            disp_own.start()
-
-    row_peer = (rep_at ^ 2, exp_at)
-    late_copy = remote(
-        w_outer.at[block - DEFER :],
-        outer_w.at[2 * block - DEFER :],
-        early_s.at[0],
-        early_r.at[0],
-        row_peer,
-    )
-    late_copy.start()
 
     gate_copy = remote(gates, gates, gate_s.at[0], gate_r.at[0], side_peer)
 
@@ -989,15 +997,15 @@
 
     @pl.when(first)
     def _():
-        logit = lax.dot_general(
-            own_x[...], cent_b[...], (((1,), (1,)), ((), ())), preferred_element_type=wide
-        )
-        gates[...] = jax.nn.sigmoid(logit)
-        gate_copy.start()
-
         @pl.loop(0, CHUNKS)
         def _(at):
             norm_rows(at)
+
+        logit = lax.dot_general(
+            own_x[...], cent_b[...], (((1,), (1,)), ((), ())), preferred_element_type=wide
+        )
+        gates[...] = jax.nn.sigmoid(logit)
+        gate_copy.start()
 
     @pl.when(second)
     def _():
@@ -1470,7 +1478,7 @@
 
 
 def run_experts(
-    exp_size, rep_size, slots, own_rows, arrived, packed, inner_w, outer_w, w_inner, w_outer, counts_all, cents, gains_e
+    exp_size, rep_size, slots, own_rows, arrived, packed, inner_w, outer_w, w_inner, w_outer, spread, cents, gains_e
 ):
     width = arrived.shape[1]
     depth = width // rep_size
@@ -1488,7 +1496,6 @@
     scratch = [
         pltpu.VMEM((total, width), low),
         pltpu.VMEM((total, own_rows), low),
-        pltpu.VMEM((2, exp_size * 16, 128), wide),
         pltpu.VMEM((128, width), low),
         pltpu.VMEM((1, width), wide),
         pltpu.VMEM((1, width), wide),
@@ -1513,7 +1520,7 @@
         pltpu.VMEM((block, width), low),
         pltpu.VMEM((block, width), low),
         pltpu.VMEM((rep_size, 2, depth, block), low),
-        dma((8,)),
+        dma((9,)),
         dma((exp_size // 2,)),
         dma((exp_size,)),
         dma((exp_size // 2,)),
@@ -1540,7 +1547,7 @@
             jax.ShapeDtypeStruct((2, depth, rep_size * block), low),
             jax.ShapeDtypeStruct((rep_size * 8, piece), wide),
         ),
-        in_specs=[anyplace] * 6 + [inside] * 3,
+        in_specs=[anyplace] * 7 + [inside] * 2,
         out_specs=(anyplace,) * 8,
         scratch_shapes=scratch,
         compiler_params=pltpu.CompilerParams(
@@ -1550,7 +1557,7 @@
             flops=flops, bytes_accessed=40 << 20, transcendentals=2 * all_rows * 2 * block
         ),
         name="experts",
-    )(arrived, packed, inner_w, outer_w, w_inner, w_outer, counts_all, cents, gains_e)
+    )(arrived, packed, inner_w, outer_w, w_inner, w_outer, spread, cents, gains_e)
 
 
 def finish_kernel(
@@ -2069,7 +2076,7 @@
         inner_w,
         outer_w,
         arrived,
-        counts_all,
+        spread,
         cents,
         gains_e,
         packed,
@@ -2106,7 +2113,7 @@
         outer_w,
         w_inner[0],
         w_outer[0],
-        counts_all,
+        spread,
         cents,
         gains_e,
     )

time: 315 us -> 312 us (level)
  no operation moved by 1% of the time
where the time goes in v9:
time: 312 us
  Pallas kernels  296 us (95%)
  other arithmetic  11.8 us (4%)
  local copies, waits for them, and re-layouts  3.15 us (1%)
    pallas_call x1, Pallas kernels, run_experts(): pl.pallas_call(functools.partial(expert_kernel, exp_size, rep_size, slots...  113 us
    pallas_call x1, Pallas kernels, run_finish(): pl.pallas_call(functools.partial(finish_kernel, exp_size, rep_size), out_...  97.5 us
    pallas_call x1, Pallas kernels, run_attend(): pl.pallas_call(functools.partial(attend_kernel, exp_size, rep_size, slots...  85.9 us

profile of v9, /device:TPU:11, one launch (start us, length us, event | category | flops | bytes accessed | tf_op | source)
XLA Modules:
  0.0 311.8 jit_solution(16603026678805943625)
XLA Ops:
  0.6 85.9 %attend.1 = (bf16[4,1024,1024]{2,1,0:T(8,128)(2,1)}, bf16[1024,2048]{1,0:T(8,128)(2,1)}, bf16[640,1024]{1,0:T(8,128)(2,1)}, bf16[768,1024]{1,0:T(8,128)(2,1)}, b...) custom-call(bf16[256,1024]{1,0:T(8,128)(2,1)} %tokens_h.1, ...), custom_call_target="tpu_custom_call" | custom-call | flops 2684354560 | bytes 41943040 | tf_op jit(solution)/shard_map/attend/pallas_call | solution.py:660
  86.6 112.7 %experts.1 = (bf16[384,1024]{1,0:T(8,128)(2,1)}, bf16[768,1024]{1,0:T(8,128)(2,1)}, bf16[384,1024]{1,0:T(8,128)(2,1)}, bf16[1024,1024]{1,0:T(8,128)(2,1)}, bf16[...) custom-call(bf16[768,1024]{1,0:T(8,128)(2,1)} %get-tuple-element.39.arrived, ...), custom_call_target="tpu_custom_call" | custom-call | flops 25769803776 | bytes 41943040 | tf_op jit(solution)/shard_map/experts/pallas_call | solution.py:1538
  199.3 0.0 copy-start.1
  199.3 97.5 %finish.1 = (bf16[256,1024]{1,0:T(8,128)(2,1)}, f32[256,1024]{1,0:T(8,128)}, f32[4,128,1024]{2,1,0:T(8,128)}, bf16[1024,1024]{1,0:T(8,128)(2,1)}, bf16[256,4096]{1,0:T(8,128)(2,1)}) custom-call(bf16[384,1024]{1,0:T(8,128)(2,1)} %get-tuple-element.46.home, bf16[768,1024]{1,0:T(8,128)(2,1)} %get-tuple-element.47.branch, ...), custom_call_target="tpu_custom_call" | custom-call | flops 5368709120 | bytes 62914560 | tf_op jit(solution)/shard_map/finish/pallas_call | solution.py:1970
  296.9 1.2 slice_reduce_fusion
  298.1 0.0 copy-done.1
  298.1 0.0 copy-start.9
  298.1 0.0 copy-start
  298.1 0.0 copy-start.6
  298.1 0.0 copy-start.7
  298.1 0.0 copy-start.8
  298.1 5.2 %multiply_reduce_fusion = (f32[256]{0:T(256)S(1)}, f32[1,256,4096]{2,1,0:T(8,128)}) fusion(bf16[256,4096]{1,0:T(8,128)(2,1)} %get-tuple-element.63, bf16[2,256,4096]{2,1,0:T(8,128)(2,1)} %get-tuple-element.59.inner_sum, bf16[1,256,4096]{2,1,0:T(8,128)(2,1)S(1)} %copy-done.1), kind=kLoop, calls=%fused_computation.1 | loop fusion | flops 6291200 | bytes 10486784 | tf_op jit(solution)/shard_map/reduce_sum | solution.py:2144
  303.3 0.0 copy-done.9
  303.3 0.6 convert_divide_fusion
  303.9 0.0 copy-done
  303.9 0.0 copy-start.3
  303.9 0.8 slice_bitcast_fusion
  304.8 0.0 copy-done.6
  304.8 0.0 copy-done.7
  304.8 0.0 copy-done.8
  304.8 0.0 copy-start.10
  304.8 0.0 copy-start.2
  304.8 1.3 multiply_reduce_fusion.1
  306.1 0.0 copy-done.10
  306.1 0.5 convert_divide_fusion.1
  306.6 0.0 copy-done.3
  306.6 0.5 copy-done.2
  307.1 0.0 copy-start.5
  307.1 0.0 copy-start.4
  307.1 2.9 add_bitcast_fusion
  310.0 0.0 copy-done.5
  310.0 0.8 copy.26
  310.8 0.0 copy-done.4
  310.8 1.0 copy.27
Async XLA Ops:
  199.3 98.8 %copy-start.1 = (bf16[1,256,4096]{2,1,0:T(8,128)(2,1)S(1)}, bf16[1,256,4096]{2,1,0:T(8,128)(2,1)}, u32[]{:S(2)}) copy-start(bf16[1,256,4096]{2,1,0:T(8,128)(2,1)} %param.22) | copy-start | bytes 6291460
  298.1 5.2 %copy-start.9 = (bf16[1,256]{1,0:T(2,128)(2,1)S(1)}, bf16[1,256]{1,0:T(2,128)(2,1)}, u32[]{:S(2)}) copy-start(bf16[1,256]{1,0:T(2,128)(2,1)} %gain_e.1) | copy-start | bytes 1540
  298.1 5.8 %copy-start = (f32[4,128,1024]{2,1,0:T(8,128)S(1)}, f32[4,128,1024]{2,1,0:T(8,128)}, u32[]{:S(2)}) copy-start(f32[4,128,1024]{2,1,0:T(8,128)} %get-tuple-element.62) | copy-start | bytes 6291460
  298.1 6.6 %copy-start.6 = (bf16[128,1024]{1,0:T(8,128)(2,1)S(1)}, bf16[128,1024]{1,0:T(8,128)(2,1)}, u32[]{:S(2)}) copy-start(bf16[128,1024]{1,0:T(8,128)(2,1)} %w_query.1) | copy-start | bytes 786436
  298.1 6.6 %copy-start.7 = (bf16[128,1024]{1,0:T(8,128)(2,1)S(1)}, bf16[128,1024]{1,0:T(8,128)(2,1)}, u32[]{:S(2)}) copy-start(bf16[128,1024]{1,0:T(8,128)(2,1)} %w_key.1) | copy-start | bytes 786436
  298.1 6.6 %copy-start.8 = (bf16[128,1024]{1,0:T(8,128)(2,1)S(1)}, bf16[128,1024]{1,0:T(8,128)(2,1)}, u32[]{:S(2)}) copy-start(bf16[128,1024]{1,0:T(8,128)(2,1)} %w_value.1) | copy-start | bytes 786436
  303.9 2.7 copy-start.3
  304.8 1.3 copy-start.10
  304.8 2.3 copy-start.2
  307.1 2.9 copy-start.5
  307.1 3.7 %copy-start.4 = (f32[256,1024]{1,0:T(8,128)S(1)}, f32[256,1024]{1,0:T(8,128)}, u32[]{:S(2)}) copy-start(f32[256,1024]{1,0:T(8,128)} %get-tuple-element.91) | copy-start | bytes 3145732

commit v10 on v9

--- a/solution.py
+++ b/solution.py
@@ -332,6 +332,7 @@
     pick[...] = (
         lax.broadcasted_iota(jnp.int32, pick.shape, 0) == position
     ).astype(wide).astype(low)
+    counts_v[...] = jnp.zeros_like(counts_v)
     counts_v[:8, :] = lax.dot_general(
         jnp.ones((8, rows_n), low),
         onehot.astype(low),

time: 312 us -> 312 us (level)
  no operation moved by 1% of the time
where the time goes in v10:
time: 312 us
  Pallas kernels  296 us (95%)
  other arithmetic  11.8 us (4%)
  local copies, waits for them, and re-layouts  3.15 us (1%)
    pallas_call x1, Pallas kernels, run_experts(): pl.pallas_call(functools.partial(expert_kernel, exp_size, rep_size, slots...  113 us
    pallas_call x1, Pallas kernels, run_finish(): pl.pallas_call(functools.partial(finish_kernel, exp_size, rep_size), out_...  97.5 us
    pallas_call x1, Pallas kernels, run_attend(): pl.pallas_call(functools.partial(attend_kernel, exp_size, rep_size, slots...  85.9 us

profile of v10, /device:TPU:11, one launch (start us, length us, event | category | flops | bytes accessed | tf_op | source)
XLA Modules:
  0.0 311.8 jit_solution(16603026678805943625)
XLA Ops:
  0.6 85.9 %attend.1 = (bf16[4,1024,1024]{2,1,0:T(8,128)(2,1)}, bf16[1024,2048]{1,0:T(8,128)(2,1)}, bf16[640,1024]{1,0:T(8,128)(2,1)}, bf16[768,1024]{1,0:T(8,128)(2,1)}, b...) custom-call(bf16[256,1024]{1,0:T(8,128)(2,1)} %tokens_h.1, ...), custom_call_target="tpu_custom_call" | custom-call | flops 2684354560 | bytes 41943040 | tf_op jit(solution)/shard_map/attend/pallas_call | solution.py:661
  86.6 112.7 %experts.1 = (bf16[384,1024]{1,0:T(8,128)(2,1)}, bf16[768,1024]{1,0:T(8,128)(2,1)}, bf16[384,1024]{1,0:T(8,128)(2,1)}, bf16[1024,1024]{1,0:T(8,128)(2,1)}, bf16[...) custom-call(bf16[768,1024]{1,0:T(8,128)(2,1)} %get-tuple-element.39.arrived, ...), custom_call_target="tpu_custom_call" | custom-call | flops 25769803776 | bytes 41943040 | tf_op jit(solution)/shard_map/experts/pallas_call | solution.py:1539
  199.3 0.0 copy-start.1
  199.3 97.5 %finish.1 = (bf16[256,1024]{1,0:T(8,128)(2,1)}, f32[256,1024]{1,0:T(8,128)}, f32[4,128,1024]{2,1,0:T(8,128)}, bf16[1024,1024]{1,0:T(8,128)(2,1)}, bf16[256,4096]{1,0:T(8,128)(2,1)}) custom-call(bf16[384,1024]{1,0:T(8,128)(2,1)} %get-tuple-element.46.home, bf16[768,1024]{1,0:T(8,128)(2,1)} %get-tuple-element.47.branch, ...), custom_call_target="tpu_custom_call" | custom-call | flops 5368709120 | bytes 62914560 | tf_op jit(solution)/shard_map/finish/pallas_call | solution.py:1971
  296.9 1.2 slice_reduce_fusion
  298.1 0.0 copy-done.1
  298.1 0.0 copy-start.9
  298.1 0.0 copy-start
  298.1 0.0 copy-start.6
  298.1 0.0 copy-start.7
  298.1 0.0 copy-start.8
  298.1 5.2 %multiply_reduce_fusion = (f32[256]{0:T(256)S(1)}, f32[1,256,4096]{2,1,0:T(8,128)}) fusion(bf16[256,4096]{1,0:T(8,128)(2,1)} %get-tuple-element.63, bf16[2,256,4096]{2,1,0:T(8,128)(2,1)} %get-tuple-element.59.inner_sum, bf16[1,256,4096]{2,1,0:T(8,128)(2,1)S(1)} %copy-done.1), kind=kLoop, calls=%fused_computation.1 | loop fusion | flops 6291200 | bytes 10486784 | tf_op jit(solution)/shard_map/reduce_sum | solution.py:2145
  303.3 0.0 copy-done.9
  303.3 0.6 convert_divide_fusion
  303.9 0.0 copy-done
  303.9 0.0 copy-start.3
  303.9 0.8 slice_bitcast_fusion
  304.8 0.0 copy-done.6
  304.8 0.0 copy-done.7
  304.8 0.0 copy-done.8
  304.8 0.0 copy-start.10
  304.8 0.0 copy-start.2
  304.8 1.3 multiply_reduce_fusion.1
  306.1 0.0 copy-done.10
  306.1 0.5 convert_divide_fusion.1
  306.6 0.0 copy-done.3
  306.6 0.5 copy-done.2
  307.1 0.0 copy-start.5
  307.1 0.0 copy-start.4
  307.1 2.9 add_bitcast_fusion
  310.0 0.0 copy-done.5
  310.0 0.8 copy.26
  310.8 0.0 copy-done.4
  310.8 1.0 copy.27
Async XLA Ops:
  199.3 98.8 %copy-start.1 = (bf16[1,256,4096]{2,1,0:T(8,128)(2,1)S(1)}, bf16[1,256,4096]{2,1,0:T(8,128)(2,1)}, u32[]{:S(2)}) copy-start(bf16[1,256,4096]{2,1,0:T(8,128)(2,1)} %param.22) | copy-start | bytes 6291460
  298.1 5.2 %copy-start.9 = (bf16[1,256]{1,0:T(2,128)(2,1)S(1)}, bf16[1,256]{1,0:T(2,128)(2,1)}, u32[]{:S(2)}) copy-start(bf16[1,256]{1,0:T(2,128)(2,1)} %gain_e.1) | copy-start | bytes 1540
  298.1 5.8 %copy-start = (f32[4,128,1024]{2,1,0:T(8,128)S(1)}, f32[4,128,1024]{2,1,0:T(8,128)}, u32[]{:S(2)}) copy-start(f32[4,128,1024]{2,1,0:T(8,128)} %get-tuple-element.62) | copy-start | bytes 6291460
  298.1 6.6 %copy-start.6 = (bf16[128,1024]{1,0:T(8,128)(2,1)S(1)}, bf16[128,1024]{1,0:T(8,128)(2,1)}, u32[]{:S(2)}) copy-start(bf16[128,1024]{1,0:T(8,128)(2,1)} %w_query.1) | copy-start | bytes 786436
  298.1 6.6 %copy-start.7 = (bf16[128,1024]{1,0:T(8,128)(2,1)S(1)}, bf16[128,1024]{1,0:T(8,128)(2,1)}, u32[]{:S(2)}) copy-start(bf16[128,1024]{1,0:T(8,128)(2,1)} %w_key.1) | copy-start | bytes 786436
  298.1 6.6 %copy-start.8 = (bf16[128,1024]{1,0:T(8,128)(2,1)S(1)}, bf16[128,1024]{1,0:T(8,128)(2,1)}, u32[]{:S(2)}) copy-start(bf16[128,1024]{1,0:T(8,128)(2,1)} %w_value.1) | copy-start | bytes 786436
  303.9 2.7 copy-start.3
  304.8 1.3 copy-start.10
  304.8 2.3 copy-start.2
  307.1 2.9 copy-start.5
  307.1 3.7 %copy-start.4 = (f32[256,1024]{1,0:T(8,128)S(1)}, f32[256,1024]{1,0:T(8,128)}, u32[]{:S(2)}) copy-start(f32[256,1024]{1,0:T(8,128)} %get-tuple-element.91) | copy-start | bytes 3145732

commit v11 on v10

--- a/solution.py
+++ b/solution.py
@@ -12,7 +12,7 @@
 ROOT_HALF = 0.7071067811865476
 INV_ROOT_TAU = 0.3989422804014327
 CHUNKS = 4
-DEFER = 384
+DEFER = 448
 EARLY = 512
 
 

time: 312 us -> 315 us (level)
  no operation moved by 1% of the time
where the time goes in v11:
time: 315 us; the launch traced here: 314 us
  Pallas kernels  298 us (95%)
  other arithmetic  11.8 us (4%)
  local copies, waits for them, and re-layouts  3.15 us (1%)
    pallas_call x1, Pallas kernels, run_experts(): pl.pallas_call(functools.partial(expert_kernel, exp_size, rep_size, slots...  116 us
    pallas_call x1, Pallas kernels, run_finish(): pl.pallas_call(functools.partial(finish_kernel, exp_size, rep_size), out_...  96.2 us
    pallas_call x1, Pallas kernels, run_attend(): pl.pallas_call(functools.partial(attend_kernel, exp_size, rep_size, slots...  85.9 us

profile of v11, /device:TPU:11, one launch (start us, length us, event | category | flops | bytes accessed | tf_op | source)
XLA Modules:
  0.0 313.5 jit_solution(13279243353551334922)
XLA Ops:
  0.6 85.9 %attend.1 = (bf16[4,1024,1024]{2,1,0:T(8,128)(2,1)}, bf16[1024,2048]{1,0:T(8,128)(2,1)}, bf16[576,1024]{1,0:T(8,128)(2,1)}, bf16[768,1024]{1,0:T(8,128)(2,1)}, b...) custom-call(bf16[256,1024]{1,0:T(8,128)(2,1)} %tokens_h.1, ...), custom_call_target="tpu_custom_call" | custom-call | flops 2684354560 | bytes 41943040 | tf_op jit(solution)/shard_map/attend/pallas_call | solution.py:661
  86.6 115.7 %experts.1 = (bf16[384,1024]{1,0:T(8,128)(2,1)}, bf16[768,1024]{1,0:T(8,128)(2,1)}, bf16[384,1024]{1,0:T(8,128)(2,1)}, bf16[1024,1024]{1,0:T(8,128)(2,1)}, bf16[...) custom-call(bf16[768,1024]{1,0:T(8,128)(2,1)} %get-tuple-element.39.arrived, ...), custom_call_target="tpu_custom_call" | custom-call | flops 25769803776 | bytes 41943040 | tf_op jit(solution)/shard_map/experts/pallas_call | solution.py:1539
  202.3 0.0 copy-start.1
  202.3 96.2 %finish.1 = (bf16[256,1024]{1,0:T(8,128)(2,1)}, f32[256,1024]{1,0:T(8,128)}, f32[4,128,1024]{2,1,0:T(8,128)}, bf16[1024,1024]{1,0:T(8,128)(2,1)}, bf16[256,4096]{1,0:T(8,128)(2,1)}) custom-call(bf16[384,1024]{1,0:T(8,128)(2,1)} %get-tuple-element.46.home, bf16[768,1024]{1,0:T(8,128)(2,1)} %get-tuple-element.47.branch, ...), custom_call_target="tpu_custom_call" | custom-call | flops 5368709120 | bytes 62914560 | tf_op jit(solution)/shard_map/finish/pallas_call | solution.py:1971
  298.6 1.2 slice_reduce_fusion
  299.8 0.0 copy-done.1
  299.8 0.0 copy-start.9
  299.8 0.0 copy-start
  299.8 0.0 copy-start.6
  299.8 0.0 copy-start.7
  299.8 0.0 copy-start.8
  299.8 5.2 %multiply_reduce_fusion = (f32[256]{0:T(256)S(1)}, f32[1,256,4096]{2,1,0:T(8,128)}) fusion(bf16[256,4096]{1,0:T(8,128)(2,1)} %get-tuple-element.63, bf16[2,256,4096]{2,1,0:T(8,128)(2,1)} %get-tuple-element.59.inner_sum, bf16[1,256,4096]{2,1,0:T(8,128)(2,1)S(1)} %copy-done.1), kind=kLoop, calls=%fused_computation.1 | loop fusion | flops 6291200 | bytes 10486784 | tf_op jit(solution)/shard_map/reduce_sum | solution.py:2145
  305.0 0.0 copy-done.9
  305.0 0.6 convert_divide_fusion
  305.6 0.0 copy-done
  305.6 0.0 copy-start.3
  305.6 0.8 slice_bitcast_fusion
  306.5 0.0 copy-done.6
  306.5 0.0 copy-done.7
  306.5 0.0 copy-done.8
  306.5 0.0 copy-start.10
  306.5 0.0 copy-start.2
  306.5 1.3 multiply_reduce_fusion.1
  307.8 0.0 copy-done.10
  307.8 0.5 convert_divide_fusion.1
  308.3 0.0 copy-done.3
  308.3 0.5 copy-done.2
  308.8 0.0 copy-start.5
  308.8 0.0 copy-start.4
  308.8 2.9 add_bitcast_fusion
  311.7 0.0 copy-done.5
  311.7 0.8 copy.26
  312.5 0.0 copy-done.4
  312.5 1.0 copy.27
Async XLA Ops:
  202.3 97.5 %copy-start.1 = (bf16[1,256,4096]{2,1,0:T(8,128)(2,1)S(1)}, bf16[1,256,4096]{2,1,0:T(8,128)(2,1)}, u32[]{:S(2)}) copy-start(bf16[1,256,4096]{2,1,0:T(8,128)(2,1)} %param.22) | copy-start | bytes 6291460
  299.8 5.2 %copy-start.9 = (bf16[1,256]{1,0:T(2,128)(2,1)S(1)}, bf16[1,256]{1,0:T(2,128)(2,1)}, u32[]{:S(2)}) copy-start(bf16[1,256]{1,0:T(2,128)(2,1)} %gain_e.1) | copy-start | bytes 1540
  299.8 5.8 %copy-start = (f32[4,128,1024]{2,1,0:T(8,128)S(1)}, f32[4,128,1024]{2,1,0:T(8,128)}, u32[]{:S(2)}) copy-start(f32[4,128,1024]{2,1,0:T(8,128)} %get-tuple-element.62) | copy-start | bytes 6291460
  299.8 6.6 %copy-start.6 = (bf16[128,1024]{1,0:T(8,128)(2,1)S(1)}, bf16[128,1024]{1,0:T(8,128)(2,1)}, u32[]{:S(2)}) copy-start(bf16[128,1024]{1,0:T(8,128)(2,1)} %w_query.1) | copy-start | bytes 786436
  299.8 6.6 %copy-start.7 = (bf16[128,1024]{1,0:T(8,128)(2,1)S(1)}, bf16[128,1024]{1,0:T(8,128)(2,1)}, u32[]{:S(2)}) copy-start(bf16[128,1024]{1,0:T(8,128)(2,1)} %w_key.1) | copy-start | bytes 786436
  299.8 6.6 %copy-start.8 = (bf16[128,1024]{1,0:T(8,128)(2,1)S(1)}, bf16[128,1024]{1,0:T(8,128)(2,1)}, u32[]{:S(2)}) copy-start(bf16[128,1024]{1,0:T(8,128)(2,1)} %w_value.1) | copy-start | bytes 786436
  305.6 2.7 copy-start.3
  306.5 1.3 copy-start.10
  306.5 2.3 copy-start.2
  308.8 2.9 copy-start.5
  308.8 3.7 %copy-start.4 = (f32[256,1024]{1,0:T(8,128)S(1)}, f32[256,1024]{1,0:T(8,128)}, u32[]{:S(2)}) copy-start(f32[256,1024]{1,0:T(8,128)} %get-tuple-element.91) | copy-start | bytes 3145732
